TPU v7x, 512 devices: a whole 4x8x8 slice. The times are simulated.
512 devices in a mesh: seq: 64 (over y, x, z_hi), tp: 8 (over z_lo, core).
Axes of the slice: x: 4, y: 8, z: 8 (z_hi: 2, z_lo: 4; z = z_hi * 4 + z_lo), core: 2. Of those that a mesh axis runs over, the one named last changes fastest.
Arguments:
- queries: bfloat16 [16384, 4096], P('seq', 'tp'), may hold values from -90 to 90
- key_rows: bfloat16 [16384, 4096], P('seq', 'tp'), may hold values from -4 to 4
- value_rows: bfloat16 [16384, 4096], P('seq', 'tp'), may hold values from -5 to 5
- residual: bfloat16 [16384, 4096], P('seq', 'tp'), may hold values from -1.5 to 1.5
- out_weight: bfloat16 [4096, 4096], P('tp', 'seq'), may hold values from -0.09375 to 0.09375
- norm_gain: float32 [4096], P('tp'), may hold values from 0.5 to 1.5
- norm_bias: float32 [4096], P('tp'), may hold values from -1 to 1
- global_list: int32 [2], replicated, may hold values from 0 to 1023
- random_device: int32 [1024, 3], P('seq'), may hold values from 0 to 63, all different within a row; in each aligned block of 16 rows (0 to 15, 16 to 31, ...) at most 2 rows name the same one
- random_offset: int32 [1024, 3], P('seq'), may hold values from 0 to 15
- drop_seed: int32 [1], replicated, may hold values from 0 to 65535
- drop_offsets: int32 [1024], P('seq'), may hold values from 0 to 8388607
Outputs:
- encoded: bfloat16 [16384, 4096], P('seq', 'tp')
Inputs may be any that keep to these rules, and one draw needn't show every extreme that they name: `random_device`: each row names 3 different indices; among the 16 rows of one index of seq no index is named more than 2 times.
All inputs are finite; a program needn't handle non-finite values.
Results may differ from a plain program's by a relative error of at most 0.013.
Values may be sent and summed in bfloat16 or wider, within the bound.
No kernel may reach another device: no remote copies, remote signals or barrier semaphores. Data moves between devices by JAX's collectives and lax.ppermute only.
A program may use at most 64 MiB of HBM per device.

v0:
```python
import jax
import jax.numpy as jnp
from jax import lax
from jax.sharding import PartitionSpec as P

D = 4096
DH = 128
BLOCK = 16


def padded_2(x, sides, width):
    for axis, dim in sides:
        devices, length = (lax.axis_size(axis), x.shape[dim])
        up = [(i, (i + 1) % devices) for i in range(devices)]
        down = [(j, i) for i, j in up]
        last = lax.slice_in_dim(x, length - width, length, axis=dim)
        first = lax.slice_in_dim(x, 0, width, axis=dim)
        before = lax.ppermute(last, axis, up)
        after = lax.ppermute(first, axis, down)
        x = jnp.concatenate([before, x, after], axis=dim)
    return x


def broadcast(value, axis, source):
    kept = jnp.where(lax.axis_index(axis) == source, value, 0).astype(value.dtype)
    return lax.psum(kept, axis)


def mix_bits(counter, seed_value):
    hashed = counter + seed_value * 1000003
    for rounds in range(2):
        hashed = jnp.bitwise_xor(hashed, lax.shift_right_logical(hashed, jnp.int32(16)))
        hashed = hashed * 73244475
    hashed = jnp.bitwise_xor(hashed, lax.shift_right_logical(hashed, jnp.int32(16)))
    return hashed


def keep_table(counter, seed_value):
    hashed = mix_bits(counter, seed_value)
    kept = jnp.bitwise_and(hashed, 1023) >= 102
    return jnp.where(kept, jnp.float32(1024.0 / 922.0), jnp.float32(0.0))


def on_device(
    queries,
    key_rows,
    value_rows,
    residual,
    out_weight,
    norm_gain,
    norm_bias,
    global_list,
    random_device,
    random_offset,
    drop_seed,
    drop_offsets,
):
    row_count, width_here = queries.shape
    heads_here = width_here // DH
    block_count = row_count // BLOCK
    seq_count = lax.axis_size("seq")
    paired = jnp.concatenate([key_rows, value_rows], axis=1).reshape(
        block_count, BLOCK, 2 * width_here
    )
    padded = padded_2(paired, (("seq", 0),), 1)
    window = jnp.stack(
        [padded[0:block_count], padded[1 : block_count + 1], padded[2 : block_count + 2]], axis=1
    )
    glob_count = global_list.shape[0]
    fetched = []
    for which in range(glob_count):
        wanted_block = global_list[which]
        local_block = jnp.take(paired, wanted_block % block_count, axis=0)
        fetched.append(broadcast(local_block, "seq", wanted_block // block_count))
    glob_blocks = jnp.stack(fetched, axis=0)
    glob_blocks = jnp.broadcast_to(glob_blocks[None], (block_count,) + glob_blocks.shape)
    rand_count = random_device.shape[1]
    request_count = block_count * rand_count
    target = random_device.reshape(request_count)
    wanted = random_offset.reshape(request_count)
    request_rank = jnp.arange(request_count, dtype=jnp.int32)
    same_dest = target[:, None] == target[None, :]
    earlier = request_rank[None, :] < request_rank[:, None]
    slot_index = jnp.sum(jnp.logical_and(same_dest, earlier), axis=1)
    capacity = max(2, -(-request_count // seq_count))
    dest_ids = jnp.arange(seq_count, dtype=jnp.int32)
    slot_ids = jnp.arange(capacity, dtype=jnp.int32)
    matched = jnp.logical_and(
        target[None, None, :] == dest_ids[:, None, None],
        slot_index[None, None, :] == slot_ids[None, :, None],
    )
    request_table = jnp.sum(jnp.where(matched, wanted[None, None, :], 0), axis=2)
    picked = jnp.take(
        paired,
        lax.all_to_all(request_table, "seq", split_axis=0, concat_axis=0, tiled=True),
        axis=0,
    )
    replies = lax.all_to_all(picked, "seq", split_axis=0, concat_axis=0, tiled=True)
    flat_replies = replies.reshape(seq_count * capacity, BLOCK, 2 * width_here)
    chosen = jnp.take(flat_replies, target * capacity + slot_index, axis=0)
    chosen = chosen.reshape(block_count, rand_count, BLOCK, 2 * width_here)
    all_keys = jnp.concatenate([window, glob_blocks, chosen], axis=1)
    key_total = all_keys.shape[1] * BLOCK
    all_keys = all_keys.reshape(block_count, key_total, 2 * width_here)
    key_heads = all_keys[:, :, :width_here].reshape(block_count, key_total, heads_here, DH)
    value_heads = all_keys[:, :, width_here:].reshape(block_count, key_total, heads_here, DH)
    query_heads = queries.reshape(block_count, BLOCK, heads_here, DH)
    score_scale = jnp.float32(1.0 / DH**0.5)
    scores = (
        jnp.einsum("bqhd,bkhd->bhqk", query_heads, key_heads, preferred_element_type=jnp.float32)
        * score_scale
    )
    top_score = jnp.max(scores, axis=-1, keepdims=True)
    expo = jnp.exp(scores - top_score)
    attn_probs = (expo / jnp.sum(expo, axis=-1, keepdims=True)).astype(jnp.bfloat16)
    context = jnp.einsum(
        "bhqk,bkhd->bqhd", attn_probs, value_heads, preferred_element_type=jnp.float32
    )
    context = context.astype(jnp.bfloat16).reshape(row_count, width_here)
    partial_terms = jnp.dot(
        context,
        lax.all_gather(out_weight, "seq", axis=1, tiled=True),
        preferred_element_type=jnp.float32,
    )
    attended = lax.psum_scatter(
        partial_terms.astype(jnp.bfloat16), "tp", scatter_dimension=1, tiled=True
    ).astype(jnp.float32)
    cols_here = attended.shape[1]
    first_col = lax.axis_index("tp") * cols_here
    inner = jnp.arange(BLOCK, dtype=jnp.int32)
    columns = first_col + jnp.arange(cols_here, dtype=jnp.int32)
    counter = drop_offsets[:, None, None] + inner[None, :, None] * D + columns[None, None, :]
    keep_factor = keep_table(counter, drop_seed[0]).reshape(row_count, cols_here)
    summed_rows = residual.astype(jnp.float32) + keep_factor * attended
    row_total = lax.psum(jnp.sum(summed_rows, axis=1), "tp")
    row_mean = row_total / D
    centered = summed_rows - row_mean[:, None]
    spread = lax.psum(jnp.sum(centered * centered, axis=1), "tp")
    row_var = spread / D
    encoded = (
        centered * lax.rsqrt(row_var + 1e-05)[:, None] * norm_gain[None, :] + norm_bias[None, :]
    )
    return encoded.astype(jnp.bfloat16)


def solution(mesh):
    placed = (
        P("seq", "tp"),
        P("seq", "tp"),
        P("seq", "tp"),
        P("seq", "tp"),
        P("tp", "seq"),
        P("tp"),
        P("tp"),
        P(),
        P("seq", None),
        P("seq", None),
        P(),
        P("seq"),
    )
    return jax.shard_map(
        on_device, mesh=mesh, in_specs=placed, out_specs=P("seq", "tp"), check_vma=False
    )
```

profile of v0, /device:TPU:1, one launch (start us, length us, event | category | flops | bytes accessed | tf_op | source)
XLA Modules:
  0.0 1136.7 jit_solution(4310646254590320187)
XLA Ops:
  6.5 0.8 copy.68
  7.3 0.1 reshape.205
  7.4 0.2 convert_reduce_fusion
  7.6 0.1 iota_compare_fusion
  7.7 0.8 copy.70
  8.4 0.1 broadcast_in_dim.81
  8.5 0.1 select_reduce_fusion
  8.6 0.7 copy.71
  9.3 19.6 %all-to-all-start = ((s32[64,1,2]{2,1,0:T(1,128)}), s32[64,1,2]{2,1,0:T(1,128)S(1)}, u32[]{:S(2)}, u32[]{:S(2)}) async-start(s32[64,1,2]{2,1,0:T(1,128)} %copy.71), calls=%async_computation | async-start | bytes 65536 | tf_op jit(solution)/shard_map/all_to_all | solution.py:95
  28.9 1.0 constant_dynamic-update-slice_fusion.1
  29.9 1.0 constant_dynamic-update-slice_fusion
  30.9 11.2 all-to-all-done
  42.0 0.1 copy.72
  42.1 0.1 copy.75
  42.2 0.1 reshape.259
  42.4 0.1 copy.73
  42.5 2.7 gather_fusion
  45.2 4.6 broadcast_select_fusion
  49.9 5.8 all-to-all-start.1
  55.7 0.0 all-reduce.3.cloned.1.call-start
  55.7 0.0 copy-done.4
  55.7 0.7 fusion.24
  61.8 0.6 fusion.18
  62.4 0.0 all-reduce.3.cloned.1.call-update
  62.5 0.0 all-gather.2.cloned.1.call-start
  62.5 0.7 all-gather.2.cloned.1.call-update
  63.2 0.0 reduce-scatter.2.cloned.1.call-start
  63.3 6.6 collective-permute-start
  69.9 6.8 collective-permute-start.1
  76.7 0.1 reduce_sum.50
  76.8 0.1 mul.83
  76.9 0.1 reshape.210
  77.0 73.8 %collective-permute-done = bf16[1,16,1024]{2,1,0:T(8,128)(2,1)S(1)} collective-permute-done((bf16[1,16,1024]{2,1,0:T(8,128)(2,1)S(1)}, bf16[1,16,1024]{2,1,0:T(8,128)(2,1)S(1)}, u32[]{:S(2)}, u32[]{:S(2)}) %collective-permute-start) | collective-permute-done | bytes 32800 | tf_op jit(solution)/shard_map/ppermute | solution.py:18
  150.8 0.8 fusion.12
  151.7 0.8 constant_dynamic-update-slice_fusion.2
  152.5 0.0 collective-permute-done.1
  152.5 0.8 fusion.10
  153.4 702.0 %all-reduce.3.cloned.1.call-done = (bf16[1,16,1024]{2,1,0:T(8,128)(2,1)}, bf16[1,16,1024]{2,1,0:T(8,128)(2,1)}) async-done(((bf16[1,16,1024]{2,1,0:T(8,128)(2,1)}, bf16[1,16,1024]{2,1,0:T(8,128)(2,1)}), (bf16[1,16,1024]{2,1,0:T(8,128)(2,1)}, bf16[1,16,1024]{2,1,0:T(8,128)(2,1)})) %all-reduce.3.cloned.1.call-update) | async-done | bytes 65552 | tf_op jit(solution)/shard_map/psum | solution.py:26
  855.4 0.8 pad_maximum_fusion.2
  856.2 1.1 broadcast_dynamic-update-slice_fusion
  857.3 0.0 all-to-all-done.1
  857.3 2.8 gather_fusion.1
  860.1 1.5 select_dynamic-update-slice_fusion
  861.6 4.6 fusion.23
  866.3 3.0 copy.80
  869.3 3.9 copy.79
  873.2 0.7 fusion.3
  873.9 0.4 fusion.25
  874.3 3.4 fusion.4
  877.6 0.1 copy.84
  877.8 175.0 %all-gather.2.cloned.1.call-done = bf16[512,4096]{0,1:T(8,128)(2,1)} async-done(((bf16[512,64]{0,1:T(8,128)(2,1)}), bf16[512,4096]{0,1:T(8,128)(2,1)}) %all-gather.2.cloned.1.call-update) | async-done | bytes 4194320 | tf_op jit(solution)/shard_map/all_gather | solution.py:122
  1052.8 4.8 convolution_convert_fusion
  1057.6 0.0 reduce-scatter.2.cloned.1.call-update
  1057.7 0.1 add.153
  1057.8 0.0 copy-done.5
  1057.8 0.1 add.150
  1057.8 0.1 add.151
  1058.6 38.0 %reduce-scatter.2.cloned.1.call-done = bf16[256,512]{1,0:T(8,128)(2,1)} async-done(((bf16[256,4096]{1,0:T(8,128)(2,1)}), bf16[256,512]{1,0:T(8,128)(2,1)}) %reduce-scatter.2.cloned.1.call-update) | async-done | bytes 262160 | tf_op jit(solution)/shard_map/reduce_scatter | solution.py:125
  1096.6 1.4 fusion.22
  1098.1 16.2 %psum.30 = f32[256]{0:T(256)S(1)} all-reduce(f32[256]{0:T(256)S(1)} %get-tuple-element.19), channel_id=1, replica_groups=mesh['seq'=64,'tp'=8] {'tp'}, use_global_device_ids=true, to_apply=%region_8.10 | all-reduce | flops 256 | bytes 2048 | tf_op jit(solution)/shard_map/psum | solution.py:135
  1114.3 0.2 multiply_reduce_fusion
  1114.5 14.8 %psum.31 = f32[256]{0:T(256)S(1)} all-reduce(f32[256]{0:T(256)S(1)} %multiply_reduce_fusion), channel_id=1, replica_groups=mesh['seq'=64,'tp'=8] {'tp'}, use_global_device_ids=true, to_apply=%region_10.12 | all-reduce | flops 256 | bytes 2048 | tf_op jit(solution)/shard_map/psum | solution.py:138
  1129.3 0.0 copy-done.2
  1129.3 0.9 add_convert_fusion
  (24 shorter events, 0.1 us)
Async XLA Ops:
  9.3 32.7 %all-to-all-start = ((s32[64,1,2]{2,1,0:T(1,128)}), s32[64,1,2]{2,1,0:T(1,128)S(1)}, u32[]{:S(2)}, u32[]{:S(2)}) async-start(s32[64,1,2]{2,1,0:T(1,128)} %copy.71), calls=%async_computation | async-start | bytes 65536 | tf_op jit(solution)/shard_map/all_to_all | solution.py:95
  49.9 5.9 copy-start.4
  49.9 27.1 %copy-start = (bf16[256,512]{1,0:T(8,128)(2,1)S(1)}, bf16[256,512]{1,0:T(8,128)(2,1)}, u32[]{:S(2)}) copy-start(bf16[256,512]{1,0:T(8,128)(2,1)} %param.14) | copy-start | bytes 786436
  49.9 807.4 %all-to-all-start.1 = ((bf16[64,2,16,1024]{3,2,1,0:T(8,128)(2,1)}), bf16[64,2,16,1024]{3,2,1,0:T(8,128)(2,1)}, u32[]{:S(2)}, u32[]{:S(2)}) async-start(bf16[64,2,16,1024]{3,2,1,0:T(8,128)(2,1)} %broadcast_select_fusion), calls=%async_computation.1 | async-start | bytes 8388608 | tf_op jit(solution)/shard_map/all_to_all | solution.py:98
  55.7 799.7 %all-reduce.3.cloned.1.call-start = ((), (), s32[]{:S(2)}) async-start(), calls=%async_computation.5 | async-start | bytes 131072 | tf_op jit(solution)/shard_map/psum | solution.py:26
  62.5 990.3 %all-gather.2.cloned.1.call-start = ((), (), s32[]{:S(2)}) async-start(), calls=%async_computation.3 | async-start | bytes 4259840 | tf_op jit(solution)/shard_map/all_gather | solution.py:122
  63.2 1033.4 %reduce-scatter.2.cloned.1.call-start = ((), (), s32[]{:S(2)}) async-start(), calls=%async_computation.4 | async-start | bytes 2359296 | tf_op jit(solution)/shard_map/reduce_scatter | solution.py:125
  63.3 87.6 %collective-permute-start = (bf16[1,16,1024]{2,1,0:T(8,128)(2,1)S(1)}, bf16[1,16,1024]{2,1,0:T(8,128)(2,1)S(1)}, u32[]{:S(2)}, u32[]{:S(2)}) collective-permute-start(bf16[1,16,1024]{2,1,0:T(8,128)(2,1)S(1)} %get-tuple-element.26), channel_id=1, source_target_pairs={{0,8},{8,16},{16,24},{24,32},{32,40},{40,48},{48,56},{56,64},{64,7... | collective-permute-start | bytes 98312 | tf_op jit(solution)/shard_map/ppermute | solution.py:18
  69.9 82.6 %collective-permute-start.1 = (bf16[1,16,1024]{2,1,0:T(8,128)(2,1)S(1)}, bf16[1,16,1024]{2,1,0:T(8,128)(2,1)S(1)}, u32[]{:S(2)}, u32[]{:S(2)}) collective-permute-start(bf16[1,16,1024]{2,1,0:T(8,128)(2,1)S(1)} %get-tuple-element.25), channel_id=1, source_target_pairs={{8,0},{16,8},{24,16},{32,24},{40,32},{48,40},{56,48},{64,56},{72,6... | collective-permute-start | bytes 98312 | tf_op jit(solution)/shard_map/ppermute | solution.py:19
  1052.8 5.0 copy-start.5
  1052.8 43.9 %copy-start.1 = (bf16[256,512]{1,0:T(8,128)(2,1)S(1)}, bf16[256,512]{1,0:T(8,128)(2,1)}, u32[]{:S(2)}) copy-start(bf16[256,512]{1,0:T(8,128)(2,1)} %param.17) | copy-start | bytes 786436
  1052.8 76.6 %copy-start.2 = (f32[512]{0:T(512)S(1)}, f32[512]{0:T(512)}, u32[]{:S(2)}) copy-start(f32[512]{0:T(512)} %param.20) | copy-start | bytes 6148
  1052.8 76.6 %copy-start.3 = (f32[512]{0:T(512)S(1)}, f32[512]{0:T(512)}, u32[]{:S(2)}) copy-start(f32[512]{0:T(512)} %param.19) | copy-start | bytes 6148
Sparse Core Ops, SparseCore 0:
  62.6 792.7 all-reduce.2
  860.7 191.9 all-gather.1
  1057.8 38.8 reduce-scatter.1
where the time goes:
time: 1140 us
  waiting for transfers between devices  1000 us (88%)
  starting transfers between devices  38.9 us (3%)
  blocking collectives  31.1 us (3%)
  local copies, waits for them, and re-layouts  25.2 us (2%)
  between operations  19.4 us (2%)
  other arithmetic  12.5 us (1%)
    psum x1, waiting for transfers between devices, broadcast(): return lax.psum(kept, axis)  702 us
    all_gather x1, waiting for transfers between devices, on_device(): lax.all_gather(out_weight, 'seq', axis=1, tiled=True)  175 us
    ppermute x1, waiting for transfers between devices, padded_2(): before = lax.ppermute(last, axis, up)  73.8 us
    reduce_scatter x1, waiting for transfers between devices, on_device(): lax.psum_scatter(partial_terms.astype(jnp.bfloat16), 'tp', scatter_dimens...  38 us
  transfers between devices with their start and end apart: 7, of which 5 were waited for; matrix products, arithmetic and copies ran while one was open for 3% of the time, Pallas kernels for 0%

commit v1 on v0

v1 whole, which is shorter than its diff:
```python
import functools

import jax
import jax.numpy as jnp
from jax import lax
from jax.experimental import pallas as pl
from jax.experimental.pallas import tpu as pltpu
from jax.sharding import PartitionSpec as P

D = 4096
DH = 128
BLOCK = 16
GLOB = 2
RAND = 3
CAP = 2
BF = jnp.bfloat16
F32 = jnp.float32
VMEM_LIMIT = 48 * 1024 * 1024


def whole(shape):
    return pl.BlockSpec(shape, lambda *a: (0,) * len(shape))


def params():
    return pltpu.CompilerParams(vmem_limit_bytes=VMEM_LIMIT)


def pack_kernel(want_ref, k_ref, v_ref, out_ref):
    width = k_ref.shape[1]

    def step(i, carry):
        rows = pl.ds(pl.multiple_of(want_ref[i] * BLOCK, BLOCK), BLOCK)
        out_ref[i, :, :width] = k_ref[rows, :]
        out_ref[i, :, width:] = v_ref[rows, :]
        return carry

    lax.fori_loop(0, out_ref.shape[0], step, 0, unroll=8)


def pack(want, k, v):
    slots = want.shape[0]
    width = k.shape[1]
    out = (slots, BLOCK, 2 * width)
    return pl.pallas_call(
        pack_kernel,
        grid_spec=pltpu.PrefetchScalarGridSpec(
            num_scalar_prefetch=1,
            grid=(1,),
            in_specs=[whole(k.shape), whole(v.shape)],
            out_specs=whole(out),
        ),
        out_shape=jax.ShapeDtypeStruct(out, BF),
        compiler_params=params(),
        cost_estimate=pl.CostEstimate(flops=0, transcendentals=0, bytes_accessed=5 << 20),
        name="pack",
    )(want, k, v)


def attend_kernel(
    pick_ref, q_ref, k_ref, v_ref, prev_ref, next_ref, glob_ref, rep_ref, out_ref
):
    width = q_ref.shape[1]
    blocks = q_ref.shape[0] // BLOCK
    scale = jnp.float32(1.0 / DH**0.5)

    def pieces(local_ref, offset, b, h):
        lo, hi = h * DH, (h + 1) * DH
        olo, ohi = offset + lo, offset + hi
        parts = []
        if b == 0:
            parts.append(prev_ref[:, olo:ohi])
            parts.append(local_ref[0 : 2 * BLOCK, lo:hi])
        elif b == blocks - 1:
            parts.append(local_ref[(b - 1) * BLOCK : (b + 1) * BLOCK, lo:hi])
            parts.append(next_ref[:, olo:ohi])
        else:
            parts.append(local_ref[(b - 1) * BLOCK : (b + 2) * BLOCK, lo:hi])
        tile = olo // DH
        chunk, inner = tile // 2, tile % 2
        for g in range(GLOB):
            at = (2 * g + inner) * DH
            parts.append(glob_ref[chunk * BLOCK : (chunk + 1) * BLOCK, at : at + DH])
        for r in range(RAND):
            parts.append(rep_ref[pick_ref[b * RAND + r], :, olo:ohi])
        return jnp.concatenate(parts, axis=0)

    for b in range(blocks):
        rows = slice(b * BLOCK, (b + 1) * BLOCK)
        for h in range(width // DH):
            keys = pieces(k_ref, 0, b, h)
            vals = pieces(v_ref, width, b, h)
            query = q_ref[rows, h * DH : (h + 1) * DH]
            scores = (
                lax.dot_general(
                    query, keys, (((1,), (1,)), ((), ())), preferred_element_type=F32
                )
                * scale
            )
            expo = jnp.exp(scores - jnp.max(scores, axis=-1, keepdims=True))
            probs = (expo / jnp.sum(expo, axis=-1, keepdims=True)).astype(BF)
            got = jnp.dot(probs, vals, preferred_element_type=F32)
            out_ref[rows, h * DH : (h + 1) * DH] = got.astype(BF)


def attend(pick, q, k, v, prev, after, glob, rep):
    args = (q, k, v, prev, after, glob, rep)
    return pl.pallas_call(
        attend_kernel,
        grid_spec=pltpu.PrefetchScalarGridSpec(
            num_scalar_prefetch=1,
            grid=(1,),
            in_specs=[whole(a.shape) for a in args],
            out_specs=whole(q.shape),
        ),
        out_shape=jax.ShapeDtypeStruct(q.shape, BF),
        compiler_params=params(),
        cost_estimate=pl.CostEstimate(
            flops=4 * 256 * 128 * 512, transcendentals=256 * 128 * 4, bytes_accessed=6 << 20
        ),
        name="attend",
    )(pick, *args)


def project_kernel(
    where_ref, drop_ref, mine_ref, other_ref, w_ref, res_ref, sum_ref, stat_ref, acc_ref
):
    step = pl.program_id(0)
    half = mine_ref.shape[0]
    lhs = jnp.where(step < half, 0, 1)

    @pl.when(step == 0)
    def _():
        acc_ref[...] = jnp.zeros_like(acc_ref)

    def add(ref, at):
        acc_ref[...] += lax.dot_general(
            ref[at], w_ref[0], (((1,), (1,)), ((), ())), preferred_element_type=F32
        )

    @pl.when(lhs == 0)
    def _():
        add(mine_ref, step)

    @pl.when(lhs == 1)
    def _():
        add(other_ref, step - half)

    @pl.when(step == pl.num_programs(0) - 1)
    def _():
        cols = acc_ref.shape[1]
        blocks = acc_ref.shape[0] // BLOCK
        seed = where_ref[1] * 1000003 + where_ref[2] * cols
        inner = lax.broadcasted_iota(jnp.int32, (BLOCK, cols), 0) * D
        inner = inner + lax.broadcasted_iota(jnp.int32, (BLOCK, cols), 1) + seed
        lane = lax.broadcasted_iota(jnp.int32, (BLOCK, DH), 1)
        for b in range(blocks):
            rows = slice(b * BLOCK, (b + 1) * BLOCK)
            hashed = inner + drop_ref[b]
            for _ in range(2):
                hashed = hashed ^ lax.shift_right_logical(hashed, jnp.int32(16))
                hashed = hashed * 73244475
            hashed = hashed ^ lax.shift_right_logical(hashed, jnp.int32(16))
            kept = (hashed & 1023) >= 102
            keep = jnp.where(kept, jnp.float32(1024.0 / 922.0), jnp.float32(0.0))
            total = res_ref[rows, :].astype(F32) + keep * acc_ref[rows, :]
            sum_ref[rows, :] = total
            mean = jnp.sum(total, axis=1, keepdims=True) * jnp.float32(1.0 / cols)
            dev = total - mean
            spread = jnp.sum(dev * dev, axis=1, keepdims=True)
            stat_ref[rows, :] = jnp.where(lane == 0, mean, spread)


def project(where, drops, mine, other, weight, residual):
    rows, cols = residual.shape
    half = mine.shape[0]
    steps = 2 * half

    def w_map(i, where_ref, drop_ref):
        core = where_ref[0]
        own = 2 * i + core
        far = 2 * (i - half) + (1 - core)
        return (jnp.where(i < half, own, far), 0, 0)

    return pl.pallas_call(
        project_kernel,
        grid_spec=pltpu.PrefetchScalarGridSpec(
            num_scalar_prefetch=2,
            grid=(steps,),
            in_specs=[
                whole(mine.shape),
                whole(other.shape),
                pl.BlockSpec((1,) + weight.shape[1:], w_map),
                whole(residual.shape),
            ],
            out_specs=[whole((rows, cols)), whole((rows, DH))],
            scratch_shapes=[pltpu.VMEM((rows, cols), F32)],
        ),
        out_shape=[
            jax.ShapeDtypeStruct((rows, cols), F32),
            jax.ShapeDtypeStruct((rows, DH), F32),
        ],
        compiler_params=params(),
        cost_estimate=pl.CostEstimate(
            flops=2 * rows * D * cols, transcendentals=0, bytes_accessed=8 << 20
        ),
        name="project",
    )(where, drops, mine, other, weight, residual)


def on_device(
    queries,
    key_rows,
    value_rows,
    residual,
    out_weight,
    norm_gain,
    norm_bias,
    global_list,
    random_device,
    random_offset,
    drop_seed,
    drop_offsets,
):
    row_count, width_here = queries.shape
    block_count = row_count // BLOCK
    seq_count = lax.axis_size("seq")
    tp_count = lax.axis_size("tp")
    tp_at = lax.axis_index("tp")
    cols_here = out_weight.shape[1]

    per = seq_count // tp_count
    moves = [
        (s * tp_count + t, (t * per + s % per) * tp_count + s // per)
        for s in range(seq_count)
        for t in range(tp_count)
    ]
    moved = lax.ppermute(out_weight.T, ("seq", "tp"), moves)
    weight = lax.all_gather(moved, "seq", axis=0, tiled=True)
    weight = weight.reshape(tp_count, per * cols_here, width_here)

    request_count = block_count * RAND
    target = random_device.reshape(request_count)
    wanted = random_offset.reshape(request_count)
    rank = jnp.arange(request_count, dtype=jnp.int32)
    same = target[:, None] == target[None, :]
    earlier = rank[None, :] < rank[:, None]
    slot = jnp.sum(jnp.logical_and(same, earlier), axis=1).astype(jnp.int32)
    dest_ids = jnp.arange(seq_count, dtype=jnp.int32)
    matched = jnp.logical_and(
        target[None, None, :] == dest_ids[:, None, None],
        slot[None, None, :] == jnp.arange(CAP, dtype=jnp.int32)[None, :, None],
    )
    table = jnp.sum(jnp.where(matched, wanted[None, None, :], 0), axis=2)
    chunks = seq_count // BLOCK
    share = 2 * width_here // chunks
    sent = []
    for which in range(GLOB):
        first = (global_list[which] % block_count) * BLOCK
        block = jnp.concatenate(
            [
                lax.dynamic_slice_in_dim(key_rows, first, BLOCK, axis=0),
                lax.dynamic_slice_in_dim(value_rows, first, BLOCK, axis=0),
            ],
            axis=1,
        )
        block = block.reshape(BLOCK, chunks, share).transpose(1, 0, 2)
        sent.append(block.reshape(seq_count, share))
    sent.append(jnp.pad(table.astype(BF), ((0, 0), (0, 2 * share - CAP))))
    first_payload = jnp.concatenate(sent, axis=1).reshape(seq_count, 8, DH)
    first_got = lax.all_to_all(first_payload, "seq", split_axis=0, concat_axis=0, tiled=True)
    want = first_got[:, 4, :CAP].astype(jnp.int32).reshape(seq_count * CAP)

    replies = pack(want, key_rows, value_rows)
    replies = lax.all_to_all(
        replies.reshape(seq_count, CAP, BLOCK, 2 * width_here),
        "seq",
        split_axis=0,
        concat_axis=0,
        tiled=True,
    ).reshape(seq_count * CAP, BLOCK, 2 * width_here)

    held = jnp.concatenate(
        [
            lax.dynamic_index_in_dim(first_got, global_list[g] // block_count, 0)[
                :, 2 * g : 2 * g + 2
            ]
            for g in range(GLOB)
        ]
        + [jnp.zeros((1, 4, DH), BF)],
        axis=1,
    )
    held = jnp.broadcast_to(held, (seq_count, 8, DH))
    glob = lax.all_to_all(held, "seq", split_axis=0, concat_axis=0, tiled=True)
    glob = glob.reshape(seq_count, 8 * DH)

    up = [(i, (i + 1) % seq_count) for i in range(seq_count)]
    down = [(j, i) for i, j in up]
    tail = row_count - BLOCK
    last = jnp.concatenate([key_rows[tail:], value_rows[tail:]], axis=1)
    head = jnp.concatenate([key_rows[:BLOCK], value_rows[:BLOCK]], axis=1)
    prev = lax.ppermute(last, "seq", up)
    after = lax.ppermute(head, "seq", down)

    context = attend(
        target * CAP + slot, queries, key_rows, value_rows, prev, after, glob, replies
    )

    pairs = tp_count // 2
    groups = [[2 * z + c for z in range(pairs)] for c in range(2)]
    mine = lax.all_to_all(
        jnp.broadcast_to(context[None], (pairs,) + context.shape),
        "tp",
        split_axis=0,
        concat_axis=0,
        tiled=True,
        axis_index_groups=groups,
    )
    other = lax.ppermute(mine, "tp", [(i, i ^ 1) for i in range(tp_count)])

    where = jnp.stack([tp_at % 2, drop_seed[0], tp_at]).astype(jnp.int32)
    summed, stats = project(where, drop_offsets, mine, other, weight, residual)

    stats = jnp.broadcast_to(stats[:, :2].T[None], (tp_count, 2, row_count))
    stats = lax.all_to_all(stats, "tp", split_axis=0, concat_axis=0, tiled=True)
    means, spreads = stats[:, 0], stats[:, 1]
    mean = jnp.sum(means, axis=0) / tp_count
    away = means - mean[None]
    cols = summed.shape[1]
    spread = jnp.sum(spreads, axis=0) + cols * jnp.sum(away * away, axis=0)
    factor = lax.rsqrt(spread / D + 1e-05)
    encoded = (summed - mean[:, None]) * factor[:, None] * norm_gain[None] + norm_bias[None]
    return encoded.astype(BF)


def solution(mesh):
    placed = (
        P("seq", "tp"),
        P("seq", "tp"),
        P("seq", "tp"),
        P("seq", "tp"),
        P("tp", "seq"),
        P("tp"),
        P("tp"),
        P(),
        P("seq", None),
        P("seq", None),
        P(),
        P("seq"),
    )
    return jax.shard_map(
        on_device, mesh=mesh, in_specs=placed, out_specs=P("seq", "tp"), check_vma=False
    )
```

time: 1140 us -> 358 us (0.31)
  waiting for transfers between devices: 1000 us -> 187 us
  Pallas kernels: 0 us -> 30.9 us
  blocking collectives: 31.1 us -> 51.6 us
  starting transfers between devices: 38.9 us -> 56.2 us
  local copies, waits for them, and re-layouts: 25.2 us -> 10.6 us
    psum x1 -> x0, waiting for transfers between devices: 702 us -> none  [broadcast(): return lax.psum(kept, axis)]
    all_gather x1, waiting for transfers between devices: 175 us -> 78.9 us  [on_device(): weight = lax.all_gather(moved, 'seq', axis=0, tiled=True)]
    all_to_all x0 -> x2, blocking collectives: none -> 51.6 us  [the longest x1 40.4 us: on_device(): lax.all_to_all(jnp.broadcast_to(context[None], (pairs,) + context.shape),...]
    reduce_scatter x1 -> x0, waiting for transfers between devices: 38 us -> none  [on_device(): lax.psum_scatter(partial_terms.astype(jnp.bfloat16), 'tp', scatter_dimens...]
    psum x2 -> x0, blocking collectives: 31.1 us -> none  [the longest x1 16.2 us: on_device(): row_total = lax.psum(jnp.sum(summed_rows, axis=1), 'tp')]
    pallas_call x0 -> x3, Pallas kernels: none -> 30.9 us  [the longest x1 22.9 us: attend(): pl.pallas_call(attend_kernel, grid_spec=pltpu.PrefetchScalarGridSpec(num_...]
    ppermute x2 -> x4, waiting for transfers between devices: 73.8 us -> 87.2 us  [the longest x1 85 us: on_device(): moved = lax.ppermute(out_weight.T, ('seq', 'tp'), moves)]
    ppermute x2 -> x4, starting transfers between devices: 13.4 us -> 25.8 us  [the longest x1 8.36 us: on_device(): after = lax.ppermute(head, 'seq', down)]
  transfers between devices with their start and end apart: 7 -> 8, of which waited for: 5 -> 5; matrix products, arithmetic and copies ran while one was open for 3% -> 0% of each run, Pallas kernels for 0% -> 7%
where the time goes in v1:
time: 358 us
  waiting for transfers between devices  187 us (52%)
  starting transfers between devices  56.2 us (16%)
  blocking collectives  51.6 us (14%)
  Pallas kernels  30.9 us (9%)
  between operations  19.3 us (5%)
  local copies, waits for them, and re-layouts  10.6 us (3%)
    ppermute x1, waiting for transfers between devices, on_device(): moved = lax.ppermute(out_weight.T, ('seq', 'tp'), moves)  85 us
    all_gather x1, waiting for transfers between devices, on_device(): weight = lax.all_gather(moved, 'seq', axis=0, tiled=True)  78.9 us
    all_to_all x1, blocking collectives, on_device(): lax.all_to_all(jnp.broadcast_to(context[None], (pairs,) + context.shape),...  40.4 us
    pallas_call x1, Pallas kernels, attend(): pl.pallas_call(attend_kernel, grid_spec=pltpu.PrefetchScalarGridSpec(num_...  22.9 us
    all_to_all x1, starting transfers between devices, on_device(): lax.all_to_all(first_payload, 'seq', split_axis=0, concat_axis=0, tiled=T...  19.6 us
    all_to_all x1, waiting for transfers between devices, on_device(): lax.all_to_all(first_payload, 'seq', split_axis=0, concat_axis=0, tiled=T...  12.5 us
    all_to_all x1, blocking collectives, on_device(): stats = lax.all_to_all(stats, 'tp', split_axis=0, concat_axis=0, tiled=True)  11.3 us
    all_to_all x1, waiting for transfers between devices, on_device(): glob = lax.all_to_all(held, 'seq', split_axis=0, concat_axis=0, tiled=True)  8.84 us
  transfers between devices with their start and end apart: 8, of which 5 were waited for; matrix products, arithmetic and copies ran while one was open for 0% of the time, Pallas kernels for 7%

profile of v1, /device:TPU:1, one launch (start us, length us, event | category | flops | bytes accessed | tf_op | source)
XLA Modules:
  0.0 357.6 jit_solution(7075475910761539908)
XLA Ops:
  6.5 1.3 fusion.6
  11.5 0.8 copy.34
  12.2 0.1 reshape.105
  12.3 0.2 convert_reduce_fusion
  12.5 0.1 iota_compare_fusion.1
  12.6 0.8 copy.37
  13.4 0.1 broadcast_in_dim.24
  13.5 0.1 select_reduce_fusion
  13.6 0.9 constant_dynamic-slice_fusion.4
  14.5 0.1 copy.39
  14.7 0.1 copy.38
  14.8 0.8 copy.44
  15.6 19.6 %all-to-all-start = ((bf16[64,8,128]{2,1,0:T(8,128)(2,1)}), bf16[64,8,128]{2,1,0:T(8,128)(2,1)S(1)}, u32[]{:S(2)}, u32[]{:S(2)}) async-start(bf16[64,8,128]{2,1,0:T(8,128)(2,1)} %copy.44), calls=%async_computation | async-start | bytes 262144 | tf_op jit(solution)/shard_map/all_to_all | solution.py:271
  36.5 0.1 pad.7.clone
  36.5 12.5 %all-to-all-done = bf16[64,8,128]{2,1,0:T(8,128)(2,1)S(1)} async-done(((bf16[64,8,128]{2,1,0:T(8,128)(2,1)}), bf16[64,8,128]{2,1,0:T(8,128)(2,1)S(1)}, u32[]{:S(2)}, u32[]{:S(2)}) %all-to-all-start) | async-done | bytes 131104 | tf_op jit(solution)/shard_map/all_to_all | solution.py:271
  49.0 0.1 maximum_bitcast_fusion
  49.1 0.7 broadcast_in_dim.29
  49.8 4.6 %all-to-all-start.1 = ((bf16[64,8,128]{2,1,0:T(8,128)(2,1)}), bf16[64,8,128]{2,1,0:T(8,128)(2,1)S(1)}, u32[]{:S(2)}, u32[]{:S(2)}) async-start(bf16[64,8,128]{2,1,0:T(8,128)(2,1)} %broadcast_in_dim.29), calls=%async_computation.1 | async-start | bytes 262144 | tf_op jit(solution)/shard_map/all_to_all | solution.py:294
  54.4 0.1 fusion.2
  54.5 0.1 reshape.115.want_ref
  54.7 0.0 copy-start.1
  54.7 0.9 copy-done.1
  55.6 0.0 copy-start.3
  55.6 0.9 copy-done.3
  56.6 0.9 pack.1
  57.5 0.0 copy-start
  57.5 1.9 copy-done
  59.4 8.8 %all-to-all-done.1 = bf16[64,8,128]{2,1,0:T(8,128)(2,1)S(1)} async-done(((bf16[64,8,128]{2,1,0:T(8,128)(2,1)}), bf16[64,8,128]{2,1,0:T(8,128)(2,1)S(1)}, u32[]{:S(2)}, u32[]{:S(2)}) %all-to-all-start.1) | async-done | bytes 131104 | tf_op jit(solution)/shard_map/all_to_all | solution.py:294
  68.3 0.0 copy-start.11
  68.3 0.0 copy-start.2
  68.3 6.1 %all-to-all-start.2 = ((bf16[64,2,16,1024]{3,2,1,0:T(8,128)(2,1)}), bf16[64,2,16,1024]{3,2,1,0:T(8,128)(2,1)}, u32[]{:S(2)}, u32[]{:S(2)}) async-start(bf16[64,2,16,1024]{3,2,1,0:T(8,128)(2,1)} %bitcast.27), calls=%async_computation.2 | async-start | bytes 8388608 | tf_op jit(solution)/shard_map/all_to_all | solution.py:275
  74.4 0.0 all-gather.2.cloned.1.call-start
  74.5 0.0 copy-done.11
  74.5 5.8 %collective-permute-start.3 = (bf16[64,512]{1,0:T(8,128)(2,1)S(1)}, bf16[64,512]{1,0:T(8,128)(2,1)S(1)}, u32[]{:S(2)}, u32[]{:S(2)}) collective-permute-start(bf16[64,512]{1,0:T(8,128)(2,1)S(1)} %bitcast.36), channel_id=1, source_target_pairs={{0,0},{1,64},{2,128},{3,192},{4,256},{5,320},{6,384},{7,448},{8,8}... | collective-permute-start | bytes 196616 | tf_op jit(solution)/shard_map/ppermute | solution.py:238
  80.3 85.0 %collective-permute-done.3 = bf16[64,512]{1,0:T(8,128)(2,1)S(1)} collective-permute-done((bf16[64,512]{1,0:T(8,128)(2,1)S(1)}, bf16[64,512]{1,0:T(8,128)(2,1)S(1)}, u32[]{:S(2)}, u32[]{:S(2)}) %collective-permute-start.3) | collective-permute-done | bytes 65568 | tf_op jit(solution)/shard_map/ppermute | solution.py:238
  165.3 0.6 copy-done.8
  165.9 0.0 all-gather.2.cloned.1.call-update
  166.0 7.9 %collective-permute-start = (bf16[16,1024]{1,0:T(8,128)(2,1)S(1)}, bf16[16,1024]{1,0:T(8,128)(2,1)S(1)}, u32[]{:S(2)}, u32[]{:S(2)}) collective-permute-start(bf16[16,1024]{1,0:T(8,128)(2,1)S(1)} %pad_maximum_fusion), channel_id=1, source_target_pairs={{0,8},{8,16},{16,24},{24,32},{32,40},{40,48},{48,56},{56,64},{64,7... | collective-permute-start | bytes 98312 | tf_op jit(solution)/shard_map/ppermute | solution.py:302
  173.9 8.4 %collective-permute-start.1 = (bf16[16,1024]{1,0:T(8,128)(2,1)S(1)}, bf16[16,1024]{1,0:T(8,128)(2,1)S(1)}, u32[]{:S(2)}, u32[]{:S(2)}) collective-permute-start(bf16[16,1024]{1,0:T(8,128)(2,1)S(1)} %pad_maximum_fusion.1), channel_id=1, source_target_pairs={{8,0},{16,8},{24,16},{32,24},{40,32},{48,40},{56,48},{64,56},{72,6... | collective-permute-start | bytes 98312 | tf_op jit(solution)/shard_map/ppermute | solution.py:303
  182.3 0.0 collective-permute-done.prev_ref
  182.3 2.2 collective-permute-done.1.next_ref
  184.5 0.0 all-to-all-done.2
  184.5 0.0 copy-done.2
  184.5 0.0 copy-done.4
  184.5 0.0 copy-done.5
  184.5 0.0 copy-start.6
  184.6 0.0 copy-start.7
  184.6 22.9 %attend.1 = bf16[256,512]{1,0:T(8,128)(2,1)S(1)} custom-call(s32[48]{0:T(128)S(1)} %multiply_add_fusion.pick_ref, bf16[256,512]{1,0:T(8,128)(2,1)S(1)} %copy-done.5, bf16[256,512]{1,0:T(8,128)(2,1)S(1)} %copy-done.2, bf16[256,512]{1,0:T(8,128)(2,1)S(1)} %copy-done.4, bf16[16,1024]{1,0:T(8,128)(2,1)S(1)} %collective-permute-done.prev_ref, ...), custom_call_target="tpu_custom_call" | custom-call | flops 67108864 | bytes 6291456 | tf_op jit(solution)/shard_map/attend/pallas_call | solution.py:108
  207.5 0.1 broadcast_in_dim.52
  207.6 0.0 copy-start.9
  207.6 0.0 copy-start.10
  207.6 40.4 %all_to_all.25.mine_ref = bf16[4,256,512]{2,1,0:T(8,128)(2,1)S(1)} all-to-all(bf16[4,256,512]{2,1,0:T(8,128)(2,1)S(1)} %broadcast_in_dim.52), channel_id=1, replica_groups={{0,2,4,6},{1,3,5,7},{8,10,12,14},{9,11,13,15},{16,18,20,22},{17,19,21,2..., dimensions={0} | all-to-all | bytes 2097152 | tf_op jit(solution)/shard_map/all_to_all | solution.py:311
  248.0 3.7 %collective-permute-start.2 = (bf16[4,256,512]{2,1,0:T(8,128)(2,1)S(1)}, bf16[4,256,512]{2,1,0:T(8,128)(2,1)S(1)}, u32[]{:S(2)}, u32[]{:S(2)}) collective-permute-start(bf16[4,256,512]{2,1,0:T(8,128)(2,1)S(1)} %all_to_all.25.mine_ref), channel_id=1, source_target_pairs={{0,1},{1,0},{2,3},{3,2},{4,5},{5,4},{6,7},{7,6},{8,9},{9,8},{10,11... | collective-permute-start | bytes 3145736 | tf_op jit(solution)/shard_map/ppermute | solution.py:319
  252.4 0.1 pad_add_fusion.where_ref
  252.5 78.9 %all-gather.2.cloned.1.call-done = bf16[4096,512]{1,0:T(8,128)(2,1)} async-done(((bf16[64,512]{1,0:T(8,128)(2,1)}), bf16[4096,512]{1,0:T(8,128)(2,1)}) %all-gather.2.cloned.1.call-update) | async-done | bytes 4194320 | tf_op jit(solution)/shard_map/all_gather | solution.py:239
  331.3 0.0 collective-permute-done.2.other_ref
  331.3 0.0 copy-done.6
  331.3 0.0 copy-done.7
  331.3 7.1 %project.1 = (f32[256,512]{1,0:T(8,128)S(1)}, f32[256,128]{1,0:T(8,128)S(1)}) custom-call(s32[3]{0:T(128)S(1)} %pad_add_fusion.where_ref, s32[16]{0:T(128)S(1)} %copy-done.7, bf16[4,256,512]{2,1,0:T(8,128)(2,1)S(1)} %all_to_all.25.mine_ref, bf16[4,256,512]{2,1,0:T(8,128)(2,1)S(1)} %collective-permute-done.2.other_ref, bf16[8,512,512]{2,1,0:T(8,128)(2,1)} %bitcast.29, ...), custom_call_target="tpu_custom_call" | custom-call | flops 1073741824 | bytes 8388608 | tf_op jit(solution)/shard_map/project/pallas_call | solution.py:185
  338.4 0.1 copy.41
  338.5 11.3 %all_to_all.26 = f32[8,2,256]{2,1,0:T(2,128)S(1)} all-to-all(f32[8,2,256]{2,1,0:T(2,128)S(1)} %broadcast_in_dim.53), channel_id=1, replica_groups=mesh['seq'=64,'tp'=8] {'tp'}, dimensions={0} | all-to-all | bytes 32768 | tf_op jit(solution)/shard_map/all_to_all | solution.py:325
  349.8 0.0 copy-done.9
  349.9 0.0 copy-done.10
  349.9 0.9 add_convert_fusion
  (26 shorter events, 0.3 us)
Async XLA Ops:
  15.6 33.4 %all-to-all-start = ((bf16[64,8,128]{2,1,0:T(8,128)(2,1)}), bf16[64,8,128]{2,1,0:T(8,128)(2,1)S(1)}, u32[]{:S(2)}, u32[]{:S(2)}) async-start(bf16[64,8,128]{2,1,0:T(8,128)(2,1)} %copy.44), calls=%async_computation | async-start | bytes 262144 | tf_op jit(solution)/shard_map/all_to_all | solution.py:271
  49.8 18.5 %all-to-all-start.1 = ((bf16[64,8,128]{2,1,0:T(8,128)(2,1)}), bf16[64,8,128]{2,1,0:T(8,128)(2,1)S(1)}, u32[]{:S(2)}, u32[]{:S(2)}) async-start(bf16[64,8,128]{2,1,0:T(8,128)(2,1)} %broadcast_in_dim.29), calls=%async_computation.1 | async-start | bytes 262144 | tf_op jit(solution)/shard_map/all_to_all | solution.py:294
  54.7 1.0 copy-start.1
  55.6 0.9 copy-start.3
  57.5 2.0 copy-start
  68.3 6.2 %copy-start.11 = (bf16[512,64]{0,1:T(8,128)(2,1)S(1)}, bf16[512,64]{0,1:T(8,128)(2,1)}, u32[]{:S(2)}) copy-start(bf16[512,64]{0,1:T(8,128)(2,1)} %param.16) | copy-start | bytes 196612
  68.3 116.2 %copy-start.2 = (bf16[256,512]{1,0:T(8,128)(2,1)S(1)}, bf16[256,512]{1,0:T(8,128)(2,1)}, u32[]{:S(2)}) copy-start(bf16[256,512]{1,0:T(8,128)(2,1)} %k_ref.3) | copy-start | bytes 786436
  68.3 116.2 %copy-start.4 = (bf16[256,512]{1,0:T(8,128)(2,1)S(1)}, bf16[256,512]{1,0:T(8,128)(2,1)}, u32[]{:S(2)}) copy-start(bf16[256,512]{1,0:T(8,128)(2,1)} %v_ref.3) | copy-start | bytes 786436
  68.3 116.2 %copy-start.5 = (bf16[256,512]{1,0:T(8,128)(2,1)S(1)}, bf16[256,512]{1,0:T(8,128)(2,1)}, u32[]{:S(2)}) copy-start(bf16[256,512]{1,0:T(8,128)(2,1)} %q_ref.1) | copy-start | bytes 786436
  68.3 116.2 %all-to-all-start.2 = ((bf16[64,2,16,1024]{3,2,1,0:T(8,128)(2,1)}), bf16[64,2,16,1024]{3,2,1,0:T(8,128)(2,1)}, u32[]{:S(2)}, u32[]{:S(2)}) async-start(bf16[64,2,16,1024]{3,2,1,0:T(8,128)(2,1)} %bitcast.27), calls=%async_computation.2 | async-start | bytes 8388608 | tf_op jit(solution)/shard_map/all_to_all | solution.py:275
  74.4 256.9 %all-gather.2.cloned.1.call-start = ((), (), s32[]{:S(2)}) async-start(), calls=%async_computation.5 | async-start | bytes 4259840 | tf_op jit(solution)/shard_map/all_gather | solution.py:239
  74.5 90.8 %collective-permute-start.3 = (bf16[64,512]{1,0:T(8,128)(2,1)S(1)}, bf16[64,512]{1,0:T(8,128)(2,1)S(1)}, u32[]{:S(2)}, u32[]{:S(2)}) collective-permute-start(bf16[64,512]{1,0:T(8,128)(2,1)S(1)} %bitcast.36), channel_id=1, source_target_pairs={{0,0},{1,64},{2,128},{3,192},{4,256},{5,320},{6,384},{7,448},{8,8}... | collective-permute-start | bytes 196616 | tf_op jit(solution)/shard_map/ppermute | solution.py:238
  165.3 0.6 copy-start.8
  166.0 16.3 %collective-permute-start = (bf16[16,1024]{1,0:T(8,128)(2,1)S(1)}, bf16[16,1024]{1,0:T(8,128)(2,1)S(1)}, u32[]{:S(2)}, u32[]{:S(2)}) collective-permute-start(bf16[16,1024]{1,0:T(8,128)(2,1)S(1)} %pad_maximum_fusion), channel_id=1, source_target_pairs={{0,8},{8,16},{16,24},{24,32},{32,40},{40,48},{48,56},{56,64},{64,7... | collective-permute-start | bytes 98312 | tf_op jit(solution)/shard_map/ppermute | solution.py:302
  173.9 10.6 %collective-permute-start.1 = (bf16[16,1024]{1,0:T(8,128)(2,1)S(1)}, bf16[16,1024]{1,0:T(8,128)(2,1)S(1)}, u32[]{:S(2)}, u32[]{:S(2)}) collective-permute-start(bf16[16,1024]{1,0:T(8,128)(2,1)S(1)} %pad_maximum_fusion.1), channel_id=1, source_target_pairs={{8,0},{16,8},{24,16},{32,24},{40,32},{48,40},{56,48},{64,56},{72,6... | collective-permute-start | bytes 98312 | tf_op jit(solution)/shard_map/ppermute | solution.py:303
  184.5 146.8 %copy-start.6 = (bf16[256,512]{1,0:T(8,128)(2,1)S(1)}, bf16[256,512]{1,0:T(8,128)(2,1)}, u32[]{:S(2)}) copy-start(bf16[256,512]{1,0:T(8,128)(2,1)} %res_ref.1) | copy-start | bytes 786436
  184.6 146.8 %copy-start.7 = (s32[16]{0:T(128)S(1)}, s32[16]{0:T(128)}, u32[]{:S(2)}) copy-start(s32[16]{0:T(128)} %drop_ref.1) | copy-start | bytes 196
  207.6 142.2 %copy-start.9 = (f32[512]{0:T(512)S(1)}, f32[512]{0:T(512)}, u32[]{:S(2)}) copy-start(f32[512]{0:T(512)} %param.18) | copy-start | bytes 6148
  207.6 142.2 %copy-start.10 = (f32[512]{0:T(512)S(1)}, f32[512]{0:T(512)}, u32[]{:S(2)}) copy-start(f32[512]{0:T(512)} %param.17) | copy-start | bytes 6148
  248.0 83.3 %collective-permute-start.2 = (bf16[4,256,512]{2,1,0:T(8,128)(2,1)S(1)}, bf16[4,256,512]{2,1,0:T(8,128)(2,1)S(1)}, u32[]{:S(2)}, u32[]{:S(2)}) collective-permute-start(bf16[4,256,512]{2,1,0:T(8,128)(2,1)S(1)} %all_to_all.25.mine_ref), channel_id=1, source_target_pairs={{0,1},{1,0},{2,3},{3,2},{4,5},{5,4},{6,7},{7,6},{8,9},{9,8},{10,11... | collective-permute-start | bytes 3145736 | tf_op jit(solution)/shard_map/ppermute | solution.py:319
Sparse Core Ops, SparseCore 0:
  166.1 165.1 all-gather.1

commit v2 on v1

v2 whole, which is shorter than its diff:
```python
import jax
import jax.numpy as jnp
from jax import lax
from jax.experimental import pallas as pl
from jax.experimental.pallas import tpu as pltpu
from jax.sharding import Mesh
from jax.sharding import PartitionSpec as P

D = 4096
DH = 128
BLOCK = 16
GLOB = 2
RAND = 3
CAP = 2
BF = jnp.bfloat16
F32 = jnp.float32
SEQ = ("y", "x", "zh")
TP = ("zl", "core")
PLANE = ("x", "zh")
VMEM_LIMIT = 48 * 1024 * 1024


def whole(shape):
    return pl.BlockSpec(shape, lambda *a: (0,) * len(shape))


def params():
    return pltpu.CompilerParams(vmem_limit_bytes=VMEM_LIMIT)


def pack_kernel(want_ref, pool_ref, out_ref):
    def step(i, carry):
        rows = pl.ds(pl.multiple_of(want_ref[i] * BLOCK, BLOCK), BLOCK)
        out_ref[i] = pool_ref[rows, :]
        return carry

    lax.fori_loop(0, out_ref.shape[0], step, 0, unroll=8)


def pack(want, pool):
    out = (want.shape[0], BLOCK, pool.shape[1])
    return pl.pallas_call(
        pack_kernel,
        grid_spec=pltpu.PrefetchScalarGridSpec(
            num_scalar_prefetch=1,
            grid=(1,),
            in_specs=[whole(pool.shape)],
            out_specs=whole(out),
        ),
        out_shape=jax.ShapeDtypeStruct(out, BF),
        compiler_params=params(),
        cost_estimate=pl.CostEstimate(flops=0, transcendentals=0, bytes_accessed=9 << 20),
        name="pack",
    )(want, pool)


def attend_kernel(pick_ref, q_ref, k_ref, v_ref, prev_ref, next_ref, rep_ref, out_ref):
    width = q_ref.shape[1]
    blocks = q_ref.shape[0] // BLOCK
    heads = width // DH
    scale = jnp.float32(1.0 / DH**0.5)

    def listed(local_ref, offset, b, h):
        lo, hi = h * DH, (h + 1) * DH
        olo, ohi = offset + lo, offset + hi
        parts = []
        if b == 0:
            parts.append(prev_ref[:, olo:ohi])
            parts.append(local_ref[0 : 2 * BLOCK, lo:hi])
        elif b == blocks - 1:
            parts.append(local_ref[(b - 1) * BLOCK : (b + 1) * BLOCK, lo:hi])
            parts.append(next_ref[:, olo:ohi])
        else:
            parts.append(local_ref[(b - 1) * BLOCK : (b + 2) * BLOCK, lo:hi])
        for g in range(GLOB):
            parts.append(rep_ref[pick_ref[blocks * RAND + g], :, olo:ohi])
        for r in range(RAND):
            parts.append(rep_ref[pick_ref[b * RAND + r], :, olo:ohi])
        return jnp.concatenate(parts, axis=0)

    for first in range(0, blocks, 4):
        pairs = [(b, h) for b in range(first, first + 4) for h in range(heads)]
        scores = []
        for b, h in pairs:
            query = q_ref[b * BLOCK : (b + 1) * BLOCK, h * DH : (h + 1) * DH]
            scores.append(
                lax.dot_general(
                    query,
                    listed(k_ref, 0, b, h),
                    (((1,), (1,)), ((), ())),
                    preferred_element_type=F32,
                )
            )
        scores = jnp.concatenate(scores, axis=0) * scale
        expo = jnp.exp(scores - jnp.max(scores, axis=-1, keepdims=True))
        probs = (expo / jnp.sum(expo, axis=-1, keepdims=True)).astype(BF)
        for i, (b, h) in enumerate(pairs):
            got = jnp.dot(
                probs[i * BLOCK : (i + 1) * BLOCK],
                listed(v_ref, width, b, h),
                preferred_element_type=F32,
            )
            out_ref[b * BLOCK : (b + 1) * BLOCK, h * DH : (h + 1) * DH] = got.astype(BF)


def attend(pick, q, k, v, prev, after, rep):
    args = (q, k, v, prev, after, rep)
    return pl.pallas_call(
        attend_kernel,
        grid_spec=pltpu.PrefetchScalarGridSpec(
            num_scalar_prefetch=1,
            grid=(1,),
            in_specs=[whole(a.shape) for a in args],
            out_specs=whole(q.shape),
        ),
        out_shape=jax.ShapeDtypeStruct(q.shape, BF),
        compiler_params=params(),
        cost_estimate=pl.CostEstimate(
            flops=4 * 256 * 128 * 512, transcendentals=256 * 128 * 4, bytes_accessed=6 << 20
        ),
        name="attend",
    )(pick, *args)


def project_kernel(
    where_ref, drop_ref, mine_ref, other_ref, w_ref, res_ref, sum_ref, stat_ref, acc_ref
):
    step = pl.program_id(0)
    half = mine_ref.shape[0]
    lhs = jnp.where(step < half, 0, 1)

    @pl.when(step == 0)
    def _():
        acc_ref[...] = jnp.zeros_like(acc_ref)

    def add(ref, at):
        acc_ref[...] += lax.dot_general(
            ref[at], w_ref[0], (((1,), (1,)), ((), ())), preferred_element_type=F32
        )

    @pl.when(lhs == 0)
    def _():
        add(mine_ref, step)

    @pl.when(lhs == 1)
    def _():
        add(other_ref, step - half)

    @pl.when(step == pl.num_programs(0) - 1)
    def _():
        cols = acc_ref.shape[1]
        blocks = acc_ref.shape[0] // BLOCK
        seed = where_ref[1] * 1000003 + where_ref[2] * cols
        inner = lax.broadcasted_iota(jnp.int32, (BLOCK, cols), 0) * D
        inner = inner + lax.broadcasted_iota(jnp.int32, (BLOCK, cols), 1) + seed
        lane = lax.broadcasted_iota(jnp.int32, (BLOCK, DH), 1)
        for b in range(blocks):
            rows = slice(b * BLOCK, (b + 1) * BLOCK)
            hashed = inner + drop_ref[b]
            for _ in range(2):
                hashed = hashed ^ lax.shift_right_logical(hashed, jnp.int32(16))
                hashed = hashed * 73244475
            hashed = hashed ^ lax.shift_right_logical(hashed, jnp.int32(16))
            kept = (hashed & 1023) >= 102
            keep = jnp.where(kept, jnp.float32(1024.0 / 922.0), jnp.float32(0.0))
            total = res_ref[rows, :].astype(F32) + keep * acc_ref[rows, :]
            sum_ref[rows, :] = total
            mean = jnp.sum(total, axis=1, keepdims=True) * jnp.float32(1.0 / cols)
            dev = total - mean
            spread = jnp.sum(dev * dev, axis=1, keepdims=True)
            stat_ref[rows, :] = jnp.where(lane == 0, mean, spread)


def project(where, drops, mine, other, weight, residual):
    rows, cols = residual.shape
    half = mine.shape[0]
    steps = 2 * half

    def w_map(i, where_ref, drop_ref):
        core = where_ref[0]
        own = 2 * i + core
        far = 2 * (i - half) + (1 - core)
        return (jnp.where(i < half, own, far), 0, 0)

    return pl.pallas_call(
        project_kernel,
        grid_spec=pltpu.PrefetchScalarGridSpec(
            num_scalar_prefetch=2,
            grid=(steps,),
            in_specs=[
                whole(mine.shape),
                whole(other.shape),
                pl.BlockSpec((1,) + weight.shape[1:], w_map),
                whole(residual.shape),
            ],
            out_specs=[whole((rows, cols)), whole((rows, DH))],
            scratch_shapes=[pltpu.VMEM((rows, cols), F32)],
        ),
        out_shape=[
            jax.ShapeDtypeStruct((rows, cols), F32),
            jax.ShapeDtypeStruct((rows, DH), F32),
        ],
        compiler_params=params(),
        cost_estimate=pl.CostEstimate(
            flops=2 * rows * D * cols, transcendentals=0, bytes_accessed=8 << 20
        ),
        name="project",
    )(where, drops, mine, other, weight, residual)


def on_device(
    queries,
    key_rows,
    value_rows,
    residual,
    out_weight,
    norm_gain,
    norm_bias,
    global_list,
    random_device,
    random_offset,
    drop_seed,
    drop_offsets,
):
    row_count, width_here = queries.shape
    block_count = row_count // BLOCK
    n_y, n_x, n_zh = (lax.axis_size(a) for a in SEQ)
    plane = n_x * n_zh
    seq_count = n_y * plane
    n_zl = lax.axis_size("zl")
    tp_count = n_zl * lax.axis_size("core")
    tp_at = lax.axis_index(TP)
    cols_here = out_weight.shape[1]

    paired = jnp.concatenate([key_rows, value_rows], axis=1)
    pool = lax.all_gather(paired, "y", axis=0, tiled=True)

    moves = [
        ((y * plane + p) * tp_count + t, (t * plane + p) * tp_count + y)
        for y in range(n_y)
        for p in range(plane)
        for t in range(tp_count)
    ]
    moved = lax.ppermute(out_weight.T, SEQ + TP, moves)

    request_count = block_count * RAND
    target = random_device.reshape(request_count)
    wanted = random_offset.reshape(request_count)
    rank = jnp.arange(request_count, dtype=jnp.int32)
    same = target[:, None] == target[None, :]
    earlier = rank[None, :] < rank[:, None]
    slot = jnp.sum(jnp.logical_and(same, earlier), axis=1).astype(jnp.int32)
    place = (target // plane) * CAP + slot
    column = target % plane
    slots = n_y * CAP
    matched = jnp.logical_and(
        column[None, None, :] == jnp.arange(plane, dtype=jnp.int32)[:, None, None],
        place[None, None, :] == jnp.arange(slots, dtype=jnp.int32)[None, :, None],
    )
    table = jnp.sum(jnp.where(matched, wanted[None, None, :], 0), axis=2)
    asked = jnp.pad(table.astype(BF)[:, None, :], ((0, 0), (0, 7), (0, width_here - slots)))
    spread_w = jnp.broadcast_to(moved[None], (plane,) + moved.shape)
    got = lax.all_to_all(
        jnp.concatenate([spread_w, asked], axis=1),
        PLANE,
        split_axis=0,
        concat_axis=0,
        tiled=True,
    )
    want = got[:, cols_here, :slots].astype(jnp.int32)
    weight = lax.all_gather(
        got[:, :cols_here].reshape(plane * cols_here, width_here), "y", axis=0, tiled=True
    )
    weight = weight.reshape(tp_count, plane * cols_here, width_here)

    base = (jnp.arange(slots, dtype=jnp.int32) // CAP) * block_count
    owner = global_list // block_count
    glob_row = (owner // plane) * block_count + global_list % block_count
    want = jnp.concatenate(
        [want + base[None], jnp.broadcast_to(glob_row[None], (plane, GLOB))], axis=1
    )
    sent = slots + GLOB
    replies = pack(want.reshape(plane * sent), pool)
    replies = lax.all_to_all(
        replies.reshape(plane, sent, BLOCK, 2 * width_here),
        PLANE,
        split_axis=0,
        concat_axis=0,
        tiled=True,
    ).reshape(plane * sent, BLOCK, 2 * width_here)

    up = [(i, (i + 1) % seq_count) for i in range(seq_count)]
    down = [(j, i) for i, j in up]
    tail = row_count - BLOCK
    prev = lax.ppermute(paired[tail:], SEQ, up)
    after = lax.ppermute(paired[:BLOCK], SEQ, down)

    pick = jnp.concatenate(
        [
            column * sent + place,
            (owner % plane) * sent + slots + jnp.arange(GLOB, dtype=jnp.int32),
        ]
    )
    context = attend(pick, queries, key_rows, value_rows, prev, after, replies)

    mine = lax.all_to_all(
        jnp.broadcast_to(context[None], (n_zl,) + context.shape),
        "zl",
        split_axis=0,
        concat_axis=0,
        tiled=True,
    )
    other = lax.ppermute(mine, "core", [(0, 1), (1, 0)])

    where = jnp.stack([tp_at % 2, drop_seed[0], tp_at]).astype(jnp.int32)
    summed, stats = project(where, drop_offsets, mine, other, weight, residual)

    stats = jnp.broadcast_to(stats[:, :2].T[None], (tp_count, 2, row_count))
    stats = lax.all_to_all(stats, TP, split_axis=0, concat_axis=0, tiled=True)
    means, spreads = stats[:, 0], stats[:, 1]
    mean = jnp.sum(means, axis=0) / tp_count
    away = means - mean[None]
    cols = summed.shape[1]
    spread = jnp.sum(spreads, axis=0) + cols * jnp.sum(away * away, axis=0)
    factor = lax.rsqrt(spread / D + 1e-05)
    encoded = (summed - mean[:, None]) * factor[:, None] * norm_gain[None] + norm_bias[None]
    return encoded.astype(BF)


def solution(mesh):
    fine = Mesh(mesh.devices.reshape(8, 4, 2, 4, 2), SEQ + TP)
    placed = (
        P(SEQ, TP),
        P(SEQ, TP),
        P(SEQ, TP),
        P(SEQ, TP),
        P(TP, SEQ),
        P(TP),
        P(TP),
        P(),
        P(SEQ, None),
        P(SEQ, None),
        P(),
        P(SEQ),
    )
    return jax.shard_map(
        on_device, mesh=fine, in_specs=placed, out_specs=P(SEQ, TP), check_vma=False
    )
```

time: 358 us -> 265 us (0.74)
  waiting for transfers between devices: 187 us -> 141 us
  Pallas kernels: 30.9 us -> 15.4 us
  starting transfers between devices: 56.2 us -> 44 us
  blocking collectives: 51.6 us -> 40.2 us
  between operations: 19.3 us -> 14.3 us
    all_gather x1 -> x2, waiting for transfers between devices: 78.9 us -> 30.5 us  [the longest x1 30.5 us: on_device(): pool = lax.all_gather(paired, 'y', axis=0, tiled=True)]
    pallas_call x1, Pallas kernels: 22.9 us -> 5.2 us  [attend(): pl.pallas_call(attend_kernel, grid_spec=pltpu.PrefetchScalarGridSpec(num_...]
    all_to_all x2, blocking collectives: 51.6 us -> 40.2 us  [the longest x1 32.4 us: on_device(): lax.all_to_all(jnp.broadcast_to(context[None], (n_zl,) + context.shape),...]
    ppermute x4, waiting for transfers between devices: 87.2 us -> 98.2 us  [the longest x1 95.6 us: on_device(): prev = lax.ppermute(paired[tail:], SEQ, up)]
    all_to_all x3 -> x2, waiting for transfers between devices: 21.3 us -> 12.1 us  [the longest x1 12.1 us: on_device(): lax.all_to_all(jnp.concatenate([spread_w, asked], axis=1), PLANE, split_a...]
    all_to_all x3 -> x2, starting transfers between devices: 30.3 us -> 22 us  [the longest x1 12.5 us: on_device(): lax.all_to_all(jnp.concatenate([spread_w, asked], axis=1), PLANE, split_a...]
    ppermute x4, starting transfers between devices: 25.8 us -> 22 us  [the longest x1 7.25 us: on_device(): prev = lax.ppermute(paired[tail:], SEQ, up)]
  transfers between devices with their start and end apart: 8 -> 8, of which waited for: 5 -> 5; matrix products, arithmetic and copies ran while one was open for 0% -> 1% of each run, Pallas kernels for 7% -> 2%
where the time goes in v2:
time: 265 us
  waiting for transfers between devices  141 us (53%)
  starting transfers between devices  44 us (17%)
  blocking collectives  40.2 us (15%)
  Pallas kernels  15.4 us (6%)
  between operations  14.3 us (5%)
  local copies, waits for them, and re-layouts  7.39 us (3%)
    ppermute x1, waiting for transfers between devices, on_device(): prev = lax.ppermute(paired[tail:], SEQ, up)  95.6 us
    all_to_all x1, blocking collectives, on_device(): lax.all_to_all(jnp.broadcast_to(context[None], (n_zl,) + context.shape),...  32.4 us
    all_gather x1, waiting for transfers between devices, on_device(): pool = lax.all_gather(paired, 'y', axis=0, tiled=True)  30.5 us
    all_to_all x1, starting transfers between devices, on_device(): lax.all_to_all(jnp.concatenate([spread_w, asked], axis=1), PLANE, split_a...  12.5 us
    all_to_all x1, waiting for transfers between devices, on_device(): lax.all_to_all(jnp.concatenate([spread_w, asked], axis=1), PLANE, split_a...  12.1 us
    all_to_all x1, starting transfers between devices, on_device(): lax.all_to_all(replies.reshape(plane, sent, BLOCK, 2 * width_here), PLANE...  9.51 us
    all_to_all x1, blocking collectives, on_device(): stats = lax.all_to_all(stats, TP, split_axis=0, concat_axis=0, tiled=True)  7.83 us
    ppermute x1, starting transfers between devices, on_device(): prev = lax.ppermute(paired[tail:], SEQ, up)  7.25 us
  transfers between devices with their start and end apart: 8, of which 5 were waited for; matrix products, arithmetic and copies ran while one was open for 1% of the time, Pallas kernels for 2%

profile of v2, /device:TPU:1, one launch (start us, length us, event | category | flops | bytes accessed | tf_op | source)
XLA Modules:
  0.0 264.6 jit_solution(1060396241387115958)
XLA Ops:
  6.5 0.0 copy-start.11
  6.5 0.0 copy-start.9
  6.5 0.0 all-gather.3.cloned.1.call-start
  6.5 1.0 constant_dynamic-update-slice_fusion.1
  7.6 1.0 constant_dynamic-update-slice_fusion
  8.5 0.0 copy-start.6
  8.5 0.8 copy-done.6
  9.4 0.0 all-gather.3.cloned.1.call-update
  9.4 0.0 copy-done.11
  9.4 4.6 %collective-permute-start.2 = (bf16[64,512]{1,0:T(8,128)(2,1)S(1)}, bf16[64,512]{1,0:T(8,128)(2,1)S(1)}, u32[]{:S(2)}, u32[]{:S(2)}) collective-permute-start(bf16[64,512]{1,0:T(8,128)(2,1)S(1)} %bitcast.25), channel_id=1, source_target_pairs={{0,0},{1,64},{2,128},{3,192},{4,256},{5,320},{6,384},{7,448},{8,8}... | collective-permute-start | bytes 196616 | tf_op jit(solution)/shard_map/ppermute | solution.py:244
  14.0 0.0 copy-done.9
  14.0 0.1 copy.30
  14.1 0.1 reshape.165
  14.2 0.0 copy-done.10
  14.2 0.1 copy.31
  14.3 0.1 broadcast_in_dim.23
  14.4 0.2 convert_reduce_fusion
  14.6 0.2 select_reduce_fusion
  14.8 1.1 collective-permute-done.2
  16.0 0.0 copy-start.12
  16.0 0.9 fusion.1
  16.9 12.5 %all-to-all-start = ((bf16[8,72,512]{2,1,0:T(8,128)(2,1)}), bf16[8,72,512]{2,1,0:T(8,128)(2,1)S(1)}, u32[]{:S(2)}, u32[]{:S(2)}) async-start(bf16[8,72,512]{2,1,0:T(8,128)(2,1)} %fusion.1), calls=%async_computation | async-start | bytes 1179648 | tf_op jit(solution)/shard_map/all_to_all | solution.py:263
  29.3 0.0 copy-done.12
  29.4 0.1 pad.6.clone
  29.4 12.1 %all-to-all-done = bf16[8,72,512]{2,1,0:T(8,128)(2,1)S(1)} async-done(((bf16[8,72,512]{2,1,0:T(8,128)(2,1)}), bf16[8,72,512]{2,1,0:T(8,128)(2,1)S(1)}, u32[]{:S(2)}, u32[]{:S(2)}) %all-to-all-start) | async-done | bytes 589856 | tf_op jit(solution)/shard_map/all_to_all | solution.py:263
  41.5 0.1 reshape.166.want_ref
  41.6 30.5 %all-gather.3.cloned.1.call-done.pool_ref = bf16[2048,1024]{1,0:T(8,128)(2,1)} async-done(((bf16[256,1024]{1,0:T(8,128)(2,1)}), bf16[2048,1024]{1,0:T(8,128)(2,1)}) %all-gather.3.cloned.1.call-update) | async-done | bytes 4194320 | tf_op jit(solution)/shard_map/all_gather | solution.py:236
  72.2 0.0 copy-start
  72.2 2.2 copy-done
  74.4 3.1 %pack.1 = bf16[144,16,1024]{2,1,0:T(8,128)(2,1)} custom-call(s32[144]{0:T(256)S(1)} %reshape.166.want_ref, bf16[2048,1024]{1,0:T(8,128)(2,1)S(1)} %copy-done), custom_call_target="tpu_custom_call" | custom-call | bytes 9437184 | tf_op jit(solution)/shard_map/pack/pallas_call | solution.py:42
  77.5 9.5 %all-to-all-start.1 = ((bf16[8,18,16,1024]{3,2,1,0:T(8,128)(2,1)}), bf16[8,18,16,1024]{3,2,1,0:T(8,128)(2,1)}, u32[]{:S(2)}, u32[]{:S(2)}) async-start(bf16[8,18,16,1024]{3,2,1,0:T(8,128)(2,1)} %bitcast.22), calls=%async_computation.1 | async-start | bytes 9437184 | tf_op jit(solution)/shard_map/all_to_all | solution.py:284
  87.0 0.0 copy-start.1
  87.0 0.0 copy-start.2
  87.0 0.0 copy-start.3
  87.0 0.0 all-gather.5.cloned.1.call-start
  87.1 0.8 slice.31
  87.9 0.0 all-gather.5.cloned.1.call-update
  88.0 0.8 fusion.10
  88.7 7.2 %collective-permute-start = (bf16[16,1024]{1,0:T(8,128)(2,1)S(1)}, bf16[16,1024]{1,0:T(8,128)(2,1)S(1)}, u32[]{:S(2)}, u32[]{:S(2)}) collective-permute-start(bf16[16,1024]{1,0:T(8,128)(2,1)S(1)} %get-tuple-element.17), channel_id=1, source_target_pairs={{0,8},{8,16},{16,24},{24,32},{32,40},{40,48},{48,56},{56,64},{64,7... | collective-permute-start | bytes 98312 | tf_op jit(solution)/shard_map/ppermute | solution.py:295
  96.0 6.1 %collective-permute-start.1 = (bf16[16,1024]{1,0:T(8,128)(2,1)S(1)}, bf16[16,1024]{1,0:T(8,128)(2,1)S(1)}, u32[]{:S(2)}, u32[]{:S(2)}) collective-permute-start(bf16[16,1024]{1,0:T(8,128)(2,1)S(1)} %get-tuple-element.16), channel_id=1, source_target_pairs={{8,0},{16,8},{24,16},{32,24},{40,32},{48,40},{56,48},{64,56},{72,6... | collective-permute-start | bytes 98312 | tf_op jit(solution)/shard_map/ppermute | solution.py:296
  102.2 0.1 pad_add_fusion.2.pick_ref
  102.2 95.6 %collective-permute-done.prev_ref = bf16[16,1024]{1,0:T(8,128)(2,1)S(1)} collective-permute-done((bf16[16,1024]{1,0:T(8,128)(2,1)S(1)}, bf16[16,1024]{1,0:T(8,128)(2,1)S(1)}, u32[]{:S(2)}, u32[]{:S(2)}) %collective-permute-start) | collective-permute-done | bytes 32800 | tf_op jit(solution)/shard_map/ppermute | solution.py:295
  197.8 0.0 collective-permute-done.1.next_ref
  197.8 0.0 all-to-all-done.1
  197.8 0.0 copy-done.1
  197.8 0.0 copy-done.2
  197.8 0.0 copy-done.3
  197.9 5.2 %attend.1 = bf16[256,512]{1,0:T(8,128)(2,1)S(1)} custom-call(s32[50]{0:T(128)S(1)} %pad_add_fusion.2.pick_ref, bf16[256,512]{1,0:T(8,128)(2,1)S(1)} %copy-done.3, bf16[256,512]{1,0:T(8,128)(2,1)S(1)} %copy-done.1, bf16[256,512]{1,0:T(8,128)(2,1)S(1)} %copy-done.2, bf16[16,1024]{1,0:T(8,128)(2,1)S(1)} %collective-permute-done.prev_ref, ...), custom_call_target="tpu_custom_call" | custom-call | flops 67108864 | bytes 6291456 | tf_op jit(solution)/shard_map/attend/pallas_call | solution.py:108
  203.1 0.1 broadcast_in_dim.27
  203.2 0.0 copy-start.4
  203.2 0.0 copy-start.5
  203.2 32.4 %all_to_all.20.mine_ref = bf16[4,256,512]{2,1,0:T(8,128)(2,1)S(1)} all-to-all(bf16[4,256,512]{2,1,0:T(8,128)(2,1)S(1)} %broadcast_in_dim.27), channel_id=1, replica_groups=mesh['y'=8,'x'=4,'zh'=2,'zl'=4,'core'=2] {'zl'}, dimensions={0} | all-to-all | bytes 2097152 | tf_op jit(solution)/shard_map/all_to_all | solution.py:306
  235.5 4.0 %collective-permute-start.3 = (bf16[4,256,512]{2,1,0:T(8,128)(2,1)S(1)}, bf16[4,256,512]{2,1,0:T(8,128)(2,1)S(1)}, u32[]{:S(2)}, u32[]{:S(2)}) collective-permute-start(bf16[4,256,512]{2,1,0:T(8,128)(2,1)S(1)} %all_to_all.20.mine_ref), channel_id=1, source_target_pairs={{0,1},{1,0},{2,3},{3,2},{4,5},{5,4},{6,7},{7,6},{8,9},{9,8},{10,11... | collective-permute-start | bytes 3145736 | tf_op jit(solution)/shard_map/ppermute | solution.py:313
  240.2 0.1 pad_add_fusion.1.where_ref
  240.3 0.0 all-gather.5.cloned.1.call-done
  240.3 1.5 collective-permute-done.3.other_ref
  241.8 0.0 copy-done.4
  241.8 0.0 copy-done.5
  241.8 7.1 %project.1 = (f32[256,512]{1,0:T(8,128)S(1)}, f32[256,128]{1,0:T(8,128)S(1)}) custom-call(s32[3]{0:T(128)S(1)} %pad_add_fusion.1.where_ref, s32[16]{0:T(128)S(1)} %copy-done.5, bf16[4,256,512]{2,1,0:T(8,128)(2,1)S(1)} %all_to_all.20.mine_ref, bf16[4,256,512]{2,1,0:T(8,128)(2,1)S(1)} %collective-permute-done.3.other_ref, bf16[8,512,512]{2,1,0:T(8,128)(2,1)} %bitcast.23, ...), custom_call_target="tpu_custom_call" | custom-call | flops 1073741824 | bytes 8388608 | tf_op jit(solution)/shard_map/project/pallas_call | solution.py:185
  248.9 0.1 copy.34
  249.0 7.8 %all_to_all.21 = f32[8,2,256]{2,1,0:T(2,128)S(1)} all-to-all(f32[8,2,256]{2,1,0:T(2,128)S(1)} %broadcast_in_dim.28), channel_id=1, replica_groups=mesh['y'=8,'x'=4,'zh'=2,'zl'=4,'core'=2] {'zl','core'}, dimensions={0} | all-to-all | bytes 32768 | tf_op jit(solution)/shard_map/all_to_all | solution.py:319
  256.9 0.0 copy-done.7
  256.9 0.0 copy-done.8
  256.9 0.9 add_convert_fusion
  (21 shorter events, 0.2 us)
Async XLA Ops:
  6.5 2.9 %copy-start.11 = (bf16[512,64]{0,1:T(8,128)(2,1)S(1)}, bf16[512,64]{0,1:T(8,128)(2,1)}, u32[]{:S(2)}) copy-start(bf16[512,64]{0,1:T(8,128)(2,1)} %param.16) | copy-start | bytes 196612
  6.5 7.5 %copy-start.9 = (s32[16,3]{0,1:T(4,128)S(1)}, s32[16,3]{0,1:T(4,128)}, u32[]{:S(2)}) copy-start(s32[16,3]{0,1:T(4,128)} %param.20) | copy-start | bytes 580
  6.5 7.6 %copy-start.10 = (s32[16,3]{0,1:T(4,128)S(1)}, s32[16,3]{0,1:T(4,128)}, u32[]{:S(2)}) copy-start(s32[16,3]{0,1:T(4,128)} %param.21) | copy-start | bytes 580
  6.5 65.6 %all-gather.3.cloned.1.call-start = ((), (), s32[]{:S(2)}) async-start(), calls=%async_computation.4 | async-start | bytes 4718592 | tf_op jit(solution)/shard_map/all_gather | solution.py:236
  8.5 0.8 copy-start.6
  9.4 6.5 %collective-permute-start.2 = (bf16[64,512]{1,0:T(8,128)(2,1)S(1)}, bf16[64,512]{1,0:T(8,128)(2,1)S(1)}, u32[]{:S(2)}, u32[]{:S(2)}) collective-permute-start(bf16[64,512]{1,0:T(8,128)(2,1)S(1)} %bitcast.25), channel_id=1, source_target_pairs={{0,0},{1,64},{2,128},{3,192},{4,256},{5,320},{6,384},{7,448},{8,8}... | collective-permute-start | bytes 196616 | tf_op jit(solution)/shard_map/ppermute | solution.py:244
  16.0 13.4 %copy-start.12 = (s32[2]{0:T(128)S(1)}, s32[2]{0:T(128)}, u32[]{:S(2)}) copy-start(s32[2]{0:T(128)} %param.19) | copy-start | bytes 28
  16.9 24.7 %all-to-all-start = ((bf16[8,72,512]{2,1,0:T(8,128)(2,1)}), bf16[8,72,512]{2,1,0:T(8,128)(2,1)S(1)}, u32[]{:S(2)}, u32[]{:S(2)}) async-start(bf16[8,72,512]{2,1,0:T(8,128)(2,1)} %fusion.1), calls=%async_computation | async-start | bytes 1179648 | tf_op jit(solution)/shard_map/all_to_all | solution.py:263
  72.2 2.2 copy-start
  77.5 120.3 %all-to-all-start.1 = ((bf16[8,18,16,1024]{3,2,1,0:T(8,128)(2,1)}), bf16[8,18,16,1024]{3,2,1,0:T(8,128)(2,1)}, u32[]{:S(2)}, u32[]{:S(2)}) async-start(bf16[8,18,16,1024]{3,2,1,0:T(8,128)(2,1)} %bitcast.22), calls=%async_computation.1 | async-start | bytes 9437184 | tf_op jit(solution)/shard_map/all_to_all | solution.py:284
  87.0 110.8 %copy-start.1 = (bf16[256,512]{1,0:T(8,128)(2,1)S(1)}, bf16[256,512]{1,0:T(8,128)(2,1)}, u32[]{:S(2)}) copy-start(bf16[256,512]{1,0:T(8,128)(2,1)} %k_ref.1) | copy-start | bytes 786436
  87.0 110.8 %copy-start.2 = (bf16[256,512]{1,0:T(8,128)(2,1)S(1)}, bf16[256,512]{1,0:T(8,128)(2,1)}, u32[]{:S(2)}) copy-start(bf16[256,512]{1,0:T(8,128)(2,1)} %v_ref.1) | copy-start | bytes 786436
  87.0 110.8 %copy-start.3 = (bf16[256,512]{1,0:T(8,128)(2,1)S(1)}, bf16[256,512]{1,0:T(8,128)(2,1)}, u32[]{:S(2)}) copy-start(bf16[256,512]{1,0:T(8,128)(2,1)} %q_ref.1) | copy-start | bytes 786436
  87.0 153.2 %all-gather.5.cloned.1.call-start = ((), (), s32[]{:S(2)}) async-start(), calls=%async_computation.5 | async-start | bytes 4718592 | tf_op jit(solution)/shard_map/all_gather | solution.py:271
  88.7 109.1 %collective-permute-start = (bf16[16,1024]{1,0:T(8,128)(2,1)S(1)}, bf16[16,1024]{1,0:T(8,128)(2,1)S(1)}, u32[]{:S(2)}, u32[]{:S(2)}) collective-permute-start(bf16[16,1024]{1,0:T(8,128)(2,1)S(1)} %get-tuple-element.17), channel_id=1, source_target_pairs={{0,8},{8,16},{16,24},{24,32},{32,40},{40,48},{48,56},{56,64},{64,7... | collective-permute-start | bytes 98312 | tf_op jit(solution)/shard_map/ppermute | solution.py:295
  96.0 101.8 %collective-permute-start.1 = (bf16[16,1024]{1,0:T(8,128)(2,1)S(1)}, bf16[16,1024]{1,0:T(8,128)(2,1)S(1)}, u32[]{:S(2)}, u32[]{:S(2)}) collective-permute-start(bf16[16,1024]{1,0:T(8,128)(2,1)S(1)} %get-tuple-element.16), channel_id=1, source_target_pairs={{8,0},{16,8},{24,16},{32,24},{40,32},{48,40},{56,48},{64,56},{72,6... | collective-permute-start | bytes 98312 | tf_op jit(solution)/shard_map/ppermute | solution.py:296
  203.2 38.7 %copy-start.4 = (bf16[256,512]{1,0:T(8,128)(2,1)S(1)}, bf16[256,512]{1,0:T(8,128)(2,1)}, u32[]{:S(2)}) copy-start(bf16[256,512]{1,0:T(8,128)(2,1)} %res_ref.1) | copy-start | bytes 786436
  203.2 38.6 %copy-start.5 = (s32[16]{0:T(128)S(1)}, s32[16]{0:T(128)}, u32[]{:S(2)}) copy-start(s32[16]{0:T(128)} %drop_ref.1) | copy-start | bytes 196
  235.5 6.3 %collective-permute-start.3 = (bf16[4,256,512]{2,1,0:T(8,128)(2,1)S(1)}, bf16[4,256,512]{2,1,0:T(8,128)(2,1)S(1)}, u32[]{:S(2)}, u32[]{:S(2)}) collective-permute-start(bf16[4,256,512]{2,1,0:T(8,128)(2,1)S(1)} %all_to_all.20.mine_ref), channel_id=1, source_target_pairs={{0,1},{1,0},{2,3},{3,2},{4,5},{5,4},{6,7},{7,6},{8,9},{9,8},{10,11... | collective-permute-start | bytes 3145736 | tf_op jit(solution)/shard_map/ppermute | solution.py:313
  241.8 15.1 %copy-start.7 = (f32[512]{0:T(512)S(1)}, f32[512]{0:T(512)}, u32[]{:S(2)}) copy-start(f32[512]{0:T(512)} %param.18) | copy-start | bytes 6148
  241.8 15.1 %copy-start.8 = (f32[512]{0:T(512)S(1)}, f32[512]{0:T(512)}, u32[]{:S(2)}) copy-start(f32[512]{0:T(512)} %param.17) | copy-start | bytes 6148
Sparse Core Ops, SparseCore 0:
  9.5 62.6 all-gather.2
  90.0 56.2 all-gather.4

commit v3 on v2

v3 whole, which is shorter than its diff:
```python
import functools

import jax
import jax.numpy as jnp
from jax import lax
from jax.experimental import pallas as pl
from jax.experimental.pallas import tpu as pltpu
from jax.sharding import Mesh
from jax.sharding import PartitionSpec as P

D = 4096
DH = 128
BLOCK = 16
GLOB = 2
RAND = 3
CAP = 2
BF = jnp.bfloat16
F32 = jnp.float32
SEQ = ("y", "x", "zh")
TP = ("zl", "core")
PLANE = ("x", "zh")
PARTS = 2
STAT_ROWS = 16
NEG = -1e30
VMEM_LIMIT = 48 * 1024 * 1024


def whole(shape):
    return pl.BlockSpec(shape, lambda *a: (0,) * len(shape))


def params():
    return pltpu.CompilerParams(vmem_limit_bytes=VMEM_LIMIT)


def partial(scores, listed, values):
    scores = jnp.where(listed, scores, NEG)
    top = jnp.max(scores, axis=0, keepdims=True)
    expo = jnp.where(listed, jnp.exp(scores - top), 0.0)
    total = jnp.sum(expo, axis=0, keepdims=True)
    got = lax.dot_general(
        expo.astype(BF), values, (((0,), (0,)), ((), ())), preferred_element_type=F32
    )
    return top, total, got


def dot_t(a, b):
    return lax.dot_general(a, b, (((1,), (1,)), ((), ())), preferred_element_type=F32)


def split(x, parts):
    out = []
    for _ in range(parts):
        out.append(x.astype(BF))
        x = x - out[-1].astype(F32)
    return out


def serve_kernel(row_ref, mark_ref, zh_ref, q_ref, pool_ref, out_ref):
    peer = pl.program_id(0)
    rows = q_ref.shape[2]
    wide = q_ref.shape[3]
    listings = row_ref.shape[0] // pl.num_programs(0)
    scale = jnp.float32(1.0 / DH**0.5)
    block_of = lax.broadcasted_iota(jnp.int32, (BLOCK, rows), 1) // BLOCK
    places, listed = [], []
    for i in range(listings):
        at = peer * listings + i
        places.append(pl.ds(pl.multiple_of(row_ref[at] * BLOCK, BLOCK), BLOCK))
        mark = mark_ref[at]
        listed.append(jnp.logical_or(block_of == mark, jnp.full(block_of.shape, mark) < 0))
    listed = jnp.concatenate(listed, axis=0)
    stats = []
    for h in range(wide // DH):
        lanes = slice(h * DH, (h + 1) * DH)
        keys = jnp.concatenate([pool_ref[p, lanes] for p in places], axis=0)
        after = slice(wide + h * DH, wide + (h + 1) * DH)
        values = jnp.concatenate([pool_ref[p, after] for p in places], axis=0)
        top, total, got = partial(
            dot_t(keys, q_ref[0, 0, :, lanes]) * scale, listed, values
        )
        out_ref[0, :rows, lanes] = got.astype(BF)
        stats += split(top, 3) + split(total, 2)
    stats.append(jnp.zeros((STAT_ROWS - len(stats), rows), BF))
    out_ref[0, rows:, :] = jnp.concatenate([x.astype(F32) for x in stats], axis=0).astype(BF)


def serve(row, mark, zh, q, pool, out_rows):
    n_x, _, _, wide = q.shape
    rows = out_rows
    peers = 2 * n_x
    out = (peers, rows + STAT_ROWS, wide)
    return pl.pallas_call(
        serve_kernel,
        grid_spec=pltpu.PrefetchScalarGridSpec(
            num_scalar_prefetch=3,
            grid=(peers,),
            in_specs=[
                pl.BlockSpec((1, 1, rows, wide), lambda i, a, b, c: (i // 2, i % 2, 0, 0)),
                whole(pool.shape),
            ],
            out_specs=pl.BlockSpec(
                (1,) + out[1:], lambda i, a, b, zh_ref: (2 * (i // 2) + (i % 2 + zh_ref[0]) % 2, 0, 0)
            ),
        ),
        out_shape=jax.ShapeDtypeStruct(out, BF),
        compiler_params=params(),
        cost_estimate=pl.CostEstimate(
            flops=4 * peers * rows * 320 * wide,
            transcendentals=peers * rows * 320 * wide // DH,
            bytes_accessed=4 << 20,
        ),
        name="serve",
    )(row, mark, zh, q, pool)


def local_kernel(q_ref, k_ref, v_ref, out_ref, stat_ref):
    rows = q_ref.shape[0]
    heads = q_ref.shape[1] // DH
    scale = jnp.float32(1.0 / DH**0.5)
    key_block = lax.broadcasted_iota(jnp.int32, (rows, rows), 0) // BLOCK
    query_block = lax.broadcasted_iota(jnp.int32, (rows, rows), 1) // BLOCK
    listed = jnp.abs(key_block - query_block) <= 1
    tops, totals = [], []
    for h in range(heads):
        lanes = slice(h * DH, (h + 1) * DH)
        top, total, got = partial(
            dot_t(k_ref[:, lanes], q_ref[:, lanes]) * scale, listed, v_ref[:, lanes]
        )
        out_ref[:, lanes] = got
        tops.append(top)
        totals.append(total)
    stat_ref[...] = jnp.concatenate(tops + totals, axis=0)


def local(q, k, v):
    rows, width = q.shape
    stat = (2 * (width // DH), rows)
    return pl.pallas_call(
        local_kernel,
        grid=(1,),
        in_specs=[whole(q.shape)] * 3,
        out_specs=[whole(q.shape), whole(stat)],
        out_shape=[jax.ShapeDtypeStruct(q.shape, F32), jax.ShapeDtypeStruct(stat, F32)],
        compiler_params=params(),
        cost_estimate=pl.CostEstimate(
            flops=4 * rows * rows * width,
            transcendentals=rows * rows * width // DH,
            bytes_accessed=2 << 20,
        ),
        name="local",
    )(q, k, v)


def merge_kernel(first, got_ref, near_ref, stat_ref, out_ref):
    peers, rows, wide = got_ref.shape
    rows = rows - STAT_ROWS
    heads = wide // DH
    all_heads = stat_ref.shape[0] // 2
    weights = []
    for h in range(heads):
        tops, totals = [], []
        for s in range(peers):
            stats = got_ref[s, rows:, :].astype(F32)
            at = 5 * h
            tops.append(stats[at : at + 1] + stats[at + 1 : at + 2] + stats[at + 2 : at + 3])
            totals.append(stats[at + 3 : at + 4] + stats[at + 4 : at + 5])
        tops.append(stat_ref[first + h : first + h + 1, :])
        totals.append(stat_ref[all_heads + first + h : all_heads + first + h + 1, :])
        top = functools.reduce(jnp.maximum, tops)
        factors = [jnp.exp(t - top) for t in tops]
        total = sum(f * t for f, t in zip(factors, totals))
        weights += [f / total for f in factors]
    weights.append(jnp.zeros((DH - len(weights), rows), F32))
    weights = jnp.concatenate(weights, axis=0).T
    for h in range(heads):
        lanes = slice(h * DH, (h + 1) * DH)
        at = h * (peers + 1)
        total = weights[:, at + peers : at + peers + 1] * near_ref[:, lanes]
        for s in range(peers):
            total += weights[:, at + s : at + s + 1] * got_ref[s, :rows, lanes].astype(F32)
        out_ref[:, lanes] = total.astype(BF)


def merge(part, got, near, stat):
    peers, rows, wide = got.shape
    rows = rows - STAT_ROWS
    return pl.pallas_call(
        functools.partial(merge_kernel, part * (wide // DH)),
        grid=(1,),
        in_specs=[
            whole(got.shape),
            pl.BlockSpec((rows, wide), lambda i: (0, part)),
            whole(stat.shape),
        ],
        out_specs=whole((rows, wide)),
        out_shape=jax.ShapeDtypeStruct((rows, wide), BF),
        compiler_params=params(),
        cost_estimate=pl.CostEstimate(
            flops=2 * peers * rows * wide, transcendentals=0, bytes_accessed=2 << 20
        ),
        name="merge",
    )(got, near, stat)


def project_kernel(
    where_ref, drop_ref, mine_ref, other_ref, w_ref, res_ref, sum_ref, stat_ref, acc_ref
):
    step = pl.program_id(0)
    half = mine_ref.shape[0]
    lhs = jnp.where(step < half, 0, 1)

    @pl.when(step == 0)
    def _():
        acc_ref[...] = jnp.zeros_like(acc_ref)

    def add(ref, at):
        acc_ref[...] += lax.dot_general(
            ref[at], w_ref[0], (((1,), (1,)), ((), ())), preferred_element_type=F32
        )

    @pl.when(lhs == 0)
    def _():
        add(mine_ref, step)

    @pl.when(lhs == 1)
    def _():
        add(other_ref, step - half)

    @pl.when(step == pl.num_programs(0) - 1)
    def _():
        cols = acc_ref.shape[1]
        blocks = acc_ref.shape[0] // BLOCK
        seed = where_ref[1] * 1000003 + where_ref[2] * cols
        inner = lax.broadcasted_iota(jnp.int32, (BLOCK, cols), 0) * D
        inner = inner + lax.broadcasted_iota(jnp.int32, (BLOCK, cols), 1) + seed
        lane = lax.broadcasted_iota(jnp.int32, (BLOCK, DH), 1)
        for b in range(blocks):
            rows = slice(b * BLOCK, (b + 1) * BLOCK)
            hashed = inner + drop_ref[b]
            for _ in range(2):
                hashed = hashed ^ lax.shift_right_logical(hashed, jnp.int32(16))
                hashed = hashed * 73244475
            hashed = hashed ^ lax.shift_right_logical(hashed, jnp.int32(16))
            kept = (hashed & 1023) >= 102
            keep = jnp.where(kept, jnp.float32(1024.0 / 922.0), jnp.float32(0.0))
            total = res_ref[rows, :].astype(F32) + keep * acc_ref[rows, :]
            sum_ref[rows, :] = total
            mean = jnp.sum(total, axis=1, keepdims=True) * jnp.float32(1.0 / cols)
            dev = total - mean
            spread = jnp.sum(dev * dev, axis=1, keepdims=True)
            stat_ref[rows, :] = jnp.where(lane == 0, mean, spread)


def project(where, drops, mine, other, weight, residual):
    rows, cols = residual.shape
    half = mine.shape[0]
    steps = 2 * half

    def w_map(i, where_ref, drop_ref):
        core = where_ref[0]
        own = 2 * i + core
        far = 2 * (i - half) + (1 - core)
        return (jnp.where(i < half, own, far), 0, 0)

    return pl.pallas_call(
        project_kernel,
        grid_spec=pltpu.PrefetchScalarGridSpec(
            num_scalar_prefetch=2,
            grid=(steps,),
            in_specs=[
                whole(mine.shape),
                whole(other.shape),
                pl.BlockSpec((1,) + weight.shape[1:], w_map),
                whole(residual.shape),
            ],
            out_specs=[whole((rows, cols)), whole((rows, DH))],
            scratch_shapes=[pltpu.VMEM((rows, cols), F32)],
        ),
        out_shape=[
            jax.ShapeDtypeStruct((rows, cols), F32),
            jax.ShapeDtypeStruct((rows, DH), F32),
        ],
        compiler_params=params(),
        cost_estimate=pl.CostEstimate(
            flops=2 * rows * D * cols, transcendentals=0, bytes_accessed=8 << 20
        ),
        name="project",
    )(where, drops, mine, other, weight, residual)


def on_device(
    queries,
    key_rows,
    value_rows,
    residual,
    out_weight,
    norm_gain,
    norm_bias,
    global_list,
    random_device,
    random_offset,
    drop_seed,
    drop_offsets,
):
    row_count, width_here = queries.shape
    block_count = row_count // BLOCK
    n_y, n_x, n_zh = (lax.axis_size(a) for a in SEQ)
    plane = n_x * n_zh
    seq_count = n_y * plane
    n_zl = lax.axis_size("zl")
    tp_count = n_zl * lax.axis_size("core")
    tp_at = lax.axis_index(TP)
    cols_here = out_weight.shape[1]

    plane_at = lax.axis_index(PLANE)
    y_at = lax.axis_index("y")
    zh_at = lax.axis_index("zh")
    wide = width_here // PARTS

    def cut(x, part):
        return x[:, part * wide : (part + 1) * wide]

    pools = []
    for part in range(PARTS):
        paired = jnp.concatenate([cut(key_rows, part), cut(value_rows, part)], axis=1)
        pools.append(lax.all_gather(paired, "y", axis=0, tiled=True))

    def moves(flip):
        return [
            ((y * plane + p) * tp_count + t, (t * plane + (p ^ flip)) * tp_count + y)
            for y in range(n_y)
            for p in range(plane)
            for t in range(tp_count)
        ]

    same_zh = lax.ppermute(out_weight.T, SEQ + TP, moves(0))
    other_zh = lax.ppermute(out_weight.T, SEQ + TP, moves(1))
    shards = jnp.concatenate(
        [
            jnp.where(zh_at == 0, same_zh, other_zh),
            jnp.where(zh_at == 0, other_zh, same_zh),
        ],
        axis=0,
    )
    shards = jnp.concatenate([shards[:, :wide], shards[:, wide:]], axis=0)

    request_count = block_count * RAND
    target = random_device.reshape(request_count)
    wanted = random_offset.reshape(request_count)
    rank = jnp.arange(request_count, dtype=jnp.int32)
    same = target[:, None] == target[None, :]
    earlier = rank[None, :] < rank[:, None]
    slot = jnp.sum(jnp.logical_and(same, earlier), axis=1).astype(jnp.int32)
    slots = n_y * CAP
    place = (target // plane) * CAP + slot
    column = target % plane
    entry = column * (2 * slots) + place
    cells = jnp.arange(plane * 2 * slots, dtype=jnp.int32)
    is_offset = entry[:, None] == cells[None, :]
    is_asker = entry[:, None] + slots == cells[None, :]
    asker = rank // RAND + 1
    table = jnp.sum(
        jnp.where(is_offset, wanted[:, None], jnp.where(is_asker, asker[:, None], 0)), axis=0
    )
    table = jnp.pad(table.astype(BF)[None], ((0, 7), (0, 0)))

    flip = [(0, 1), (1, 0)]
    asked = []
    for part in range(PARTS):
        mine = cut(queries, part)
        if part == 0:
            mine = jnp.concatenate([mine, table], axis=0)
        both = jnp.stack([mine, lax.ppermute(mine, "zh", flip)])
        if part == PARTS - 1:
            both = jnp.concatenate([both, shards[None]], axis=0)
        both = jnp.broadcast_to(both[None], (n_x,) + both.shape)
        asked.append(lax.all_to_all(both, "x", split_axis=0, concat_axis=0, tiled=True))
    shards = asked[-1][:, 2]
    shards = jnp.concatenate(
        [shards[:, : shards.shape[1] // 2], shards[:, shards.shape[1] // 2 :]], axis=2
    )
    weight = lax.all_gather(
        shards.reshape(plane * cols_here, width_here), "y", axis=0, tiled=True
    )
    weight = weight.reshape(tp_count, plane * cols_here, width_here)

    lists = asked[0][:, :, row_count].reshape(plane, plane, 2 * slots)
    lists = lax.dynamic_index_in_dim(lists, plane_at, 1, keepdims=False).astype(jnp.int32)
    base = (jnp.arange(slots, dtype=jnp.int32) // CAP) * block_count
    order = jnp.arange(plane, dtype=jnp.int32)
    peer = jnp.bitwise_xor(order, zh_at)
    nothing = jnp.int32(block_count)
    owner = global_list // block_count
    glob_row = (owner // plane) * block_count + global_list % block_count
    glob_mark = jnp.where(owner % plane == plane_at, -1, nothing)
    here = y_at * plane + peer
    low = (here + seq_count - 1) % seq_count
    high = (here + 1) % seq_count
    low_row = (low // plane) * block_count + block_count - 1
    high_row = (high // plane) * block_count
    low_mark = jnp.where(low % plane == plane_at, 0, nothing)
    high_mark = jnp.where(high % plane == plane_at, block_count - 1, nothing)
    marks = lists[:, slots:] - 1
    row = jnp.concatenate(
        [
            lists[:, :slots] + base[None],
            jnp.broadcast_to(glob_row[None], (plane, GLOB)),
            low_row[:, None],
            high_row[:, None],
        ],
        axis=1,
    ).reshape(-1)
    mark = jnp.concatenate(
        [
            jnp.where(marks < 0, nothing, marks),
            jnp.broadcast_to(glob_mark[None], (plane, GLOB)),
            low_mark[:, None],
            high_mark[:, None],
        ],
        axis=1,
    ).reshape(-1)
    zh = zh_at[None].astype(jnp.int32)

    near, stat = local(queries, key_rows, value_rows)
    context = []
    for part in range(PARTS):
        partials = serve(row, mark, zh, asked[part], pools[part], row_count)
        got = lax.all_to_all(partials, PLANE, split_axis=0, concat_axis=0, tiled=True)
        context.append(merge(part, got, near, stat))
    context = jnp.concatenate(context, axis=1)

    mine = lax.all_to_all(
        jnp.broadcast_to(context[None], (n_zl,) + context.shape),
        "zl",
        split_axis=0,
        concat_axis=0,
        tiled=True,
    )
    other = lax.ppermute(mine, "core", [(0, 1), (1, 0)])

    where = jnp.stack([tp_at % 2, drop_seed[0], tp_at]).astype(jnp.int32)
    summed, stats = project(where, drop_offsets, mine, other, weight, residual)

    stats = jnp.broadcast_to(stats[:, :2].T[None], (tp_count, 2, row_count))
    stats = lax.all_to_all(stats, TP, split_axis=0, concat_axis=0, tiled=True)
    means, spreads = stats[:, 0], stats[:, 1]
    mean = jnp.sum(means, axis=0) / tp_count
    away = means - mean[None]
    cols = summed.shape[1]
    spread = jnp.sum(spreads, axis=0) + cols * jnp.sum(away * away, axis=0)
    factor = lax.rsqrt(spread / D + 1e-05)
    encoded = (summed - mean[:, None]) * factor[:, None] * norm_gain[None] + norm_bias[None]
    return encoded.astype(BF)


def solution(mesh):
    fine = Mesh(mesh.devices.reshape(8, 4, 2, 4, 2), SEQ + TP)
    placed = (
        P(SEQ, TP),
        P(SEQ, TP),
        P(SEQ, TP),
        P(SEQ, TP),
        P(TP, SEQ),
        P(TP),
        P(TP),
        P(),
        P(SEQ, None),
        P(SEQ, None),
        P(),
        P(SEQ),
    )
    return jax.shard_map(
        on_device, mesh=fine, in_specs=placed, out_specs=P(SEQ, TP), check_vma=False
    )
```

time: 265 us -> 218 us (0.82)
  waiting for transfers between devices: 141 us -> 57.7 us
  blocking collectives: 40.2 us -> 55.7 us
  starting transfers between devices: 44 us -> 52.6 us
  Pallas kernels: 15.4 us -> 22 us
  local copies, waits for them, and re-layouts: 7.39 us -> 10.9 us
    ppermute x3 -> x4, waiting for transfers between devices: 96.7 us -> 11.5 us  [the longest x2 8.94 us: on_device(): both = jnp.stack([mine, lax.ppermute(mine, 'zh', flip)])]
    all_to_all x2 -> x4, waiting for transfers between devices: 12.1 us -> 33.2 us  [the longest x2 20.8 us: on_device(): lax.all_to_all(both, 'x', split_axis=0, concat_axis=0, tiled=True)]
    all_gather x2 -> x3, waiting for transfers between devices: 30.5 us -> 11.4 us  [the longest x2 11.4 us: on_device(): pools.append(lax.all_gather(paired, 'y', axis=0, tiled=True))]
    all_to_all x1, blocking collectives: 32.4 us -> 47.9 us  [on_device(): lax.all_to_all(jnp.broadcast_to(context[None], (n_zl,) + context.shape),...]
    ppermute x3 -> x4, starting transfers between devices: 18 us -> 28 us  [the longest x2 13.7 us: on_device(): both = jnp.stack([mine, lax.ppermute(mine, 'zh', flip)])]
    pallas_call x2 -> x5, Pallas kernels: 8.34 us -> 14.9 us  [the longest x2 12.2 us: serve(): pl.pallas_call(serve_kernel, grid_spec=pltpu.PrefetchScalarGridSpec(num_s...]
    unnamed x30 -> x32, local copies, waits for them, and re-layouts: 4.23 us -> 6.38 us
    all_to_all x2 -> x4, starting transfers between devices: 22 us -> 21.2 us  [the longest x2 13 us: on_device(): lax.all_to_all(partials, PLANE, split_axis=0, concat_axis=0, tiled=True)]
  transfers between devices with their start and end apart: 8 -> 12, of which waited for: 5 -> 7; matrix products, arithmetic and copies ran while one was open for 1% -> 3% of each run, Pallas kernels for 2% -> 7%
where the time goes in v3:
time: 218 us; the launch traced here: 217 us
  waiting for transfers between devices  57.7 us (26%)
  blocking collectives  55.7 us (26%)
  starting transfers between devices  52.6 us (24%)
  Pallas kernels  22 us (10%)
  between operations  14.1 us (6%)
  local copies, waits for them, and re-layouts  10.9 us (5%)
  other arithmetic  4.15 us (2%)
    all_to_all x1, blocking collectives, on_device(): lax.all_to_all(jnp.broadcast_to(context[None], (n_zl,) + context.shape),...  47.9 us
    all_to_all x2, waiting for transfers between devices, on_device(): lax.all_to_all(both, 'x', split_axis=0, concat_axis=0, tiled=True)  20.8 us
    ppermute x2, starting transfers between devices, on_device(): both = jnp.stack([mine, lax.ppermute(mine, 'zh', flip)])  13.7 us
    all_to_all x2, starting transfers between devices, on_device(): lax.all_to_all(partials, PLANE, split_axis=0, concat_axis=0, tiled=True)  13 us
    all_to_all x2, waiting for transfers between devices, on_device(): lax.all_to_all(partials, PLANE, split_axis=0, concat_axis=0, tiled=True)  12.4 us
    pallas_call x2, Pallas kernels, serve(): pl.pallas_call(serve_kernel, grid_spec=pltpu.PrefetchScalarGridSpec(num_s...  12.2 us
    all_gather x2, waiting for transfers between devices, on_device(): pools.append(lax.all_gather(paired, 'y', axis=0, tiled=True))  11.4 us
    ppermute x1, starting transfers between devices, on_device(): other_zh = lax.ppermute(out_weight.T, SEQ + TP, moves(1))  9.8 us
  transfers between devices with their start and end apart: 12, of which 7 were waited for; matrix products, arithmetic and copies ran while one was open for 3% of the time, Pallas kernels for 7%

profile of v3, /device:TPU:1, one launch (start us, length us, event | category | flops | bytes accessed | tf_op | source)
XLA Modules:
  0.0 217.1 jit_solution(2249717489757335228)
XLA Ops:
  6.5 1.2 fusion.29
  7.7 0.7 pad_maximum_fusion.3
  8.4 0.0 all-gather.4.cloned.1.call-update
  8.5 0.0 all-gather.6.cloned.1.call-start
  8.5 0.7 pad_maximum_fusion.4
  9.2 0.0 all-gather.6.cloned.1.call-update
  9.3 0.1 copy.22
  9.4 0.1 reshape.386
  9.5 0.1 copy.23
  9.5 0.1 broadcast_in_dim.52
  9.6 0.2 convert_reduce_fusion
  9.8 0.1 select_reduce_fusion
  10.0 11.5 %collective-permute-start = (bf16[264,256]{1,0:T(8,128)(2,1)S(1)}, bf16[264,256]{1,0:T(8,128)(2,1)S(1)}, u32[]{:S(2)}, u32[]{:S(2)}) collective-permute-start(bf16[264,256]{1,0:T(8,128)(2,1)S(1)} %get-tuple-element.29), channel_id=1, source_target_pairs={{0,8},{8,0},{1,9},{9,1},{2,10},{10,2},{3,11},{11,3},{4,12},{12,4},... | collective-permute-start | bytes 405512 | tf_op jit(solution)/shard_map/ppermute | solution.py:374
  21.5 3.9 %collective-permute-done = bf16[264,256]{1,0:T(8,128)(2,1)S(1)} collective-permute-done((bf16[264,256]{1,0:T(8,128)(2,1)S(1)}, bf16[264,256]{1,0:T(8,128)(2,1)S(1)}, u32[]{:S(2)}, u32[]{:S(2)}) %collective-permute-start) | collective-permute-done | bytes 135200 | tf_op jit(solution)/shard_map/ppermute | solution.py:374
  25.5 1.1 broadcast_in_dim.56
  26.6 3.7 %all-to-all-start = ((bf16[4,2,264,256]{3,2,1,0:T(8,128)(2,1)}), bf16[4,2,264,256]{3,2,1,0:T(8,128)(2,1)S(1)}, u32[]{:S(2)}, u32[]{:S(2)}) async-start(bf16[4,2,264,256]{3,2,1,0:T(8,128)(2,1)} %broadcast_in_dim.56), calls=%async_computation | async-start | bytes 2162688 | tf_op jit(solution)/shard_map/all_to_all | solution.py:378
  30.3 4.5 %collective-permute-start.2 = (bf16[64,512]{1,0:T(8,128)(2,1)S(1)}, bf16[64,512]{1,0:T(8,128)(2,1)S(1)}, u32[]{:S(2)}, u32[]{:S(2)}) collective-permute-start(bf16[64,512]{1,0:T(8,128)(2,1)S(1)} %bitcast.30), channel_id=1, source_target_pairs={{0,0},{1,64},{2,128},{3,192},{4,256},{5,320},{6,384},{7,448},{8,8}... | collective-permute-start | bytes 196616 | tf_op jit(solution)/shard_map/ppermute | solution.py:337
  34.8 9.8 %collective-permute-start.3 = (bf16[64,512]{1,0:T(8,128)(2,1)S(1)}, bf16[64,512]{1,0:T(8,128)(2,1)S(1)}, u32[]{:S(2)}, u32[]{:S(2)}) collective-permute-start(bf16[64,512]{1,0:T(8,128)(2,1)S(1)} %bitcast.31), channel_id=1, source_target_pairs={{0,8},{1,72},{2,136},{3,200},{4,264},{5,328},{6,392},{7,456},{8,0}... | collective-permute-start | bytes 196616 | tf_op jit(solution)/shard_map/ppermute | solution.py:338
  44.6 2.2 %collective-permute-start.1 = (bf16[256,256]{1,0:T(8,128)(2,1)S(1)}, bf16[256,256]{1,0:T(8,128)(2,1)S(1)}, u32[]{:S(2)}, u32[]{:S(2)}) collective-permute-start(bf16[256,256]{1,0:T(8,128)(2,1)S(1)} %get-tuple-element.27), channel_id=1, source_target_pairs={{0,8},{8,0},{1,9},{9,1},{2,10},{10,2},{3,11},{11,3},{4,12},{12,4},... | collective-permute-start | bytes 393224 | tf_op jit(solution)/shard_map/ppermute | solution.py:374
  46.8 0.0 collective-permute-done.2
  46.8 2.5 %collective-permute-done.3 = bf16[64,512]{1,0:T(8,128)(2,1)S(1)} collective-permute-done((bf16[64,512]{1,0:T(8,128)(2,1)S(1)}, bf16[64,512]{1,0:T(8,128)(2,1)S(1)}, u32[]{:S(2)}, u32[]{:S(2)}) %collective-permute-start.3) | collective-permute-done | bytes 65568 | tf_op jit(solution)/shard_map/ppermute | solution.py:338
  49.4 5.0 %collective-permute-done.1 = bf16[256,256]{1,0:T(8,128)(2,1)S(1)} collective-permute-done((bf16[256,256]{1,0:T(8,128)(2,1)S(1)}, bf16[256,256]{1,0:T(8,128)(2,1)S(1)}, u32[]{:S(2)}, u32[]{:S(2)}) %collective-permute-start.1) | collective-permute-done | bytes 131104 | tf_op jit(solution)/shard_map/ppermute | solution.py:374
  54.4 0.0 all-to-all-done.q_ref
  54.5 1.3 broadcast_in_dim.62
  55.8 4.6 %all-to-all-start.2 = ((bf16[4,3,256,256]{3,2,1,0:T(8,128)(2,1)}), bf16[4,3,256,256]{3,2,1,0:T(8,128)(2,1)S(1)}, u32[]{:S(2)}, u32[]{:S(2)}) async-start(bf16[4,3,256,256]{3,2,1,0:T(8,128)(2,1)} %broadcast_in_dim.62), calls=%async_computation.2 | async-start | bytes 3145728 | tf_op jit(solution)/shard_map/all_to_all | solution.py:378
  60.4 0.1 pad.21.clone
  60.5 0.1 pad.25.clone
  60.6 0.1 reshape_squeeze.3
  60.7 20.8 %all-to-all-done.2.q_ref = bf16[4,3,256,256]{3,2,1,0:T(8,128)(2,1)S(1)} async-done(((bf16[4,3,256,256]{3,2,1,0:T(8,128)(2,1)}), bf16[4,3,256,256]{3,2,1,0:T(8,128)(2,1)S(1)}, u32[]{:S(2)}, u32[]{:S(2)}) %all-to-all-start.2) | async-done | bytes 1572896 | tf_op jit(solution)/shard_map/all_to_all | solution.py:378
  81.6 0.9 pad_maximum_fusion
  82.5 0.0 all-gather.8.cloned.1.call-update
  82.6 0.1 compare_select_fusion
  82.6 0.1 pad_add_fusion.1
  82.7 0.1 reshape.388.mark_ref
  82.8 0.1 pad_add_fusion
  82.9 0.1 reshape.387.row_ref
  83.0 1.6 copy-done.2
  84.6 6.1 %serve.2 = bf16[8,272,256]{2,1,0:T(8,128)(2,1)S(1)} custom-call(s32[160]{0:T(256)S(1)} %reshape.387.row_ref, s32[160]{0:T(256)S(1)} %reshape.388.mark_ref, s32[1]{0:T(128)} %bitcast.5.zh_ref, bf16[4,2,264,256]{3,2,1,0:T(8,128)(2,1)S(1)} %all-to-all-done.q_ref, bf16[2048,512]{1,0:T(8,128)(2,1)S(1)} %copy-done.2), custom_call_target="tpu_custom_call" | custom-call | flops 671088640 | bytes 4194304 | tf_op jit(solution)/shard_map/serve/pallas_call | solution.py:93
  90.7 1.0 copy-done.1
  91.6 3.6 %all-to-all-start.1 = ((bf16[8,272,256]{2,1,0:T(8,128)(2,1)}), bf16[8,272,256]{2,1,0:T(8,128)(2,1)S(1)}, u32[]{:S(2)}, u32[]{:S(2)}) async-start(bf16[8,272,256]{2,1,0:T(8,128)(2,1)} %copy-done.1), calls=%async_computation.1 | async-start | bytes 2228224 | tf_op jit(solution)/shard_map/all_to_all | solution.py:429
  95.2 11.4 %all-gather.6.cloned.1.call-done.pool_ref = bf16[2048,512]{1,0:T(8,128)(2,1)} async-done(((bf16[256,512]{1,0:T(8,128)(2,1)}), bf16[2048,512]{1,0:T(8,128)(2,1)}) %all-gather.6.cloned.1.call-update) | async-done | bytes 2097168 | tf_op jit(solution)/shard_map/all_gather | solution.py:327
  106.6 1.6 copy-done.3
  108.2 6.1 %serve.3 = bf16[8,272,256]{2,1,0:T(8,128)(2,1)S(1)} custom-call(s32[160]{0:T(256)S(1)} %reshape.387.row_ref, s32[160]{0:T(256)S(1)} %reshape.388.mark_ref, s32[1]{0:T(128)} %bitcast.5.zh_ref, bf16[4,3,256,256]{3,2,1,0:T(8,128)(2,1)S(1)} %all-to-all-done.2.q_ref, bf16[2048,512]{1,0:T(8,128)(2,1)S(1)} %copy-done.3), custom_call_target="tpu_custom_call" | custom-call | flops 671088640 | bytes 4194304 | tf_op jit(solution)/shard_map/serve/pallas_call | solution.py:93
  114.3 1.0 copy-done
  115.3 0.0 all-to-all-done.1.got_ref
  115.3 9.4 %all-to-all-start.3 = ((bf16[8,272,256]{2,1,0:T(8,128)(2,1)}), bf16[8,272,256]{2,1,0:T(8,128)(2,1)S(1)}, u32[]{:S(2)}, u32[]{:S(2)}) async-start(bf16[8,272,256]{2,1,0:T(8,128)(2,1)} %copy-done), calls=%async_computation.3 | async-start | bytes 2228224 | tf_op jit(solution)/shard_map/all_to_all | solution.py:429
  124.8 0.0 copy-start.6
  124.8 1.0 copy-done.6
  125.8 1.0 local.1
  126.8 0.9 merge.2
  127.7 12.4 %all-to-all-done.3.got_ref = bf16[8,272,256]{2,1,0:T(8,128)(2,1)S(1)} async-done(((bf16[8,272,256]{2,1,0:T(8,128)(2,1)}), bf16[8,272,256]{2,1,0:T(8,128)(2,1)S(1)}, u32[]{:S(2)}, u32[]{:S(2)}) %all-to-all-start.3) | async-done | bytes 1114144 | tf_op jit(solution)/shard_map/all_to_all | solution.py:429
  140.1 0.9 merge.3
  141.0 0.1 broadcast_in_dim.63
  141.1 0.0 copy-start.7
  141.1 0.0 copy-start.8
  141.1 47.9 %all_to_all.30.mine_ref = bf16[4,256,512]{2,1,0:T(8,128)(2,1)S(1)} all-to-all(bf16[4,256,512]{2,1,0:T(8,128)(2,1)S(1)} %broadcast_in_dim.63), channel_id=1, replica_groups=mesh['y'=8,'x'=4,'zh'=2,'zl'=4,'core'=2] {'zl'}, dimensions={0} | all-to-all | bytes 2097152 | tf_op jit(solution)/shard_map/all_to_all | solution.py:433
  189.0 3.3 %collective-permute-start.4 = (bf16[4,256,512]{2,1,0:T(8,128)(2,1)S(1)}, bf16[4,256,512]{2,1,0:T(8,128)(2,1)S(1)}, u32[]{:S(2)}, u32[]{:S(2)}) collective-permute-start(bf16[4,256,512]{2,1,0:T(8,128)(2,1)S(1)} %all_to_all.30.mine_ref), channel_id=1, source_target_pairs={{0,1},{1,0},{2,3},{3,2},{4,5},{5,4},{6,7},{7,6},{8,9},{9,8},{10,11... | collective-permute-start | bytes 3145736 | tf_op jit(solution)/shard_map/ppermute | solution.py:440
  193.0 0.1 pad_add_fusion.2.where_ref
  193.1 1.5 collective-permute-done.4.other_ref
  194.6 0.0 copy-start.10
  194.6 7.1 %project.1 = (f32[256,512]{1,0:T(8,128)S(1)}, f32[256,128]{1,0:T(8,128)S(1)}) custom-call(s32[3]{0:T(128)S(1)} %pad_add_fusion.2.where_ref, s32[16]{0:T(128)S(1)} %copy-done.8, bf16[4,256,512]{2,1,0:T(8,128)(2,1)S(1)} %all_to_all.30.mine_ref, bf16[4,256,512]{2,1,0:T(8,128)(2,1)S(1)} %collective-permute-done.4.other_ref, bf16[8,512,512]{2,1,0:T(8,128)(2,1)} %bitcast.25, ...), custom_call_target="tpu_custom_call" | custom-call | flops 1073741824 | bytes 8388608 | tf_op jit(solution)/shard_map/project/pallas_call | solution.py:266
  201.7 0.1 copy.24
  201.8 7.8 %all_to_all.31 = f32[8,2,256]{2,1,0:T(2,128)S(1)} all-to-all(f32[8,2,256]{2,1,0:T(2,128)S(1)} %broadcast_in_dim.64), channel_id=1, replica_groups=mesh['y'=8,'x'=4,'zh'=2,'zl'=4,'core'=2] {'zl','core'}, dimensions={0} | all-to-all | bytes 32768 | tf_op jit(solution)/shard_map/all_to_all | solution.py:446
  209.7 0.9 add_convert_fusion
  (51 shorter events, 0.5 us)
Async XLA Ops:
  6.5 2.7 %copy-start.11 = (s32[16,3]{0,1:T(4,128)S(1)}, s32[16,3]{0,1:T(4,128)}, u32[]{:S(2)}) copy-start(s32[16,3]{0,1:T(4,128)} %param.20) | copy-start | bytes 580
  6.5 2.9 %copy-start.12 = (s32[16,3]{0,1:T(4,128)S(1)}, s32[16,3]{0,1:T(4,128)}, u32[]{:S(2)}) copy-start(s32[16,3]{0,1:T(4,128)} %param.21) | copy-start | bytes 580
  6.5 3.4 %copy-start.4 = (bf16[256,512]{1,0:T(8,128)(2,1)S(1)}, bf16[256,512]{1,0:T(8,128)(2,1)}, u32[]{:S(2)}) copy-start(bf16[256,512]{1,0:T(8,128)(2,1)} %q_ref.1) | copy-start | bytes 786436
  6.5 76.4 %all-gather.4.cloned.1.call-start = ((), (), s32[]{:S(2)}) async-start(), calls=%async_computation.6 | async-start | bytes 2359296 | tf_op jit(solution)/shard_map/all_gather | solution.py:327
  8.5 98.1 %all-gather.6.cloned.1.call-start = ((), (), s32[]{:S(2)}) async-start(), calls=%async_computation.7 | async-start | bytes 2359296 | tf_op jit(solution)/shard_map/all_gather | solution.py:327
  10.0 15.4 %collective-permute-start = (bf16[264,256]{1,0:T(8,128)(2,1)S(1)}, bf16[264,256]{1,0:T(8,128)(2,1)S(1)}, u32[]{:S(2)}, u32[]{:S(2)}) collective-permute-start(bf16[264,256]{1,0:T(8,128)(2,1)S(1)} %get-tuple-element.29), channel_id=1, source_target_pairs={{0,8},{8,0},{1,9},{9,1},{2,10},{10,2},{3,11},{11,3},{4,12},{12,4},... | collective-permute-start | bytes 405512 | tf_op jit(solution)/shard_map/ppermute | solution.py:374
  26.6 3.7 %copy-start.14 = (bf16[512,64]{0,1:T(8,128)(2,1)S(1)}, bf16[512,64]{0,1:T(8,128)(2,1)}, u32[]{:S(2)}) copy-start(bf16[512,64]{0,1:T(8,128)(2,1)} %param.16) | copy-start | bytes 196612
  26.6 27.9 %all-to-all-start = ((bf16[4,2,264,256]{3,2,1,0:T(8,128)(2,1)}), bf16[4,2,264,256]{3,2,1,0:T(8,128)(2,1)S(1)}, u32[]{:S(2)}, u32[]{:S(2)}) async-start(bf16[4,2,264,256]{3,2,1,0:T(8,128)(2,1)} %broadcast_in_dim.56), calls=%async_computation | async-start | bytes 2162688 | tf_op jit(solution)/shard_map/all_to_all | solution.py:378
  30.3 16.5 %collective-permute-start.2 = (bf16[64,512]{1,0:T(8,128)(2,1)S(1)}, bf16[64,512]{1,0:T(8,128)(2,1)S(1)}, u32[]{:S(2)}, u32[]{:S(2)}) collective-permute-start(bf16[64,512]{1,0:T(8,128)(2,1)S(1)} %bitcast.30), channel_id=1, source_target_pairs={{0,0},{1,64},{2,128},{3,192},{4,256},{5,320},{6,384},{7,448},{8,8}... | collective-permute-start | bytes 196616 | tf_op jit(solution)/shard_map/ppermute | solution.py:337
  34.8 14.6 %collective-permute-start.3 = (bf16[64,512]{1,0:T(8,128)(2,1)S(1)}, bf16[64,512]{1,0:T(8,128)(2,1)S(1)}, u32[]{:S(2)}, u32[]{:S(2)}) collective-permute-start(bf16[64,512]{1,0:T(8,128)(2,1)S(1)} %bitcast.31), channel_id=1, source_target_pairs={{0,8},{1,72},{2,136},{3,200},{4,264},{5,328},{6,392},{7,456},{8,0}... | collective-permute-start | bytes 196616 | tf_op jit(solution)/shard_map/ppermute | solution.py:338
  44.6 9.8 %collective-permute-start.1 = (bf16[256,256]{1,0:T(8,128)(2,1)S(1)}, bf16[256,256]{1,0:T(8,128)(2,1)S(1)}, u32[]{:S(2)}, u32[]{:S(2)}) collective-permute-start(bf16[256,256]{1,0:T(8,128)(2,1)S(1)} %get-tuple-element.27), channel_id=1, source_target_pairs={{0,8},{8,0},{1,9},{9,1},{2,10},{10,2},{3,11},{11,3},{4,12},{12,4},... | collective-permute-start | bytes 393224 | tf_op jit(solution)/shard_map/ppermute | solution.py:374
  55.8 4.6 %copy-start.13 = (s32[2]{0:T(128)S(1)}, s32[2]{0:T(128)}, u32[]{:S(2)}) copy-start(s32[2]{0:T(128)} %param.19) | copy-start | bytes 28
  55.8 25.7 %all-to-all-start.2 = ((bf16[4,3,256,256]{3,2,1,0:T(8,128)(2,1)}), bf16[4,3,256,256]{3,2,1,0:T(8,128)(2,1)S(1)}, u32[]{:S(2)}, u32[]{:S(2)}) async-start(bf16[4,3,256,256]{3,2,1,0:T(8,128)(2,1)} %broadcast_in_dim.62), calls=%async_computation.2 | async-start | bytes 3145728 | tf_op jit(solution)/shard_map/all_to_all | solution.py:378
  60.4 134.3 %all-gather.8.cloned.1.call-start = ((), (), s32[]{:S(2)}) async-start(), calls=%async_computation.8 | async-start | bytes 4718592 | tf_op jit(solution)/shard_map/all_gather | solution.py:383
  82.9 1.6 copy-start.2
  90.7 1.0 copy-start.1
  91.6 23.7 %all-to-all-start.1 = ((bf16[8,272,256]{2,1,0:T(8,128)(2,1)}), bf16[8,272,256]{2,1,0:T(8,128)(2,1)S(1)}, u32[]{:S(2)}, u32[]{:S(2)}) async-start(bf16[8,272,256]{2,1,0:T(8,128)(2,1)} %copy-done.1), calls=%async_computation.1 | async-start | bytes 2228224 | tf_op jit(solution)/shard_map/all_to_all | solution.py:429
  106.6 1.6 copy-start.3
  114.3 1.1 copy-start
  115.3 9.4 %copy-start.5 = (bf16[256,512]{1,0:T(8,128)(2,1)S(1)}, bf16[256,512]{1,0:T(8,128)(2,1)}, u32[]{:S(2)}) copy-start(bf16[256,512]{1,0:T(8,128)(2,1)} %k_ref.1) | copy-start | bytes 786436
  115.3 24.8 %all-to-all-start.3 = ((bf16[8,272,256]{2,1,0:T(8,128)(2,1)}), bf16[8,272,256]{2,1,0:T(8,128)(2,1)S(1)}, u32[]{:S(2)}, u32[]{:S(2)}) async-start(bf16[8,272,256]{2,1,0:T(8,128)(2,1)} %copy-done), calls=%async_computation.3 | async-start | bytes 2228224 | tf_op jit(solution)/shard_map/all_to_all | solution.py:429
  124.8 1.0 copy-start.6
  141.1 53.5 %copy-start.7 = (bf16[256,512]{1,0:T(8,128)(2,1)S(1)}, bf16[256,512]{1,0:T(8,128)(2,1)}, u32[]{:S(2)}) copy-start(bf16[256,512]{1,0:T(8,128)(2,1)} %res_ref.1) | copy-start | bytes 786436
  141.1 53.5 %copy-start.8 = (s32[16]{0:T(128)S(1)}, s32[16]{0:T(128)}, u32[]{:S(2)}) copy-start(s32[16]{0:T(128)} %drop_ref.1) | copy-start | bytes 196
  189.0 5.6 %collective-permute-start.4 = (bf16[4,256,512]{2,1,0:T(8,128)(2,1)S(1)}, bf16[4,256,512]{2,1,0:T(8,128)(2,1)S(1)}, u32[]{:S(2)}, u32[]{:S(2)}) collective-permute-start(bf16[4,256,512]{2,1,0:T(8,128)(2,1)S(1)} %all_to_all.30.mine_ref), channel_id=1, source_target_pairs={{0,1},{1,0},{2,3},{3,2},{4,5},{5,4},{6,7},{7,6},{8,9},{9,8},{10,11... | collective-permute-start | bytes 3145736 | tf_op jit(solution)/shard_map/ppermute | solution.py:440
  194.6 15.1 %copy-start.9 = (f32[512]{0:T(512)S(1)}, f32[512]{0:T(512)}, u32[]{:S(2)}) copy-start(f32[512]{0:T(512)} %param.18) | copy-start | bytes 6148
  194.6 15.1 %copy-start.10 = (f32[512]{0:T(512)S(1)}, f32[512]{0:T(512)}, u32[]{:S(2)}) copy-start(f32[512]{0:T(512)} %param.17) | copy-start | bytes 6148
Sparse Core Ops, SparseCore 0:
  9.4 53.0 all-gather.3
  64.6 41.9 all-gather.5
  108.7 59.6 all-gather.7

commit v4 on v3

--- a/solution.py
+++ b/solution.py
@@ -56,7 +56,7 @@
     return out
 
 
-def serve_kernel(row_ref, mark_ref, zh_ref, q_ref, pool_ref, out_ref):
+def serve_kernel(row_ref, mark_ref, zh_ref, q_ref, key_ref, value_ref, out_ref):
     peer = pl.program_id(0)
     rows = q_ref.shape[2]
     wide = q_ref.shape[3]
@@ -73,9 +73,8 @@
     stats = []
     for h in range(wide // DH):
         lanes = slice(h * DH, (h + 1) * DH)
-        keys = jnp.concatenate([pool_ref[p, lanes] for p in places], axis=0)
-        after = slice(wide + h * DH, wide + (h + 1) * DH)
-        values = jnp.concatenate([pool_ref[p, after] for p in places], axis=0)
+        keys = jnp.concatenate([key_ref[p, lanes] for p in places], axis=0)
+        values = jnp.concatenate([value_ref[p, lanes] for p in places], axis=0)
         top, total, got = partial(
             dot_t(keys, q_ref[0, 0, :, lanes]) * scale, listed, values
         )
@@ -85,8 +84,9 @@
     out_ref[0, rows:, :] = jnp.concatenate([x.astype(F32) for x in stats], axis=0).astype(BF)
 
 
-def serve(row, mark, zh, q, pool, out_rows):
-    n_x, _, _, wide = q.shape
+def serve(part, row, mark, zh, q, pool, out_rows):
+    n_x = q.shape[0]
+    wide = q.shape[3] // PARTS
     rows = out_rows
     peers = 2 * n_x
     out = (peers, rows + STAT_ROWS, wide)
@@ -96,8 +96,9 @@
             num_scalar_prefetch=3,
             grid=(peers,),
             in_specs=[
-                pl.BlockSpec((1, 1, rows, wide), lambda i, a, b, c: (i // 2, i % 2, 0, 0)),
-                whole(pool.shape),
+                pl.BlockSpec((1, 1, rows, wide), lambda i, a, b, c: (i // 2, i % 2, 0, part)),
+                pl.BlockSpec((pool.shape[0], wide), lambda i, a, b, c: (0, part)),
+                pl.BlockSpec((pool.shape[0], wide), lambda i, a, b, c: (0, PARTS + part)),
             ],
             out_specs=pl.BlockSpec(
                 (1,) + out[1:], lambda i, a, b, zh_ref: (2 * (i // 2) + (i % 2 + zh_ref[0]) % 2, 0, 0)
@@ -111,7 +112,7 @@
             bytes_accessed=4 << 20,
         ),
         name="serve",
-    )(row, mark, zh, q, pool)
+    )(row, mark, zh, q, pool, pool)
 
 
 def local_kernel(q_ref, k_ref, v_ref, out_ref, stat_ref):
@@ -152,141 +153,220 @@
     )(q, k, v)
 
 
-def merge_kernel(first, got_ref, near_ref, stat_ref, out_ref):
-    peers, rows, wide = got_ref.shape
+def stats_of(block, rows, h):
+    stats = block[rows:, :].astype(F32)
+    at = 5 * h
+    top = stats[at : at + 1] + stats[at + 1 : at + 2] + stats[at + 2 : at + 3]
+    return top, stats[at + 3 : at + 4] + stats[at + 4 : at + 5]
+
+
+def columns(lines):
+    rows = lines[0].shape[1]
+    lines = lines + [jnp.zeros((DH - len(lines), rows), F32)]
+    return jnp.concatenate(lines, axis=0).T
+
+
+def fold_kernel(zh_ref, got_ref, out_ref):
+    peers, _, rows, wide = got_ref.shape
+    rows = rows - STAT_ROWS
+    heads = wide // DH
+    factors, stats = [], []
+    for h in range(heads):
+        pairs = [stats_of(got_ref[s, 0], rows, h) for s in range(peers)]
+        top = functools.reduce(jnp.maximum, [t for t, _ in pairs])
+        factor = [jnp.exp(t - top) for t, _ in pairs]
+        total = sum(f * l for f, (_, l) in zip(factor, pairs))
+        factors += factor
+        stats += split(top, 3) + split(total, 2)
+    stats.append(jnp.zeros((STAT_ROWS - len(stats), rows), BF))
+    out_ref[rows:, :] = jnp.concatenate([x.astype(F32) for x in stats], axis=0).astype(BF)
+    factors = columns(factors)
+    for h in range(heads):
+        lanes = slice(h * DH, (h + 1) * DH)
+        out_ref[:rows, lanes] = sum(
+            factors[:, h * peers + s : h * peers + s + 1] * got_ref[s, 0, :rows, lanes].astype(F32)
+            for s in range(peers)
+        ).astype(BF)
+
+
+def fold(zh, got):
+    peers, _, rows, wide = got.shape
+    return pl.pallas_call(
+        fold_kernel,
+        grid_spec=pltpu.PrefetchScalarGridSpec(
+            num_scalar_prefetch=1,
+            grid=(1,),
+            in_specs=[
+                pl.BlockSpec((peers, 1, rows, wide), lambda i, zh_ref: (0, 1 - zh_ref[0], 0, 0))
+            ],
+            out_specs=whole((rows, wide)),
+        ),
+        out_shape=jax.ShapeDtypeStruct((rows, wide), BF),
+        compiler_params=params(),
+        cost_estimate=pl.CostEstimate(
+            flops=2 * peers * rows * wide, transcendentals=0, bytes_accessed=1 << 20
+        ),
+        name="fold",
+    )(zh, got)
+
+
+def merge_kernel(first, zh_ref, got_ref, far_ref, near_ref, stat_ref, out_ref):
+    peers, _, rows, wide = got_ref.shape
     rows = rows - STAT_ROWS
     heads = wide // DH
     all_heads = stat_ref.shape[0] // 2
     weights = []
     for h in range(heads):
-        tops, totals = [], []
-        for s in range(peers):
-            stats = got_ref[s, rows:, :].astype(F32)
-            at = 5 * h
-            tops.append(stats[at : at + 1] + stats[at + 1 : at + 2] + stats[at + 2 : at + 3])
-            totals.append(stats[at + 3 : at + 4] + stats[at + 4 : at + 5])
-        tops.append(stat_ref[first + h : first + h + 1, :])
-        totals.append(stat_ref[all_heads + first + h : all_heads + first + h + 1, :])
-        top = functools.reduce(jnp.maximum, tops)
-        factors = [jnp.exp(t - top) for t in tops]
-        total = sum(f * t for f, t in zip(factors, totals))
+        pairs = [stats_of(got_ref[s, 0], rows, h) for s in range(peers)]
+        pairs.append(stats_of(far_ref[...], rows, h))
+        at = first + h
+        pairs.append((stat_ref[at : at + 1, :], stat_ref[all_heads + at : all_heads + at + 1, :]))
+        top = functools.reduce(jnp.maximum, [t for t, _ in pairs])
+        factors = [jnp.exp(t - top) for t, _ in pairs]
+        total = sum(f * l for f, (_, l) in zip(factors, pairs))
         weights += [f / total for f in factors]
-    weights.append(jnp.zeros((DH - len(weights), rows), F32))
-    weights = jnp.concatenate(weights, axis=0).T
+    weights = columns(weights)
     for h in range(heads):
         lanes = slice(h * DH, (h + 1) * DH)
-        at = h * (peers + 1)
-        total = weights[:, at + peers : at + peers + 1] * near_ref[:, lanes]
+        at = h * (peers + 2)
+        total = weights[:, at + peers + 1 : at + peers + 2] * near_ref[:, lanes]
+        total += weights[:, at + peers : at + peers + 1] * far_ref[:rows, lanes].astype(F32)
         for s in range(peers):
-            total += weights[:, at + s : at + s + 1] * got_ref[s, :rows, lanes].astype(F32)
+            total += weights[:, at + s : at + s + 1] * got_ref[s, 0, :rows, lanes].astype(F32)
         out_ref[:, lanes] = total.astype(BF)
 
 
-def merge(part, got, near, stat):
-    peers, rows, wide = got.shape
-    rows = rows - STAT_ROWS
+def merge(part, zh, got, far, near, stat):
+    peers, _, rows, wide = got.shape
+    out = (rows - STAT_ROWS, wide)
     return pl.pallas_call(
         functools.partial(merge_kernel, part * (wide // DH)),
-        grid=(1,),
-        in_specs=[
-            whole(got.shape),
-            pl.BlockSpec((rows, wide), lambda i: (0, part)),
-            whole(stat.shape),
-        ],
-        out_specs=whole((rows, wide)),
-        out_shape=jax.ShapeDtypeStruct((rows, wide), BF),
+        grid_spec=pltpu.PrefetchScalarGridSpec(
+            num_scalar_prefetch=1,
+            grid=(1,),
+            in_specs=[
+                pl.BlockSpec((peers, 1, rows, wide), lambda i, zh_ref: (0, zh_ref[0], 0, 0)),
+                whole(far.shape),
+                pl.BlockSpec(out, lambda i, zh_ref: (0, part)),
+                whole(stat.shape),
+            ],
+            out_specs=whole(out),
+        ),
+        out_shape=jax.ShapeDtypeStruct(out, BF),
         compiler_params=params(),
         cost_estimate=pl.CostEstimate(
-            flops=2 * peers * rows * wide, transcendentals=0, bytes_accessed=2 << 20
+            flops=2 * peers * rows * wide, transcendentals=0, bytes_accessed=1 << 20
         ),
         name="merge",
-    )(got, near, stat)
-
-
-def project_kernel(
-    where_ref, drop_ref, mine_ref, other_ref, w_ref, res_ref, sum_ref, stat_ref, acc_ref
-):
+    )(zh, got, far, near, stat)
+
+
+def keep_kernel(where_ref, drop_ref, out_ref):
+    rows, cols = out_ref.shape
+    seed = where_ref[1] * 1000003 + where_ref[2] * cols
+    inner = lax.broadcasted_iota(jnp.int32, (BLOCK, cols), 0) * D
+    inner = inner + lax.broadcasted_iota(jnp.int32, (BLOCK, cols), 1) + seed
+    for b in range(rows // BLOCK):
+        hashed = inner + drop_ref[b]
+        for _ in range(2):
+            hashed = hashed ^ lax.shift_right_logical(hashed, jnp.int32(16))
+            hashed = hashed * 73244475
+        hashed = hashed ^ lax.shift_right_logical(hashed, jnp.int32(16))
+        kept = (hashed & 1023) >= 102
+        out_ref[b * BLOCK : (b + 1) * BLOCK, :] = jnp.where(
+            kept, jnp.float32(1024.0 / 922.0), jnp.float32(0.0)
+        )
+
+
+def keep(where, drops, shape):
+    return pl.pallas_call(
+        keep_kernel,
+        grid_spec=pltpu.PrefetchScalarGridSpec(
+            num_scalar_prefetch=2, grid=(1,), in_specs=[], out_specs=whole(shape)
+        ),
+        out_shape=jax.ShapeDtypeStruct(shape, F32),
+        compiler_params=params(),
+        cost_estimate=pl.CostEstimate(
+            flops=20 * shape[0] * shape[1], transcendentals=0, bytes_accessed=1 << 19
+        ),
+        name="keep",
+    )(where, drops)
+
+
+def project_kernel(shifts, last, where_ref, *refs):
+    count = len(shifts)
+    contexts, w_ref = refs[:count], refs[count]
+    rest = refs[count + 1 :]
+    acc_ref = rest[-1]
     step = pl.program_id(0)
-    half = mine_ref.shape[0]
-    lhs = jnp.where(step < half, 0, 1)
+    half = contexts[0].shape[0]
 
     @pl.when(step == 0)
     def _():
-        acc_ref[...] = jnp.zeros_like(acc_ref)
-
-    def add(ref, at):
-        acc_ref[...] += lax.dot_general(
-            ref[at], w_ref[0], (((1,), (1,)), ((), ())), preferred_element_type=F32
-        )
-
-    @pl.when(lhs == 0)
-    def _():
-        add(mine_ref, step)
-
-    @pl.when(lhs == 1)
-    def _():
-        add(other_ref, step - half)
-
-    @pl.when(step == pl.num_programs(0) - 1)
-    def _():
-        cols = acc_ref.shape[1]
-        blocks = acc_ref.shape[0] // BLOCK
-        seed = where_ref[1] * 1000003 + where_ref[2] * cols
-        inner = lax.broadcasted_iota(jnp.int32, (BLOCK, cols), 0) * D
-        inner = inner + lax.broadcasted_iota(jnp.int32, (BLOCK, cols), 1) + seed
-        lane = lax.broadcasted_iota(jnp.int32, (BLOCK, DH), 1)
-        for b in range(blocks):
-            rows = slice(b * BLOCK, (b + 1) * BLOCK)
-            hashed = inner + drop_ref[b]
-            for _ in range(2):
-                hashed = hashed ^ lax.shift_right_logical(hashed, jnp.int32(16))
-                hashed = hashed * 73244475
-            hashed = hashed ^ lax.shift_right_logical(hashed, jnp.int32(16))
-            kept = (hashed & 1023) >= 102
-            keep = jnp.where(kept, jnp.float32(1024.0 / 922.0), jnp.float32(0.0))
-            total = res_ref[rows, :].astype(F32) + keep * acc_ref[rows, :]
-            sum_ref[rows, :] = total
+        acc_ref[...] = jnp.zeros_like(acc_ref) if rest[0] is acc_ref else rest[0][...]
+
+    for i, ref in enumerate(contexts):
+
+        @pl.when(step // half == i)
+        def _():
+            acc_ref[...] += dot_t(ref[step % half], w_ref[0])
+
+    if last:
+        _, keep_ref, res_ref, sum_ref, stat_ref, _ = rest
+
+        @pl.when(step == pl.num_programs(0) - 1)
+        def _():
+            cols = acc_ref.shape[1]
+            total = res_ref[...].astype(F32) + keep_ref[...] * acc_ref[...]
+            sum_ref[...] = total
             mean = jnp.sum(total, axis=1, keepdims=True) * jnp.float32(1.0 / cols)
             dev = total - mean
             spread = jnp.sum(dev * dev, axis=1, keepdims=True)
-            stat_ref[rows, :] = jnp.where(lane == 0, mean, spread)
-
-
-def project(where, drops, mine, other, weight, residual):
-    rows, cols = residual.shape
-    half = mine.shape[0]
-    steps = 2 * half
-
-    def w_map(i, where_ref, drop_ref):
+            lane = lax.broadcasted_iota(jnp.int32, stat_ref.shape, 1)
+            stat_ref[...] = jnp.where(lane == 0, mean, spread)
+
+
+def project(part, shifts, where, contexts, weight, before=None, finish=None):
+    half, rows, wide = contexts[0].shape
+    cols = weight.shape[1]
+    out = (rows, cols)
+
+    def w_map(i, where_ref):
         core = where_ref[0]
-        own = 2 * i + core
-        far = 2 * (i - half) + (1 - core)
-        return (jnp.where(i < half, own, far), 0, 0)
-
+        parity = jnp.int32(0)
+        for at, shift in enumerate(shifts):
+            parity = jnp.where(i // half == at, (core + shift) % 2, parity)
+        return (2 * (i % half) + parity, 0, part)
+
+    args = list(contexts) + [weight]
+    specs = [whole(c.shape) for c in contexts] + [pl.BlockSpec((1, cols, wide), w_map)]
+    scratch, out_specs, out_shape = [], [whole(out)], [jax.ShapeDtypeStruct(out, F32)]
+    if before is not None:
+        args.append(before)
+        specs.append(whole(out))
+    if finish is not None:
+        args += list(finish)
+        specs += [whole(x.shape) for x in finish]
+        out_specs.append(whole((rows, DH)))
+        out_shape.append(jax.ShapeDtypeStruct((rows, DH), F32))
+        scratch.append(pltpu.VMEM(out, F32))
+    steps = half * len(contexts)
     return pl.pallas_call(
-        project_kernel,
+        functools.partial(project_kernel, shifts, finish is not None),
         grid_spec=pltpu.PrefetchScalarGridSpec(
-            num_scalar_prefetch=2,
+            num_scalar_prefetch=1,
             grid=(steps,),
-            in_specs=[
-                whole(mine.shape),
-                whole(other.shape),
-                pl.BlockSpec((1,) + weight.shape[1:], w_map),
-                whole(residual.shape),
-            ],
-            out_specs=[whole((rows, cols)), whole((rows, DH))],
-            scratch_shapes=[pltpu.VMEM((rows, cols), F32)],
-        ),
-        out_shape=[
-            jax.ShapeDtypeStruct((rows, cols), F32),
-            jax.ShapeDtypeStruct((rows, DH), F32),
-        ],
+            in_specs=specs,
+            out_specs=out_specs,
+            scratch_shapes=scratch,
+        ),
+        out_shape=out_shape,
         compiler_params=params(),
         cost_estimate=pl.CostEstimate(
-            flops=2 * rows * D * cols, transcendentals=0, bytes_accessed=8 << 20
+            flops=2 * rows * steps * wide * cols, transcendentals=0, bytes_accessed=2 << 20
         ),
         name="project",
-    )(where, drops, mine, other, weight, residual)
+    )(where, *args)
 
 
 def on_device(
@@ -318,13 +398,8 @@
     zh_at = lax.axis_index("zh")
     wide = width_here // PARTS
 
-    def cut(x, part):
-        return x[:, part * wide : (part + 1) * wide]
-
-    pools = []
-    for part in range(PARTS):
-        paired = jnp.concatenate([cut(key_rows, part), cut(value_rows, part)], axis=1)
-        pools.append(lax.all_gather(paired, "y", axis=0, tiled=True))
+    paired = jnp.concatenate([key_rows, value_rows], axis=1)
+    pool = lax.all_gather(paired, "y", axis=0, tiled=True)
 
     def moves(flip):
         return [
@@ -343,7 +418,6 @@
         ],
         axis=0,
     )
-    shards = jnp.concatenate([shards[:, :wide], shards[:, wide:]], axis=0)
 
     request_count = block_count * RAND
     target = random_device.reshape(request_count)
@@ -363,29 +437,23 @@
     table = jnp.sum(
         jnp.where(is_offset, wanted[:, None], jnp.where(is_asker, asker[:, None], 0)), axis=0
     )
-    table = jnp.pad(table.astype(BF)[None], ((0, 7), (0, 0)))
+    table = jnp.pad(table.astype(BF)[None], ((0, 7), (0, width_here - cells.shape[0])))
 
     flip = [(0, 1), (1, 0)]
-    asked = []
-    for part in range(PARTS):
-        mine = cut(queries, part)
-        if part == 0:
-            mine = jnp.concatenate([mine, table], axis=0)
-        both = jnp.stack([mine, lax.ppermute(mine, "zh", flip)])
-        if part == PARTS - 1:
-            both = jnp.concatenate([both, shards[None]], axis=0)
-        both = jnp.broadcast_to(both[None], (n_x,) + both.shape)
-        asked.append(lax.all_to_all(both, "x", split_axis=0, concat_axis=0, tiled=True))
-    shards = asked[-1][:, 2]
-    shards = jnp.concatenate(
-        [shards[:, : shards.shape[1] // 2], shards[:, shards.shape[1] // 2 :]], axis=2
-    )
+
+    def over_x(x):
+        x = jnp.broadcast_to(x[None], (n_x,) + x.shape)
+        return lax.all_to_all(x, "x", split_axis=0, concat_axis=0, tiled=True)
+
+    asking = jnp.concatenate([queries, table], axis=0)
+    asked = over_x(jnp.stack([asking, lax.ppermute(asking, "zh", flip)]))
+    shards = over_x(shards)
     weight = lax.all_gather(
         shards.reshape(plane * cols_here, width_here), "y", axis=0, tiled=True
     )
     weight = weight.reshape(tp_count, plane * cols_here, width_here)
 
-    lists = asked[0][:, :, row_count].reshape(plane, plane, 2 * slots)
+    lists = asked[:, :, row_count, : cells.shape[0]].reshape(plane, plane, 2 * slots)
     lists = lax.dynamic_index_in_dim(lists, plane_at, 1, keepdims=False).astype(jnp.int32)
     base = (jnp.arange(slots, dtype=jnp.int32) // CAP) * block_count
     order = jnp.arange(plane, dtype=jnp.int32)
@@ -423,24 +491,25 @@
     zh = zh_at[None].astype(jnp.int32)
 
     near, stat = local(queries, key_rows, value_rows)
-    context = []
+    where = jnp.stack([tp_at % 2, drop_seed[0], tp_at]).astype(jnp.int32)
+    kept = keep(where, drop_offsets, residual.shape)
+    folded = []
     for part in range(PARTS):
-        partials = serve(row, mark, zh, asked[part], pools[part], row_count)
-        got = lax.all_to_all(partials, PLANE, split_axis=0, concat_axis=0, tiled=True)
-        context.append(merge(part, got, near, stat))
-    context = jnp.concatenate(context, axis=1)
-
-    mine = lax.all_to_all(
-        jnp.broadcast_to(context[None], (n_zl,) + context.shape),
-        "zl",
-        split_axis=0,
-        concat_axis=0,
-        tiled=True,
-    )
-    other = lax.ppermute(mine, "core", [(0, 1), (1, 0)])
-
-    where = jnp.stack([tp_at % 2, drop_seed[0], tp_at]).astype(jnp.int32)
-    summed, stats = project(where, drop_offsets, mine, other, weight, residual)
+        partials = serve(part, row, mark, zh, asked, pool, row_count)
+        partials = partials.reshape((n_x, 2) + partials.shape[1:])
+        got = lax.all_to_all(partials, "x", split_axis=0, concat_axis=0, tiled=True)
+        folded.append((got, lax.ppermute(fold(zh, got), "zh", flip)))
+    mine, other = [], []
+    for part in range(PARTS):
+        context = merge(part, zh, *folded[part], near, stat)
+        context = jnp.broadcast_to(context[None], (n_zl,) + context.shape)
+        mine.append(lax.all_to_all(context, "zl", split_axis=0, concat_axis=0, tiled=True))
+        other.append(lax.ppermute(mine[part], "core", flip))
+    (acc,) = project(0, (0, 1), where, (mine[0], other[0]), weight)
+    (acc,) = project(1, (0,), where, (mine[1],), weight, before=acc)
+    summed, stats = project(
+        1, (1,), where, (other[1],), weight, before=acc, finish=(kept, residual)
+    )
 
     stats = jnp.broadcast_to(stats[:, :2].T[None], (tp_count, 2, row_count))
     stats = lax.all_to_all(stats, TP, split_axis=0, concat_axis=0, tiled=True)

time: 218 us -> 214 us (0.982)
  blocking collectives: 55.7 us -> 18.4 us
  starting transfers between devices: 52.6 us -> 84.1 us
  Pallas kernels: 22 us -> 28.8 us
  waiting for transfers between devices: 57.7 us -> 54.2 us
    all_to_all x1, blocking collectives: 47.9 us -> 10.9 us  [over_x(): return lax.all_to_all(x, 'x', split_axis=0, concat_axis=0, tiled=True)]
    ppermute x3 -> x5, starting transfers between devices: 17 us -> 36.5 us  [the longest x2 14 us: on_device(): folded.append((got, lax.ppermute(fold(zh, got), 'zh', flip)))]
    all_to_all x4 -> x5, starting transfers between devices: 21.2 us -> 32.6 us  [the longest x2 21.8 us: on_device(): lax.all_to_all(context, 'zl', split_axis=0, concat_axis=0, tiled=True)]
    all_gather x2 -> x1, waiting for transfers between devices: 11.4 us -> 0.01 us  [on_device(): pool = lax.all_gather(paired, 'y', axis=0, tiled=True)]
    ppermute x3 -> x5, waiting for transfers between devices: 10.5 us -> 16.6 us  [the longest x2 10.7 us: on_device(): folded.append((got, lax.ppermute(fold(zh, got), 'zh', flip)))]
    pallas_call x1 -> x6, Pallas kernels: 7.06 us -> 10.7 us  [the longest x3 8.88 us: project(): pl.pallas_call(functools.partial(project_kernel, shifts, finish is not No...]
    pallas_call x2, Pallas kernels: 12.2 us -> 15.8 us  [serve(): pl.pallas_call(serve_kernel, grid_spec=pltpu.PrefetchScalarGridSpec(num_s...]
    all_to_all x4 -> x5, waiting for transfers between devices: 33.2 us -> 35.4 us  [the longest x1 25.1 us: over_x(): return lax.all_to_all(x, 'x', split_axis=0, concat_axis=0, tiled=True)]
  transfers between devices with their start and end apart: 12 -> 14, of which waited for: 7 -> 8; matrix products, arithmetic and copies ran while one was open for 3% -> 2% of each run, Pallas kernels for 7% -> 12%
where the time goes in v4:
time: 214 us; the launch traced here: 213 us
  starting transfers between devices  84.1 us (39%)
  waiting for transfers between devices  54.2 us (25%)
  Pallas kernels  28.8 us (13%)
  blocking collectives  18.4 us (9%)
  between operations  14.5 us (7%)
  local copies, waits for them, and re-layouts  9.58 us (4%)
  other arithmetic  3.67 us (2%)
    all_to_all x1, waiting for transfers between devices, over_x(): return lax.all_to_all(x, 'x', split_axis=0, concat_axis=0, tiled=True)  25.1 us
    all_to_all x2, starting transfers between devices, on_device(): lax.all_to_all(context, 'zl', split_axis=0, concat_axis=0, tiled=True)  21.8 us
    pallas_call x2, Pallas kernels, serve(): pl.pallas_call(serve_kernel, grid_spec=pltpu.PrefetchScalarGridSpec(num_s...  15.8 us
    ppermute x2, starting transfers between devices, on_device(): folded.append((got, lax.ppermute(fold(zh, got), 'zh', flip)))  14 us
    ppermute x2, starting transfers between devices, on_device(): other.append(lax.ppermute(mine[part], 'core', flip))  11.6 us
    ppermute x1, starting transfers between devices, on_device(): asked = over_x(jnp.stack([asking, lax.ppermute(asking, 'zh', flip)]))  10.9 us
    all_to_all x1, blocking collectives, over_x(): return lax.all_to_all(x, 'x', split_axis=0, concat_axis=0, tiled=True)  10.9 us
    ppermute x2, waiting for transfers between devices, on_device(): folded.append((got, lax.ppermute(fold(zh, got), 'zh', flip)))  10.7 us
  transfers between devices with their start and end apart: 14, of which 8 were waited for; matrix products, arithmetic and copies ran while one was open for 2% of the time, Pallas kernels for 12%

profile of v4, /device:TPU:1, one launch (start us, length us, event | category | flops | bytes accessed | tf_op | source)
XLA Modules:
  0.0 213.3 jit_solution(17339675959446657130)
XLA Ops:
  6.5 1.9 pad_maximum_fusion.1
  8.5 0.0 all-gather.3.cloned.1.call-update
  8.5 0.0 all-gather.5.cloned.1.call-start
  8.5 4.6 %collective-permute-start.3 = (bf16[64,512]{1,0:T(8,128)(2,1)}, bf16[64,512]{1,0:T(8,128)(2,1)S(1)}, u32[]{:S(2)}, u32[]{:S(2)}) collective-permute-start(bf16[64,512]{1,0:T(8,128)(2,1)} %bitcast.28), channel_id=1, source_target_pairs={{0,0},{1,64},{2,128},{3,192},{4,256},{5,320},{6,384},{7,448},{8,8}... | collective-permute-start | bytes 196616 | tf_op jit(solution)/shard_map/ppermute | solution.py:412
  13.1 10.4 %collective-permute-start.4 = (bf16[64,512]{1,0:T(8,128)(2,1)}, bf16[64,512]{1,0:T(8,128)(2,1)S(1)}, u32[]{:S(2)}, u32[]{:S(2)}) collective-permute-start(bf16[64,512]{1,0:T(8,128)(2,1)} %bitcast.29), channel_id=1, source_target_pairs={{0,8},{1,72},{2,136},{3,200},{4,264},{5,328},{6,392},{7,456},{8,0}... | collective-permute-start | bytes 196616 | tf_op jit(solution)/shard_map/ppermute | solution.py:413
  23.5 2.1 collective-permute-done.4
  25.7 10.9 %all_to_all.35 = bf16[4,128,512]{2,1,0:T(8,128)(2,1)} all-to-all(bf16[4,128,512]{2,1,0:T(8,128)(2,1)S(1)} %broadcast_in_dim.62), channel_id=1, replica_groups=mesh['y'=8,'x'=4,'zh'=2,'zl'=4,'core'=2] {'x'}, dimensions={0} | all-to-all | bytes 1048576 | tf_op jit(solution)/shard_map/all_to_all | solution.py:446
  36.6 0.0 all-gather.5.cloned.1.call-update
  36.6 0.1 copy.22
  36.7 0.1 reshape.393
  36.8 0.1 copy.23
  36.9 0.1 broadcast_in_dim.53
  37.0 0.2 convert_reduce_fusion
  37.2 0.1 select_reduce_fusion
  37.4 10.9 %collective-permute-start = (bf16[264,512]{1,0:T(8,128)(2,1)S(1)}, bf16[264,512]{1,0:T(8,128)(2,1)S(1)}, u32[]{:S(2)}, u32[]{:S(2)}) collective-permute-start(bf16[264,512]{1,0:T(8,128)(2,1)S(1)} %get-tuple-element.20), channel_id=1, source_target_pairs={{0,8},{8,0},{1,9},{9,1},{2,10},{10,2},{3,11},{11,3},{4,12},{12,4},... | collective-permute-start | bytes 811016 | tf_op jit(solution)/shard_map/ppermute | solution.py:449
  48.3 5.8 %collective-permute-done = bf16[264,512]{1,0:T(8,128)(2,1)S(1)} collective-permute-done((bf16[264,512]{1,0:T(8,128)(2,1)S(1)}, bf16[264,512]{1,0:T(8,128)(2,1)S(1)}, u32[]{:S(2)}, u32[]{:S(2)}) %collective-permute-start) | collective-permute-done | bytes 270368 | tf_op jit(solution)/shard_map/ppermute | solution.py:449
  54.1 0.1 pad_maximum_fusion
  54.2 1.6 broadcast_in_dim.57
  55.8 3.8 %all-to-all-start = ((bf16[4,2,264,512]{3,2,1,0:T(8,128)(2,1)}), bf16[4,2,264,512]{3,2,1,0:T(8,128)(2,1)S(1)}, u32[]{:S(2)}, u32[]{:S(2)}) async-start(bf16[4,2,264,512]{3,2,1,0:T(8,128)(2,1)} %broadcast_in_dim.57), calls=%async_computation | async-start | bytes 4325376 | tf_op jit(solution)/shard_map/all_to_all | solution.py:446
  59.6 0.1 pad.10.clone
  59.7 0.1 pad.14.clone
  59.8 25.1 %all-to-all-done.q_ref = bf16[4,2,264,512]{3,2,1,0:T(8,128)(2,1)S(1)} async-done(((bf16[4,2,264,512]{3,2,1,0:T(8,128)(2,1)}), bf16[4,2,264,512]{3,2,1,0:T(8,128)(2,1)S(1)}, u32[]{:S(2)}, u32[]{:S(2)}) %all-to-all-start) | async-done | bytes 2162720 | tf_op jit(solution)/shard_map/all_to_all | solution.py:446
  84.9 0.1 reshape_squeeze.3
  85.0 0.1 compare_select_fusion
  85.1 0.1 pad_add_fusion.1
  85.2 0.1 reshape.395.mark_ref
  85.2 0.1 pad_add_fusion
  85.3 0.1 reshape.394.row_ref
  85.4 7.9 %serve.3 = bf16[8,272,256]{2,1,0:T(8,128)(2,1)S(1)} custom-call(s32[160]{0:T(256)S(1)} %reshape.394.row_ref, s32[160]{0:T(256)S(1)} %reshape.395.mark_ref, s32[1]{0:T(128)} %bitcast.2.zh_ref, bf16[4,2,264,512]{3,2,1,0:T(8,128)(2,1)S(1)} %all-to-all-done.q_ref, bf16[2048,1024]{1,0:T(8,128)(2,1)} %all-gather.3.cloned.1.call-done.key_ref.value_ref, ...), custom_call_target="tpu_custom_call" | custom-call | flops 671088640 | bytes 4194304 | tf_op jit(solution)/shard_map/serve/pallas_call | solution.py:93
  93.3 1.1 copy-done.3
  94.4 3.5 %all-to-all-start.4 = ((bf16[4,2,272,256]{3,2,1,0:T(8,128)(2,1)}), bf16[4,2,272,256]{3,2,1,0:T(8,128)(2,1)S(1)}, u32[]{:S(2)}, u32[]{:S(2)}) async-start(bf16[4,2,272,256]{3,2,1,0:T(8,128)(2,1)} %bitcast.24), calls=%async_computation.4 | async-start | bytes 2228224 | tf_op jit(solution)/shard_map/all_to_all | solution.py:500
  97.9 7.9 %serve.2 = bf16[8,272,256]{2,1,0:T(8,128)(2,1)S(1)} custom-call(s32[160]{0:T(256)S(1)} %reshape.394.row_ref, s32[160]{0:T(256)S(1)} %reshape.395.mark_ref, s32[1]{0:T(128)} %bitcast.2.zh_ref, bf16[4,2,264,512]{3,2,1,0:T(8,128)(2,1)S(1)} %all-to-all-done.q_ref, bf16[2048,1024]{1,0:T(8,128)(2,1)} %all-gather.3.cloned.1.call-done.key_ref.value_ref, ...), custom_call_target="tpu_custom_call" | custom-call | flops 671088640 | bytes 4194304 | tf_op jit(solution)/shard_map/serve/pallas_call | solution.py:93
  105.8 1.0 copy-done.2
  106.9 3.9 %all-to-all-done.4.got_ref = bf16[4,2,272,256]{3,2,1,0:T(8,128)(2,1)S(1)} async-done(((bf16[4,2,272,256]{3,2,1,0:T(8,128)(2,1)}), bf16[4,2,272,256]{3,2,1,0:T(8,128)(2,1)S(1)}, u32[]{:S(2)}, u32[]{:S(2)}) %all-to-all-start.4) | async-done | bytes 1114144 | tf_op jit(solution)/shard_map/all_to_all | solution.py:500
  110.7 3.5 %all-to-all-start.1 = ((bf16[4,2,272,256]{3,2,1,0:T(8,128)(2,1)}), bf16[4,2,272,256]{3,2,1,0:T(8,128)(2,1)S(1)}, u32[]{:S(2)}, u32[]{:S(2)}) async-start(bf16[4,2,272,256]{3,2,1,0:T(8,128)(2,1)} %bitcast.23), calls=%async_computation.1 | async-start | bytes 2228224 | tf_op jit(solution)/shard_map/all_to_all | solution.py:500
  114.3 0.6 fold.3
  114.8 12.1 %collective-permute-start.5 = (bf16[272,256]{1,0:T(8,128)(2,1)S(1)}, bf16[272,256]{1,0:T(8,128)(2,1)S(1)}, u32[]{:S(2)}, u32[]{:S(2)}) collective-permute-start(bf16[272,256]{1,0:T(8,128)(2,1)S(1)} %fold.3), channel_id=1, source_target_pairs={{0,8},{8,0},{1,9},{9,1},{2,10},{10,2},{3,11},{11,3},{4,12},{12,4},... | collective-permute-start | bytes 417800 | tf_op jit(solution)/shard_map/ppermute | solution.py:501
  126.9 1.0 local.1
  128.0 1.4 collective-permute-done.5.far_ref
  129.3 0.6 merge.3
  130.0 0.9 broadcast_in_dim.63
  130.8 14.4 %all-to-all-start.5 = ((bf16[4,256,256]{2,1,0:T(8,128)(2,1)}), bf16[4,256,256]{2,1,0:T(8,128)(2,1)S(1)}, u32[]{:S(2)}, u32[]{:S(2)}) async-start(bf16[4,256,256]{2,1,0:T(8,128)(2,1)} %broadcast_in_dim.63), calls=%async_computation.5 | async-start | bytes 1048576 | tf_op jit(solution)/shard_map/all_to_all | solution.py:506
  145.2 0.5 fold.2
  145.8 1.9 collective-permute-start.1
  147.7 9.4 %collective-permute-done.1.far_ref = bf16[272,256]{1,0:T(8,128)(2,1)S(1)} collective-permute-done((bf16[272,256]{1,0:T(8,128)(2,1)S(1)}, bf16[272,256]{1,0:T(8,128)(2,1)S(1)}, u32[]{:S(2)}, u32[]{:S(2)}) %collective-permute-start.1) | collective-permute-done | bytes 139296 | tf_op jit(solution)/shard_map/ppermute | solution.py:501
  157.0 1.0 copy-done.5
  158.1 0.6 merge.2
  158.7 0.7 all-to-all-done.5.refs_0_
  159.4 0.9 broadcast_in_dim.61
  160.3 7.5 %all-to-all-start.2 = ((bf16[4,256,256]{2,1,0:T(8,128)(2,1)}), bf16[4,256,256]{2,1,0:T(8,128)(2,1)S(1)}, u32[]{:S(2)}, u32[]{:S(2)}) async-start(bf16[4,256,256]{2,1,0:T(8,128)(2,1)} %broadcast_in_dim.61), calls=%async_computation.2 | async-start | bytes 1048576 | tf_op jit(solution)/shard_map/all_to_all | solution.py:506
  167.8 5.2 %collective-permute-start.6 = (bf16[4,256,256]{2,1,0:T(8,128)(2,1)S(1)}, bf16[4,256,256]{2,1,0:T(8,128)(2,1)S(1)}, u32[]{:S(2)}, u32[]{:S(2)}) collective-permute-start(bf16[4,256,256]{2,1,0:T(8,128)(2,1)S(1)} %all-to-all-done.5.refs_0_), channel_id=1, source_target_pairs={{0,1},{1,0},{2,3},{3,2},{4,5},{5,4},{6,7},{7,6},{8,9},{9,8},{10,11... | collective-permute-start | bytes 1572872 | tf_op jit(solution)/shard_map/ppermute | solution.py:507
  173.0 5.8 %all-to-all-done.2.refs_0_ = bf16[4,256,256]{2,1,0:T(8,128)(2,1)S(1)} async-done(((bf16[4,256,256]{2,1,0:T(8,128)(2,1)}), bf16[4,256,256]{2,1,0:T(8,128)(2,1)S(1)}, u32[]{:S(2)}, u32[]{:S(2)}) %all-to-all-start.2) | async-done | bytes 524320 | tf_op jit(solution)/shard_map/all_to_all | solution.py:506
  178.7 6.4 %collective-permute-start.2 = (bf16[4,256,256]{2,1,0:T(8,128)(2,1)S(1)}, bf16[4,256,256]{2,1,0:T(8,128)(2,1)S(1)}, u32[]{:S(2)}, u32[]{:S(2)}) collective-permute-start(bf16[4,256,256]{2,1,0:T(8,128)(2,1)S(1)} %all-to-all-done.2.refs_0_), channel_id=1, source_target_pairs={{0,1},{1,0},{2,3},{3,2},{4,5},{5,4},{6,7},{7,6},{8,9},{9,8},{10,11... | collective-permute-start | bytes 1572872 | tf_op jit(solution)/shard_map/ppermute | solution.py:507
  185.8 0.1 pad_add_fusion.2.where_ref
  185.8 0.8 keep.1.refs_3_
  186.6 0.0 all-gather.5.cloned.1.call-done
  186.7 2.2 %copy-done = bf16[4096,512]{1,0:T(8,128)(2,1)S(1)} copy-done((bf16[4096,512]{1,0:T(8,128)(2,1)S(1)}, bf16[4096,512]{1,0:T(8,128)(2,1)}, u32[]{:S(2)}) %copy-start) | copy-done | bytes 4194328
  188.8 3.3 %project.3.refs_2_ = f32[256,512]{1,0:T(8,128)S(1)} custom-call(s32[3]{0:T(128)S(1)} %pad_add_fusion.2.where_ref, bf16[4,256,256]{2,1,0:T(8,128)(2,1)S(1)} %all-to-all-done.5.refs_0_, bf16[4,256,256]{2,1,0:T(8,128)(2,1)S(1)} %collective-permute-done.6.refs_1_, bf16[8,512,512]{2,1,0:T(8,128)(2,1)S(1)} %bitcast.21), custom_call_target="tpu_custom_call" | custom-call | flops 536870912 | bytes 2097152 | tf_op jit(solution)/shard_map/project/pallas_call | solution.py:354
  192.2 0.0 copy-start.9
  192.2 1.9 project.4.refs_2_
  194.2 3.6 %project.5 = (f32[256,512]{1,0:T(8,128)S(1)}, f32[256,128]{1,0:T(8,128)S(1)}) custom-call(s32[3]{0:T(128)S(1)} %pad_add_fusion.2.where_ref, bf16[4,256,256]{2,1,0:T(8,128)(2,1)S(1)} %collective-permute-done.2.refs_0_, bf16[8,512,512]{2,1,0:T(8,128)(2,1)} %bitcast.20, f32[256,512]{1,0:T(8,128)S(1)} %project.4.refs_2_, f32[256,512]{1,0:T(8,128)S(1)} %keep.1.refs_3_, ...), custom_call_target="tpu_custom_call" | custom-call | flops 268435456 | bytes 2097152 | tf_op jit(solution)/shard_map/project/pallas_call | solution.py:354
  197.8 0.1 copy.24
  197.9 7.6 %all_to_all.36 = f32[8,2,256]{2,1,0:T(2,128)S(1)} all-to-all(f32[8,2,256]{2,1,0:T(2,128)S(1)} %broadcast_in_dim.64), channel_id=1, replica_groups=mesh['y'=8,'x'=4,'zh'=2,'zl'=4,'core'=2] {'zl','core'}, dimensions={0} | all-to-all | bytes 32768 | tf_op jit(solution)/shard_map/all_to_all | solution.py:515
  205.6 0.9 add_convert_fusion
  (53 shorter events, 0.4 us)
Async XLA Ops:
  6.5 30.1 %copy-start.13 = (s32[16,3]{0,1:T(4,128)S(1)}, s32[16,3]{0,1:T(4,128)}, u32[]{:S(2)}) copy-start(s32[16,3]{0,1:T(4,128)} %param.20) | copy-start | bytes 580
  6.5 30.3 %copy-start.14 = (s32[16,3]{0,1:T(4,128)S(1)}, s32[16,3]{0,1:T(4,128)}, u32[]{:S(2)}) copy-start(s32[16,3]{0,1:T(4,128)} %param.21) | copy-start | bytes 580
  6.5 30.8 %copy-start.6 = (bf16[256,512]{1,0:T(8,128)(2,1)S(1)}, bf16[256,512]{1,0:T(8,128)(2,1)}, u32[]{:S(2)}) copy-start(bf16[256,512]{1,0:T(8,128)(2,1)} %q_ref.1) | copy-start | bytes 786436
  6.5 78.9 %all-gather.3.cloned.1.call-start = ((), (), s32[]{:S(2)}) async-start(), calls=%async_computation.7 | async-start | bytes 4718592 | tf_op jit(solution)/shard_map/all_gather | solution.py:402
  8.5 178.1 %all-gather.5.cloned.1.call-start = ((), (), s32[]{:S(2)}) async-start(), calls=%async_computation.8 | async-start | bytes 4718592 | tf_op jit(solution)/shard_map/all_gather | solution.py:451
  8.5 15.0 %collective-permute-start.3 = (bf16[64,512]{1,0:T(8,128)(2,1)}, bf16[64,512]{1,0:T(8,128)(2,1)S(1)}, u32[]{:S(2)}, u32[]{:S(2)}) collective-permute-start(bf16[64,512]{1,0:T(8,128)(2,1)} %bitcast.28), channel_id=1, source_target_pairs={{0,0},{1,64},{2,128},{3,192},{4,256},{5,320},{6,384},{7,448},{8,8}... | collective-permute-start | bytes 196616 | tf_op jit(solution)/shard_map/ppermute | solution.py:412
  13.1 12.5 %collective-permute-start.4 = (bf16[64,512]{1,0:T(8,128)(2,1)}, bf16[64,512]{1,0:T(8,128)(2,1)S(1)}, u32[]{:S(2)}, u32[]{:S(2)}) collective-permute-start(bf16[64,512]{1,0:T(8,128)(2,1)} %bitcast.29), channel_id=1, source_target_pairs={{0,8},{1,72},{2,136},{3,200},{4,264},{5,328},{6,392},{7,456},{8,0}... | collective-permute-start | bytes 196616 | tf_op jit(solution)/shard_map/ppermute | solution.py:413
  37.4 16.8 %collective-permute-start = (bf16[264,512]{1,0:T(8,128)(2,1)S(1)}, bf16[264,512]{1,0:T(8,128)(2,1)S(1)}, u32[]{:S(2)}, u32[]{:S(2)}) collective-permute-start(bf16[264,512]{1,0:T(8,128)(2,1)S(1)} %get-tuple-element.20), channel_id=1, source_target_pairs={{0,8},{8,0},{1,9},{9,1},{2,10},{10,2},{3,11},{11,3},{4,12},{12,4},... | collective-permute-start | bytes 811016 | tf_op jit(solution)/shard_map/ppermute | solution.py:449
  55.8 3.8 %copy-start.15 = (s32[2]{0:T(128)S(1)}, s32[2]{0:T(128)}, u32[]{:S(2)}) copy-start(s32[2]{0:T(128)} %param.19) | copy-start | bytes 28
  55.8 29.1 %all-to-all-start = ((bf16[4,2,264,512]{3,2,1,0:T(8,128)(2,1)}), bf16[4,2,264,512]{3,2,1,0:T(8,128)(2,1)S(1)}, u32[]{:S(2)}, u32[]{:S(2)}) async-start(bf16[4,2,264,512]{3,2,1,0:T(8,128)(2,1)} %broadcast_in_dim.57), calls=%async_computation | async-start | bytes 4325376 | tf_op jit(solution)/shard_map/all_to_all | solution.py:446
  93.3 1.1 copy-start.3
  94.4 16.4 %all-to-all-start.4 = ((bf16[4,2,272,256]{3,2,1,0:T(8,128)(2,1)}), bf16[4,2,272,256]{3,2,1,0:T(8,128)(2,1)S(1)}, u32[]{:S(2)}, u32[]{:S(2)}) async-start(bf16[4,2,272,256]{3,2,1,0:T(8,128)(2,1)} %bitcast.24), calls=%async_computation.4 | async-start | bytes 2228224 | tf_op jit(solution)/shard_map/all_to_all | solution.py:500
  105.8 1.1 copy-start.2
  106.9 20.0 %copy-start.7 = (bf16[256,512]{1,0:T(8,128)(2,1)S(1)}, bf16[256,512]{1,0:T(8,128)(2,1)}, u32[]{:S(2)}) copy-start(bf16[256,512]{1,0:T(8,128)(2,1)} %v_ref.1) | copy-start | bytes 786436
  106.9 20.1 %copy-start.8 = (bf16[256,512]{1,0:T(8,128)(2,1)S(1)}, bf16[256,512]{1,0:T(8,128)(2,1)}, u32[]{:S(2)}) copy-start(bf16[256,512]{1,0:T(8,128)(2,1)} %k_ref.1) | copy-start | bytes 786436
  110.7 19.2 %all-to-all-start.1 = ((bf16[4,2,272,256]{3,2,1,0:T(8,128)(2,1)}), bf16[4,2,272,256]{3,2,1,0:T(8,128)(2,1)S(1)}, u32[]{:S(2)}, u32[]{:S(2)}) async-start(bf16[4,2,272,256]{3,2,1,0:T(8,128)(2,1)} %bitcast.23), calls=%async_computation.1 | async-start | bytes 2228224 | tf_op jit(solution)/shard_map/all_to_all | solution.py:500
  114.8 14.5 %collective-permute-start.5 = (bf16[272,256]{1,0:T(8,128)(2,1)S(1)}, bf16[272,256]{1,0:T(8,128)(2,1)S(1)}, u32[]{:S(2)}, u32[]{:S(2)}) collective-permute-start(bf16[272,256]{1,0:T(8,128)(2,1)S(1)} %fold.3), channel_id=1, source_target_pairs={{0,8},{8,0},{1,9},{9,1},{2,10},{10,2},{3,11},{11,3},{4,12},{12,4},... | collective-permute-start | bytes 417800 | tf_op jit(solution)/shard_map/ppermute | solution.py:501
  127.9 2.9 %copy-start.4 = (f32[256,512]{1,0:T(8,128)}, f32[256,512]{1,0:T(8,128)S(1)}, u32[]{:S(2)}) copy-start(f32[256,512]{1,0:T(8,128)S(1)} %get-tuple-element.9.near_ref) | copy-start | bytes 1572868
  130.8 28.6 %all-to-all-start.5 = ((bf16[4,256,256]{2,1,0:T(8,128)(2,1)}), bf16[4,256,256]{2,1,0:T(8,128)(2,1)S(1)}, u32[]{:S(2)}, u32[]{:S(2)}) async-start(bf16[4,256,256]{2,1,0:T(8,128)(2,1)} %broadcast_in_dim.63), calls=%async_computation.5 | async-start | bytes 1048576 | tf_op jit(solution)/shard_map/all_to_all | solution.py:506
  145.2 40.6 %copy-start.10 = (s32[16]{0:T(128)S(1)}, s32[16]{0:T(128)}, u32[]{:S(2)}) copy-start(s32[16]{0:T(128)} %drop_ref.1) | copy-start | bytes 196
  145.8 11.3 %collective-permute-start.1 = (bf16[272,256]{1,0:T(8,128)(2,1)S(1)}, bf16[272,256]{1,0:T(8,128)(2,1)S(1)}, u32[]{:S(2)}, u32[]{:S(2)}) collective-permute-start(bf16[272,256]{1,0:T(8,128)(2,1)S(1)} %fold.2), channel_id=1, source_target_pairs={{0,8},{8,0},{1,9},{9,1},{2,10},{10,2},{3,11},{11,3},{4,12},{12,4},... | collective-permute-start | bytes 417800 | tf_op jit(solution)/shard_map/ppermute | solution.py:501
  157.0 1.0 copy-start.5
  160.3 18.5 %all-to-all-start.2 = ((bf16[4,256,256]{2,1,0:T(8,128)(2,1)}), bf16[4,256,256]{2,1,0:T(8,128)(2,1)S(1)}, u32[]{:S(2)}, u32[]{:S(2)}) async-start(bf16[4,256,256]{2,1,0:T(8,128)(2,1)} %broadcast_in_dim.61), calls=%async_computation.2 | async-start | bytes 1048576 | tf_op jit(solution)/shard_map/all_to_all | solution.py:506
  167.8 18.9 %collective-permute-start.6 = (bf16[4,256,256]{2,1,0:T(8,128)(2,1)S(1)}, bf16[4,256,256]{2,1,0:T(8,128)(2,1)S(1)}, u32[]{:S(2)}, u32[]{:S(2)}) collective-permute-start(bf16[4,256,256]{2,1,0:T(8,128)(2,1)S(1)} %all-to-all-done.5.refs_0_), channel_id=1, source_target_pairs={{0,1},{1,0},{2,3},{3,2},{4,5},{5,4},{6,7},{7,6},{8,9},{9,8},{10,11... | collective-permute-start | bytes 1572872 | tf_op jit(solution)/shard_map/ppermute | solution.py:507
  178.7 15.4 %collective-permute-start.2 = (bf16[4,256,256]{2,1,0:T(8,128)(2,1)S(1)}, bf16[4,256,256]{2,1,0:T(8,128)(2,1)S(1)}, u32[]{:S(2)}, u32[]{:S(2)}) collective-permute-start(bf16[4,256,256]{2,1,0:T(8,128)(2,1)S(1)} %all-to-all-done.2.refs_0_), channel_id=1, source_target_pairs={{0,1},{1,0},{2,3},{3,2},{4,5},{5,4},{6,7},{7,6},{8,9},{9,8},{10,11... | collective-permute-start | bytes 1572872 | tf_op jit(solution)/shard_map/ppermute | solution.py:507
  186.6 2.2 %copy-start = (bf16[4096,512]{1,0:T(8,128)(2,1)S(1)}, bf16[4096,512]{1,0:T(8,128)(2,1)}, u32[]{:S(2)}) copy-start(bf16[4096,512]{1,0:T(8,128)(2,1)} %all-gather.5.cloned.1.call-done) | copy-start | bytes 12582916
  188.8 3.3 %copy-start.1 = (bf16[4096,512]{1,0:T(8,128)(2,1)S(1)}, bf16[4096,512]{1,0:T(8,128)(2,1)}, u32[]{:S(2)}) copy-start(bf16[4096,512]{1,0:T(8,128)(2,1)} %all-gather.5.cloned.1.call-done) | copy-start | bytes 12582916
  192.2 2.0 copy-start.9
  194.1 11.4 %copy-start.11 = (f32[512]{0:T(512)S(1)}, f32[512]{0:T(512)}, u32[]{:S(2)}) copy-start(f32[512]{0:T(512)} %param.18) | copy-start | bytes 6148
  194.1 11.4 %copy-start.12 = (f32[512]{0:T(512)S(1)}, f32[512]{0:T(512)}, u32[]{:S(2)}) copy-start(f32[512]{0:T(512)} %param.17) | copy-start | bytes 6148
Sparse Core Ops, SparseCore 0:
  9.4 65.0 all-gather.2
  76.6 53.7 all-gather.4

commit v5 on v4

--- a/solution.py
+++ b/solution.py
@@ -166,7 +166,7 @@
     return jnp.concatenate(lines, axis=0).T
 
 
-def fold_kernel(zh_ref, got_ref, out_ref):
+def fold_kernel(zh_ref, got_ref, _, out_ref):
     peers, _, rows, wide = got_ref.shape
     rows = rows - STAT_ROWS
     heads = wide // DH
@@ -189,7 +189,7 @@
         ).astype(BF)
 
 
-def fold(zh, got):
+def fold(zh, got, after):
     peers, _, rows, wide = got.shape
     return pl.pallas_call(
         fold_kernel,
@@ -197,7 +197,8 @@
             num_scalar_prefetch=1,
             grid=(1,),
             in_specs=[
-                pl.BlockSpec((peers, 1, rows, wide), lambda i, zh_ref: (0, 1 - zh_ref[0], 0, 0))
+                pl.BlockSpec((peers, 1, rows, wide), lambda i, zh_ref: (0, 1 - zh_ref[0], 0, 0)),
+                pl.BlockSpec(memory_space=pl.ANY),
             ],
             out_specs=whole((rows, wide)),
         ),
@@ -207,10 +208,10 @@
             flops=2 * peers * rows * wide, transcendentals=0, bytes_accessed=1 << 20
         ),
         name="fold",
-    )(zh, got)
-
-
-def merge_kernel(first, zh_ref, got_ref, far_ref, near_ref, stat_ref, out_ref):
+    )(zh, got, after)
+
+
+def merge_kernel(first, zh_ref, got_ref, far_ref, near_ref, stat_ref, _, out_ref):
     peers, _, rows, wide = got_ref.shape
     rows = rows - STAT_ROWS
     heads = wide // DH
@@ -236,7 +237,7 @@
         out_ref[:, lanes] = total.astype(BF)
 
 
-def merge(part, zh, got, far, near, stat):
+def merge(part, zh, got, far, near, stat, after):
     peers, _, rows, wide = got.shape
     out = (rows - STAT_ROWS, wide)
     return pl.pallas_call(
@@ -249,6 +250,7 @@
                 whole(far.shape),
                 pl.BlockSpec(out, lambda i, zh_ref: (0, part)),
                 whole(stat.shape),
+                pl.BlockSpec(memory_space=pl.ANY),
             ],
             out_specs=whole(out),
         ),
@@ -258,7 +260,7 @@
             flops=2 * peers * rows * wide, transcendentals=0, bytes_accessed=1 << 20
         ),
         name="merge",
-    )(zh, got, far, near, stat)
+    )(zh, got, far, near, stat, after)
 
 
 def keep_kernel(where_ref, drop_ref, out_ref):
@@ -293,54 +295,43 @@
     )(where, drops)
 
 
-def project_kernel(shifts, last, where_ref, *refs):
-    count = len(shifts)
-    contexts, w_ref = refs[:count], refs[count]
-    rest = refs[count + 1 :]
-    acc_ref = rest[-1]
-    step = pl.program_id(0)
-    half = contexts[0].shape[0]
-
-    @pl.when(step == 0)
-    def _():
-        acc_ref[...] = jnp.zeros_like(acc_ref) if rest[0] is acc_ref else rest[0][...]
-
-    for i, ref in enumerate(contexts):
-
-        @pl.when(step // half == i)
-        def _():
-            acc_ref[...] += dot_t(ref[step % half], w_ref[0])
-
-    if last:
-        _, keep_ref, res_ref, sum_ref, stat_ref, _ = rest
-
-        @pl.when(step == pl.num_programs(0) - 1)
-        def _():
-            cols = acc_ref.shape[1]
-            total = res_ref[...].astype(F32) + keep_ref[...] * acc_ref[...]
-            sum_ref[...] = total
-            mean = jnp.sum(total, axis=1, keepdims=True) * jnp.float32(1.0 / cols)
-            dev = total - mean
-            spread = jnp.sum(dev * dev, axis=1, keepdims=True)
-            lane = lax.broadcasted_iota(jnp.int32, stat_ref.shape, 1)
-            stat_ref[...] = jnp.where(lane == 0, mean, spread)
+def project_kernel(count, last, where_ref, *refs):
+    contexts, weights = refs[:count], refs[count : 2 * count]
+    rest = refs[2 * count :]
+    acc = sum(
+        dot_t(c_ref[z], w_ref[z, 0])
+        for c_ref, w_ref in zip(contexts, weights)
+        for z in range(c_ref.shape[0])
+    )
+    if len(rest) > 1:
+        acc = acc + rest[0][...]
+    if not last:
+        rest[-1][...] = acc
+        return
+    _, keep_ref, res_ref, sum_ref, stat_ref = rest
+    cols = acc.shape[1]
+    total = res_ref[...].astype(F32) + keep_ref[...] * acc
+    sum_ref[...] = total
+    mean = jnp.sum(total, axis=1, keepdims=True) * jnp.float32(1.0 / cols)
+    dev = total - mean
+    spread = jnp.sum(dev * dev, axis=1, keepdims=True)
+    lane = lax.broadcasted_iota(jnp.int32, stat_ref.shape, 1)
+    stat_ref[...] = jnp.where(lane == 0, mean, spread)
 
 
 def project(part, shifts, where, contexts, weight, before=None, finish=None):
     half, rows, wide = contexts[0].shape
-    cols = weight.shape[1]
+    cols = weight.shape[2]
     out = (rows, cols)
-
-    def w_map(i, where_ref):
-        core = where_ref[0]
-        parity = jnp.int32(0)
-        for at, shift in enumerate(shifts):
-            parity = jnp.where(i // half == at, (core + shift) % 2, parity)
-        return (2 * (i % half) + parity, 0, part)
-
-    args = list(contexts) + [weight]
-    specs = [whole(c.shape) for c in contexts] + [pl.BlockSpec((1, cols, wide), w_map)]
-    scratch, out_specs, out_shape = [], [whole(out)], [jax.ShapeDtypeStruct(out, F32)]
+    args = list(contexts) + [weight] * len(contexts)
+    specs = [whole(c.shape) for c in contexts] + [
+        pl.BlockSpec(
+            (half, 1, cols, wide),
+            lambda i, where_ref, shift=shift: (0, (where_ref[0] + shift) % 2, 0, part),
+        )
+        for shift in shifts
+    ]
+    out_specs, out_shape = [whole(out)], [jax.ShapeDtypeStruct(out, F32)]
     if before is not None:
         args.append(before)
         specs.append(whole(out))
@@ -349,21 +340,17 @@
         specs += [whole(x.shape) for x in finish]
         out_specs.append(whole((rows, DH)))
         out_shape.append(jax.ShapeDtypeStruct((rows, DH), F32))
-        scratch.append(pltpu.VMEM(out, F32))
-    steps = half * len(contexts)
     return pl.pallas_call(
-        functools.partial(project_kernel, shifts, finish is not None),
+        functools.partial(project_kernel, len(contexts), finish is not None),
         grid_spec=pltpu.PrefetchScalarGridSpec(
-            num_scalar_prefetch=1,
-            grid=(steps,),
-            in_specs=specs,
-            out_specs=out_specs,
-            scratch_shapes=scratch,
+            num_scalar_prefetch=1, grid=(1,), in_specs=specs, out_specs=out_specs
         ),
         out_shape=out_shape,
         compiler_params=params(),
         cost_estimate=pl.CostEstimate(
-            flops=2 * rows * steps * wide * cols, transcendentals=0, bytes_accessed=2 << 20
+            flops=2 * rows * half * len(contexts) * wide * cols,
+            transcendentals=0,
+            bytes_accessed=2 << 20,
         ),
         name="project",
     )(where, *args)
@@ -445,13 +432,17 @@
         x = jnp.broadcast_to(x[None], (n_x,) + x.shape)
         return lax.all_to_all(x, "x", split_axis=0, concat_axis=0, tiled=True)
 
-    asking = jnp.concatenate([queries, table], axis=0)
-    asked = over_x(jnp.stack([asking, lax.ppermute(asking, "zh", flip)]))
-    shards = over_x(shards)
+    near_q = jnp.concatenate([queries, table], axis=0)
+    far_q = jnp.concatenate(
+        [lax.ppermute(queries, "zh", flip), lax.ppermute(table, "zh", flip)], axis=0
+    )
+    asked = over_x(jnp.stack([near_q, far_q]))
+    after = asked[0, 0, row_count, 0] * 0
+    shards = over_x(shards + after)
     weight = lax.all_gather(
         shards.reshape(plane * cols_here, width_here), "y", axis=0, tiled=True
     )
-    weight = weight.reshape(tp_count, plane * cols_here, width_here)
+    weight = weight.reshape(n_zl, 2, plane * cols_here, width_here)
 
     lists = asked[:, :, row_count, : cells.shape[0]].reshape(plane, plane, 2 * slots)
     lists = lax.dynamic_index_in_dim(lists, plane_at, 1, keepdims=False).astype(jnp.int32)
@@ -498,10 +489,11 @@
         partials = serve(part, row, mark, zh, asked, pool, row_count)
         partials = partials.reshape((n_x, 2) + partials.shape[1:])
         got = lax.all_to_all(partials, "x", split_axis=0, concat_axis=0, tiled=True)
-        folded.append((got, lax.ppermute(fold(zh, got), "zh", flip)))
+        gone = fold(zh, got, kept)
+        folded.append((got, lax.ppermute(gone, "zh", flip)))
     mine, other = [], []
     for part in range(PARTS):
-        context = merge(part, zh, *folded[part], near, stat)
+        context = merge(part, zh, *folded[part], near, stat, gone)
         context = jnp.broadcast_to(context[None], (n_zl,) + context.shape)
         mine.append(lax.all_to_all(context, "zl", split_axis=0, concat_axis=0, tiled=True))
         other.append(lax.ppermute(mine[part], "core", flip))

time: 214 us -> 200 us (0.935)
  waiting for transfers between devices: 54.2 us -> 44.4 us
  starting transfers between devices: 84.1 us -> 75.3 us
  local copies, waits for them, and re-layouts: 9.58 us -> 15 us
  Pallas kernels: 28.8 us -> 26.4 us
    all_to_all x1, waiting for transfers between devices: 25.1 us -> 6.11 us  [over_x(): return lax.all_to_all(x, 'x', split_axis=0, concat_axis=0, tiled=True)]
    all_to_all x2, starting transfers between devices: 21.8 us -> 9.15 us  [on_device(): lax.all_to_all(context, 'zl', split_axis=0, concat_axis=0, tiled=True)]
    all_gather x1, waiting for transfers between devices: 0.01 us -> 7.6 us  [on_device(): pool = lax.all_gather(paired, 'y', axis=0, tiled=True)]
    unnamed x34 -> x32, local copies, waits for them, and re-layouts: 5.55 us -> 10.5 us
    pallas_call x3, Pallas kernels: 8.88 us -> 4.74 us  [project(): pl.pallas_call(functools.partial(project_kernel, len(contexts), finish is...]
    ppermute x3 -> x4, starting transfers between devices: 24.9 us -> 28.5 us  [the longest x2 15.1 us: on_device(): folded.append((got, lax.ppermute(gone, 'zh', flip)))]
    ppermute x1, waiting for transfers between devices: 2.13 us -> 5.04 us  [on_device(): other_zh = lax.ppermute(out_weight.T, SEQ + TP, moves(1))]
    ppermute x1, starting transfers between devices: 10.4 us -> 7.73 us  [on_device(): other_zh = lax.ppermute(out_weight.T, SEQ + TP, moves(1))]
  transfers between devices with their start and end apart: 14 -> 15, of which waited for: 8 -> 8; matrix products, arithmetic and copies ran while one was open for 2% -> 4% of each run, Pallas kernels for 12% -> 12%
where the time goes in v5:
time: 200 us; the launch traced here: 199 us
  starting transfers between devices  75.3 us (38%)
  waiting for transfers between devices  44.4 us (22%)
  Pallas kernels  26.4 us (13%)
  blocking collectives  17.6 us (9%)
  between operations  15.1 us (8%)
  local copies, waits for them, and re-layouts  15 us (8%)
  other arithmetic  4.69 us (2%)
    pallas_call x2, Pallas kernels, serve(): pl.pallas_call(serve_kernel, grid_spec=pltpu.PrefetchScalarGridSpec(num_s...  15.9 us
    ppermute x2, starting transfers between devices, on_device(): folded.append((got, lax.ppermute(gone, 'zh', flip)))  15.1 us
    ppermute x2, starting transfers between devices, on_device(): other.append(lax.ppermute(mine[part], 'core', flip))  12.6 us
    ppermute x1, starting transfers between devices, on_device(): lax.ppermute(queries, 'zh', flip)  11.5 us
    unnamed x32, local copies, waits for them, and re-layouts  10.5 us
    all_to_all x1, blocking collectives, over_x(): return lax.all_to_all(x, 'x', split_axis=0, concat_axis=0, tiled=True)  10 us
    ppermute x2, waiting for transfers between devices, on_device(): folded.append((got, lax.ppermute(gone, 'zh', flip)))  9.54 us
    all_to_all x2, starting transfers between devices, on_device(): lax.all_to_all(context, 'zl', split_axis=0, concat_axis=0, tiled=True)  9.15 us
  transfers between devices with their start and end apart: 15, of which 8 were waited for; matrix products, arithmetic and copies ran while one was open for 4% of the time, Pallas kernels for 12%

profile of v5, /device:TPU:1, one launch (start us, length us, event | category | flops | bytes accessed | tf_op | source)
XLA Modules:
  0.0 198.6 jit_solution(13291003154103089499)
XLA Ops:
  6.5 2.0 pad_maximum_fusion.1
  8.5 11.5 %collective-permute-start = (bf16[256,512]{1,0:T(8,128)(2,1)}, bf16[256,512]{1,0:T(8,128)(2,1)S(1)}, u32[]{:S(2)}, u32[]{:S(2)}) collective-permute-start(bf16[256,512]{1,0:T(8,128)(2,1)} %q_ref.1), channel_id=1, source_target_pairs={{0,8},{8,0},{1,9},{9,1},{2,10},{10,2},{3,11},{11,3},{4,12},{12,4},... | collective-permute-start | bytes 786440 | tf_op jit(solution)/shard_map/ppermute | solution.py:437
  20.0 0.8 copy.22
  20.8 0.1 reshape.409
  20.9 0.2 convert_reduce_fusion
  21.1 0.8 copy.23
  21.8 0.1 broadcast_in_dim.53
  21.9 0.1 select_reduce_fusion
  22.1 1.9 collective-permute-start.1
  24.0 1.0 maximum_bitcast_fusion
  25.0 5.5 %collective-permute-done.1 = bf16[8,512]{1,0:T(8,128)(2,1)S(1)} collective-permute-done((bf16[8,512]{1,0:T(8,128)(2,1)S(1)}, bf16[8,512]{1,0:T(8,128)(2,1)S(1)}, u32[]{:S(2)}, u32[]{:S(2)}) %collective-permute-start.1) | collective-permute-done | bytes 8224 | tf_op jit(solution)/shard_map/ppermute | solution.py:437
  30.6 1.6 broadcast_in_dim.57
  32.2 4.1 %all-to-all-start = ((bf16[4,2,264,512]{3,2,1,0:T(8,128)(2,1)}), bf16[4,2,264,512]{3,2,1,0:T(8,128)(2,1)S(1)}, u32[]{:S(2)}, u32[]{:S(2)}) async-start(bf16[4,2,264,512]{3,2,1,0:T(8,128)(2,1)} %broadcast_in_dim.57), calls=%async_computation | async-start | bytes 4325376 | tf_op jit(solution)/shard_map/all_to_all | solution.py:433
  36.3 5.6 %collective-permute-start.4 = (bf16[64,512]{1,0:T(8,128)(2,1)S(1)}, bf16[64,512]{1,0:T(8,128)(2,1)S(1)}, u32[]{:S(2)}, u32[]{:S(2)}) collective-permute-start(bf16[64,512]{1,0:T(8,128)(2,1)S(1)} %bitcast.30), channel_id=1, source_target_pairs={{0,0},{1,64},{2,128},{3,192},{4,256},{5,320},{6,384},{7,448},{8,8}... | collective-permute-start | bytes 196616 | tf_op jit(solution)/shard_map/ppermute | solution.py:399
  41.9 7.7 %collective-permute-start.5 = (bf16[64,512]{1,0:T(8,128)(2,1)S(1)}, bf16[64,512]{1,0:T(8,128)(2,1)S(1)}, u32[]{:S(2)}, u32[]{:S(2)}) collective-permute-start(bf16[64,512]{1,0:T(8,128)(2,1)S(1)} %bitcast.31), channel_id=1, source_target_pairs={{0,8},{1,72},{2,136},{3,200},{4,264},{5,328},{6,392},{7,456},{8,0}... | collective-permute-start | bytes 196616 | tf_op jit(solution)/shard_map/ppermute | solution.py:400
  49.6 5.0 %collective-permute-done.5 = bf16[64,512]{1,0:T(8,128)(2,1)S(1)} collective-permute-done((bf16[64,512]{1,0:T(8,128)(2,1)S(1)}, bf16[64,512]{1,0:T(8,128)(2,1)S(1)}, u32[]{:S(2)}, u32[]{:S(2)}) %collective-permute-start.5) | collective-permute-done | bytes 65568 | tf_op jit(solution)/shard_map/ppermute | solution.py:400
  54.7 6.1 %all-to-all-done.q_ref = bf16[4,2,264,512]{3,2,1,0:T(8,128)(2,1)S(1)} async-done(((bf16[4,2,264,512]{3,2,1,0:T(8,128)(2,1)}), bf16[4,2,264,512]{3,2,1,0:T(8,128)(2,1)S(1)}, u32[]{:S(2)}, u32[]{:S(2)}) %all-to-all-start) | async-done | bytes 2162720 | tf_op jit(solution)/shard_map/all_to_all | solution.py:433
  60.8 0.5 slice.29
  62.1 10.0 %all_to_all.35 = bf16[4,128,512]{2,1,0:T(8,128)(2,1)} all-to-all(bf16[4,128,512]{2,1,0:T(8,128)(2,1)S(1)} %broadcast_in_dim.62), channel_id=1, replica_groups=mesh['y'=8,'x'=4,'zh'=2,'zl'=4,'core'=2] {'x'}, dimensions={0} | all-to-all | bytes 1048576 | tf_op jit(solution)/shard_map/all_to_all | solution.py:433
  72.2 0.1 pad.10.clone
  72.2 0.1 pad.14.clone
  72.4 0.1 reshape_squeeze.3
  72.5 0.1 compare_select_fusion
  72.6 0.1 pad_add_fusion.1
  72.7 0.1 reshape.411.mark_ref
  72.8 0.1 pad_add_fusion
  72.8 0.1 reshape.410.row_ref
  72.9 7.6 %all-gather.3.cloned.1.call-done.key_ref.value_ref = bf16[2048,1024]{1,0:T(8,128)(2,1)} async-done(((bf16[256,1024]{1,0:T(8,128)(2,1)}), bf16[2048,1024]{1,0:T(8,128)(2,1)}) %all-gather.3.cloned.1.call-update) | async-done | bytes 4194320 | tf_op jit(solution)/shard_map/all_gather | solution.py:389
  80.5 7.9 %serve.3 = bf16[8,272,256]{2,1,0:T(8,128)(2,1)S(1)} custom-call(s32[160]{0:T(256)S(1)} %reshape.410.row_ref, s32[160]{0:T(256)S(1)} %reshape.411.mark_ref, s32[1]{0:T(128)} %bitcast.2.zh_ref, bf16[4,2,264,512]{3,2,1,0:T(8,128)(2,1)S(1)} %all-to-all-done.q_ref, bf16[2048,1024]{1,0:T(8,128)(2,1)} %all-gather.3.cloned.1.call-done.key_ref.value_ref, ...), custom_call_target="tpu_custom_call" | custom-call | flops 671088640 | bytes 4194304 | tf_op jit(solution)/shard_map/serve/pallas_call | solution.py:93
  88.4 1.1 copy-done.3
  89.5 4.0 %all-to-all-start.4 = ((bf16[4,2,272,256]{3,2,1,0:T(8,128)(2,1)}), bf16[4,2,272,256]{3,2,1,0:T(8,128)(2,1)S(1)}, u32[]{:S(2)}, u32[]{:S(2)}) async-start(bf16[4,2,272,256]{3,2,1,0:T(8,128)(2,1)} %bitcast.27), calls=%async_computation.4 | async-start | bytes 2228224 | tf_op jit(solution)/shard_map/all_to_all | solution.py:491
  93.5 8.0 %serve.2 = bf16[8,272,256]{2,1,0:T(8,128)(2,1)S(1)} custom-call(s32[160]{0:T(256)S(1)} %reshape.410.row_ref, s32[160]{0:T(256)S(1)} %reshape.411.mark_ref, s32[1]{0:T(128)} %bitcast.2.zh_ref, bf16[4,2,264,512]{3,2,1,0:T(8,128)(2,1)S(1)} %all-to-all-done.q_ref, bf16[2048,1024]{1,0:T(8,128)(2,1)} %all-gather.3.cloned.1.call-done.key_ref.value_ref, ...), custom_call_target="tpu_custom_call" | custom-call | flops 671088640 | bytes 4194304 | tf_op jit(solution)/shard_map/serve/pallas_call | solution.py:93
  101.5 1.1 copy-done.2
  102.6 5.8 %all-to-all-done.4.got_ref = bf16[4,2,272,256]{3,2,1,0:T(8,128)(2,1)S(1)} async-done(((bf16[4,2,272,256]{3,2,1,0:T(8,128)(2,1)}), bf16[4,2,272,256]{3,2,1,0:T(8,128)(2,1)S(1)}, u32[]{:S(2)}, u32[]{:S(2)}) %all-to-all-start.4) | async-done | bytes 1114144 | tf_op jit(solution)/shard_map/all_to_all | solution.py:491
  108.4 3.7 %all-to-all-start.1 = ((bf16[4,2,272,256]{3,2,1,0:T(8,128)(2,1)}), bf16[4,2,272,256]{3,2,1,0:T(8,128)(2,1)S(1)}, u32[]{:S(2)}, u32[]{:S(2)}) async-start(bf16[4,2,272,256]{3,2,1,0:T(8,128)(2,1)} %bitcast.26), calls=%async_computation.1 | async-start | bytes 2228224 | tf_op jit(solution)/shard_map/all_to_all | solution.py:491
  112.7 0.1 pad_add_fusion.2.where_ref
  112.8 0.8 keep.1._.refs_3_
  113.5 1.2 fold.3
  114.7 7.7 %collective-permute-start.6 = (bf16[272,256]{1,0:T(8,128)(2,1)}, bf16[272,256]{1,0:T(8,128)(2,1)}, u32[]{:S(2)}, u32[]{:S(2)}) collective-permute-start(bf16[272,256]{1,0:T(8,128)(2,1)} %fold.3), channel_id=1, source_target_pairs={{0,8},{8,0},{1,9},{9,1},{2,10},{10,2},{3,11},{11,3},{4,12},{12,4},... | collective-permute-start | bytes 417800 | tf_op jit(solution)/shard_map/ppermute | solution.py:493
  122.5 0.9 copy-done.7
  123.4 0.9 copy-done.8
  124.4 1.0 local.1
  125.4 0.8 copy-done.4
  126.2 0.5 fold.2._
  126.8 0.2 collective-permute-done.6.far_ref
  126.9 1.1 copy-done.5
  128.0 1.6 merge.3
  129.6 0.9 broadcast_in_dim.63
  130.4 3.5 %all-to-all-start.5 = ((bf16[4,256,256]{2,1,0:T(8,128)(2,1)}), bf16[4,256,256]{2,1,0:T(8,128)(2,1)S(1)}, u32[]{:S(2)}, u32[]{:S(2)}) async-start(bf16[4,256,256]{2,1,0:T(8,128)(2,1)} %broadcast_in_dim.63), calls=%async_computation.5 | async-start | bytes 1048576 | tf_op jit(solution)/shard_map/all_to_all | solution.py:498
  133.9 7.4 %collective-permute-start.2 = (bf16[272,256]{1,0:T(8,128)(2,1)S(1)}, bf16[272,256]{1,0:T(8,128)(2,1)S(1)}, u32[]{:S(2)}, u32[]{:S(2)}) collective-permute-start(bf16[272,256]{1,0:T(8,128)(2,1)S(1)} %fold.2._), channel_id=1, source_target_pairs={{0,8},{8,0},{1,9},{9,1},{2,10},{10,2},{3,11},{11,3},{4,12},{12,4},... | collective-permute-start | bytes 417800 | tf_op jit(solution)/shard_map/ppermute | solution.py:493
  141.3 9.4 %collective-permute-done.2.far_ref = bf16[272,256]{1,0:T(8,128)(2,1)S(1)} collective-permute-done((bf16[272,256]{1,0:T(8,128)(2,1)S(1)}, bf16[272,256]{1,0:T(8,128)(2,1)S(1)}, u32[]{:S(2)}, u32[]{:S(2)}) %collective-permute-start.2) | collective-permute-done | bytes 139296 | tf_op jit(solution)/shard_map/ppermute | solution.py:493
  150.7 0.6 merge.2
  151.3 0.9 broadcast_in_dim.61
  152.2 5.7 %all-to-all-start.2 = ((bf16[4,256,256]{2,1,0:T(8,128)(2,1)}), bf16[4,256,256]{2,1,0:T(8,128)(2,1)S(1)}, u32[]{:S(2)}, u32[]{:S(2)}) async-start(bf16[4,256,256]{2,1,0:T(8,128)(2,1)} %broadcast_in_dim.61), calls=%async_computation.2 | async-start | bytes 1048576 | tf_op jit(solution)/shard_map/all_to_all | solution.py:498
  157.9 6.1 %collective-permute-start.7 = (bf16[4,256,256]{2,1,0:T(8,128)(2,1)S(1)}, bf16[4,256,256]{2,1,0:T(8,128)(2,1)S(1)}, u32[]{:S(2)}, u32[]{:S(2)}) collective-permute-start(bf16[4,256,256]{2,1,0:T(8,128)(2,1)S(1)} %all-to-all-done.5.refs_0_), channel_id=1, source_target_pairs={{0,1},{1,0},{2,3},{3,2},{4,5},{5,4},{6,7},{7,6},{8,9},{9,8},{10,11... | collective-permute-start | bytes 1572872 | tf_op jit(solution)/shard_map/ppermute | solution.py:499
  164.0 4.7 %all-to-all-done.2.refs_0_ = bf16[4,256,256]{2,1,0:T(8,128)(2,1)S(1)} async-done(((bf16[4,256,256]{2,1,0:T(8,128)(2,1)}), bf16[4,256,256]{2,1,0:T(8,128)(2,1)S(1)}, u32[]{:S(2)}, u32[]{:S(2)}) %all-to-all-start.2) | async-done | bytes 524320 | tf_op jit(solution)/shard_map/all_to_all | solution.py:498
  168.7 6.5 %collective-permute-start.3 = (bf16[4,256,256]{2,1,0:T(8,128)(2,1)S(1)}, bf16[4,256,256]{2,1,0:T(8,128)(2,1)S(1)}, u32[]{:S(2)}, u32[]{:S(2)}) collective-permute-start(bf16[4,256,256]{2,1,0:T(8,128)(2,1)S(1)} %all-to-all-done.2.refs_0_), channel_id=1, source_target_pairs={{0,1},{1,0},{2,3},{3,2},{4,5},{5,4},{6,7},{7,6},{8,9},{9,8},{10,11... | collective-permute-start | bytes 1572872 | tf_op jit(solution)/shard_map/ppermute | solution.py:499
  175.3 2.2 %copy-done = bf16[4096,512]{1,0:T(8,128)(2,1)S(1)} copy-done((bf16[4096,512]{1,0:T(8,128)(2,1)S(1)}, bf16[4096,512]{1,0:T(8,128)(2,1)}, u32[]{:S(2)}) %copy-start) | copy-done | bytes 4194328
  177.5 1.3 project.3.refs_2_
  178.7 0.9 copy-done.1
  179.6 1.0 project.4.refs_2_
  180.7 2.4 %project.5 = (f32[256,512]{1,0:T(8,128)S(1)}, f32[256,128]{1,0:T(8,128)S(1)}) custom-call(s32[3]{0:T(128)S(1)} %pad_add_fusion.2.where_ref, bf16[4,256,256]{2,1,0:T(8,128)(2,1)S(1)} %collective-permute-done.3.refs_0_, bf16[4,2,512,512]{3,2,1,0:T(8,128)(2,1)} %bitcast.22, f32[256,512]{1,0:T(8,128)S(1)} %project.4.refs_2_, f32[256,512]{1,0:T(8,128)S(1)} %keep.1._.refs_3_, ...), custom_call_target="tpu_custom_call" | custom-call | flops 268435456 | bytes 2097152 | tf_op jit(solution)/shard_map/project/pallas_call | solution.py:343
  183.3 7.6 %all_to_all.36 = f32[8,2,256]{2,1,0:T(2,128)S(1)} all-to-all(f32[8,2,256]{2,1,0:T(2,128)S(1)} %broadcast_in_dim.64), channel_id=1, replica_groups=mesh['y'=8,'x'=4,'zh'=2,'zl'=4,'core'=2] {'zl','core'}, dimensions={0} | all-to-all | bytes 32768 | tf_op jit(solution)/shard_map/all_to_all | solution.py:507
  190.9 0.9 add_convert_fusion
  (56 shorter events, 0.6 us)
Async XLA Ops:
  6.5 74.0 %all-gather.3.cloned.1.call-start = ((), (), s32[]{:S(2)}) async-start(), calls=%async_computation.7 | async-start | bytes 4718592 | tf_op jit(solution)/shard_map/all_gather | solution.py:389
  8.5 22.0 %collective-permute-start = (bf16[256,512]{1,0:T(8,128)(2,1)}, bf16[256,512]{1,0:T(8,128)(2,1)S(1)}, u32[]{:S(2)}, u32[]{:S(2)}) collective-permute-start(bf16[256,512]{1,0:T(8,128)(2,1)} %q_ref.1), channel_id=1, source_target_pairs={{0,8},{8,0},{1,9},{9,1},{2,10},{10,2},{3,11},{11,3},{4,12},{12,4},... | collective-permute-start | bytes 786440 | tf_op jit(solution)/shard_map/ppermute | solution.py:437
  22.1 8.4 %collective-permute-start.1 = (bf16[8,512]{1,0:T(8,128)(2,1)S(1)}, bf16[8,512]{1,0:T(8,128)(2,1)S(1)}, u32[]{:S(2)}, u32[]{:S(2)}) collective-permute-start(bf16[8,512]{1,0:T(8,128)(2,1)S(1)} %pad.4), channel_id=1, source_target_pairs={{0,8},{8,0},{1,9},{9,1},{2,10},{10,2},{3,11},{11,3},{4,12},{12,4},... | collective-permute-start | bytes 24584 | tf_op jit(solution)/shard_map/ppermute | solution.py:437
  32.2 4.1 %copy-start.14 = (bf16[512,64]{0,1:T(8,128)(2,1)S(1)}, bf16[512,64]{0,1:T(8,128)(2,1)}, u32[]{:S(2)}) copy-start(bf16[512,64]{0,1:T(8,128)(2,1)} %param.16) | copy-start | bytes 196612
  32.2 28.7 %all-to-all-start = ((bf16[4,2,264,512]{3,2,1,0:T(8,128)(2,1)}), bf16[4,2,264,512]{3,2,1,0:T(8,128)(2,1)S(1)}, u32[]{:S(2)}, u32[]{:S(2)}) async-start(bf16[4,2,264,512]{3,2,1,0:T(8,128)(2,1)} %broadcast_in_dim.57), calls=%async_computation | async-start | bytes 4325376 | tf_op jit(solution)/shard_map/all_to_all | solution.py:433
  36.3 35.9 %copy-start.13 = (s32[2]{0:T(128)S(1)}, s32[2]{0:T(128)}, u32[]{:S(2)}) copy-start(s32[2]{0:T(128)} %param.19) | copy-start | bytes 28
  36.3 139.0 %all-gather.5.cloned.1.call-start = ((), (), s32[]{:S(2)}) async-start(), calls=%async_computation.8 | async-start | bytes 4718592 | tf_op jit(solution)/shard_map/all_gather | solution.py:442
  36.3 13.4 %collective-permute-start.4 = (bf16[64,512]{1,0:T(8,128)(2,1)S(1)}, bf16[64,512]{1,0:T(8,128)(2,1)S(1)}, u32[]{:S(2)}, u32[]{:S(2)}) collective-permute-start(bf16[64,512]{1,0:T(8,128)(2,1)S(1)} %bitcast.30), channel_id=1, source_target_pairs={{0,0},{1,64},{2,128},{3,192},{4,256},{5,320},{6,384},{7,448},{8,8}... | collective-permute-start | bytes 196616 | tf_op jit(solution)/shard_map/ppermute | solution.py:399
  41.9 12.8 %collective-permute-start.5 = (bf16[64,512]{1,0:T(8,128)(2,1)S(1)}, bf16[64,512]{1,0:T(8,128)(2,1)S(1)}, u32[]{:S(2)}, u32[]{:S(2)}) collective-permute-start(bf16[64,512]{1,0:T(8,128)(2,1)S(1)} %bitcast.31), channel_id=1, source_target_pairs={{0,8},{1,72},{2,136},{3,200},{4,264},{5,328},{6,392},{7,456},{8,0}... | collective-permute-start | bytes 196616 | tf_op jit(solution)/shard_map/ppermute | solution.py:400
  88.4 1.1 copy-start.3
  89.5 18.9 %all-to-all-start.4 = ((bf16[4,2,272,256]{3,2,1,0:T(8,128)(2,1)}), bf16[4,2,272,256]{3,2,1,0:T(8,128)(2,1)S(1)}, u32[]{:S(2)}, u32[]{:S(2)}) async-start(bf16[4,2,272,256]{3,2,1,0:T(8,128)(2,1)} %bitcast.27), calls=%async_computation.4 | async-start | bytes 2228224 | tf_op jit(solution)/shard_map/all_to_all | solution.py:491
  101.5 1.1 copy-start.2
  102.6 10.2 %copy-start.10 = (s32[16]{0:T(128)S(1)}, s32[16]{0:T(128)}, u32[]{:S(2)}) copy-start(s32[16]{0:T(128)} %drop_ref.1) | copy-start | bytes 196
  108.4 14.1 %copy-start.6 = (bf16[256,512]{1,0:T(8,128)(2,1)S(1)}, bf16[256,512]{1,0:T(8,128)(2,1)}, u32[]{:S(2)}) copy-start(bf16[256,512]{1,0:T(8,128)(2,1)} %q_ref.1) | copy-start | bytes 786436
  108.4 17.8 %all-to-all-start.1 = ((bf16[4,2,272,256]{3,2,1,0:T(8,128)(2,1)}), bf16[4,2,272,256]{3,2,1,0:T(8,128)(2,1)S(1)}, u32[]{:S(2)}, u32[]{:S(2)}) async-start(bf16[4,2,272,256]{3,2,1,0:T(8,128)(2,1)} %bitcast.26), calls=%async_computation.1 | async-start | bytes 2228224 | tf_op jit(solution)/shard_map/all_to_all | solution.py:491
  114.7 12.2 %collective-permute-start.6 = (bf16[272,256]{1,0:T(8,128)(2,1)}, bf16[272,256]{1,0:T(8,128)(2,1)}, u32[]{:S(2)}, u32[]{:S(2)}) collective-permute-start(bf16[272,256]{1,0:T(8,128)(2,1)} %fold.3), channel_id=1, source_target_pairs={{0,8},{8,0},{1,9},{9,1},{2,10},{10,2},{3,11},{11,3},{4,12},{12,4},... | collective-permute-start | bytes 417800 | tf_op jit(solution)/shard_map/ppermute | solution.py:493
  122.5 1.0 copy-start.7
  123.4 0.9 copy-start.8
  125.4 0.8 copy-start.4
  126.9 1.1 copy-start.5
  130.4 20.9 %all-to-all-start.5 = ((bf16[4,256,256]{2,1,0:T(8,128)(2,1)}), bf16[4,256,256]{2,1,0:T(8,128)(2,1)S(1)}, u32[]{:S(2)}, u32[]{:S(2)}) async-start(bf16[4,256,256]{2,1,0:T(8,128)(2,1)} %broadcast_in_dim.63), calls=%async_computation.5 | async-start | bytes 1048576 | tf_op jit(solution)/shard_map/all_to_all | solution.py:498
  133.9 16.8 %collective-permute-start.2 = (bf16[272,256]{1,0:T(8,128)(2,1)S(1)}, bf16[272,256]{1,0:T(8,128)(2,1)S(1)}, u32[]{:S(2)}, u32[]{:S(2)}) collective-permute-start(bf16[272,256]{1,0:T(8,128)(2,1)S(1)} %fold.2._), channel_id=1, source_target_pairs={{0,8},{8,0},{1,9},{9,1},{2,10},{10,2},{3,11},{11,3},{4,12},{12,4},... | collective-permute-start | bytes 417800 | tf_op jit(solution)/shard_map/ppermute | solution.py:493
  152.2 16.5 %all-to-all-start.2 = ((bf16[4,256,256]{2,1,0:T(8,128)(2,1)}), bf16[4,256,256]{2,1,0:T(8,128)(2,1)S(1)}, u32[]{:S(2)}, u32[]{:S(2)}) async-start(bf16[4,256,256]{2,1,0:T(8,128)(2,1)} %broadcast_in_dim.61), calls=%async_computation.2 | async-start | bytes 1048576 | tf_op jit(solution)/shard_map/all_to_all | solution.py:498
  157.9 17.4 %collective-permute-start.7 = (bf16[4,256,256]{2,1,0:T(8,128)(2,1)S(1)}, bf16[4,256,256]{2,1,0:T(8,128)(2,1)S(1)}, u32[]{:S(2)}, u32[]{:S(2)}) collective-permute-start(bf16[4,256,256]{2,1,0:T(8,128)(2,1)S(1)} %all-to-all-done.5.refs_0_), channel_id=1, source_target_pairs={{0,1},{1,0},{2,3},{3,2},{4,5},{5,4},{6,7},{7,6},{8,9},{9,8},{10,11... | collective-permute-start | bytes 1572872 | tf_op jit(solution)/shard_map/ppermute | solution.py:499
  168.7 12.0 %collective-permute-start.3 = (bf16[4,256,256]{2,1,0:T(8,128)(2,1)S(1)}, bf16[4,256,256]{2,1,0:T(8,128)(2,1)S(1)}, u32[]{:S(2)}, u32[]{:S(2)}) collective-permute-start(bf16[4,256,256]{2,1,0:T(8,128)(2,1)S(1)} %all-to-all-done.2.refs_0_), channel_id=1, source_target_pairs={{0,1},{1,0},{2,3},{3,2},{4,5},{5,4},{6,7},{7,6},{8,9},{9,8},{10,11... | collective-permute-start | bytes 1572872 | tf_op jit(solution)/shard_map/ppermute | solution.py:499
  175.3 2.2 %copy-start = (bf16[4096,512]{1,0:T(8,128)(2,1)S(1)}, bf16[4096,512]{1,0:T(8,128)(2,1)}, u32[]{:S(2)}) copy-start(bf16[4096,512]{1,0:T(8,128)(2,1)} %all-gather.5.cloned.1.call-done) | copy-start | bytes 12582916
  177.5 2.2 %copy-start.1 = (bf16[4096,512]{1,0:T(8,128)(2,1)S(1)}, bf16[4096,512]{1,0:T(8,128)(2,1)}, u32[]{:S(2)}) copy-start(bf16[4096,512]{1,0:T(8,128)(2,1)} %all-gather.5.cloned.1.call-done) | copy-start | bytes 12582916
  179.6 1.1 copy-start.9
  180.7 10.3 %copy-start.11 = (f32[512]{0:T(512)S(1)}, f32[512]{0:T(512)}, u32[]{:S(2)}) copy-start(f32[512]{0:T(512)} %param.18) | copy-start | bytes 6148
  180.7 10.2 %copy-start.12 = (f32[512]{0:T(512)S(1)}, f32[512]{0:T(512)}, u32[]{:S(2)}) copy-start(f32[512]{0:T(512)} %param.17) | copy-start | bytes 6148
Sparse Core Ops, SparseCore 0:
  9.4 71.0 all-gather.2
  82.6 55.4 all-gather.4

commit v6 on v5

--- a/solution.py
+++ b/solution.py
@@ -1,4 +1,5 @@
 import functools
+import math
 
 import jax
 import jax.numpy as jnp
@@ -22,6 +23,7 @@
 PARTS = 2
 STAT_ROWS = 16
 NEG = -1e30
+EMPTY = -1e20
 VMEM_LIMIT = 48 * 1024 * 1024
 
 
@@ -29,19 +31,23 @@
     return pl.BlockSpec(shape, lambda *a: (0,) * len(shape))
 
 
-def params():
-    return pltpu.CompilerParams(vmem_limit_bytes=VMEM_LIMIT)
+def params(limit=VMEM_LIMIT):
+    return pltpu.CompilerParams(vmem_limit_bytes=limit)
 
 
 def partial(scores, listed, values):
     scores = jnp.where(listed, scores, NEG)
-    top = jnp.max(scores, axis=0, keepdims=True)
-    expo = jnp.where(listed, jnp.exp(scores - top), 0.0)
+    top = jnp.maximum(jnp.max(scores, axis=0, keepdims=True), EMPTY)
+    expo = weight_of(scores, top)
     total = jnp.sum(expo, axis=0, keepdims=True)
     got = lax.dot_general(
-        expo.astype(BF), values, (((0,), (0,)), ((), ())), preferred_element_type=F32
+        values, expo.astype(BF), (((0,), (0,)), ((), ())), preferred_element_type=F32
     )
     return top, total, got
+
+
+def weight_of(score, top):
+    return jnp.exp2((score - top) * jnp.float32(math.log2(math.e) / DH**0.5))
 
 
 def dot_t(a, b):
@@ -61,7 +67,6 @@
     rows = q_ref.shape[2]
     wide = q_ref.shape[3]
     listings = row_ref.shape[0] // pl.num_programs(0)
-    scale = jnp.float32(1.0 / DH**0.5)
     block_of = lax.broadcasted_iota(jnp.int32, (BLOCK, rows), 1) // BLOCK
     places, listed = [], []
     for i in range(listings):
@@ -75,13 +80,11 @@
         lanes = slice(h * DH, (h + 1) * DH)
         keys = jnp.concatenate([key_ref[p, lanes] for p in places], axis=0)
         values = jnp.concatenate([value_ref[p, lanes] for p in places], axis=0)
-        top, total, got = partial(
-            dot_t(keys, q_ref[0, 0, :, lanes]) * scale, listed, values
-        )
-        out_ref[0, :rows, lanes] = got.astype(BF)
+        top, total, got = partial(dot_t(keys, q_ref[0, 0, :, lanes]), listed, values)
+        out_ref[0, lanes, :] = got.astype(BF)
         stats += split(top, 3) + split(total, 2)
     stats.append(jnp.zeros((STAT_ROWS - len(stats), rows), BF))
-    out_ref[0, rows:, :] = jnp.concatenate([x.astype(F32) for x in stats], axis=0).astype(BF)
+    out_ref[0, wide:, :] = jnp.concatenate([x.astype(F32) for x in stats], axis=0).astype(BF)
 
 
 def serve(part, row, mark, zh, q, pool, out_rows):
@@ -89,7 +92,7 @@
     wide = q.shape[3] // PARTS
     rows = out_rows
     peers = 2 * n_x
-    out = (peers, rows + STAT_ROWS, wide)
+    out = (peers, wide + STAT_ROWS, rows)
     return pl.pallas_call(
         serve_kernel,
         grid_spec=pltpu.PrefetchScalarGridSpec(
@@ -118,7 +121,6 @@
 def local_kernel(q_ref, k_ref, v_ref, out_ref, stat_ref):
     rows = q_ref.shape[0]
     heads = q_ref.shape[1] // DH
-    scale = jnp.float32(1.0 / DH**0.5)
     key_block = lax.broadcasted_iota(jnp.int32, (rows, rows), 0) // BLOCK
     query_block = lax.broadcasted_iota(jnp.int32, (rows, rows), 1) // BLOCK
     listed = jnp.abs(key_block - query_block) <= 1
@@ -126,131 +128,118 @@
     for h in range(heads):
         lanes = slice(h * DH, (h + 1) * DH)
         top, total, got = partial(
-            dot_t(k_ref[:, lanes], q_ref[:, lanes]) * scale, listed, v_ref[:, lanes]
+            dot_t(k_ref[:, lanes], q_ref[:, lanes]), listed, v_ref[:, lanes]
         )
-        out_ref[:, lanes] = got
+        out_ref[lanes, :] = got
         tops.append(top)
         totals.append(total)
     stat_ref[...] = jnp.concatenate(tops + totals, axis=0)
 
 
-def local(q, k, v):
-    rows, width = q.shape
-    stat = (2 * (width // DH), rows)
+def local(part, q, k, v):
+    rows = q.shape[0]
+    wide = q.shape[1] // PARTS
+    stat = (2 * (wide // DH), rows)
     return pl.pallas_call(
         local_kernel,
         grid=(1,),
-        in_specs=[whole(q.shape)] * 3,
-        out_specs=[whole(q.shape), whole(stat)],
-        out_shape=[jax.ShapeDtypeStruct(q.shape, F32), jax.ShapeDtypeStruct(stat, F32)],
+        in_specs=[pl.BlockSpec((rows, wide), lambda i: (0, part))] * 3,
+        out_specs=[whole((wide, rows)), whole(stat)],
+        out_shape=[jax.ShapeDtypeStruct((wide, rows), F32), jax.ShapeDtypeStruct(stat, F32)],
         compiler_params=params(),
         cost_estimate=pl.CostEstimate(
-            flops=4 * rows * rows * width,
-            transcendentals=rows * rows * width // DH,
-            bytes_accessed=2 << 20,
+            flops=4 * rows * rows * wide,
+            transcendentals=rows * rows * wide // DH,
+            bytes_accessed=1 << 20,
         ),
         name="local",
     )(q, k, v)
 
 
-def stats_of(block, rows, h):
-    stats = block[rows:, :].astype(F32)
+def stats_of(block, wide, h):
+    stats = block[wide:, :].astype(F32)
     at = 5 * h
     top = stats[at : at + 1] + stats[at + 1 : at + 2] + stats[at + 2 : at + 3]
     return top, stats[at + 3 : at + 4] + stats[at + 4 : at + 5]
 
 
-def columns(lines):
-    rows = lines[0].shape[1]
-    lines = lines + [jnp.zeros((DH - len(lines), rows), F32)]
-    return jnp.concatenate(lines, axis=0).T
-
-
 def fold_kernel(zh_ref, got_ref, _, out_ref):
-    peers, _, rows, wide = got_ref.shape
-    rows = rows - STAT_ROWS
-    heads = wide // DH
-    factors, stats = [], []
-    for h in range(heads):
-        pairs = [stats_of(got_ref[s, 0], rows, h) for s in range(peers)]
+    peers, _, wide, rows = got_ref.shape
+    wide = wide - STAT_ROWS
+    stats = []
+    for h in range(wide // DH):
+        lines = slice(h * DH, (h + 1) * DH)
+        pairs = [stats_of(got_ref[s, 0], wide, h) for s in range(peers)]
         top = functools.reduce(jnp.maximum, [t for t, _ in pairs])
-        factor = [jnp.exp(t - top) for t, _ in pairs]
-        total = sum(f * l for f, (_, l) in zip(factor, pairs))
-        factors += factor
+        factors = [weight_of(t, top) for t, _ in pairs]
+        total = sum(f * l for f, (_, l) in zip(factors, pairs))
         stats += split(top, 3) + split(total, 2)
+        out_ref[lines, :] = sum(
+            f * got_ref[s, 0, lines, :].astype(F32) for s, f in enumerate(factors)
+        ).astype(BF)
     stats.append(jnp.zeros((STAT_ROWS - len(stats), rows), BF))
-    out_ref[rows:, :] = jnp.concatenate([x.astype(F32) for x in stats], axis=0).astype(BF)
-    factors = columns(factors)
-    for h in range(heads):
-        lanes = slice(h * DH, (h + 1) * DH)
-        out_ref[:rows, lanes] = sum(
-            factors[:, h * peers + s : h * peers + s + 1] * got_ref[s, 0, :rows, lanes].astype(F32)
-            for s in range(peers)
-        ).astype(BF)
+    out_ref[wide:, :] = jnp.concatenate([x.astype(F32) for x in stats], axis=0).astype(BF)
 
 
 def fold(zh, got, after):
-    peers, _, rows, wide = got.shape
+    peers, _, lines, rows = got.shape
     return pl.pallas_call(
         fold_kernel,
         grid_spec=pltpu.PrefetchScalarGridSpec(
             num_scalar_prefetch=1,
             grid=(1,),
             in_specs=[
-                pl.BlockSpec((peers, 1, rows, wide), lambda i, zh_ref: (0, 1 - zh_ref[0], 0, 0)),
-                pl.BlockSpec(memory_space=pl.ANY),
+                pl.BlockSpec((peers, 1, lines, rows), lambda i, zh_ref: (0, 1 - zh_ref[0], 0, 0)),
+                pl.BlockSpec((BLOCK, DH), lambda i, zh_ref: (0, 0)),
             ],
-            out_specs=whole((rows, wide)),
-        ),
-        out_shape=jax.ShapeDtypeStruct((rows, wide), BF),
+            out_specs=whole((lines, rows)),
+        ),
+        out_shape=jax.ShapeDtypeStruct((lines, rows), BF),
         compiler_params=params(),
         cost_estimate=pl.CostEstimate(
-            flops=2 * peers * rows * wide, transcendentals=0, bytes_accessed=1 << 20
+            flops=2 * peers * rows * lines, transcendentals=0, bytes_accessed=1 << 20
         ),
         name="fold",
     )(zh, got, after)
 
 
-def merge_kernel(first, zh_ref, got_ref, far_ref, near_ref, stat_ref, _, out_ref):
-    peers, _, rows, wide = got_ref.shape
-    rows = rows - STAT_ROWS
+def merge_kernel(zh_ref, got_ref, far_ref, near_ref, stat_ref, _, out_ref):
+    peers, _, wide, rows = got_ref.shape
+    wide = wide - STAT_ROWS
     heads = wide // DH
-    all_heads = stat_ref.shape[0] // 2
-    weights = []
     for h in range(heads):
-        pairs = [stats_of(got_ref[s, 0], rows, h) for s in range(peers)]
-        pairs.append(stats_of(far_ref[...], rows, h))
-        at = first + h
-        pairs.append((stat_ref[at : at + 1, :], stat_ref[all_heads + at : all_heads + at + 1, :]))
+        lines = slice(h * DH, (h + 1) * DH)
+        pairs = [stats_of(got_ref[s, 0], wide, h) for s in range(peers)]
+        pairs.append(stats_of(far_ref[...], wide, h))
+        pairs.append((stat_ref[h : h + 1, :], stat_ref[heads + h : heads + h + 1, :]))
         top = functools.reduce(jnp.maximum, [t for t, _ in pairs])
-        factors = [jnp.exp(t - top) for t, _ in pairs]
+        factors = [weight_of(t, top) for t, _ in pairs]
         total = sum(f * l for f, (_, l) in zip(factors, pairs))
-        weights += [f / total for f in factors]
-    weights = columns(weights)
-    for h in range(heads):
-        lanes = slice(h * DH, (h + 1) * DH)
-        at = h * (peers + 2)
-        total = weights[:, at + peers + 1 : at + peers + 2] * near_ref[:, lanes]
-        total += weights[:, at + peers : at + peers + 1] * far_ref[:rows, lanes].astype(F32)
+        factors = [f / total for f in factors]
+        context = factors[-1] * near_ref[lines, :]
+        context += factors[-2] * far_ref[lines, :].astype(F32)
         for s in range(peers):
-            total += weights[:, at + s : at + s + 1] * got_ref[s, 0, :rows, lanes].astype(F32)
-        out_ref[:, lanes] = total.astype(BF)
-
-
-def merge(part, zh, got, far, near, stat, after):
-    peers, _, rows, wide = got.shape
-    out = (rows - STAT_ROWS, wide)
+            context += factors[s] * got_ref[s, 0, lines, :].astype(F32)
+        context = context.T.astype(BF)
+        for copy in range(out_ref.shape[0]):
+            out_ref[copy, :, lines] = context
+
+
+def merge(zh, got, far, near, stat, after, copies):
+    peers, _, lines, rows = got.shape
+    wide = lines - STAT_ROWS
+    out = (copies, rows, wide)
     return pl.pallas_call(
-        functools.partial(merge_kernel, part * (wide // DH)),
+        merge_kernel,
         grid_spec=pltpu.PrefetchScalarGridSpec(
             num_scalar_prefetch=1,
             grid=(1,),
             in_specs=[
-                pl.BlockSpec((peers, 1, rows, wide), lambda i, zh_ref: (0, zh_ref[0], 0, 0)),
+                pl.BlockSpec((peers, 1, lines, rows), lambda i, zh_ref: (0, zh_ref[0], 0, 0)),
                 whole(far.shape),
-                pl.BlockSpec(out, lambda i, zh_ref: (0, part)),
+                whole(near.shape),
                 whole(stat.shape),
-                pl.BlockSpec(memory_space=pl.ANY),
+                pl.BlockSpec((BLOCK, DH), lambda i, zh_ref: (0, 0)),
             ],
             out_specs=whole(out),
         ),
@@ -260,7 +249,7 @@
             flops=2 * peers * rows * wide, transcendentals=0, bytes_accessed=1 << 20
         ),
         name="merge",
-    )(zh, got, far, near, stat, after)
+    )(zh, got, far, near, stat, after.reshape(-1, after.shape[-1]))
 
 
 def keep_kernel(where_ref, drop_ref, out_ref):
@@ -295,16 +284,29 @@
     )(where, drops)
 
 
-def project_kernel(count, last, where_ref, *refs):
-    contexts, weights = refs[:count], refs[count : 2 * count]
-    rest = refs[2 * count :]
-    acc = sum(
-        dot_t(c_ref[z], w_ref[z, 0])
-        for c_ref, w_ref in zip(contexts, weights)
-        for z in range(c_ref.shape[0])
-    )
-    if len(rest) > 1:
-        acc = acc + rest[0][...]
+def project_kernel(part, shifts, last, where_ref, *refs):
+    count = len(shifts)
+    contexts, w_ref = refs[:count], refs[count]
+    rest, held_ref, sems = refs[count + 1 : -2], refs[-2], refs[-1]
+    half, _, wide = contexts[0].shape
+    copies = []
+    for i, shift in enumerate(shifts):
+        parity = lax.rem(where_ref[0] + shift, 2)
+        for z in range(half):
+            at = i * half + z
+            copies.append(
+                pltpu.make_async_copy(
+                    w_ref.at[z, parity, :, part * wide : (part + 1) * wide],
+                    held_ref.at[at],
+                    sems.at[at],
+                )
+            )
+            copies[-1].start()
+    acc = rest[0][...] if len(rest) > 1 else None
+    for at, copy in enumerate(copies):
+        copy.wait()
+        term = dot_t(contexts[at // half][at % half], held_ref[at])
+        acc = term if acc is None else acc + term
     if not last:
         rest[-1][...] = acc
         return
@@ -323,14 +325,9 @@
     half, rows, wide = contexts[0].shape
     cols = weight.shape[2]
     out = (rows, cols)
-    args = list(contexts) + [weight] * len(contexts)
-    specs = [whole(c.shape) for c in contexts] + [
-        pl.BlockSpec(
-            (half, 1, cols, wide),
-            lambda i, where_ref, shift=shift: (0, (where_ref[0] + shift) % 2, 0, part),
-        )
-        for shift in shifts
-    ]
+    pieces = half * len(contexts)
+    args = list(contexts) + [weight]
+    specs = [whole(c.shape) for c in contexts] + [pl.BlockSpec(memory_space=pltpu.HBM)]
     out_specs, out_shape = [whole(out)], [jax.ShapeDtypeStruct(out, F32)]
     if before is not None:
         args.append(before)
@@ -341,16 +338,21 @@
         out_specs.append(whole((rows, DH)))
         out_shape.append(jax.ShapeDtypeStruct((rows, DH), F32))
     return pl.pallas_call(
-        functools.partial(project_kernel, len(contexts), finish is not None),
+        functools.partial(project_kernel, part, shifts, finish is not None),
         grid_spec=pltpu.PrefetchScalarGridSpec(
-            num_scalar_prefetch=1, grid=(1,), in_specs=specs, out_specs=out_specs
+            num_scalar_prefetch=1,
+            grid=(1,),
+            in_specs=specs,
+            out_specs=out_specs,
+            scratch_shapes=[
+                pltpu.VMEM((pieces, cols, wide), BF),
+                pltpu.SemaphoreType.DMA((pieces,)),
+            ],
         ),
         out_shape=out_shape,
         compiler_params=params(),
         cost_estimate=pl.CostEstimate(
-            flops=2 * rows * half * len(contexts) * wide * cols,
-            transcendentals=0,
-            bytes_accessed=2 << 20,
+            flops=2 * rows * pieces * wide * cols, transcendentals=0, bytes_accessed=2 << 20
         ),
         name="project",
     )(where, *args)
@@ -481,7 +483,7 @@
     ).reshape(-1)
     zh = zh_at[None].astype(jnp.int32)
 
-    near, stat = local(queries, key_rows, value_rows)
+    near = [local(part, queries, key_rows, value_rows) for part in range(PARTS)]
     where = jnp.stack([tp_at % 2, drop_seed[0], tp_at]).astype(jnp.int32)
     kept = keep(where, drop_offsets, residual.shape)
     folded = []
@@ -493,8 +495,7 @@
         folded.append((got, lax.ppermute(gone, "zh", flip)))
     mine, other = [], []
     for part in range(PARTS):
-        context = merge(part, zh, *folded[part], near, stat, gone)
-        context = jnp.broadcast_to(context[None], (n_zl,) + context.shape)
+        context = merge(zh, *folded[part], *near[part], (gone, weight)[part], n_zl)
         mine.append(lax.all_to_all(context, "zl", split_axis=0, concat_axis=0, tiled=True))
         other.append(lax.ppermute(mine[part], "core", flip))
     (acc,) = project(0, (0, 1), where, (mine[0], other[0]), weight)

time: 200 us -> 200 us (level)
  Pallas kernels: 26.4 us -> 29.4 us
  waiting for transfers between devices: 44.4 us -> 41.4 us
    pallas_call x2, Pallas kernels: 15.9 us -> 18.3 us  [serve(): pl.pallas_call(serve_kernel, grid_spec=pltpu.PrefetchScalarGridSpec(num_s...]
    unnamed x32 -> x44, local copies, waits for them, and re-layouts: 10.5 us -> 12.9 us
    ppermute x2, waiting for transfers between devices: 9.54 us -> 7.27 us  [on_device(): folded.append((got, lax.ppermute(gone, 'zh', flip)))]
    pallas_call x6 -> x7, Pallas kernels: 7.95 us -> 9.41 us  [the longest x3 5.85 us: project(): pl.pallas_call(functools.partial(project_kernel, part, shifts, finish is...]
  transfers between devices with their start and end apart: 15 -> 15, of which waited for: 8 -> 9; matrix products, arithmetic and copies ran while one was open for 4% -> 3% of each run, Pallas kernels for 12% -> 14%
where the time goes in v6:
time: 200 us; the launch traced here: 199 us
  starting transfers between devices  75.1 us (38%)
  waiting for transfers between devices  41.4 us (21%)
  Pallas kernels  29.4 us (15%)
  blocking collectives  17.6 us (9%)
  local copies, waits for them, and re-layouts  15.7 us (8%)
  between operations  15.2 us (8%)
  other arithmetic  4.64 us (2%)
    pallas_call x2, Pallas kernels, serve(): pl.pallas_call(serve_kernel, grid_spec=pltpu.PrefetchScalarGridSpec(num_s...  18.3 us
    ppermute x2, starting transfers between devices, on_device(): folded.append((got, lax.ppermute(gone, 'zh', flip)))  14.9 us
    unnamed x44, local copies, waits for them, and re-layouts  12.9 us
    ppermute x2, starting transfers between devices, on_device(): other.append(lax.ppermute(mine[part], 'core', flip))  12.7 us
    ppermute x1, starting transfers between devices, on_device(): lax.ppermute(queries, 'zh', flip)  11.5 us
    all_to_all x1, blocking collectives, over_x(): return lax.all_to_all(x, 'x', split_axis=0, concat_axis=0, tiled=True)  10 us
    all_to_all x2, starting transfers between devices, on_device(): lax.all_to_all(context, 'zl', split_axis=0, concat_axis=0, tiled=True)  9.15 us
    ppermute x1, starting transfers between devices, on_device(): other_zh = lax.ppermute(out_weight.T, SEQ + TP, moves(1))  7.73 us
  transfers between devices with their start and end apart: 15, of which 9 were waited for; matrix products, arithmetic and copies ran while one was open for 3% of the time, Pallas kernels for 14%

profile of v6, /device:TPU:1, one launch (start us, length us, event | category | flops | bytes accessed | tf_op | source)
XLA Modules:
  0.0 199.0 jit_solution(17692646391278228746)
XLA Ops:
  6.5 1.9 pad_maximum_fusion.1
  8.5 11.5 %collective-permute-start = (bf16[256,512]{1,0:T(8,128)(2,1)}, bf16[256,512]{1,0:T(8,128)(2,1)S(1)}, u32[]{:S(2)}, u32[]{:S(2)}) collective-permute-start(bf16[256,512]{1,0:T(8,128)(2,1)} %q_ref.3), channel_id=1, source_target_pairs={{0,8},{8,0},{1,9},{9,1},{2,10},{10,2},{3,11},{11,3},{4,12},{12,4},... | collective-permute-start | bytes 786440 | tf_op jit(solution)/shard_map/ppermute | solution.py:439
  19.9 0.8 copy.22
  20.7 0.1 reshape.407
  20.8 0.2 convert_reduce_fusion
  21.0 0.8 copy.23
  21.8 0.1 broadcast_in_dim.49
  21.9 0.1 select_reduce_fusion
  22.0 1.9 collective-permute-start.1
  23.9 1.0 maximum_bitcast_fusion
  24.9 5.5 %collective-permute-done.1 = bf16[8,512]{1,0:T(8,128)(2,1)S(1)} collective-permute-done((bf16[8,512]{1,0:T(8,128)(2,1)S(1)}, bf16[8,512]{1,0:T(8,128)(2,1)S(1)}, u32[]{:S(2)}, u32[]{:S(2)}) %collective-permute-start.1) | collective-permute-done | bytes 8224 | tf_op jit(solution)/shard_map/ppermute | solution.py:439
  30.5 1.6 broadcast_in_dim.53
  32.1 4.1 %all-to-all-start = ((bf16[4,2,264,512]{3,2,1,0:T(8,128)(2,1)}), bf16[4,2,264,512]{3,2,1,0:T(8,128)(2,1)S(1)}, u32[]{:S(2)}, u32[]{:S(2)}) async-start(bf16[4,2,264,512]{3,2,1,0:T(8,128)(2,1)} %broadcast_in_dim.53), calls=%async_computation | async-start | bytes 4325376 | tf_op jit(solution)/shard_map/all_to_all | solution.py:435
  36.2 5.6 %collective-permute-start.3 = (bf16[64,512]{1,0:T(8,128)(2,1)S(1)}, bf16[64,512]{1,0:T(8,128)(2,1)S(1)}, u32[]{:S(2)}, u32[]{:S(2)}) collective-permute-start(bf16[64,512]{1,0:T(8,128)(2,1)S(1)} %bitcast.29), channel_id=1, source_target_pairs={{0,0},{1,64},{2,128},{3,192},{4,256},{5,320},{6,384},{7,448},{8,8}... | collective-permute-start | bytes 196616 | tf_op jit(solution)/shard_map/ppermute | solution.py:401
  41.8 7.7 %collective-permute-start.4 = (bf16[64,512]{1,0:T(8,128)(2,1)S(1)}, bf16[64,512]{1,0:T(8,128)(2,1)S(1)}, u32[]{:S(2)}, u32[]{:S(2)}) collective-permute-start(bf16[64,512]{1,0:T(8,128)(2,1)S(1)} %bitcast.30), channel_id=1, source_target_pairs={{0,8},{1,72},{2,136},{3,200},{4,264},{5,328},{6,392},{7,456},{8,0}... | collective-permute-start | bytes 196616 | tf_op jit(solution)/shard_map/ppermute | solution.py:402
  49.6 5.0 %collective-permute-done.4 = bf16[64,512]{1,0:T(8,128)(2,1)S(1)} collective-permute-done((bf16[64,512]{1,0:T(8,128)(2,1)S(1)}, bf16[64,512]{1,0:T(8,128)(2,1)S(1)}, u32[]{:S(2)}, u32[]{:S(2)}) %collective-permute-start.4) | collective-permute-done | bytes 65568 | tf_op jit(solution)/shard_map/ppermute | solution.py:402
  54.6 6.1 %all-to-all-done.q_ref = bf16[4,2,264,512]{3,2,1,0:T(8,128)(2,1)S(1)} async-done(((bf16[4,2,264,512]{3,2,1,0:T(8,128)(2,1)}), bf16[4,2,264,512]{3,2,1,0:T(8,128)(2,1)S(1)}, u32[]{:S(2)}, u32[]{:S(2)}) %all-to-all-start) | async-done | bytes 2162720 | tf_op jit(solution)/shard_map/all_to_all | solution.py:435
  60.8 0.5 slice.29
  62.0 10.0 %all_to_all.35 = bf16[4,128,512]{2,1,0:T(8,128)(2,1)} all-to-all(bf16[4,128,512]{2,1,0:T(8,128)(2,1)S(1)} %broadcast_in_dim.57), channel_id=1, replica_groups=mesh['y'=8,'x'=4,'zh'=2,'zl'=4,'core'=2] {'x'}, dimensions={0} | all-to-all | bytes 1048576 | tf_op jit(solution)/shard_map/all_to_all | solution.py:435
  72.4 0.1 reshape_squeeze.3
  72.5 0.1 pad_add_fusion.1
  72.6 0.1 reshape.409.mark_ref
  72.8 0.1 reshape.408.row_ref
  72.9 7.7 %all-gather.3.cloned.1.call-done.key_ref.value_ref = bf16[2048,1024]{1,0:T(8,128)(2,1)} async-done(((bf16[256,1024]{1,0:T(8,128)(2,1)}), bf16[2048,1024]{1,0:T(8,128)(2,1)}) %all-gather.3.cloned.1.call-update) | async-done | bytes 4194320 | tf_op jit(solution)/shard_map/all_gather | solution.py:391
  80.5 9.2 %serve.3 = bf16[8,272,256]{2,1,0:T(8,128)(2,1)S(1)} custom-call(s32[160]{0:T(256)S(1)} %reshape.408.row_ref, s32[160]{0:T(256)S(1)} %reshape.409.mark_ref, s32[1]{0:T(128)} %bitcast.2.zh_ref, bf16[4,2,264,512]{3,2,1,0:T(8,128)(2,1)S(1)} %all-to-all-done.q_ref, bf16[2048,1024]{1,0:T(8,128)(2,1)} %all-gather.3.cloned.1.call-done.key_ref.value_ref, ...), custom_call_target="tpu_custom_call" | custom-call | flops 671088640 | bytes 4194304 | tf_op jit(solution)/shard_map/serve/pallas_call | solution.py:96
  89.7 1.0 copy-done.2
  90.7 4.0 %all-to-all-start.4 = ((bf16[4,2,272,256]{3,2,1,0:T(8,128)(2,1)}), bf16[4,2,272,256]{3,2,1,0:T(8,128)(2,1)S(1)}, u32[]{:S(2)}, u32[]{:S(2)}) async-start(bf16[4,2,272,256]{3,2,1,0:T(8,128)(2,1)} %bitcast.26), calls=%async_computation.4 | async-start | bytes 2228224 | tf_op jit(solution)/shard_map/all_to_all | solution.py:493
  94.7 9.2 %serve.2 = bf16[8,272,256]{2,1,0:T(8,128)(2,1)S(1)} custom-call(s32[160]{0:T(256)S(1)} %reshape.408.row_ref, s32[160]{0:T(256)S(1)} %reshape.409.mark_ref, s32[1]{0:T(128)} %bitcast.2.zh_ref, bf16[4,2,264,512]{3,2,1,0:T(8,128)(2,1)S(1)} %all-to-all-done.q_ref, bf16[2048,1024]{1,0:T(8,128)(2,1)} %all-gather.3.cloned.1.call-done.key_ref.value_ref, ...), custom_call_target="tpu_custom_call" | custom-call | flops 671088640 | bytes 4194304 | tf_op jit(solution)/shard_map/serve/pallas_call | solution.py:96
  103.9 1.0 copy-done.1
  104.9 4.7 %all-to-all-done.4.got_ref = bf16[4,2,272,256]{3,2,1,0:T(8,128)(2,1)S(1)} async-done(((bf16[4,2,272,256]{3,2,1,0:T(8,128)(2,1)}), bf16[4,2,272,256]{3,2,1,0:T(8,128)(2,1)S(1)}, u32[]{:S(2)}, u32[]{:S(2)}) %all-to-all-start.4) | async-done | bytes 1114144 | tf_op jit(solution)/shard_map/all_to_all | solution.py:493
  109.6 3.7 %all-to-all-start.1 = ((bf16[4,2,272,256]{3,2,1,0:T(8,128)(2,1)}), bf16[4,2,272,256]{3,2,1,0:T(8,128)(2,1)S(1)}, u32[]{:S(2)}, u32[]{:S(2)}) async-start(bf16[4,2,272,256]{3,2,1,0:T(8,128)(2,1)} %bitcast.25), calls=%async_computation.1 | async-start | bytes 2228224 | tf_op jit(solution)/shard_map/all_to_all | solution.py:493
  113.9 0.1 pad_add_fusion.2.where_ref
  114.0 0.8 keep.1._.refs_3_
  114.7 0.5 copy-done.12
  115.3 0.8 fold.3
  116.1 7.7 %collective-permute-start.6 = (bf16[272,256]{1,0:T(8,128)(2,1)}, bf16[272,256]{1,0:T(8,128)(2,1)S(1)}, u32[]{:S(2)}, u32[]{:S(2)}) collective-permute-start(bf16[272,256]{1,0:T(8,128)(2,1)} %fold.3), channel_id=1, source_target_pairs={{0,8},{8,0},{1,9},{9,1},{2,10},{10,2},{3,11},{11,3},{4,12},{12,4},... | collective-permute-start | bytes 417800 | tf_op jit(solution)/shard_map/ppermute | solution.py:495
  123.8 0.9 copy-done.4
  124.8 0.7 local.3
  125.5 0.7 copy-done.10
  126.2 0.6 copy-done.14
  126.8 0.4 all-to-all-done.1.got_ref
  127.2 0.1 fold.2._
  127.3 0.6 collective-permute-done.6.far_ref
  127.9 0.9 copy-done.11
  128.9 0.7 copy-done.15
  129.6 0.3 merge.3
  129.9 0.8 copy-done.8
  130.7 3.5 %all-to-all-start.5 = ((bf16[4,256,256]{2,1,0:T(8,128)(2,1)}), bf16[4,256,256]{2,1,0:T(8,128)(2,1)S(1)}, u32[]{:S(2)}, u32[]{:S(2)}) async-start(bf16[4,256,256]{2,1,0:T(8,128)(2,1)} %copy-done.8), calls=%async_computation.5 | async-start | bytes 1048576 | tf_op jit(solution)/shard_map/all_to_all | solution.py:499
  134.1 7.1 %collective-permute-start.2 = (bf16[272,256]{1,0:T(8,128)(2,1)S(1)}, bf16[272,256]{1,0:T(8,128)(2,1)S(1)}, u32[]{:S(2)}, u32[]{:S(2)}) collective-permute-start(bf16[272,256]{1,0:T(8,128)(2,1)S(1)} %fold.2._), channel_id=1, source_target_pairs={{0,8},{8,0},{1,9},{9,1},{2,10},{10,2},{3,11},{11,3},{4,12},{12,4},... | collective-permute-start | bytes 417800 | tf_op jit(solution)/shard_map/ppermute | solution.py:495
  141.3 0.9 copy-done.5
  142.2 0.9 copy-done.7
  143.2 0.7 local.2
  143.9 6.6 %collective-permute-done.2.far_ref = bf16[272,256]{1,0:T(8,128)(2,1)S(1)} collective-permute-done((bf16[272,256]{1,0:T(8,128)(2,1)S(1)}, bf16[272,256]{1,0:T(8,128)(2,1)S(1)}, u32[]{:S(2)}, u32[]{:S(2)}) %collective-permute-start.2) | collective-permute-done | bytes 139296 | tf_op jit(solution)/shard_map/ppermute | solution.py:495
  150.6 1.8 merge.2
  152.4 5.7 %all-to-all-start.3 = ((bf16[4,256,256]{2,1,0:T(8,128)(2,1)}), bf16[4,256,256]{2,1,0:T(8,128)(2,1)S(1)}, u32[]{:S(2)}, u32[]{:S(2)}) async-start(bf16[4,256,256]{2,1,0:T(8,128)(2,1)} %merge.2), calls=%async_computation.3 | async-start | bytes 1048576 | tf_op jit(solution)/shard_map/all_to_all | solution.py:499
  158.1 6.2 %collective-permute-start.7 = (bf16[4,256,256]{2,1,0:T(8,128)(2,1)S(1)}, bf16[4,256,256]{2,1,0:T(8,128)(2,1)S(1)}, u32[]{:S(2)}, u32[]{:S(2)}) collective-permute-start(bf16[4,256,256]{2,1,0:T(8,128)(2,1)S(1)} %all-to-all-done.5.refs_0_), channel_id=1, source_target_pairs={{0,1},{1,0},{2,3},{3,2},{4,5},{5,4},{6,7},{7,6},{8,9},{9,8},{10,11... | collective-permute-start | bytes 1572872 | tf_op jit(solution)/shard_map/ppermute | solution.py:500
  164.2 4.7 %all-to-all-done.3.refs_0_ = bf16[4,256,256]{2,1,0:T(8,128)(2,1)S(1)} async-done(((bf16[4,256,256]{2,1,0:T(8,128)(2,1)}), bf16[4,256,256]{2,1,0:T(8,128)(2,1)S(1)}, u32[]{:S(2)}, u32[]{:S(2)}) %all-to-all-start.3) | async-done | bytes 524320 | tf_op jit(solution)/shard_map/all_to_all | solution.py:499
  168.9 6.5 %collective-permute-start.5 = (bf16[4,256,256]{2,1,0:T(8,128)(2,1)S(1)}, bf16[4,256,256]{2,1,0:T(8,128)(2,1)S(1)}, u32[]{:S(2)}, u32[]{:S(2)}) collective-permute-start(bf16[4,256,256]{2,1,0:T(8,128)(2,1)S(1)} %all-to-all-done.3.refs_0_), channel_id=1, source_target_pairs={{0,1},{1,0},{2,3},{3,2},{4,5},{5,4},{6,7},{7,6},{8,9},{9,8},{10,11... | collective-permute-start | bytes 1572872 | tf_op jit(solution)/shard_map/ppermute | solution.py:500
  175.4 2.2 %copy-done = bf16[4096,512]{1,0:T(8,128)(2,1)S(1)} copy-done((bf16[4096,512]{1,0:T(8,128)(2,1)S(1)}, bf16[4096,512]{1,0:T(8,128)(2,1)}, u32[]{:S(2)}) %copy-start) | copy-done | bytes 4194328
  177.6 2.0 %project.3.refs_2_ = f32[256,512]{1,0:T(8,128)S(1)} custom-call(s32[3]{0:T(128)S(1)} %copy-done.13, bf16[4,256,256]{2,1,0:T(8,128)(2,1)S(1)} %all-to-all-done.5.refs_0_, bf16[4,256,256]{2,1,0:T(8,128)(2,1)S(1)} %collective-permute-done.7.refs_1_, bf16[4,2,512,512]{3,2,1,0:T(8,128)(2,1)S(1)} %bitcast.23), custom_call_target="tpu_custom_call" | custom-call | flops 536870912 | bytes 2097152 | tf_op jit(solution)/shard_map/project/pallas_call | solution.py:340
  179.7 1.4 project.4.refs_2_
  181.1 2.4 %project.5 = (f32[256,512]{1,0:T(8,128)S(1)}, f32[256,128]{1,0:T(8,128)S(1)}) custom-call(s32[3]{0:T(128)S(1)} %copy-done.13, bf16[4,256,256]{2,1,0:T(8,128)(2,1)S(1)} %collective-permute-done.5.refs_0_, bf16[4,2,512,512]{3,2,1,0:T(8,128)(2,1)} %bitcast.22, f32[256,512]{1,0:T(8,128)S(1)} %project.4.refs_2_, f32[256,512]{1,0:T(8,128)S(1)} %keep.1._.refs_3_, ...), custom_call_target="tpu_custom_call" | custom-call | flops 268435456 | bytes 2097152 | tf_op jit(solution)/shard_map/project/pallas_call | solution.py:340
  183.7 7.6 %all_to_all.36 = f32[8,2,256]{2,1,0:T(2,128)S(1)} all-to-all(f32[8,2,256]{2,1,0:T(2,128)S(1)} %broadcast_in_dim.58), channel_id=1, replica_groups=mesh['y'=8,'x'=4,'zh'=2,'zl'=4,'core'=2] {'zl','core'}, dimensions={0} | all-to-all | bytes 32768 | tf_op jit(solution)/shard_map/all_to_all | solution.py:508
  191.3 0.9 add_convert_fusion
  (67 shorter events, 0.9 us)
Async XLA Ops:
  6.5 74.0 %all-gather.3.cloned.1.call-start = ((), (), s32[]{:S(2)}) async-start(), calls=%async_computation.7 | async-start | bytes 4718592 | tf_op jit(solution)/shard_map/all_gather | solution.py:391
  8.5 22.0 %collective-permute-start = (bf16[256,512]{1,0:T(8,128)(2,1)}, bf16[256,512]{1,0:T(8,128)(2,1)S(1)}, u32[]{:S(2)}, u32[]{:S(2)}) collective-permute-start(bf16[256,512]{1,0:T(8,128)(2,1)} %q_ref.3), channel_id=1, source_target_pairs={{0,8},{8,0},{1,9},{9,1},{2,10},{10,2},{3,11},{11,3},{4,12},{12,4},... | collective-permute-start | bytes 786440 | tf_op jit(solution)/shard_map/ppermute | solution.py:439
  22.0 8.4 %collective-permute-start.1 = (bf16[8,512]{1,0:T(8,128)(2,1)S(1)}, bf16[8,512]{1,0:T(8,128)(2,1)S(1)}, u32[]{:S(2)}, u32[]{:S(2)}) collective-permute-start(bf16[8,512]{1,0:T(8,128)(2,1)S(1)} %pad.4), channel_id=1, source_target_pairs={{0,8},{8,0},{1,9},{9,1},{2,10},{10,2},{3,11},{11,3},{4,12},{12,4},... | collective-permute-start | bytes 24584 | tf_op jit(solution)/shard_map/ppermute | solution.py:439
  32.1 4.1 %copy-start.20 = (bf16[512,64]{0,1:T(8,128)(2,1)S(1)}, bf16[512,64]{0,1:T(8,128)(2,1)}, u32[]{:S(2)}) copy-start(bf16[512,64]{0,1:T(8,128)(2,1)} %param.16) | copy-start | bytes 196612
  32.1 28.7 %all-to-all-start = ((bf16[4,2,264,512]{3,2,1,0:T(8,128)(2,1)}), bf16[4,2,264,512]{3,2,1,0:T(8,128)(2,1)S(1)}, u32[]{:S(2)}, u32[]{:S(2)}) async-start(bf16[4,2,264,512]{3,2,1,0:T(8,128)(2,1)} %broadcast_in_dim.53), calls=%async_computation | async-start | bytes 4325376 | tf_op jit(solution)/shard_map/all_to_all | solution.py:435
  36.2 35.9 %copy-start.19 = (s32[2]{0:T(128)S(1)}, s32[2]{0:T(128)}, u32[]{:S(2)}) copy-start(s32[2]{0:T(128)} %param.19) | copy-start | bytes 28
  36.2 114.4 %all-gather.5.cloned.1.call-start = ((), (), s32[]{:S(2)}) async-start(), calls=%async_computation.8 | async-start | bytes 4718592 | tf_op jit(solution)/shard_map/all_gather | solution.py:444
  36.2 13.4 %collective-permute-start.3 = (bf16[64,512]{1,0:T(8,128)(2,1)S(1)}, bf16[64,512]{1,0:T(8,128)(2,1)S(1)}, u32[]{:S(2)}, u32[]{:S(2)}) collective-permute-start(bf16[64,512]{1,0:T(8,128)(2,1)S(1)} %bitcast.29), channel_id=1, source_target_pairs={{0,0},{1,64},{2,128},{3,192},{4,256},{5,320},{6,384},{7,448},{8,8}... | collective-permute-start | bytes 196616 | tf_op jit(solution)/shard_map/ppermute | solution.py:401
  41.8 12.8 %collective-permute-start.4 = (bf16[64,512]{1,0:T(8,128)(2,1)S(1)}, bf16[64,512]{1,0:T(8,128)(2,1)S(1)}, u32[]{:S(2)}, u32[]{:S(2)}) collective-permute-start(bf16[64,512]{1,0:T(8,128)(2,1)S(1)} %bitcast.30), channel_id=1, source_target_pairs={{0,8},{1,72},{2,136},{3,200},{4,264},{5,328},{6,392},{7,456},{8,0}... | collective-permute-start | bytes 196616 | tf_op jit(solution)/shard_map/ppermute | solution.py:402
  89.7 1.0 copy-start.2
  90.7 18.8 %all-to-all-start.4 = ((bf16[4,2,272,256]{3,2,1,0:T(8,128)(2,1)}), bf16[4,2,272,256]{3,2,1,0:T(8,128)(2,1)S(1)}, u32[]{:S(2)}, u32[]{:S(2)}) async-start(bf16[4,2,272,256]{3,2,1,0:T(8,128)(2,1)} %bitcast.26), calls=%async_computation.4 | async-start | bytes 2228224 | tf_op jit(solution)/shard_map/all_to_all | solution.py:493
  103.9 1.0 copy-start.1
  104.9 9.1 %copy-start.16 = (s32[16]{0:T(128)S(1)}, s32[16]{0:T(128)}, u32[]{:S(2)}) copy-start(s32[16]{0:T(128)} %drop_ref.1) | copy-start | bytes 196
  109.6 14.2 %copy-start.3 = (bf16[256,512]{1,0:T(8,128)(2,1)S(1)}, bf16[256,512]{1,0:T(8,128)(2,1)}, u32[]{:S(2)}) copy-start(bf16[256,512]{1,0:T(8,128)(2,1)} %q_ref.3) | copy-start | bytes 786436
  109.6 14.2 %copy-start.6 = (bf16[256,512]{1,0:T(8,128)(2,1)S(1)}, bf16[256,512]{1,0:T(8,128)(2,1)}, u32[]{:S(2)}) copy-start(bf16[256,512]{1,0:T(8,128)(2,1)} %k_ref.3) | copy-start | bytes 786436
  109.6 17.6 %all-to-all-start.1 = ((bf16[4,2,272,256]{3,2,1,0:T(8,128)(2,1)}), bf16[4,2,272,256]{3,2,1,0:T(8,128)(2,1)S(1)}, u32[]{:S(2)}, u32[]{:S(2)}) async-start(bf16[4,2,272,256]{3,2,1,0:T(8,128)(2,1)} %bitcast.25), calls=%async_computation.1 | async-start | bytes 2228224 | tf_op jit(solution)/shard_map/all_to_all | solution.py:493
  114.7 0.5 copy-start.12
  116.1 11.9 %collective-permute-start.6 = (bf16[272,256]{1,0:T(8,128)(2,1)}, bf16[272,256]{1,0:T(8,128)(2,1)S(1)}, u32[]{:S(2)}, u32[]{:S(2)}) collective-permute-start(bf16[272,256]{1,0:T(8,128)(2,1)} %fold.3), channel_id=1, source_target_pairs={{0,8},{8,0},{1,9},{9,1},{2,10},{10,2},{3,11},{11,3},{4,12},{12,4},... | collective-permute-start | bytes 417800 | tf_op jit(solution)/shard_map/ppermute | solution.py:495
  123.8 1.0 copy-start.4
  125.5 0.7 copy-start.10
  126.2 0.6 copy-start.14
  127.9 1.0 copy-start.11
  128.9 0.7 copy-start.15
  129.9 0.8 copy-start.8
  130.7 21.7 %all-to-all-start.5 = ((bf16[4,256,256]{2,1,0:T(8,128)(2,1)}), bf16[4,256,256]{2,1,0:T(8,128)(2,1)S(1)}, u32[]{:S(2)}, u32[]{:S(2)}) async-start(bf16[4,256,256]{2,1,0:T(8,128)(2,1)} %copy-done.8), calls=%async_computation.5 | async-start | bytes 1048576 | tf_op jit(solution)/shard_map/all_to_all | solution.py:499
  134.1 16.4 %collective-permute-start.2 = (bf16[272,256]{1,0:T(8,128)(2,1)S(1)}, bf16[272,256]{1,0:T(8,128)(2,1)S(1)}, u32[]{:S(2)}, u32[]{:S(2)}) collective-permute-start(bf16[272,256]{1,0:T(8,128)(2,1)S(1)} %fold.2._), channel_id=1, source_target_pairs={{0,8},{8,0},{1,9},{9,1},{2,10},{10,2},{3,11},{11,3},{4,12},{12,4},... | collective-permute-start | bytes 417800 | tf_op jit(solution)/shard_map/ppermute | solution.py:495
  141.3 1.0 copy-start.5
  142.2 0.9 copy-start.7
  150.6 24.8 %copy-start.13 = (s32[3]{0:T(128)S(1)}, s32[3]{0:T(128)}, u32[]{:S(2)}) copy-start(s32[3]{0:T(128)} %copy-done.12) | copy-start | bytes 40
  152.4 16.5 %all-to-all-start.3 = ((bf16[4,256,256]{2,1,0:T(8,128)(2,1)}), bf16[4,256,256]{2,1,0:T(8,128)(2,1)S(1)}, u32[]{:S(2)}, u32[]{:S(2)}) async-start(bf16[4,256,256]{2,1,0:T(8,128)(2,1)} %merge.2), calls=%async_computation.3 | async-start | bytes 1048576 | tf_op jit(solution)/shard_map/all_to_all | solution.py:499
  158.1 17.4 %collective-permute-start.7 = (bf16[4,256,256]{2,1,0:T(8,128)(2,1)S(1)}, bf16[4,256,256]{2,1,0:T(8,128)(2,1)S(1)}, u32[]{:S(2)}, u32[]{:S(2)}) collective-permute-start(bf16[4,256,256]{2,1,0:T(8,128)(2,1)S(1)} %all-to-all-done.5.refs_0_), channel_id=1, source_target_pairs={{0,1},{1,0},{2,3},{3,2},{4,5},{5,4},{6,7},{7,6},{8,9},{9,8},{10,11... | collective-permute-start | bytes 1572872 | tf_op jit(solution)/shard_map/ppermute | solution.py:500
  168.9 12.2 %collective-permute-start.5 = (bf16[4,256,256]{2,1,0:T(8,128)(2,1)S(1)}, bf16[4,256,256]{2,1,0:T(8,128)(2,1)S(1)}, u32[]{:S(2)}, u32[]{:S(2)}) collective-permute-start(bf16[4,256,256]{2,1,0:T(8,128)(2,1)S(1)} %all-to-all-done.3.refs_0_), channel_id=1, source_target_pairs={{0,1},{1,0},{2,3},{3,2},{4,5},{5,4},{6,7},{7,6},{8,9},{9,8},{10,11... | collective-permute-start | bytes 1572872 | tf_op jit(solution)/shard_map/ppermute | solution.py:500
  175.4 2.2 %copy-start = (bf16[4096,512]{1,0:T(8,128)(2,1)S(1)}, bf16[4096,512]{1,0:T(8,128)(2,1)}, u32[]{:S(2)}) copy-start(bf16[4096,512]{1,0:T(8,128)(2,1)} %all-gather.5.cloned.1.call-done._) | copy-start | bytes 12582916
  179.6 1.5 copy-start.9
  181.1 10.2 %copy-start.17 = (f32[512]{0:T(512)S(1)}, f32[512]{0:T(512)}, u32[]{:S(2)}) copy-start(f32[512]{0:T(512)} %param.18) | copy-start | bytes 6148
  181.1 10.2 %copy-start.18 = (f32[512]{0:T(512)S(1)}, f32[512]{0:T(512)}, u32[]{:S(2)}) copy-start(f32[512]{0:T(512)} %param.17) | copy-start | bytes 6148
Sparse Core Ops, SparseCore 0:
  9.4 71.0 all-gather.2
  82.6 55.4 all-gather.4

commit v7 on v6

--- a/solution.py
+++ b/solution.py
@@ -24,6 +24,7 @@
 STAT_ROWS = 16
 NEG = -1e30
 EMPTY = -1e20
+MERGE_HINT = 30_000_000_000
 VMEM_LIMIT = 48 * 1024 * 1024
 
 
@@ -63,28 +64,46 @@
 
 
 def serve_kernel(row_ref, mark_ref, zh_ref, q_ref, key_ref, value_ref, out_ref):
-    peer = pl.program_id(0)
-    rows = q_ref.shape[2]
-    wide = q_ref.shape[3]
-    listings = row_ref.shape[0] // pl.num_programs(0)
+    n_x, n_zh, rows, wide = q_ref.shape
+    listings = row_ref.shape[0] // (pl.num_programs(0) * n_x * n_zh)
     block_of = lax.broadcasted_iota(jnp.int32, (BLOCK, rows), 1) // BLOCK
-    places, listed = [], []
-    for i in range(listings):
-        at = peer * listings + i
-        places.append(pl.ds(pl.multiple_of(row_ref[at] * BLOCK, BLOCK), BLOCK))
-        mark = mark_ref[at]
-        listed.append(jnp.logical_or(block_of == mark, jnp.full(block_of.shape, mark) < 0))
-    listed = jnp.concatenate(listed, axis=0)
-    stats = []
-    for h in range(wide // DH):
+    jobs = []
+    for x in range(n_x):
+        for j in range(n_zh):
+            peer = (pl.program_id(0) * n_x + x) * n_zh + j
+            places, listed = [], []
+            for i in range(listings):
+                at = peer * listings + i
+                places.append(pl.ds(pl.multiple_of(row_ref[at] * BLOCK, BLOCK), BLOCK))
+                mark = mark_ref[at]
+                listed.append(
+                    jnp.logical_or(block_of == mark, jnp.full(block_of.shape, mark) < 0)
+                )
+            listed = jnp.concatenate(listed, axis=0)
+            jobs += [(x, j, h, places, listed) for h in range(wide // DH)]
+
+    def scores(x, j, h, places, listed):
         lanes = slice(h * DH, (h + 1) * DH)
         keys = jnp.concatenate([key_ref[p, lanes] for p in places], axis=0)
+        return dot_t(keys, q_ref[x, j, :, lanes])
+
+    stats = []
+    coming = scores(*jobs[0])
+    for k, (x, j, h, places, listed) in enumerate(jobs):
+        now = coming
+        if k + 1 < len(jobs):
+            coming = scores(*jobs[k + 1])
+        lanes = slice(h * DH, (h + 1) * DH)
         values = jnp.concatenate([value_ref[p, lanes] for p in places], axis=0)
-        top, total, got = partial(dot_t(keys, q_ref[0, 0, :, lanes]), listed, values)
-        out_ref[0, lanes, :] = got.astype(BF)
+        top, total, got = partial(now, listed, values)
+        peer = x * n_zh + lax.rem(j + zh_ref[0], n_zh)
+        out_ref[peer, lanes, :] = got.astype(BF)
         stats += split(top, 3) + split(total, 2)
-    stats.append(jnp.zeros((STAT_ROWS - len(stats), rows), BF))
-    out_ref[0, wide:, :] = jnp.concatenate([x.astype(F32) for x in stats], axis=0).astype(BF)
+        if (h + 1) * DH == wide:
+            stats.append(jnp.zeros((STAT_ROWS - len(stats), rows), BF))
+            stats = jnp.concatenate([line.astype(F32) for line in stats], axis=0)
+            out_ref[peer, wide:, :] = stats.astype(BF)
+            stats = []
 
 
 def serve(part, row, mark, zh, q, pool, out_rows):
@@ -93,19 +112,18 @@
     rows = out_rows
     peers = 2 * n_x
     out = (peers, wide + STAT_ROWS, rows)
+    steps = n_x // 2
     return pl.pallas_call(
         serve_kernel,
         grid_spec=pltpu.PrefetchScalarGridSpec(
             num_scalar_prefetch=3,
-            grid=(peers,),
+            grid=(steps,),
             in_specs=[
-                pl.BlockSpec((1, 1, rows, wide), lambda i, a, b, c: (i // 2, i % 2, 0, part)),
+                pl.BlockSpec((n_x // steps, 2, rows, wide), lambda i, a, b, c: (i, 0, 0, part)),
                 pl.BlockSpec((pool.shape[0], wide), lambda i, a, b, c: (0, part)),
                 pl.BlockSpec((pool.shape[0], wide), lambda i, a, b, c: (0, PARTS + part)),
             ],
-            out_specs=pl.BlockSpec(
-                (1,) + out[1:], lambda i, a, b, zh_ref: (2 * (i // 2) + (i % 2 + zh_ref[0]) % 2, 0, 0)
-            ),
+            out_specs=pl.BlockSpec((peers // steps,) + out[1:], lambda i, a, b, c: (i, 0, 0)),
         ),
         out_shape=jax.ShapeDtypeStruct(out, BF),
         compiler_params=params(),
@@ -246,7 +264,7 @@
         out_shape=jax.ShapeDtypeStruct(out, BF),
         compiler_params=params(),
         cost_estimate=pl.CostEstimate(
-            flops=2 * peers * rows * wide, transcendentals=0, bytes_accessed=1 << 20
+            flops=MERGE_HINT, transcendentals=0, bytes_accessed=1 << 20
         ),
         name="merge",
     )(zh, got, far, near, stat, after.reshape(-1, after.shape[-1]))
@@ -350,7 +368,7 @@
             ],
         ),
         out_shape=out_shape,
-        compiler_params=params(),
+        compiler_params=params(59 << 20),
         cost_estimate=pl.CostEstimate(
             flops=2 * rows * pieces * wide * cols, transcendentals=0, bytes_accessed=2 << 20
         ),

time: 200 us -> 205 us (1.025)
  waiting for transfers between devices: 41.4 us -> 49.9 us
  local copies, waits for them, and re-layouts: 15.7 us -> 9.23 us
  Pallas kernels: 29.4 us -> 32.6 us
    all_to_all x2, waiting for transfers between devices: 4.68 us -> 14.6 us  [on_device(): lax.all_to_all(context, 'zl', split_axis=0, concat_axis=0, tiled=True)]
    pallas_call x3, Pallas kernels: 5.85 us -> 14 us  [project(): pl.pallas_call(functools.partial(project_kernel, part, shifts, finish is...]
    unnamed x44 -> x38, local copies, waits for them, and re-layouts: 12.9 us -> 5.49 us
    ppermute x2, waiting for transfers between devices: 7.27 us -> 0.01 us  [on_device(): folded.append((got, lax.ppermute(gone, 'zh', flip)))]
    pallas_call x2, Pallas kernels: 18.3 us -> 11.6 us  [serve(): pl.pallas_call(serve_kernel, grid_spec=pltpu.PrefetchScalarGridSpec(num_s...]
    all_to_all x2, waiting for transfers between devices: 5.01 us -> 10.2 us  [on_device(): got = lax.all_to_all(partials, 'x', split_axis=0, concat_axis=0, tiled=True)]
where the time goes in v7:
time: 205 us; the launch traced here: 203 us
  starting transfers between devices  73.2 us (36%)
  waiting for transfers between devices  49.9 us (24%)
  Pallas kernels  32.6 us (16%)
  blocking collectives  17.6 us (9%)
  between operations  15.2 us (7%)
  local copies, waits for them, and re-layouts  9.23 us (5%)
  other arithmetic  5.7 us (3%)
    ppermute x2, starting transfers between devices, on_device(): folded.append((got, lax.ppermute(gone, 'zh', flip)))  15.5 us
    all_to_all x2, waiting for transfers between devices, on_device(): lax.all_to_all(context, 'zl', split_axis=0, concat_axis=0, tiled=True)  14.6 us
    pallas_call x3, Pallas kernels, project(): pl.pallas_call(functools.partial(project_kernel, part, shifts, finish is...  14 us
    pallas_call x2, Pallas kernels, serve(): pl.pallas_call(serve_kernel, grid_spec=pltpu.PrefetchScalarGridSpec(num_s...  11.6 us
    ppermute x1, starting transfers between devices, on_device(): lax.ppermute(queries, 'zh', flip)  11.5 us
    ppermute x2, starting transfers between devices, on_device(): other.append(lax.ppermute(mine[part], 'core', flip))  11.4 us
    all_to_all x2, waiting for transfers between devices, on_device(): got = lax.all_to_all(partials, 'x', split_axis=0, concat_axis=0, tiled=True)  10.2 us
    all_to_all x1, blocking collectives, over_x(): return lax.all_to_all(x, 'x', split_axis=0, concat_axis=0, tiled=True)  10 us
  transfers between devices with their start and end apart: 15, of which 9 were waited for; matrix products, arithmetic and copies ran while one was open for 3% of the time, Pallas kernels for 14%

profile of v7, /device:TPU:1, one launch (start us, length us, event | category | flops | bytes accessed | tf_op | source)
XLA Modules:
  0.0 203.4 jit_solution(6198042541850553870)
XLA Ops:
  6.5 1.9 pad_maximum_fusion.1
  8.5 11.5 %collective-permute-start = (bf16[256,512]{1,0:T(8,128)(2,1)}, bf16[256,512]{1,0:T(8,128)(2,1)S(1)}, u32[]{:S(2)}, u32[]{:S(2)}) collective-permute-start(bf16[256,512]{1,0:T(8,128)(2,1)} %q_ref.3), channel_id=1, source_target_pairs={{0,8},{8,0},{1,9},{9,1},{2,10},{10,2},{3,11},{11,3},{4,12},{12,4},... | collective-permute-start | bytes 786440 | tf_op jit(solution)/shard_map/ppermute | solution.py:457
  20.0 0.8 copy.22
  20.7 0.1 reshape.407
  20.8 0.2 convert_reduce_fusion
  21.0 0.8 copy.23
  21.8 0.1 broadcast_in_dim.49
  21.9 0.1 select_reduce_fusion
  22.0 1.9 collective-permute-start.1
  23.9 1.0 maximum_bitcast_fusion
  24.9 5.5 %collective-permute-done.1 = bf16[8,512]{1,0:T(8,128)(2,1)S(1)} collective-permute-done((bf16[8,512]{1,0:T(8,128)(2,1)S(1)}, bf16[8,512]{1,0:T(8,128)(2,1)S(1)}, u32[]{:S(2)}, u32[]{:S(2)}) %collective-permute-start.1) | collective-permute-done | bytes 8224 | tf_op jit(solution)/shard_map/ppermute | solution.py:457
  30.5 0.1 pad_maximum_fusion
  30.6 1.6 broadcast_in_dim.53
  32.1 4.1 %all-to-all-start = ((bf16[4,2,264,512]{3,2,1,0:T(8,128)(2,1)}), bf16[4,2,264,512]{3,2,1,0:T(8,128)(2,1)S(1)}, u32[]{:S(2)}, u32[]{:S(2)}) async-start(bf16[4,2,264,512]{3,2,1,0:T(8,128)(2,1)} %broadcast_in_dim.53), calls=%async_computation | async-start | bytes 4325376 | tf_op jit(solution)/shard_map/all_to_all | solution.py:453
  36.2 5.6 %collective-permute-start.3 = (bf16[64,512]{1,0:T(8,128)(2,1)S(1)}, bf16[64,512]{1,0:T(8,128)(2,1)S(1)}, u32[]{:S(2)}, u32[]{:S(2)}) collective-permute-start(bf16[64,512]{1,0:T(8,128)(2,1)S(1)} %bitcast.27), channel_id=1, source_target_pairs={{0,0},{1,64},{2,128},{3,192},{4,256},{5,320},{6,384},{7,448},{8,8}... | collective-permute-start | bytes 196616 | tf_op jit(solution)/shard_map/ppermute | solution.py:419
  41.9 7.7 %collective-permute-start.4 = (bf16[64,512]{1,0:T(8,128)(2,1)S(1)}, bf16[64,512]{1,0:T(8,128)(2,1)S(1)}, u32[]{:S(2)}, u32[]{:S(2)}) collective-permute-start(bf16[64,512]{1,0:T(8,128)(2,1)S(1)} %bitcast.28), channel_id=1, source_target_pairs={{0,8},{1,72},{2,136},{3,200},{4,264},{5,328},{6,392},{7,456},{8,0}... | collective-permute-start | bytes 196616 | tf_op jit(solution)/shard_map/ppermute | solution.py:420
  49.6 5.0 %collective-permute-done.4 = bf16[64,512]{1,0:T(8,128)(2,1)S(1)} collective-permute-done((bf16[64,512]{1,0:T(8,128)(2,1)S(1)}, bf16[64,512]{1,0:T(8,128)(2,1)S(1)}, u32[]{:S(2)}, u32[]{:S(2)}) %collective-permute-start.4) | collective-permute-done | bytes 65568 | tf_op jit(solution)/shard_map/ppermute | solution.py:420
  54.7 6.1 %all-to-all-done.q_ref = bf16[4,2,264,512]{3,2,1,0:T(8,128)(2,1)S(1)} async-done(((bf16[4,2,264,512]{3,2,1,0:T(8,128)(2,1)}), bf16[4,2,264,512]{3,2,1,0:T(8,128)(2,1)S(1)}, u32[]{:S(2)}, u32[]{:S(2)}) %all-to-all-start) | async-done | bytes 2162720 | tf_op jit(solution)/shard_map/all_to_all | solution.py:453
  60.8 0.5 slice.29
  62.0 10.0 %all_to_all.35 = bf16[4,128,512]{2,1,0:T(8,128)(2,1)} all-to-all(bf16[4,128,512]{2,1,0:T(8,128)(2,1)S(1)} %broadcast_in_dim.57), channel_id=1, replica_groups=mesh['y'=8,'x'=4,'zh'=2,'zl'=4,'core'=2] {'x'}, dimensions={0} | all-to-all | bytes 1048576 | tf_op jit(solution)/shard_map/all_to_all | solution.py:453
  72.1 0.1 pad.10.clone
  72.2 0.1 pad.14.clone
  72.4 0.1 reshape_squeeze.3
  72.5 0.1 compare_select_fusion
  72.6 0.1 pad_add_fusion.1
  72.7 0.1 reshape.409.mark_ref
  72.7 0.1 pad_add_fusion
  72.8 0.1 reshape.408.row_ref
  72.9 7.6 %all-gather.3.cloned.1.call-done.key_ref.value_ref = bf16[2048,1024]{1,0:T(8,128)(2,1)} async-done(((bf16[256,1024]{1,0:T(8,128)(2,1)}), bf16[2048,1024]{1,0:T(8,128)(2,1)}) %all-gather.3.cloned.1.call-update) | async-done | bytes 4194320 | tf_op jit(solution)/shard_map/all_gather | solution.py:409
  80.5 5.8 %serve.3 = bf16[8,272,256]{2,1,0:T(8,128)(2,1)} custom-call(s32[160]{0:T(256)S(1)} %reshape.408.row_ref, s32[160]{0:T(256)S(1)} %reshape.409.mark_ref, s32[1]{0:T(128)} %bitcast.2.zh_ref, bf16[4,2,264,512]{3,2,1,0:T(8,128)(2,1)S(1)} %all-to-all-done.q_ref, bf16[2048,1024]{1,0:T(8,128)(2,1)} %all-gather.3.cloned.1.call-done.key_ref.value_ref, ...), custom_call_target="tpu_custom_call" | custom-call | flops 671088640 | bytes 4194304 | tf_op jit(solution)/shard_map/serve/pallas_call | solution.py:116
  86.3 4.0 %all-to-all-start.4 = ((bf16[4,2,272,256]{3,2,1,0:T(8,128)(2,1)}), bf16[4,2,272,256]{3,2,1,0:T(8,128)(2,1)S(1)}, u32[]{:S(2)}, u32[]{:S(2)}) async-start(bf16[4,2,272,256]{3,2,1,0:T(8,128)(2,1)} %bitcast.11), calls=%async_computation.4 | async-start | bytes 2228224 | tf_op jit(solution)/shard_map/all_to_all | solution.py:511
  90.3 5.8 %serve.2 = bf16[8,272,256]{2,1,0:T(8,128)(2,1)} custom-call(s32[160]{0:T(256)S(1)} %reshape.408.row_ref, s32[160]{0:T(256)S(1)} %reshape.409.mark_ref, s32[1]{0:T(128)} %bitcast.2.zh_ref, bf16[4,2,264,512]{3,2,1,0:T(8,128)(2,1)S(1)} %all-to-all-done.q_ref, bf16[2048,1024]{1,0:T(8,128)(2,1)} %all-gather.3.cloned.1.call-done.key_ref.value_ref, ...), custom_call_target="tpu_custom_call" | custom-call | flops 671088640 | bytes 4194304 | tf_op jit(solution)/shard_map/serve/pallas_call | solution.py:116
  96.0 9.1 %all-to-all-done.4.got_ref = bf16[4,2,272,256]{3,2,1,0:T(8,128)(2,1)S(1)} async-done(((bf16[4,2,272,256]{3,2,1,0:T(8,128)(2,1)}), bf16[4,2,272,256]{3,2,1,0:T(8,128)(2,1)S(1)}, u32[]{:S(2)}, u32[]{:S(2)}) %all-to-all-start.4) | async-done | bytes 1114144 | tf_op jit(solution)/shard_map/all_to_all | solution.py:511
  105.2 3.7 %all-to-all-start.1 = ((bf16[4,2,272,256]{3,2,1,0:T(8,128)(2,1)}), bf16[4,2,272,256]{3,2,1,0:T(8,128)(2,1)S(1)}, u32[]{:S(2)}, u32[]{:S(2)}) async-start(bf16[4,2,272,256]{3,2,1,0:T(8,128)(2,1)} %bitcast.6), calls=%async_computation.1 | async-start | bytes 2228224 | tf_op jit(solution)/shard_map/all_to_all | solution.py:511
  109.5 0.1 pad_add_fusion.2.where_ref
  109.6 0.8 keep.1._.refs_3_
  110.4 0.8 fold.3
  111.2 7.7 %collective-permute-start.6 = (bf16[272,256]{1,0:T(8,128)(2,1)}, bf16[272,256]{1,0:T(8,128)(2,1)}, u32[]{:S(2)}, u32[]{:S(2)}) collective-permute-start(bf16[272,256]{1,0:T(8,128)(2,1)} %fold.3), channel_id=1, source_target_pairs={{0,8},{8,0},{1,9},{9,1},{2,10},{10,2},{3,11},{11,3},{4,12},{12,4},... | collective-permute-start | bytes 417800 | tf_op jit(solution)/shard_map/ppermute | solution.py:513
  118.9 0.7 local.3
  119.7 0.7 copy-done.8
  120.4 0.7 local.2
  121.1 0.7 copy-done.6
  121.8 1.1 all-to-all-done.1.got_ref
  122.9 0.1 fold.2._
  123.0 7.7 %collective-permute-start.2 = (bf16[272,256]{1,0:T(8,128)(2,1)S(1)}, bf16[272,256]{1,0:T(8,128)(2,1)S(1)}, u32[]{:S(2)}, u32[]{:S(2)}) collective-permute-start(bf16[272,256]{1,0:T(8,128)(2,1)S(1)} %fold.2._), channel_id=1, source_target_pairs={{0,8},{8,0},{1,9},{9,1},{2,10},{10,2},{3,11},{11,3},{4,12},{12,4},... | collective-permute-start | bytes 417800 | tf_op jit(solution)/shard_map/ppermute | solution.py:513
  130.8 0.9 copy-done.9
  131.7 2.1 %merge.3 = bf16[4,256,256]{2,1,0:T(8,128)(2,1)} custom-call(s32[1]{0:T(128)} %bitcast.2.zh_ref, bf16[4,2,272,256]{3,2,1,0:T(8,128)(2,1)S(1)} %all-to-all-done.4.got_ref, bf16[272,256]{1,0:T(8,128)(2,1)} %collective-permute-done.6.far_ref, f32[256,256]{1,0:T(8,128)S(1)} %copy-done.9, f32[4,256]{1,0:T(4,128)S(1)} %get-tuple-element.14.stat_ref, ...), custom_call_target="tpu_custom_call" | custom-call | flops 30000001024 | bytes 1048576 | tf_op jit(solution)/shard_map/merge/pallas_call | solution.py:250
  133.8 3.5 %all-to-all-start.5 = ((bf16[4,256,256]{2,1,0:T(8,128)(2,1)}), bf16[4,256,256]{2,1,0:T(8,128)(2,1)S(1)}, u32[]{:S(2)}, u32[]{:S(2)}) async-start(bf16[4,256,256]{2,1,0:T(8,128)(2,1)} %merge.3), calls=%async_computation.5 | async-start | bytes 1048576 | tf_op jit(solution)/shard_map/all_to_all | solution.py:517
  137.3 0.7 all-gather.5.cloned.1.call-done._
  138.1 1.8 merge.2
  139.9 8.7 %all-to-all-done.5.refs_0_ = bf16[4,256,256]{2,1,0:T(8,128)(2,1)S(1)} async-done(((bf16[4,256,256]{2,1,0:T(8,128)(2,1)}), bf16[4,256,256]{2,1,0:T(8,128)(2,1)S(1)}, u32[]{:S(2)}, u32[]{:S(2)}) %all-to-all-start.5) | async-done | bytes 524320 | tf_op jit(solution)/shard_map/all_to_all | solution.py:517
  148.5 4.4 %all-to-all-start.3 = ((bf16[4,256,256]{2,1,0:T(8,128)(2,1)}), bf16[4,256,256]{2,1,0:T(8,128)(2,1)S(1)}, u32[]{:S(2)}, u32[]{:S(2)}) async-start(bf16[4,256,256]{2,1,0:T(8,128)(2,1)} %merge.2), calls=%async_computation.3 | async-start | bytes 1048576 | tf_op jit(solution)/shard_map/all_to_all | solution.py:517
  153.0 5.1 %collective-permute-start.7 = (bf16[4,256,256]{2,1,0:T(8,128)(2,1)S(1)}, bf16[4,256,256]{2,1,0:T(8,128)(2,1)S(1)}, u32[]{:S(2)}, u32[]{:S(2)}) collective-permute-start(bf16[4,256,256]{2,1,0:T(8,128)(2,1)S(1)} %all-to-all-done.5.refs_0_), channel_id=1, source_target_pairs={{0,1},{1,0},{2,3},{3,2},{4,5},{5,4},{6,7},{7,6},{8,9},{9,8},{10,11... | collective-permute-start | bytes 1572872 | tf_op jit(solution)/shard_map/ppermute | solution.py:518
  158.1 5.9 %all-to-all-done.3.refs_0_ = bf16[4,256,256]{2,1,0:T(8,128)(2,1)S(1)} async-done(((bf16[4,256,256]{2,1,0:T(8,128)(2,1)}), bf16[4,256,256]{2,1,0:T(8,128)(2,1)S(1)}, u32[]{:S(2)}, u32[]{:S(2)}) %all-to-all-start.3) | async-done | bytes 524320 | tf_op jit(solution)/shard_map/all_to_all | solution.py:517
  164.1 6.3 %collective-permute-start.5 = (bf16[4,256,256]{2,1,0:T(8,128)(2,1)S(1)}, bf16[4,256,256]{2,1,0:T(8,128)(2,1)S(1)}, u32[]{:S(2)}, u32[]{:S(2)}) collective-permute-start(bf16[4,256,256]{2,1,0:T(8,128)(2,1)S(1)} %all-to-all-done.3.refs_0_), channel_id=1, source_target_pairs={{0,1},{1,0},{2,3},{3,2},{4,5},{5,4},{6,7},{7,6},{8,9},{9,8},{10,11... | collective-permute-start | bytes 1572872 | tf_op jit(solution)/shard_map/ppermute | solution.py:518
  170.4 0.8 copy-done.13
  171.2 5.0 %project.3.refs_2_ = f32[256,512]{1,0:T(8,128)} custom-call(s32[3]{0:T(128)} %copy-done.4, bf16[4,256,256]{2,1,0:T(8,128)(2,1)} %copy-done.10, bf16[4,256,256]{2,1,0:T(8,128)(2,1)} %copy-done.13, bf16[4,2,512,512]{3,2,1,0:T(8,128)(2,1)} %bitcast.22), custom_call_target="tpu_custom_call" | custom-call | flops 536870912 | bytes 2097152 | tf_op jit(solution)/shard_map/project/pallas_call | solution.py:358
  176.2 4.4 %project.4.refs_2_ = f32[256,512]{1,0:T(8,128)} custom-call(s32[3]{0:T(128)} %copy-done.4, bf16[4,256,256]{2,1,0:T(8,128)(2,1)} %copy-done.11, bf16[4,2,512,512]{3,2,1,0:T(8,128)(2,1)} %bitcast.23, f32[256,512]{1,0:T(8,128)} %project.3.refs_2_), custom_call_target="tpu_custom_call" | custom-call | flops 268435456 | bytes 2097152 | tf_op jit(solution)/shard_map/project/pallas_call | solution.py:358
  180.6 0.8 copy-done.12
  181.4 4.6 %project.5 = (f32[256,512]{1,0:T(8,128)}, f32[256,128]{1,0:T(8,128)}) custom-call(s32[3]{0:T(128)} %copy-done.4, bf16[4,256,256]{2,1,0:T(8,128)(2,1)} %copy-done.12, bf16[4,2,512,512]{3,2,1,0:T(8,128)(2,1)} %bitcast.24, f32[256,512]{1,0:T(8,128)} %project.4.refs_2_, f32[256,512]{1,0:T(8,128)} %copy-done, bf16[256,512]{1,0:T(8,128)(2,1)} %refs_4_.1), custom_call_target="tpu_custom_call" | custom-call | flops 268435456 | bytes 2097152 | tf_op jit(solution)/shard_map/project/pallas_call | solution.py:358
  186.0 0.9 slice_bitcast_fusion
  186.9 0.1 copy.24
  187.0 7.6 %all_to_all.36 = f32[8,2,256]{2,1,0:T(2,128)S(1)} all-to-all(f32[8,2,256]{2,1,0:T(2,128)S(1)} %broadcast_in_dim.58), channel_id=1, replica_groups=mesh['y'=8,'x'=4,'zh'=2,'zl'=4,'core'=2] {'zl','core'}, dimensions={0} | all-to-all | bytes 32768 | tf_op jit(solution)/shard_map/all_to_all | solution.py:526
  194.7 1.9 add_convert_fusion
  (61 shorter events, 0.5 us)
Async XLA Ops:
  6.5 74.0 %all-gather.3.cloned.1.call-start = ((), (), s32[]{:S(2)}) async-start(), calls=%async_computation.7 | async-start | bytes 4718592 | tf_op jit(solution)/shard_map/all_gather | solution.py:409
  8.5 22.0 %collective-permute-start = (bf16[256,512]{1,0:T(8,128)(2,1)}, bf16[256,512]{1,0:T(8,128)(2,1)S(1)}, u32[]{:S(2)}, u32[]{:S(2)}) collective-permute-start(bf16[256,512]{1,0:T(8,128)(2,1)} %q_ref.3), channel_id=1, source_target_pairs={{0,8},{8,0},{1,9},{9,1},{2,10},{10,2},{3,11},{11,3},{4,12},{12,4},... | collective-permute-start | bytes 786440 | tf_op jit(solution)/shard_map/ppermute | solution.py:457
  22.0 8.4 %collective-permute-start.1 = (bf16[8,512]{1,0:T(8,128)(2,1)S(1)}, bf16[8,512]{1,0:T(8,128)(2,1)S(1)}, u32[]{:S(2)}, u32[]{:S(2)}) collective-permute-start(bf16[8,512]{1,0:T(8,128)(2,1)S(1)} %pad.4), channel_id=1, source_target_pairs={{0,8},{8,0},{1,9},{9,1},{2,10},{10,2},{3,11},{11,3},{4,12},{12,4},... | collective-permute-start | bytes 24584 | tf_op jit(solution)/shard_map/ppermute | solution.py:457
  32.1 4.1 %copy-start.17 = (bf16[512,64]{0,1:T(8,128)(2,1)S(1)}, bf16[512,64]{0,1:T(8,128)(2,1)}, u32[]{:S(2)}) copy-start(bf16[512,64]{0,1:T(8,128)(2,1)} %param.16) | copy-start | bytes 196612
  32.1 28.7 %all-to-all-start = ((bf16[4,2,264,512]{3,2,1,0:T(8,128)(2,1)}), bf16[4,2,264,512]{3,2,1,0:T(8,128)(2,1)S(1)}, u32[]{:S(2)}, u32[]{:S(2)}) async-start(bf16[4,2,264,512]{3,2,1,0:T(8,128)(2,1)} %broadcast_in_dim.53), calls=%async_computation | async-start | bytes 4325376 | tf_op jit(solution)/shard_map/all_to_all | solution.py:453
  36.2 35.9 %copy-start.16 = (s32[2]{0:T(128)S(1)}, s32[2]{0:T(128)}, u32[]{:S(2)}) copy-start(s32[2]{0:T(128)} %param.19) | copy-start | bytes 28
  36.2 101.8 %all-gather.5.cloned.1.call-start = ((), (), s32[]{:S(2)}) async-start(), calls=%async_computation.8 | async-start | bytes 4718592 | tf_op jit(solution)/shard_map/all_gather | solution.py:462
  36.2 13.4 %collective-permute-start.3 = (bf16[64,512]{1,0:T(8,128)(2,1)S(1)}, bf16[64,512]{1,0:T(8,128)(2,1)S(1)}, u32[]{:S(2)}, u32[]{:S(2)}) collective-permute-start(bf16[64,512]{1,0:T(8,128)(2,1)S(1)} %bitcast.27), channel_id=1, source_target_pairs={{0,0},{1,64},{2,128},{3,192},{4,256},{5,320},{6,384},{7,448},{8,8}... | collective-permute-start | bytes 196616 | tf_op jit(solution)/shard_map/ppermute | solution.py:419
  41.9 12.8 %collective-permute-start.4 = (bf16[64,512]{1,0:T(8,128)(2,1)S(1)}, bf16[64,512]{1,0:T(8,128)(2,1)S(1)}, u32[]{:S(2)}, u32[]{:S(2)}) collective-permute-start(bf16[64,512]{1,0:T(8,128)(2,1)S(1)} %bitcast.28), channel_id=1, source_target_pairs={{0,8},{1,72},{2,136},{3,200},{4,264},{5,328},{6,392},{7,456},{8,0}... | collective-permute-start | bytes 196616 | tf_op jit(solution)/shard_map/ppermute | solution.py:420
  86.3 18.9 %all-to-all-start.4 = ((bf16[4,2,272,256]{3,2,1,0:T(8,128)(2,1)}), bf16[4,2,272,256]{3,2,1,0:T(8,128)(2,1)S(1)}, u32[]{:S(2)}, u32[]{:S(2)}) async-start(bf16[4,2,272,256]{3,2,1,0:T(8,128)(2,1)} %bitcast.11), calls=%async_computation.4 | async-start | bytes 2228224 | tf_op jit(solution)/shard_map/all_to_all | solution.py:511
  96.0 13.5 %copy-start.5 = (s32[16]{0:T(128)S(1)}, s32[16]{0:T(128)}, u32[]{:S(2)}) copy-start(s32[16]{0:T(128)} %drop_ref.1) | copy-start | bytes 196
  105.2 13.8 %copy-start.1 = (bf16[256,512]{1,0:T(8,128)(2,1)S(1)}, bf16[256,512]{1,0:T(8,128)(2,1)}, u32[]{:S(2)}) copy-start(bf16[256,512]{1,0:T(8,128)(2,1)} %q_ref.3) | copy-start | bytes 786436
  105.2 13.8 %copy-start.2 = (bf16[256,512]{1,0:T(8,128)(2,1)S(1)}, bf16[256,512]{1,0:T(8,128)(2,1)}, u32[]{:S(2)}) copy-start(bf16[256,512]{1,0:T(8,128)(2,1)} %v_ref.3) | copy-start | bytes 786436
  105.2 13.8 %copy-start.3 = (bf16[256,512]{1,0:T(8,128)(2,1)S(1)}, bf16[256,512]{1,0:T(8,128)(2,1)}, u32[]{:S(2)}) copy-start(bf16[256,512]{1,0:T(8,128)(2,1)} %k_ref.3) | copy-start | bytes 786436
  105.2 17.7 %all-to-all-start.1 = ((bf16[4,2,272,256]{3,2,1,0:T(8,128)(2,1)}), bf16[4,2,272,256]{3,2,1,0:T(8,128)(2,1)S(1)}, u32[]{:S(2)}, u32[]{:S(2)}) async-start(bf16[4,2,272,256]{3,2,1,0:T(8,128)(2,1)} %bitcast.6), calls=%async_computation.1 | async-start | bytes 2228224 | tf_op jit(solution)/shard_map/all_to_all | solution.py:511
  109.6 13.4 %copy-start.4 = (s32[3]{0:T(128)}, s32[3]{0:T(128)S(1)}, u32[]{:S(2)}) copy-start(s32[3]{0:T(128)S(1)} %pad_add_fusion.2.where_ref) | copy-start | bytes 40
  110.3 12.7 %copy-start = (f32[256,512]{1,0:T(8,128)}, f32[256,512]{1,0:T(8,128)S(1)}, u32[]{:S(2)}) copy-start(f32[256,512]{1,0:T(8,128)S(1)} %keep.1._.refs_3_) | copy-start | bytes 1572868
  111.2 19.6 %collective-permute-start.6 = (bf16[272,256]{1,0:T(8,128)(2,1)}, bf16[272,256]{1,0:T(8,128)(2,1)}, u32[]{:S(2)}, u32[]{:S(2)}) collective-permute-start(bf16[272,256]{1,0:T(8,128)(2,1)} %fold.3), channel_id=1, source_target_pairs={{0,8},{8,0},{1,9},{9,1},{2,10},{10,2},{3,11},{11,3},{4,12},{12,4},... | collective-permute-start | bytes 417800 | tf_op jit(solution)/shard_map/ppermute | solution.py:513
  119.7 0.7 copy-start.8
  121.1 0.7 copy-start.6
  123.0 14.3 %collective-permute-start.2 = (bf16[272,256]{1,0:T(8,128)(2,1)S(1)}, bf16[272,256]{1,0:T(8,128)(2,1)S(1)}, u32[]{:S(2)}, u32[]{:S(2)}) collective-permute-start(bf16[272,256]{1,0:T(8,128)(2,1)S(1)} %fold.2._), channel_id=1, source_target_pairs={{0,8},{8,0},{1,9},{9,1},{2,10},{10,2},{3,11},{11,3},{4,12},{12,4},... | collective-permute-start | bytes 417800 | tf_op jit(solution)/shard_map/ppermute | solution.py:513
  130.8 1.0 copy-start.9
  131.7 6.3 %copy-start.7 = (f32[256,256]{1,0:T(8,128)S(1)}, f32[256,256]{1,0:T(8,128)}, u32[]{:S(2)}) copy-start(f32[256,256]{1,0:T(8,128)} %copy-done.6) | copy-start | bytes 786436
  133.8 14.7 %all-to-all-start.5 = ((bf16[4,256,256]{2,1,0:T(8,128)(2,1)}), bf16[4,256,256]{2,1,0:T(8,128)(2,1)S(1)}, u32[]{:S(2)}, u32[]{:S(2)}) async-start(bf16[4,256,256]{2,1,0:T(8,128)(2,1)} %merge.3), calls=%async_computation.5 | async-start | bytes 1048576 | tf_op jit(solution)/shard_map/all_to_all | solution.py:517
  148.5 21.8 %copy-start.10 = (bf16[4,256,256]{2,1,0:T(8,128)(2,1)}, bf16[4,256,256]{2,1,0:T(8,128)(2,1)S(1)}, u32[]{:S(2)}) copy-start(bf16[4,256,256]{2,1,0:T(8,128)(2,1)S(1)} %all-to-all-done.5.refs_0_) | copy-start | bytes 1572868
  148.5 15.5 %all-to-all-start.3 = ((bf16[4,256,256]{2,1,0:T(8,128)(2,1)}), bf16[4,256,256]{2,1,0:T(8,128)(2,1)S(1)}, u32[]{:S(2)}, u32[]{:S(2)}) async-start(bf16[4,256,256]{2,1,0:T(8,128)(2,1)} %merge.2), calls=%async_computation.3 | async-start | bytes 1048576 | tf_op jit(solution)/shard_map/all_to_all | solution.py:517
  153.0 17.4 %collective-permute-start.7 = (bf16[4,256,256]{2,1,0:T(8,128)(2,1)S(1)}, bf16[4,256,256]{2,1,0:T(8,128)(2,1)S(1)}, u32[]{:S(2)}, u32[]{:S(2)}) collective-permute-start(bf16[4,256,256]{2,1,0:T(8,128)(2,1)S(1)} %all-to-all-done.5.refs_0_), channel_id=1, source_target_pairs={{0,1},{1,0},{2,3},{3,2},{4,5},{5,4},{6,7},{7,6},{8,9},{9,8},{10,11... | collective-permute-start | bytes 1572872 | tf_op jit(solution)/shard_map/ppermute | solution.py:518
  164.0 12.1 %copy-start.11 = (bf16[4,256,256]{2,1,0:T(8,128)(2,1)}, bf16[4,256,256]{2,1,0:T(8,128)(2,1)S(1)}, u32[]{:S(2)}) copy-start(bf16[4,256,256]{2,1,0:T(8,128)(2,1)S(1)} %all-to-all-done.3.refs_0_) | copy-start | bytes 1572868
  164.1 16.6 %collective-permute-start.5 = (bf16[4,256,256]{2,1,0:T(8,128)(2,1)S(1)}, bf16[4,256,256]{2,1,0:T(8,128)(2,1)S(1)}, u32[]{:S(2)}, u32[]{:S(2)}) collective-permute-start(bf16[4,256,256]{2,1,0:T(8,128)(2,1)S(1)} %all-to-all-done.3.refs_0_), channel_id=1, source_target_pairs={{0,1},{1,0},{2,3},{3,2},{4,5},{5,4},{6,7},{7,6},{8,9},{9,8},{10,11... | collective-permute-start | bytes 1572872 | tf_op jit(solution)/shard_map/ppermute | solution.py:518
  170.4 0.8 copy-start.13
  180.6 14.1 %copy-start.14 = (f32[512]{0:T(512)S(1)}, f32[512]{0:T(512)}, u32[]{:S(2)}) copy-start(f32[512]{0:T(512)} %param.18) | copy-start | bytes 6148
  180.6 14.1 %copy-start.15 = (f32[512]{0:T(512)S(1)}, f32[512]{0:T(512)}, u32[]{:S(2)}) copy-start(f32[512]{0:T(512)} %param.17) | copy-start | bytes 6148
  180.6 0.8 copy-start.12
Sparse Core Ops, SparseCore 0:
  9.4 71.0 all-gather.2
  82.6 55.4 all-gather.4

commit v8 on v7

--- a/solution.py
+++ b/solution.py
@@ -21,6 +21,7 @@
 TP = ("zl", "core")
 PLANE = ("x", "zh")
 PARTS = 2
+PROJECT_LIMIT = 48
 STAT_ROWS = 16
 NEG = -1e30
 EMPTY = -1e20
@@ -302,75 +303,69 @@
     )(where, drops)
 
 
-def project_kernel(part, shifts, last, where_ref, *refs):
-    count = len(shifts)
-    contexts, w_ref = refs[:count], refs[count]
-    rest, held_ref, sems = refs[count + 1 : -2], refs[-2], refs[-1]
+def project_kernel(where_ref, *refs):
+    contexts, rest = refs[: 2 * PARTS], refs[2 * PARTS :]
+    w_ref, keep_ref, res_ref, sum_ref, stat_ref, held_ref, sems = rest
     half, _, wide = contexts[0].shape
     copies = []
-    for i, shift in enumerate(shifts):
-        parity = lax.rem(where_ref[0] + shift, 2)
-        for z in range(half):
-            at = i * half + z
+    for z in range(half):
+        for shift in range(2):
+            at = 2 * z + shift
             copies.append(
                 pltpu.make_async_copy(
-                    w_ref.at[z, parity, :, part * wide : (part + 1) * wide],
+                    w_ref.at[2 * z + lax.rem(where_ref[0] + shift, 2)],
                     held_ref.at[at],
                     sems.at[at],
                 )
             )
             copies[-1].start()
-    acc = rest[0][...] if len(rest) > 1 else None
+    acc = None
     for at, copy in enumerate(copies):
         copy.wait()
-        term = dot_t(contexts[at // half][at % half], held_ref[at])
-        acc = term if acc is None else acc + term
-    if not last:
-        rest[-1][...] = acc
-        return
-    _, keep_ref, res_ref, sum_ref, stat_ref = rest
-    cols = acc.shape[1]
+        for part in range(PARTS):
+            term = dot_t(
+                contexts[2 * part + at % 2][at // 2],
+                held_ref[at, :, part * wide : (part + 1) * wide],
+            )
+            acc = term if acc is None else acc + term
+    rows, cols = acc.shape
     total = res_ref[...].astype(F32) + keep_ref[...] * acc
     sum_ref[...] = total
     mean = jnp.sum(total, axis=1, keepdims=True) * jnp.float32(1.0 / cols)
     dev = total - mean
     spread = jnp.sum(dev * dev, axis=1, keepdims=True)
-    lane = lax.broadcasted_iota(jnp.int32, stat_ref.shape, 1)
-    stat_ref[...] = jnp.where(lane == 0, mean, spread)
-
-
-def project(part, shifts, where, contexts, weight, before=None, finish=None):
-    half, rows, wide = contexts[0].shape
-    cols = weight.shape[2]
-    out = (rows, cols)
-    pieces = half * len(contexts)
-    args = list(contexts) + [weight]
-    specs = [whole(c.shape) for c in contexts] + [pl.BlockSpec(memory_space=pltpu.HBM)]
-    out_specs, out_shape = [whole(out)], [jax.ShapeDtypeStruct(out, F32)]
-    if before is not None:
-        args.append(before)
-        specs.append(whole(out))
-    if finish is not None:
-        args += list(finish)
-        specs += [whole(x.shape) for x in finish]
-        out_specs.append(whole((rows, DH)))
-        out_shape.append(jax.ShapeDtypeStruct((rows, DH), F32))
+    lane = lax.broadcasted_iota(jnp.int32, (rows, DH), 1)
+    lines = jnp.where(lane == 0, mean, spread).T[:2, :]
+    for copy in range(stat_ref.shape[0]):
+        stat_ref[copy] = lines
+
+
+def project(where, contexts, weight, kept, residual):
+    rows, cols = residual.shape
+    groups = weight.shape[0]
+    args = list(contexts) + [weight, kept, residual]
+    specs = [whole(x.shape) for x in args]
+    specs[len(contexts)] = pl.BlockSpec(memory_space=pltpu.HBM)
+    stat = (groups, 2, rows)
     return pl.pallas_call(
-        functools.partial(project_kernel, part, shifts, finish is not None),
+        project_kernel,
         grid_spec=pltpu.PrefetchScalarGridSpec(
             num_scalar_prefetch=1,
             grid=(1,),
             in_specs=specs,
-            out_specs=out_specs,
+            out_specs=[whole((rows, cols)), whole(stat)],
             scratch_shapes=[
-                pltpu.VMEM((pieces, cols, wide), BF),
-                pltpu.SemaphoreType.DMA((pieces,)),
+                pltpu.VMEM(weight.shape, BF),
+                pltpu.SemaphoreType.DMA((groups,)),
             ],
         ),
-        out_shape=out_shape,
-        compiler_params=params(59 << 20),
+        out_shape=[
+            jax.ShapeDtypeStruct((rows, cols), F32),
+            jax.ShapeDtypeStruct(stat, F32),
+        ],
+        compiler_params=params(PROJECT_LIMIT << 20),
         cost_estimate=pl.CostEstimate(
-            flops=2 * rows * pieces * wide * cols, transcendentals=0, bytes_accessed=2 << 20
+            flops=2 * rows * D * cols, transcendentals=0, bytes_accessed=6 << 20
         ),
         name="project",
     )(where, *args)
@@ -462,7 +457,7 @@
     weight = lax.all_gather(
         shards.reshape(plane * cols_here, width_here), "y", axis=0, tiled=True
     )
-    weight = weight.reshape(n_zl, 2, plane * cols_here, width_here)
+    weight = weight.reshape(tp_count, plane * cols_here, width_here)
 
     lists = asked[:, :, row_count, : cells.shape[0]].reshape(plane, plane, 2 * slots)
     lists = lax.dynamic_index_in_dim(lists, plane_at, 1, keepdims=False).astype(jnp.int32)
@@ -511,18 +506,12 @@
         got = lax.all_to_all(partials, "x", split_axis=0, concat_axis=0, tiled=True)
         gone = fold(zh, got, kept)
         folded.append((got, lax.ppermute(gone, "zh", flip)))
-    mine, other = [], []
+    contexts = []
     for part in range(PARTS):
         context = merge(zh, *folded[part], *near[part], (gone, weight)[part], n_zl)
-        mine.append(lax.all_to_all(context, "zl", split_axis=0, concat_axis=0, tiled=True))
-        other.append(lax.ppermute(mine[part], "core", flip))
-    (acc,) = project(0, (0, 1), where, (mine[0], other[0]), weight)
-    (acc,) = project(1, (0,), where, (mine[1],), weight, before=acc)
-    summed, stats = project(
-        1, (1,), where, (other[1],), weight, before=acc, finish=(kept, residual)
-    )
-
-    stats = jnp.broadcast_to(stats[:, :2].T[None], (tp_count, 2, row_count))
+        mine = lax.all_to_all(context, "zl", split_axis=0, concat_axis=0, tiled=True)
+        contexts += [mine, lax.ppermute(mine, "core", flip)]
+    summed, stats = project(where, contexts, weight, kept, residual)
     stats = lax.all_to_all(stats, TP, split_axis=0, concat_axis=0, tiled=True)
     means, spreads = stats[:, 0], stats[:, 1]
     mean = jnp.sum(means, axis=0) / tp_count

time: 205 us -> 192 us (0.937)
  Pallas kernels: 32.6 us -> 21.8 us
    pallas_call x3 -> x1, Pallas kernels: 14 us -> 3.74 us  [project(): pl.pallas_call(project_kernel, grid_spec=pltpu.PrefetchScalarGridSpec(num...]
    unnamed x38 -> x30, local copies, waits for them, and re-layouts: 5.49 us -> 5.67 us
  transfers between devices with their start and end apart: 15 -> 15, of which waited for: 9 -> 10; matrix products, arithmetic and copies ran while one was open for 3% -> 3% of each run, Pallas kernels for 14% -> 9%
where the time goes in v8:
time: 192 us; the launch traced here: 191 us
  starting transfers between devices  73.2 us (38%)
  waiting for transfers between devices  50.1 us (26%)
  Pallas kernels  21.8 us (11%)
  blocking collectives  17.9 us (9%)
  between operations  15.1 us (8%)
  local copies, waits for them, and re-layouts  8.4 us (4%)
  other arithmetic  4.69 us (2%)
    ppermute x2, starting transfers between devices, on_device(): folded.append((got, lax.ppermute(gone, 'zh', flip)))  15.5 us
    all_to_all x2, waiting for transfers between devices, on_device(): lax.all_to_all(context, 'zl', split_axis=0, concat_axis=0, tiled=True)  13.3 us
    pallas_call x2, Pallas kernels, serve(): pl.pallas_call(serve_kernel, grid_spec=pltpu.PrefetchScalarGridSpec(num_s...  11.6 us
    ppermute x1, starting transfers between devices, on_device(): lax.ppermute(queries, 'zh', flip)  11.5 us
    ppermute x2, starting transfers between devices, on_device(): contexts += [mine, lax.ppermute(mine, 'core', flip)]  11.4 us
    all_to_all x2, waiting for transfers between devices, on_device(): got = lax.all_to_all(partials, 'x', split_axis=0, concat_axis=0, tiled=True)  10.2 us
    all_to_all x1, blocking collectives, over_x(): return lax.all_to_all(x, 'x', split_axis=0, concat_axis=0, tiled=True)  10 us
    all_to_all x2, starting transfers between devices, on_device(): lax.all_to_all(context, 'zl', split_axis=0, concat_axis=0, tiled=True)  7.91 us
  transfers between devices with their start and end apart: 15, of which 10 were waited for; matrix products, arithmetic and copies ran while one was open for 3% of the time, Pallas kernels for 9%

profile of v8, /device:TPU:1, one launch (start us, length us, event | category | flops | bytes accessed | tf_op | source)
XLA Modules:
  0.0 191.2 jit_solution(12470440682146252046)
XLA Ops:
  6.5 2.0 %pad_maximum_fusion.1 = bf16[256,1024]{1,0:T(8,128)(2,1)} fusion(bf16[256,512]{1,0:T(8,128)(2,1)} %v_ref.3, bf16[256,512]{1,0:T(8,128)(2,1)} %k_ref.3), kind=kLoop, calls=%fused_computation.1 | loop fusion | flops 1048576 | bytes 1048576 | tf_op jit(solution)/shard_map/concatenate | solution.py:403
  8.5 0.0 all-gather.3.cloned.1.call-update
  8.5 11.5 %collective-permute-start = (bf16[256,512]{1,0:T(8,128)(2,1)}, bf16[256,512]{1,0:T(8,128)(2,1)S(1)}, u32[]{:S(2)}, u32[]{:S(2)}) collective-permute-start(bf16[256,512]{1,0:T(8,128)(2,1)} %q_ref.3), channel_id=1, source_target_pairs={{0,8},{8,0},{1,9},{9,1},{2,10},{10,2},{3,11},{11,3},{4,12},{12,4},... | collective-permute-start | bytes 786440 | tf_op jit(solution)/shard_map/ppermute | solution.py:452
  20.0 0.8 copy.17
  20.8 0.1 reshape.406
  20.9 0.2 convert_reduce_fusion
  21.1 0.8 copy.18
  21.8 0.1 broadcast_in_dim.47
  21.9 0.1 select_reduce_fusion
  22.1 1.9 %collective-permute-start.1 = (bf16[8,512]{1,0:T(8,128)(2,1)S(1)}, bf16[8,512]{1,0:T(8,128)(2,1)S(1)}, u32[]{:S(2)}, u32[]{:S(2)}) collective-permute-start(bf16[8,512]{1,0:T(8,128)(2,1)S(1)} %pad.4), channel_id=1, source_target_pairs={{0,8},{8,0},{1,9},{9,1},{2,10},{10,2},{3,11},{11,3},{4,12},{12,4},... | collective-permute-start | bytes 24584 | tf_op jit(solution)/shard_map/ppermute | solution.py:452
  24.0 1.0 maximum_bitcast_fusion
  25.0 5.5 %collective-permute-done.1 = bf16[8,512]{1,0:T(8,128)(2,1)S(1)} collective-permute-done((bf16[8,512]{1,0:T(8,128)(2,1)S(1)}, bf16[8,512]{1,0:T(8,128)(2,1)S(1)}, u32[]{:S(2)}, u32[]{:S(2)}) %collective-permute-start.1) | collective-permute-done | bytes 8224 | tf_op jit(solution)/shard_map/ppermute | solution.py:452
  30.5 0.1 pad_maximum_fusion
  30.6 1.6 broadcast_in_dim.51
  32.2 4.1 %all-to-all-start = ((bf16[4,2,264,512]{3,2,1,0:T(8,128)(2,1)}), bf16[4,2,264,512]{3,2,1,0:T(8,128)(2,1)S(1)}, u32[]{:S(2)}, u32[]{:S(2)}) async-start(bf16[4,2,264,512]{3,2,1,0:T(8,128)(2,1)} %broadcast_in_dim.51), calls=%async_computation | async-start | bytes 4325376 | tf_op jit(solution)/shard_map/all_to_all | solution.py:448
  36.3 5.6 %collective-permute-start.5 = (bf16[64,512]{1,0:T(8,128)(2,1)S(1)}, bf16[64,512]{1,0:T(8,128)(2,1)S(1)}, u32[]{:S(2)}, u32[]{:S(2)}) collective-permute-start(bf16[64,512]{1,0:T(8,128)(2,1)S(1)} %bitcast.23), channel_id=1, source_target_pairs={{0,0},{1,64},{2,128},{3,192},{4,256},{5,320},{6,384},{7,448},{8,8}... | collective-permute-start | bytes 196616 | tf_op jit(solution)/shard_map/ppermute | solution.py:414
  41.9 7.7 %collective-permute-start.6 = (bf16[64,512]{1,0:T(8,128)(2,1)S(1)}, bf16[64,512]{1,0:T(8,128)(2,1)S(1)}, u32[]{:S(2)}, u32[]{:S(2)}) collective-permute-start(bf16[64,512]{1,0:T(8,128)(2,1)S(1)} %bitcast.24), channel_id=1, source_target_pairs={{0,8},{1,72},{2,136},{3,200},{4,264},{5,328},{6,392},{7,456},{8,0}... | collective-permute-start | bytes 196616 | tf_op jit(solution)/shard_map/ppermute | solution.py:415
  49.6 5.0 %collective-permute-done.6 = bf16[64,512]{1,0:T(8,128)(2,1)S(1)} collective-permute-done((bf16[64,512]{1,0:T(8,128)(2,1)S(1)}, bf16[64,512]{1,0:T(8,128)(2,1)S(1)}, u32[]{:S(2)}, u32[]{:S(2)}) %collective-permute-start.6) | collective-permute-done | bytes 65568 | tf_op jit(solution)/shard_map/ppermute | solution.py:415
  54.7 6.1 %all-to-all-done.q_ref = bf16[4,2,264,512]{3,2,1,0:T(8,128)(2,1)S(1)} async-done(((bf16[4,2,264,512]{3,2,1,0:T(8,128)(2,1)}), bf16[4,2,264,512]{3,2,1,0:T(8,128)(2,1)S(1)}, u32[]{:S(2)}, u32[]{:S(2)}) %all-to-all-start) | async-done | bytes 2162720 | tf_op jit(solution)/shard_map/all_to_all | solution.py:448
  60.8 0.5 slice.25
  62.1 10.0 %all_to_all.35 = bf16[4,128,512]{2,1,0:T(8,128)(2,1)} all-to-all(bf16[4,128,512]{2,1,0:T(8,128)(2,1)S(1)} %broadcast_in_dim.55), channel_id=1, replica_groups=mesh['y'=8,'x'=4,'zh'=2,'zl'=4,'core'=2] {'x'}, dimensions={0} | all-to-all | bytes 1048576 | tf_op jit(solution)/shard_map/all_to_all | solution.py:448
  72.1 0.0 all-gather.5.cloned.1.call-update
  72.2 0.1 pad.14.clone
  72.3 0.1 pad.10.clone
  72.4 0.1 reshape_squeeze.3
  72.5 0.1 compare_select_fusion
  72.6 0.1 pad_add_fusion
  72.7 0.1 reshape.407.row_ref
  72.8 0.1 pad_add_fusion.1
  72.8 0.1 reshape.408.mark_ref
  72.9 7.6 %all-gather.3.cloned.1.call-done.key_ref.value_ref = bf16[2048,1024]{1,0:T(8,128)(2,1)} async-done(((bf16[256,1024]{1,0:T(8,128)(2,1)}), bf16[2048,1024]{1,0:T(8,128)(2,1)}) %all-gather.3.cloned.1.call-update) | async-done | bytes 4194320 | tf_op jit(solution)/shard_map/all_gather | solution.py:404
  80.5 5.8 %serve.2 = bf16[8,272,256]{2,1,0:T(8,128)(2,1)} custom-call(s32[160]{0:T(256)S(1)} %reshape.407.row_ref, s32[160]{0:T(256)S(1)} %reshape.408.mark_ref, s32[1]{0:T(128)} %bitcast.2.zh_ref, bf16[4,2,264,512]{3,2,1,0:T(8,128)(2,1)S(1)} %all-to-all-done.q_ref, bf16[2048,1024]{1,0:T(8,128)(2,1)} %all-gather.3.cloned.1.call-done.key_ref.value_ref, ...), custom_call_target="tpu_custom_call" | custom-call | flops 671088640 | bytes 4194304 | tf_op jit(solution)/shard_map/serve/pallas_call | solution.py:117
  86.3 4.0 %all-to-all-start.1 = ((bf16[4,2,272,256]{3,2,1,0:T(8,128)(2,1)}), bf16[4,2,272,256]{3,2,1,0:T(8,128)(2,1)S(1)}, u32[]{:S(2)}, u32[]{:S(2)}) async-start(bf16[4,2,272,256]{3,2,1,0:T(8,128)(2,1)} %bitcast.6), calls=%async_computation.1 | async-start | bytes 2228224 | tf_op jit(solution)/shard_map/all_to_all | solution.py:506
  90.3 5.8 %serve.3 = bf16[8,272,256]{2,1,0:T(8,128)(2,1)} custom-call(s32[160]{0:T(256)S(1)} %reshape.407.row_ref, s32[160]{0:T(256)S(1)} %reshape.408.mark_ref, s32[1]{0:T(128)} %bitcast.2.zh_ref, bf16[4,2,264,512]{3,2,1,0:T(8,128)(2,1)S(1)} %all-to-all-done.q_ref, bf16[2048,1024]{1,0:T(8,128)(2,1)} %all-gather.3.cloned.1.call-done.key_ref.value_ref, ...), custom_call_target="tpu_custom_call" | custom-call | flops 671088640 | bytes 4194304 | tf_op jit(solution)/shard_map/serve/pallas_call | solution.py:117
  96.1 9.1 %all-to-all-done.1.got_ref = bf16[4,2,272,256]{3,2,1,0:T(8,128)(2,1)S(1)} async-done(((bf16[4,2,272,256]{3,2,1,0:T(8,128)(2,1)}), bf16[4,2,272,256]{3,2,1,0:T(8,128)(2,1)S(1)}, u32[]{:S(2)}, u32[]{:S(2)}) %all-to-all-start.1) | async-done | bytes 1114144 | tf_op jit(solution)/shard_map/all_to_all | solution.py:506
  105.2 3.7 %all-to-all-start.2 = ((bf16[4,2,272,256]{3,2,1,0:T(8,128)(2,1)}), bf16[4,2,272,256]{3,2,1,0:T(8,128)(2,1)S(1)}, u32[]{:S(2)}, u32[]{:S(2)}) async-start(bf16[4,2,272,256]{3,2,1,0:T(8,128)(2,1)} %bitcast.7), calls=%async_computation.2 | async-start | bytes 2228224 | tf_op jit(solution)/shard_map/all_to_all | solution.py:506
  109.5 0.1 pad_add_fusion.2.where_ref
  109.6 0.8 keep.1._.refs_5_
  110.4 0.8 fold.2
  111.2 7.7 %collective-permute-start.2 = (bf16[272,256]{1,0:T(8,128)(2,1)}, bf16[272,256]{1,0:T(8,128)(2,1)}, u32[]{:S(2)}, u32[]{:S(2)}) collective-permute-start(bf16[272,256]{1,0:T(8,128)(2,1)} %fold.2), channel_id=1, source_target_pairs={{0,8},{8,0},{1,9},{9,1},{2,10},{10,2},{3,11},{11,3},{4,12},{12,4},... | collective-permute-start | bytes 417800 | tf_op jit(solution)/shard_map/ppermute | solution.py:508
  118.9 0.7 local.2
  119.7 0.7 copy-done.8
  120.4 0.7 local.3
  121.1 0.7 copy-done.6
  121.8 1.1 all-to-all-done.2.got_ref
  122.9 0.1 fold.3._
  123.0 7.7 %collective-permute-start.4 = (bf16[272,256]{1,0:T(8,128)(2,1)S(1)}, bf16[272,256]{1,0:T(8,128)(2,1)}, u32[]{:S(2)}, u32[]{:S(2)}) collective-permute-start(bf16[272,256]{1,0:T(8,128)(2,1)S(1)} %fold.3._), channel_id=1, source_target_pairs={{0,8},{8,0},{1,9},{9,1},{2,10},{10,2},{3,11},{11,3},{4,12},{12,4},... | collective-permute-start | bytes 417800 | tf_op jit(solution)/shard_map/ppermute | solution.py:508
  130.8 0.0 copy-start.9
  130.8 0.9 copy-done.9
  131.7 1.2 merge.2
  133.0 0.8 copy-done.3
  133.8 3.5 %all-to-all-start.3 = ((bf16[4,256,256]{2,1,0:T(8,128)(2,1)}), bf16[4,256,256]{2,1,0:T(8,128)(2,1)S(1)}, u32[]{:S(2)}, u32[]{:S(2)}) async-start(bf16[4,256,256]{2,1,0:T(8,128)(2,1)} %copy-done.3), calls=%async_computation.3 | async-start | bytes 1048576 | tf_op jit(solution)/shard_map/all_to_all | solution.py:512
  137.3 0.8 all-gather.5.cloned.1.call-done._
  138.1 0.9 copy-done.7
  139.0 2.1 %merge.3 = bf16[4,256,256]{2,1,0:T(8,128)(2,1)} custom-call(s32[1]{0:T(128)} %bitcast.2.zh_ref, bf16[4,2,272,256]{3,2,1,0:T(8,128)(2,1)S(1)} %all-to-all-done.2.got_ref, bf16[272,256]{1,0:T(8,128)(2,1)} %collective-permute-done.4.far_ref, f32[256,256]{1,0:T(8,128)S(1)} %copy-done.7, f32[4,256]{1,0:T(4,128)S(1)} %get-tuple-element.14.stat_ref, ...), custom_call_target="tpu_custom_call" | custom-call | flops 30000001024 | bytes 1048576 | tf_op jit(solution)/shard_map/merge/pallas_call | solution.py:251
  141.1 7.4 %all-to-all-done.3.refs_0_ = bf16[4,256,256]{2,1,0:T(8,128)(2,1)S(1)} async-done(((bf16[4,256,256]{2,1,0:T(8,128)(2,1)}), bf16[4,256,256]{2,1,0:T(8,128)(2,1)S(1)}, u32[]{:S(2)}, u32[]{:S(2)}) %all-to-all-start.3) | async-done | bytes 524320 | tf_op jit(solution)/shard_map/all_to_all | solution.py:512
  148.5 4.4 %all-to-all-start.5 = ((bf16[4,256,256]{2,1,0:T(8,128)(2,1)}), bf16[4,256,256]{2,1,0:T(8,128)(2,1)S(1)}, u32[]{:S(2)}, u32[]{:S(2)}) async-start(bf16[4,256,256]{2,1,0:T(8,128)(2,1)} %merge.3), calls=%async_computation.5 | async-start | bytes 1048576 | tf_op jit(solution)/shard_map/all_to_all | solution.py:512
  153.0 5.1 %collective-permute-start.3 = (bf16[4,256,256]{2,1,0:T(8,128)(2,1)S(1)}, bf16[4,256,256]{2,1,0:T(8,128)(2,1)S(1)}, u32[]{:S(2)}, u32[]{:S(2)}) collective-permute-start(bf16[4,256,256]{2,1,0:T(8,128)(2,1)S(1)} %all-to-all-done.3.refs_0_), channel_id=1, source_target_pairs={{0,1},{1,0},{2,3},{3,2},{4,5},{5,4},{6,7},{7,6},{8,9},{9,8},{10,11... | collective-permute-start | bytes 1572872 | tf_op jit(solution)/shard_map/ppermute | solution.py:513
  158.1 5.9 %all-to-all-done.5.refs_2_ = bf16[4,256,256]{2,1,0:T(8,128)(2,1)S(1)} async-done(((bf16[4,256,256]{2,1,0:T(8,128)(2,1)}), bf16[4,256,256]{2,1,0:T(8,128)(2,1)S(1)}, u32[]{:S(2)}, u32[]{:S(2)}) %all-to-all-start.5) | async-done | bytes 524320 | tf_op jit(solution)/shard_map/all_to_all | solution.py:512
  164.0 6.3 %collective-permute-start.7 = (bf16[4,256,256]{2,1,0:T(8,128)(2,1)S(1)}, bf16[4,256,256]{2,1,0:T(8,128)(2,1)S(1)}, u32[]{:S(2)}, u32[]{:S(2)}) collective-permute-start(bf16[4,256,256]{2,1,0:T(8,128)(2,1)S(1)} %all-to-all-done.5.refs_2_), channel_id=1, source_target_pairs={{0,1},{1,0},{2,3},{3,2},{4,5},{5,4},{6,7},{7,6},{8,9},{9,8},{10,11... | collective-permute-start | bytes 1572872 | tf_op jit(solution)/shard_map/ppermute | solution.py:513
  170.3 1.5 collective-permute-done.7.refs_3_
  171.8 3.7 %project.1 = (f32[256,512]{1,0:T(8,128)S(1)}, f32[8,2,256]{2,1,0:T(2,128)S(1)}) custom-call(s32[3]{0:T(128)S(1)} %pad_add_fusion.2.where_ref, bf16[4,256,256]{2,1,0:T(8,128)(2,1)S(1)} %all-to-all-done.3.refs_0_, bf16[4,256,256]{2,1,0:T(8,128)(2,1)S(1)} %collective-permute-done.3.refs_1_, bf16[4,256,256]{2,1,0:T(8,128)(2,1)S(1)} %all-to-all-done.5.refs_2_, ...), custom_call_target="tpu_custom_call" | custom-call | flops 1073741824 | bytes 6291456 | tf_op jit(solution)/shard_map/project/pallas_call | solution.py:350
  175.6 7.8 %all_to_all.36 = f32[8,2,256]{2,1,0:T(2,128)S(1)} all-to-all(f32[8,2,256]{2,1,0:T(2,128)S(1)} %get-tuple-element.16), channel_id=1, replica_groups=mesh['y'=8,'x'=4,'zh'=2,'zl'=4,'core'=2] {'zl','core'}, dimensions={0} | all-to-all | bytes 32768 | tf_op jit(solution)/shard_map/all_to_all | solution.py:515
  183.5 0.9 add_convert_fusion
  (48 shorter events, 0.4 us)
Async XLA Ops:
  6.5 74.0 %all-gather.3.cloned.1.call-start = ((), (), s32[]{:S(2)}) async-start(), calls=%async_computation.7 | async-start | bytes 4718592 | tf_op jit(solution)/shard_map/all_gather | solution.py:404
  8.5 22.0 %collective-permute-start = (bf16[256,512]{1,0:T(8,128)(2,1)}, bf16[256,512]{1,0:T(8,128)(2,1)S(1)}, u32[]{:S(2)}, u32[]{:S(2)}) collective-permute-start(bf16[256,512]{1,0:T(8,128)(2,1)} %q_ref.3), channel_id=1, source_target_pairs={{0,8},{8,0},{1,9},{9,1},{2,10},{10,2},{3,11},{11,3},{4,12},{12,4},... | collective-permute-start | bytes 786440 | tf_op jit(solution)/shard_map/ppermute | solution.py:452
  22.1 8.4 %collective-permute-start.1 = (bf16[8,512]{1,0:T(8,128)(2,1)S(1)}, bf16[8,512]{1,0:T(8,128)(2,1)S(1)}, u32[]{:S(2)}, u32[]{:S(2)}) collective-permute-start(bf16[8,512]{1,0:T(8,128)(2,1)S(1)} %pad.4), channel_id=1, source_target_pairs={{0,8},{8,0},{1,9},{9,1},{2,10},{10,2},{3,11},{11,3},{4,12},{12,4},... | collective-permute-start | bytes 24584 | tf_op jit(solution)/shard_map/ppermute | solution.py:452
  32.2 4.1 %copy-start.13 = (bf16[512,64]{0,1:T(8,128)(2,1)S(1)}, bf16[512,64]{0,1:T(8,128)(2,1)}, u32[]{:S(2)}) copy-start(bf16[512,64]{0,1:T(8,128)(2,1)} %param.16) | copy-start | bytes 196612
  32.2 28.7 %all-to-all-start = ((bf16[4,2,264,512]{3,2,1,0:T(8,128)(2,1)}), bf16[4,2,264,512]{3,2,1,0:T(8,128)(2,1)S(1)}, u32[]{:S(2)}, u32[]{:S(2)}) async-start(bf16[4,2,264,512]{3,2,1,0:T(8,128)(2,1)} %broadcast_in_dim.51), calls=%async_computation | async-start | bytes 4325376 | tf_op jit(solution)/shard_map/all_to_all | solution.py:448
  36.3 35.9 %copy-start.12 = (s32[2]{0:T(128)S(1)}, s32[2]{0:T(128)}, u32[]{:S(2)}) copy-start(s32[2]{0:T(128)} %param.19) | copy-start | bytes 28
  36.3 101.8 %all-gather.5.cloned.1.call-start = ((), (), s32[]{:S(2)}) async-start(), calls=%async_computation.8 | async-start | bytes 4718592 | tf_op jit(solution)/shard_map/all_gather | solution.py:457
  36.3 13.4 %collective-permute-start.5 = (bf16[64,512]{1,0:T(8,128)(2,1)S(1)}, bf16[64,512]{1,0:T(8,128)(2,1)S(1)}, u32[]{:S(2)}, u32[]{:S(2)}) collective-permute-start(bf16[64,512]{1,0:T(8,128)(2,1)S(1)} %bitcast.23), channel_id=1, source_target_pairs={{0,0},{1,64},{2,128},{3,192},{4,256},{5,320},{6,384},{7,448},{8,8}... | collective-permute-start | bytes 196616 | tf_op jit(solution)/shard_map/ppermute | solution.py:414
  41.9 12.8 %collective-permute-start.6 = (bf16[64,512]{1,0:T(8,128)(2,1)S(1)}, bf16[64,512]{1,0:T(8,128)(2,1)S(1)}, u32[]{:S(2)}, u32[]{:S(2)}) collective-permute-start(bf16[64,512]{1,0:T(8,128)(2,1)S(1)} %bitcast.24), channel_id=1, source_target_pairs={{0,8},{1,72},{2,136},{3,200},{4,264},{5,328},{6,392},{7,456},{8,0}... | collective-permute-start | bytes 196616 | tf_op jit(solution)/shard_map/ppermute | solution.py:415
  86.3 18.8 %all-to-all-start.1 = ((bf16[4,2,272,256]{3,2,1,0:T(8,128)(2,1)}), bf16[4,2,272,256]{3,2,1,0:T(8,128)(2,1)S(1)}, u32[]{:S(2)}, u32[]{:S(2)}) async-start(bf16[4,2,272,256]{3,2,1,0:T(8,128)(2,1)} %bitcast.6), calls=%async_computation.1 | async-start | bytes 2228224 | tf_op jit(solution)/shard_map/all_to_all | solution.py:506
  96.1 13.5 %copy-start.5 = (s32[16]{0:T(128)S(1)}, s32[16]{0:T(128)}, u32[]{:S(2)}) copy-start(s32[16]{0:T(128)} %drop_ref.1) | copy-start | bytes 196
  105.2 13.7 %copy-start = (bf16[256,512]{1,0:T(8,128)(2,1)S(1)}, bf16[256,512]{1,0:T(8,128)(2,1)}, u32[]{:S(2)}) copy-start(bf16[256,512]{1,0:T(8,128)(2,1)} %q_ref.3) | copy-start | bytes 786436
  105.2 13.7 %copy-start.1 = (bf16[256,512]{1,0:T(8,128)(2,1)S(1)}, bf16[256,512]{1,0:T(8,128)(2,1)}, u32[]{:S(2)}) copy-start(bf16[256,512]{1,0:T(8,128)(2,1)} %v_ref.3) | copy-start | bytes 786436
  105.2 13.7 %copy-start.2 = (bf16[256,512]{1,0:T(8,128)(2,1)S(1)}, bf16[256,512]{1,0:T(8,128)(2,1)}, u32[]{:S(2)}) copy-start(bf16[256,512]{1,0:T(8,128)(2,1)} %k_ref.3) | copy-start | bytes 786436
  105.2 17.7 %all-to-all-start.2 = ((bf16[4,2,272,256]{3,2,1,0:T(8,128)(2,1)}), bf16[4,2,272,256]{3,2,1,0:T(8,128)(2,1)S(1)}, u32[]{:S(2)}, u32[]{:S(2)}) async-start(bf16[4,2,272,256]{3,2,1,0:T(8,128)(2,1)} %bitcast.7), calls=%async_computation.2 | async-start | bytes 2228224 | tf_op jit(solution)/shard_map/all_to_all | solution.py:506
  111.2 19.6 %collective-permute-start.2 = (bf16[272,256]{1,0:T(8,128)(2,1)}, bf16[272,256]{1,0:T(8,128)(2,1)}, u32[]{:S(2)}, u32[]{:S(2)}) collective-permute-start(bf16[272,256]{1,0:T(8,128)(2,1)} %fold.2), channel_id=1, source_target_pairs={{0,8},{8,0},{1,9},{9,1},{2,10},{10,2},{3,11},{11,3},{4,12},{12,4},... | collective-permute-start | bytes 417800 | tf_op jit(solution)/shard_map/ppermute | solution.py:508
  119.7 0.7 copy-start.8
  121.1 0.7 copy-start.6
  123.0 14.2 %collective-permute-start.4 = (bf16[272,256]{1,0:T(8,128)(2,1)S(1)}, bf16[272,256]{1,0:T(8,128)(2,1)}, u32[]{:S(2)}, u32[]{:S(2)}) collective-permute-start(bf16[272,256]{1,0:T(8,128)(2,1)S(1)} %fold.3._), channel_id=1, source_target_pairs={{0,8},{8,0},{1,9},{9,1},{2,10},{10,2},{3,11},{11,3},{4,12},{12,4},... | collective-permute-start | bytes 417800 | tf_op jit(solution)/shard_map/ppermute | solution.py:508
  130.8 1.0 copy-start.9
  133.0 0.8 copy-start.3
  133.8 14.7 %all-to-all-start.3 = ((bf16[4,256,256]{2,1,0:T(8,128)(2,1)}), bf16[4,256,256]{2,1,0:T(8,128)(2,1)S(1)}, u32[]{:S(2)}, u32[]{:S(2)}) async-start(bf16[4,256,256]{2,1,0:T(8,128)(2,1)} %copy-done.3), calls=%async_computation.3 | async-start | bytes 1048576 | tf_op jit(solution)/shard_map/all_to_all | solution.py:512
  138.1 0.9 copy-start.7
  139.0 32.8 %copy-start.4 = (bf16[256,512]{1,0:T(8,128)(2,1)S(1)}, bf16[256,512]{1,0:T(8,128)(2,1)}, u32[]{:S(2)}) copy-start(bf16[256,512]{1,0:T(8,128)(2,1)} %refs_6_.1) | copy-start | bytes 786436
  148.5 15.5 %all-to-all-start.5 = ((bf16[4,256,256]{2,1,0:T(8,128)(2,1)}), bf16[4,256,256]{2,1,0:T(8,128)(2,1)S(1)}, u32[]{:S(2)}, u32[]{:S(2)}) async-start(bf16[4,256,256]{2,1,0:T(8,128)(2,1)} %merge.3), calls=%async_computation.5 | async-start | bytes 1048576 | tf_op jit(solution)/shard_map/all_to_all | solution.py:512
  153.0 17.4 %collective-permute-start.3 = (bf16[4,256,256]{2,1,0:T(8,128)(2,1)S(1)}, bf16[4,256,256]{2,1,0:T(8,128)(2,1)S(1)}, u32[]{:S(2)}, u32[]{:S(2)}) collective-permute-start(bf16[4,256,256]{2,1,0:T(8,128)(2,1)S(1)} %all-to-all-done.3.refs_0_), channel_id=1, source_target_pairs={{0,1},{1,0},{2,3},{3,2},{4,5},{5,4},{6,7},{7,6},{8,9},{9,8},{10,11... | collective-permute-start | bytes 1572872 | tf_op jit(solution)/shard_map/ppermute | solution.py:513
  164.0 7.8 %collective-permute-start.7 = (bf16[4,256,256]{2,1,0:T(8,128)(2,1)S(1)}, bf16[4,256,256]{2,1,0:T(8,128)(2,1)S(1)}, u32[]{:S(2)}, u32[]{:S(2)}) collective-permute-start(bf16[4,256,256]{2,1,0:T(8,128)(2,1)S(1)} %all-to-all-done.5.refs_2_), channel_id=1, source_target_pairs={{0,1},{1,0},{2,3},{3,2},{4,5},{5,4},{6,7},{7,6},{8,9},{9,8},{10,11... | collective-permute-start | bytes 1572872 | tf_op jit(solution)/shard_map/ppermute | solution.py:513
  171.8 11.7 %copy-start.10 = (f32[512]{0:T(512)S(1)}, f32[512]{0:T(512)}, u32[]{:S(2)}) copy-start(f32[512]{0:T(512)} %param.18) | copy-start | bytes 6148
  171.8 11.7 %copy-start.11 = (f32[512]{0:T(512)S(1)}, f32[512]{0:T(512)}, u32[]{:S(2)}) copy-start(f32[512]{0:T(512)} %param.17) | copy-start | bytes 6148
Sparse Core Ops, SparseCore 0:
  9.4 71.0 all-gather.2
  82.6 55.4 all-gather.4

commit v9 on v8

--- a/solution.py
+++ b/solution.py
@@ -268,7 +268,7 @@
             flops=MERGE_HINT, transcendentals=0, bytes_accessed=1 << 20
         ),
         name="merge",
-    )(zh, got, far, near, stat, after.reshape(-1, after.shape[-1]))
+    )(zh, got, far, near, stat, after)
 
 
 def keep_kernel(where_ref, drop_ref, out_ref):
@@ -323,8 +323,10 @@
     for at, copy in enumerate(copies):
         copy.wait()
         for part in range(PARTS):
+            z = at // 2
+            slot = lax.rem(where_ref[2] // 2 + half - z, half) if part == 0 else z
             term = dot_t(
-                contexts[2 * part + at % 2][at // 2],
+                contexts[2 * part + at % 2][slot],
                 held_ref[at, :, part * wide : (part + 1) * wide],
             )
             acc = term if acc is None else acc + term
@@ -499,17 +501,25 @@
     near = [local(part, queries, key_rows, value_rows) for part in range(PARTS)]
     where = jnp.stack([tp_at % 2, drop_seed[0], tp_at]).astype(jnp.int32)
     kept = keep(where, drop_offsets, residual.shape)
-    folded = []
+    folded, gone = [], []
     for part in range(PARTS):
         partials = serve(part, row, mark, zh, asked, pool, row_count)
         partials = partials.reshape((n_x, 2) + partials.shape[1:])
         got = lax.all_to_all(partials, "x", split_axis=0, concat_axis=0, tiled=True)
-        gone = fold(zh, got, kept)
-        folded.append((got, lax.ppermute(gone, "zh", flip)))
+        gone.append(fold(zh, got, kept))
+        folded.append((got, lax.ppermute(gone[part], "zh", flip)))
     contexts = []
     for part in range(PARTS):
-        context = merge(zh, *folded[part], *near[part], (gone, weight)[part], n_zl)
-        mine = lax.all_to_all(context, "zl", split_axis=0, concat_axis=0, tiled=True)
+        copies = n_zl if part else 1
+        context = merge(zh, *folded[part], *near[part], gone[1 - part], copies)
+        if part:
+            mine = lax.all_to_all(context, "zl", split_axis=0, concat_axis=0, tiled=True)
+        else:
+            shifted = [
+                lax.ppermute(context, "zl", [(z, (z + by) % n_zl) for z in range(n_zl)])
+                for by in range(1, n_zl)
+            ]
+            mine = jnp.concatenate([context] + shifted, axis=0)
         contexts += [mine, lax.ppermute(mine, "core", flip)]
     summed, stats = project(where, contexts, weight, kept, residual)
     stats = lax.all_to_all(stats, TP, split_axis=0, concat_axis=0, tiled=True)

time: 192 us -> 191 us (level)
  blocking collectives: 17.9 us -> 9.01 us
  starting transfers between devices: 73.2 us -> 79 us
    all_to_all x2 -> x1, waiting for transfers between devices: 13.3 us -> 0.01 us  [on_device(): lax.all_to_all(context, 'zl', split_axis=0, concat_axis=0, tiled=True)]
    ppermute x2 -> x5, starting transfers between devices: 15.5 us -> 25.9 us  [the longest x2 15.5 us: on_device(): folded.append((got, lax.ppermute(gone[part], 'zh', flip)))]
    all_to_all x1 -> x0, blocking collectives: 10 us -> none  [over_x(): return lax.all_to_all(x, 'x', split_axis=0, concat_axis=0, tiled=True)]
    ppermute x2 -> x5, waiting for transfers between devices: 0.01 us -> 8.7 us  [the longest x3 8.7 us: on_device(): lax.ppermute(context, 'zl', [(z, (z + by) % n_zl) for z in range(n_zl)])]
    all_gather x1, waiting for transfers between devices: 7.59 us -> 13.6 us  [on_device(): pool = lax.all_gather(paired, 'y', axis=0, tiled=True)]
    all_to_all x2 -> x1, starting transfers between devices: 7.91 us -> 3.47 us  [on_device(): lax.all_to_all(context, 'zl', split_axis=0, concat_axis=0, tiled=True)]
    ppermute x1, waiting for transfers between devices: 0.01 us -> 3.78 us  [on_device(): same_zh = lax.ppermute(out_weight.T, SEQ + TP, moves(0))]
    ppermute x2, starting transfers between devices: 11.4 us -> 7.72 us  [on_device(): contexts += [mine, lax.ppermute(mine, 'core', flip)]]
  transfers between devices with their start and end apart: 15 -> 18, of which waited for: 10 -> 9; matrix products, arithmetic and copies ran while one was open for 3% -> 4% of each run, Pallas kernels for 9% -> 9%
where the time goes in v9:
time: 191 us; the launch traced here: 190 us
  starting transfers between devices  79 us (41%)
  waiting for transfers between devices  50.9 us (27%)
  Pallas kernels  20.9 us (11%)
  between operations  15.1 us (8%)
  local copies, waits for them, and re-layouts  10 us (5%)
  blocking collectives  9.01 us (5%)
  other arithmetic  4.69 us (2%)
    ppermute x2, starting transfers between devices, on_device(): folded.append((got, lax.ppermute(gone[part], 'zh', flip)))  15.5 us
    all_gather x1, waiting for transfers between devices, on_device(): pool = lax.all_gather(paired, 'y', axis=0, tiled=True)  13.6 us
    pallas_call x2, Pallas kernels, serve(): pl.pallas_call(serve_kernel, grid_spec=pltpu.PrefetchScalarGridSpec(num_s...  11.5 us
    ppermute x1, starting transfers between devices, on_device(): lax.ppermute(queries, 'zh', flip)  11.5 us
    ppermute x1, starting transfers between devices, on_device(): other_zh = lax.ppermute(out_weight.T, SEQ + TP, moves(1))  11.4 us
    ppermute x3, starting transfers between devices, on_device(): lax.ppermute(context, 'zl', [(z, (z + by) % n_zl) for z in range(n_zl)])  10.4 us
    all_to_all x2, waiting for transfers between devices, on_device(): got = lax.all_to_all(partials, 'x', split_axis=0, concat_axis=0, tiled=True)  9.47 us
    all_to_all x1, blocking collectives, on_device(): stats = lax.all_to_all(stats, TP, split_axis=0, concat_axis=0, tiled=True)  9.01 us
  transfers between devices with their start and end apart: 18, of which 9 were waited for; matrix products, arithmetic and copies ran while one was open for 4% of the time, Pallas kernels for 9%

profile of v9, /device:TPU:1, one launch (start us, length us, event | category | flops | bytes accessed | tf_op | source)
XLA Modules:
  0.0 189.6 jit_solution(9645662099886458095)
XLA Ops:
  6.5 1.9 pad_maximum_fusion.1
  8.5 11.5 %collective-permute-start = (bf16[256,512]{1,0:T(8,128)(2,1)}, bf16[256,512]{1,0:T(8,128)(2,1)S(1)}, u32[]{:S(2)}, u32[]{:S(2)}) collective-permute-start(bf16[256,512]{1,0:T(8,128)(2,1)} %q_ref.3), channel_id=1, source_target_pairs={{0,8},{8,0},{1,9},{9,1},{2,10},{10,2},{3,11},{11,3},{4,12},{12,4},... | collective-permute-start | bytes 786440 | tf_op jit(solution)/shard_map/ppermute | solution.py:454
  19.9 0.8 copy.17
  20.7 0.1 reshape.406
  20.8 0.2 convert_reduce_fusion
  21.0 0.8 copy.18
  21.8 0.1 broadcast_in_dim.47
  21.8 0.1 select_reduce_fusion
  22.0 1.9 %collective-permute-start.1 = (bf16[8,512]{1,0:T(8,128)(2,1)S(1)}, bf16[8,512]{1,0:T(8,128)(2,1)S(1)}, u32[]{:S(2)}, u32[]{:S(2)}) collective-permute-start(bf16[8,512]{1,0:T(8,128)(2,1)S(1)} %pad.4), channel_id=1, source_target_pairs={{0,8},{8,0},{1,9},{9,1},{2,10},{10,2},{3,11},{11,3},{4,12},{12,4},... | collective-permute-start | bytes 24584 | tf_op jit(solution)/shard_map/ppermute | solution.py:454
  23.9 1.0 maximum_bitcast_fusion
  24.9 5.5 %collective-permute-done.1 = bf16[8,512]{1,0:T(8,128)(2,1)S(1)} collective-permute-done((bf16[8,512]{1,0:T(8,128)(2,1)S(1)}, bf16[8,512]{1,0:T(8,128)(2,1)S(1)}, u32[]{:S(2)}, u32[]{:S(2)}) %collective-permute-start.1) | collective-permute-done | bytes 8224 | tf_op jit(solution)/shard_map/ppermute | solution.py:454
  30.5 1.6 broadcast_in_dim.51
  32.1 4.1 %all-to-all-start = ((bf16[4,2,264,512]{3,2,1,0:T(8,128)(2,1)}), bf16[4,2,264,512]{3,2,1,0:T(8,128)(2,1)S(1)}, u32[]{:S(2)}, u32[]{:S(2)}) async-start(bf16[4,2,264,512]{3,2,1,0:T(8,128)(2,1)} %broadcast_in_dim.51), calls=%async_computation | async-start | bytes 4325376 | tf_op jit(solution)/shard_map/all_to_all | solution.py:450
  36.2 11.4 %collective-permute-start.10 = (bf16[64,512]{1,0:T(8,128)(2,1)S(1)}, bf16[64,512]{1,0:T(8,128)(2,1)S(1)}, u32[]{:S(2)}, u32[]{:S(2)}) collective-permute-start(bf16[64,512]{1,0:T(8,128)(2,1)S(1)} %bitcast.23), channel_id=1, source_target_pairs={{0,8},{1,72},{2,136},{3,200},{4,264},{5,328},{6,392},{7,456},{8,0}... | collective-permute-start | bytes 196616 | tf_op jit(solution)/shard_map/ppermute | solution.py:417
  47.6 1.9 %collective-permute-start.9 = (bf16[64,512]{1,0:T(8,128)(2,1)S(1)}, bf16[64,512]{1,0:T(8,128)(2,1)S(1)}, u32[]{:S(2)}, u32[]{:S(2)}) collective-permute-start(bf16[64,512]{1,0:T(8,128)(2,1)S(1)} %bitcast.24), channel_id=1, source_target_pairs={{0,0},{1,64},{2,128},{3,192},{4,256},{5,320},{6,384},{7,448},{8,8}... | collective-permute-start | bytes 196616 | tf_op jit(solution)/shard_map/ppermute | solution.py:416
  49.6 0.1 pad.14.clone
  49.7 0.1 pad.18.clone
  49.8 1.6 collective-permute-done.10
  51.4 3.8 %collective-permute-done.9 = bf16[64,512]{1,0:T(8,128)(2,1)S(1)} collective-permute-done((bf16[64,512]{1,0:T(8,128)(2,1)S(1)}, bf16[64,512]{1,0:T(8,128)(2,1)S(1)}, u32[]{:S(2)}, u32[]{:S(2)}) %collective-permute-start.9) | collective-permute-done | bytes 65568 | tf_op jit(solution)/shard_map/ppermute | solution.py:416
  55.2 5.6 %all-to-all-done.q_ref = bf16[4,2,264,512]{3,2,1,0:T(8,128)(2,1)S(1)} async-done(((bf16[4,2,264,512]{3,2,1,0:T(8,128)(2,1)}), bf16[4,2,264,512]{3,2,1,0:T(8,128)(2,1)S(1)}, u32[]{:S(2)}, u32[]{:S(2)}) %all-to-all-start) | async-done | bytes 2162720 | tf_op jit(solution)/shard_map/all_to_all | solution.py:450
  60.8 0.1 reshape_squeeze.3
  60.9 0.5 slice.25
  62.1 0.9 broadcast_in_dim.55
  63.0 3.5 %all-to-all-start.4 = ((bf16[4,128,512]{2,1,0:T(8,128)(2,1)}), bf16[4,128,512]{2,1,0:T(8,128)(2,1)S(1)}, u32[]{:S(2)}, u32[]{:S(2)}) async-start(bf16[4,128,512]{2,1,0:T(8,128)(2,1)} %broadcast_in_dim.55), calls=%async_computation.4 | async-start | bytes 1048576 | tf_op jit(solution)/shard_map/all_to_all | solution.py:450
  66.5 0.1 compare_select_fusion
  66.6 0.1 pad_add_fusion.1
  66.6 0.1 reshape.408.mark_ref
  66.7 0.1 pad_add_fusion
  66.8 0.1 reshape.407.row_ref
  66.9 13.6 %all-gather.3.cloned.1.call-done.key_ref.value_ref = bf16[2048,1024]{1,0:T(8,128)(2,1)} async-done(((bf16[256,1024]{1,0:T(8,128)(2,1)}), bf16[2048,1024]{1,0:T(8,128)(2,1)}) %all-gather.3.cloned.1.call-update) | async-done | bytes 4194320 | tf_op jit(solution)/shard_map/all_gather | solution.py:406
  80.5 5.8 %serve.3 = bf16[8,272,256]{2,1,0:T(8,128)(2,1)} custom-call(s32[160]{0:T(256)S(1)} %reshape.407.row_ref, s32[160]{0:T(256)S(1)} %reshape.408.mark_ref, s32[1]{0:T(128)} %bitcast.2.zh_ref, bf16[4,2,264,512]{3,2,1,0:T(8,128)(2,1)S(1)} %all-to-all-done.q_ref, bf16[2048,1024]{1,0:T(8,128)(2,1)} %all-gather.3.cloned.1.call-done.key_ref.value_ref, ...), custom_call_target="tpu_custom_call" | custom-call | flops 671088640 | bytes 4194304 | tf_op jit(solution)/shard_map/serve/pallas_call | solution.py:117
  86.3 0.8 copy-done.10
  87.1 4.0 %all-to-all-start.2 = ((bf16[4,2,272,256]{3,2,1,0:T(8,128)(2,1)}), bf16[4,2,272,256]{3,2,1,0:T(8,128)(2,1)S(1)}, u32[]{:S(2)}, u32[]{:S(2)}) async-start(bf16[4,2,272,256]{3,2,1,0:T(8,128)(2,1)} %bitcast.7), calls=%async_computation.2 | async-start | bytes 2228224 | tf_op jit(solution)/shard_map/all_to_all | solution.py:508
  91.1 0.7 all-gather.5.cloned.1.call-update
  91.8 5.8 %serve.2 = bf16[8,272,256]{2,1,0:T(8,128)(2,1)} custom-call(s32[160]{0:T(256)S(1)} %reshape.407.row_ref, s32[160]{0:T(256)S(1)} %reshape.408.mark_ref, s32[1]{0:T(128)} %bitcast.2.zh_ref, bf16[4,2,264,512]{3,2,1,0:T(8,128)(2,1)S(1)} %all-to-all-done.q_ref, bf16[2048,1024]{1,0:T(8,128)(2,1)} %all-gather.3.cloned.1.call-done.key_ref.value_ref, ...), custom_call_target="tpu_custom_call" | custom-call | flops 671088640 | bytes 4194304 | tf_op jit(solution)/shard_map/serve/pallas_call | solution.py:117
  97.6 8.4 %all-to-all-done.2.got_ref = bf16[4,2,272,256]{3,2,1,0:T(8,128)(2,1)S(1)} async-done(((bf16[4,2,272,256]{3,2,1,0:T(8,128)(2,1)}), bf16[4,2,272,256]{3,2,1,0:T(8,128)(2,1)S(1)}, u32[]{:S(2)}, u32[]{:S(2)}) %all-to-all-start.2) | async-done | bytes 1114144 | tf_op jit(solution)/shard_map/all_to_all | solution.py:508
  106.0 3.7 %all-to-all-start.1 = ((bf16[4,2,272,256]{3,2,1,0:T(8,128)(2,1)}), bf16[4,2,272,256]{3,2,1,0:T(8,128)(2,1)S(1)}, u32[]{:S(2)}, u32[]{:S(2)}) async-start(bf16[4,2,272,256]{3,2,1,0:T(8,128)(2,1)} %bitcast.6), calls=%async_computation.1 | async-start | bytes 2228224 | tf_op jit(solution)/shard_map/all_to_all | solution.py:508
  110.3 0.1 pad_add_fusion.2.where_ref
  110.4 0.8 keep.1._.refs_5_
  111.1 0.8 fold.3._
  111.9 7.7 %collective-permute-start.7 = (bf16[272,256]{1,0:T(8,128)(2,1)}, bf16[272,256]{1,0:T(8,128)(2,1)}, u32[]{:S(2)}, u32[]{:S(2)}) collective-permute-start(bf16[272,256]{1,0:T(8,128)(2,1)} %fold.3._), channel_id=1, source_target_pairs={{0,8},{8,0},{1,9},{9,1},{2,10},{10,2},{3,11},{11,3},{4,12},{12,4},... | collective-permute-start | bytes 417800 | tf_op jit(solution)/shard_map/ppermute | solution.py:510
  119.7 0.7 local.3
  120.4 0.7 copy-done.8
  121.1 0.7 local.2
  121.9 0.7 copy-done.6
  122.6 1.1 all-to-all-done.1.got_ref
  123.7 0.1 fold.2._
  123.8 7.7 %collective-permute-start.2 = (bf16[272,256]{1,0:T(8,128)(2,1)S(1)}, bf16[272,256]{1,0:T(8,128)(2,1)}, u32[]{:S(2)}, u32[]{:S(2)}) collective-permute-start(bf16[272,256]{1,0:T(8,128)(2,1)S(1)} %fold.2._), channel_id=1, source_target_pairs={{0,8},{8,0},{1,9},{9,1},{2,10},{10,2},{3,11},{11,3},{4,12},{12,4},... | collective-permute-start | bytes 417800 | tf_op jit(solution)/shard_map/ppermute | solution.py:510
  131.6 0.9 copy-done.9
  132.5 1.2 merge.3
  133.7 0.8 copy-done.3
  134.6 3.5 %all-to-all-start.3 = ((bf16[4,256,256]{2,1,0:T(8,128)(2,1)}), bf16[4,256,256]{2,1,0:T(8,128)(2,1)S(1)}, u32[]{:S(2)}, u32[]{:S(2)}) async-start(bf16[4,256,256]{2,1,0:T(8,128)(2,1)} %copy-done.3), calls=%async_computation.3 | async-start | bytes 1048576 | tf_op jit(solution)/shard_map/all_to_all | solution.py:516
  138.1 0.9 copy-done.7
  139.0 1.2 merge.2
  140.3 3.3 %collective-permute-start.3 = (bf16[1,256,256]{2,1,0:T(8,128)(2,1)S(1)}, bf16[1,256,256]{2,1,0:T(8,128)(2,1)S(1)}, u32[]{:S(2)}, u32[]{:S(2)}) collective-permute-start(bf16[1,256,256]{2,1,0:T(8,128)(2,1)S(1)} %merge.2), channel_id=1, source_target_pairs={{0,2},{2,4},{4,6},{6,0},{1,3},{3,5},{5,7},{7,1},{8,10},{10,12},{12... | collective-permute-start | bytes 393224 | tf_op jit(solution)/shard_map/ppermute | solution.py:519
  143.6 4.0 %collective-permute-start.4 = (bf16[1,256,256]{2,1,0:T(8,128)(2,1)S(1)}, bf16[1,256,256]{2,1,0:T(8,128)(2,1)S(1)}, u32[]{:S(2)}, u32[]{:S(2)}) collective-permute-start(bf16[1,256,256]{2,1,0:T(8,128)(2,1)S(1)} %merge.2), channel_id=1, source_target_pairs={{0,4},{2,6},{4,0},{6,2},{1,5},{3,7},{5,1},{7,3},{8,12},{10,14},{12... | collective-permute-start | bytes 393224 | tf_op jit(solution)/shard_map/ppermute | solution.py:519
  147.6 3.1 %collective-permute-start.5 = (bf16[1,256,256]{2,1,0:T(8,128)(2,1)S(1)}, bf16[1,256,256]{2,1,0:T(8,128)(2,1)S(1)}, u32[]{:S(2)}, u32[]{:S(2)}) collective-permute-start(bf16[1,256,256]{2,1,0:T(8,128)(2,1)S(1)} %merge.2), channel_id=1, source_target_pairs={{0,6},{2,0},{4,2},{6,4},{1,7},{3,1},{5,3},{7,5},{8,14},{10,8},{12,... | collective-permute-start | bytes 393224 | tf_op jit(solution)/shard_map/ppermute | solution.py:519
  150.7 8.7 %collective-permute-done.4 = bf16[1,256,256]{2,1,0:T(8,128)(2,1)S(1)} collective-permute-done((bf16[1,256,256]{2,1,0:T(8,128)(2,1)S(1)}, bf16[1,256,256]{2,1,0:T(8,128)(2,1)S(1)}, u32[]{:S(2)}, u32[]{:S(2)}) %collective-permute-start.4) | collective-permute-done | bytes 131104 | tf_op jit(solution)/shard_map/ppermute | solution.py:519
  159.5 5.8 %collective-permute-start.6 = (bf16[4,256,256]{2,1,0:T(8,128)(2,1)S(1)}, bf16[4,256,256]{2,1,0:T(8,128)(2,1)S(1)}, u32[]{:S(2)}, u32[]{:S(2)}) collective-permute-start(bf16[4,256,256]{2,1,0:T(8,128)(2,1)S(1)} %pad_maximum_fusion.2.refs_0_), channel_id=1, source_target_pairs={{0,1},{1,0},{2,3},{3,2},{4,5},{5,4},{6,7},{7,6},{8,9},{9,8},{10,11... | collective-permute-start | bytes 1572872 | tf_op jit(solution)/shard_map/ppermute | solution.py:523
  165.3 1.9 %collective-permute-start.8 = (bf16[4,256,256]{2,1,0:T(8,128)(2,1)S(1)}, bf16[4,256,256]{2,1,0:T(8,128)(2,1)S(1)}, u32[]{:S(2)}, u32[]{:S(2)}) collective-permute-start(bf16[4,256,256]{2,1,0:T(8,128)(2,1)S(1)} %all-to-all-done.3.refs_2_), channel_id=1, source_target_pairs={{0,1},{1,0},{2,3},{3,2},{4,5},{5,4},{6,7},{7,6},{8,9},{9,8},{10,11... | collective-permute-start | bytes 1572872 | tf_op jit(solution)/shard_map/ppermute | solution.py:523
  167.3 1.8 collective-permute-done.8.refs_3_
  169.1 3.7 %project.1 = (f32[256,512]{1,0:T(8,128)S(1)}, f32[8,2,256]{2,1,0:T(2,128)S(1)}) custom-call(s32[3]{0:T(128)S(1)} %pad_add_fusion.2.where_ref, bf16[4,256,256]{2,1,0:T(8,128)(2,1)S(1)} %pad_maximum_fusion.2.refs_0_, bf16[4,256,256]{2,1,0:T(8,128)(2,1)S(1)} %collective-permute-done.6.refs_1_, bf16[4,256,256]{2,1,0:T(8,128)(2,1)S(1)} %all-to-all-done.3.refs_2_, ...), custom_call_target="tpu_custom_call" | custom-call | flops 1073741824 | bytes 6291456 | tf_op jit(solution)/shard_map/project/pallas_call | solution.py:352
  172.8 9.0 %all_to_all.30 = f32[8,2,256]{2,1,0:T(2,128)S(1)} all-to-all(f32[8,2,256]{2,1,0:T(2,128)S(1)} %get-tuple-element.16), channel_id=1, replica_groups=mesh['y'=8,'x'=4,'zh'=2,'zl'=4,'core'=2] {'zl','core'}, dimensions={0} | all-to-all | bytes 32768 | tf_op jit(solution)/shard_map/all_to_all | solution.py:525
  181.9 0.9 add_convert_fusion
  (56 shorter events, 0.5 us)
Async XLA Ops:
  6.5 74.0 %all-gather.3.cloned.1.call-start = ((), (), s32[]{:S(2)}) async-start(), calls=%async_computation.6 | async-start | bytes 4718592 | tf_op jit(solution)/shard_map/all_gather | solution.py:406
  8.5 22.0 %collective-permute-start = (bf16[256,512]{1,0:T(8,128)(2,1)}, bf16[256,512]{1,0:T(8,128)(2,1)S(1)}, u32[]{:S(2)}, u32[]{:S(2)}) collective-permute-start(bf16[256,512]{1,0:T(8,128)(2,1)} %q_ref.3), channel_id=1, source_target_pairs={{0,8},{8,0},{1,9},{9,1},{2,10},{10,2},{3,11},{11,3},{4,12},{12,4},... | collective-permute-start | bytes 786440 | tf_op jit(solution)/shard_map/ppermute | solution.py:454
  22.0 8.4 %collective-permute-start.1 = (bf16[8,512]{1,0:T(8,128)(2,1)S(1)}, bf16[8,512]{1,0:T(8,128)(2,1)S(1)}, u32[]{:S(2)}, u32[]{:S(2)}) collective-permute-start(bf16[8,512]{1,0:T(8,128)(2,1)S(1)} %pad.4), channel_id=1, source_target_pairs={{0,8},{8,0},{1,9},{9,1},{2,10},{10,2},{3,11},{11,3},{4,12},{12,4},... | collective-permute-start | bytes 24584 | tf_op jit(solution)/shard_map/ppermute | solution.py:454
  32.1 4.1 %copy-start.14 = (bf16[512,64]{0,1:T(8,128)(2,1)S(1)}, bf16[512,64]{0,1:T(8,128)(2,1)}, u32[]{:S(2)}) copy-start(bf16[512,64]{0,1:T(8,128)(2,1)} %param.16) | copy-start | bytes 196612
  32.1 17.5 %copy-start.13 = (s32[2]{0:T(128)S(1)}, s32[2]{0:T(128)}, u32[]{:S(2)}) copy-start(s32[2]{0:T(128)} %param.19) | copy-start | bytes 28
  32.1 28.7 %all-to-all-start = ((bf16[4,2,264,512]{3,2,1,0:T(8,128)(2,1)}), bf16[4,2,264,512]{3,2,1,0:T(8,128)(2,1)S(1)}, u32[]{:S(2)}, u32[]{:S(2)}) async-start(bf16[4,2,264,512]{3,2,1,0:T(8,128)(2,1)} %broadcast_in_dim.51), calls=%async_computation | async-start | bytes 4325376 | tf_op jit(solution)/shard_map/all_to_all | solution.py:450
  36.2 15.2 %collective-permute-start.10 = (bf16[64,512]{1,0:T(8,128)(2,1)S(1)}, bf16[64,512]{1,0:T(8,128)(2,1)S(1)}, u32[]{:S(2)}, u32[]{:S(2)}) collective-permute-start(bf16[64,512]{1,0:T(8,128)(2,1)S(1)} %bitcast.23), channel_id=1, source_target_pairs={{0,8},{1,72},{2,136},{3,200},{4,264},{5,328},{6,392},{7,456},{8,0}... | collective-permute-start | bytes 196616 | tf_op jit(solution)/shard_map/ppermute | solution.py:417
  47.6 7.5 %collective-permute-start.9 = (bf16[64,512]{1,0:T(8,128)(2,1)S(1)}, bf16[64,512]{1,0:T(8,128)(2,1)S(1)}, u32[]{:S(2)}, u32[]{:S(2)}) collective-permute-start(bf16[64,512]{1,0:T(8,128)(2,1)S(1)} %bitcast.24), channel_id=1, source_target_pairs={{0,0},{1,64},{2,128},{3,192},{4,256},{5,320},{6,384},{7,448},{8,8}... | collective-permute-start | bytes 196616 | tf_op jit(solution)/shard_map/ppermute | solution.py:416
  63.0 23.3 %all-to-all-start.4 = ((bf16[4,128,512]{2,1,0:T(8,128)(2,1)}), bf16[4,128,512]{2,1,0:T(8,128)(2,1)S(1)}, u32[]{:S(2)}, u32[]{:S(2)}) async-start(bf16[4,128,512]{2,1,0:T(8,128)(2,1)} %broadcast_in_dim.55), calls=%async_computation.4 | async-start | bytes 1048576 | tf_op jit(solution)/shard_map/all_to_all | solution.py:450
  86.3 0.8 copy-start.10
  87.1 18.9 %all-to-all-start.2 = ((bf16[4,2,272,256]{3,2,1,0:T(8,128)(2,1)}), bf16[4,2,272,256]{3,2,1,0:T(8,128)(2,1)S(1)}, u32[]{:S(2)}, u32[]{:S(2)}) async-start(bf16[4,2,272,256]{3,2,1,0:T(8,128)(2,1)} %bitcast.7), calls=%async_computation.2 | async-start | bytes 2228224 | tf_op jit(solution)/shard_map/all_to_all | solution.py:508
  91.1 76.2 %all-gather.5.cloned.1.call-start = ((), (), s32[]{:S(2)}) async-start(), calls=%async_computation.7 | async-start | bytes 4718592 | tf_op jit(solution)/shard_map/all_gather | solution.py:459
  97.6 12.8 %copy-start.5 = (s32[16]{0:T(128)S(1)}, s32[16]{0:T(128)}, u32[]{:S(2)}) copy-start(s32[16]{0:T(128)} %drop_ref.1) | copy-start | bytes 196
  106.0 13.7 %copy-start = (bf16[256,512]{1,0:T(8,128)(2,1)S(1)}, bf16[256,512]{1,0:T(8,128)(2,1)}, u32[]{:S(2)}) copy-start(bf16[256,512]{1,0:T(8,128)(2,1)} %q_ref.3) | copy-start | bytes 786436
  106.0 13.7 %copy-start.1 = (bf16[256,512]{1,0:T(8,128)(2,1)S(1)}, bf16[256,512]{1,0:T(8,128)(2,1)}, u32[]{:S(2)}) copy-start(bf16[256,512]{1,0:T(8,128)(2,1)} %v_ref.3) | copy-start | bytes 786436
  106.0 13.7 %copy-start.2 = (bf16[256,512]{1,0:T(8,128)(2,1)S(1)}, bf16[256,512]{1,0:T(8,128)(2,1)}, u32[]{:S(2)}) copy-start(bf16[256,512]{1,0:T(8,128)(2,1)} %k_ref.3) | copy-start | bytes 786436
  106.0 17.7 %all-to-all-start.1 = ((bf16[4,2,272,256]{3,2,1,0:T(8,128)(2,1)}), bf16[4,2,272,256]{3,2,1,0:T(8,128)(2,1)S(1)}, u32[]{:S(2)}, u32[]{:S(2)}) async-start(bf16[4,2,272,256]{3,2,1,0:T(8,128)(2,1)} %bitcast.6), calls=%async_computation.1 | async-start | bytes 2228224 | tf_op jit(solution)/shard_map/all_to_all | solution.py:508
  111.9 19.6 %collective-permute-start.7 = (bf16[272,256]{1,0:T(8,128)(2,1)}, bf16[272,256]{1,0:T(8,128)(2,1)}, u32[]{:S(2)}, u32[]{:S(2)}) collective-permute-start(bf16[272,256]{1,0:T(8,128)(2,1)} %fold.3._), channel_id=1, source_target_pairs={{0,8},{8,0},{1,9},{9,1},{2,10},{10,2},{3,11},{11,3},{4,12},{12,4},... | collective-permute-start | bytes 417800 | tf_op jit(solution)/shard_map/ppermute | solution.py:510
  120.4 0.7 copy-start.8
  121.9 0.7 copy-start.6
  123.8 14.2 %collective-permute-start.2 = (bf16[272,256]{1,0:T(8,128)(2,1)S(1)}, bf16[272,256]{1,0:T(8,128)(2,1)}, u32[]{:S(2)}, u32[]{:S(2)}) collective-permute-start(bf16[272,256]{1,0:T(8,128)(2,1)S(1)} %fold.2._), channel_id=1, source_target_pairs={{0,8},{8,0},{1,9},{9,1},{2,10},{10,2},{3,11},{11,3},{4,12},{12,4},... | collective-permute-start | bytes 417800 | tf_op jit(solution)/shard_map/ppermute | solution.py:510
  131.6 1.0 copy-start.9
  133.7 0.8 copy-start.3
  134.6 30.7 %all-to-all-start.3 = ((bf16[4,256,256]{2,1,0:T(8,128)(2,1)}), bf16[4,256,256]{2,1,0:T(8,128)(2,1)S(1)}, u32[]{:S(2)}, u32[]{:S(2)}) async-start(bf16[4,256,256]{2,1,0:T(8,128)(2,1)} %copy-done.3), calls=%async_computation.3 | async-start | bytes 1048576 | tf_op jit(solution)/shard_map/all_to_all | solution.py:516
  138.1 1.0 copy-start.7
  139.0 30.1 %copy-start.4 = (bf16[256,512]{1,0:T(8,128)(2,1)S(1)}, bf16[256,512]{1,0:T(8,128)(2,1)}, u32[]{:S(2)}) copy-start(bf16[256,512]{1,0:T(8,128)(2,1)} %refs_6_.1) | copy-start | bytes 786436
  140.3 10.4 %collective-permute-start.3 = (bf16[1,256,256]{2,1,0:T(8,128)(2,1)S(1)}, bf16[1,256,256]{2,1,0:T(8,128)(2,1)S(1)}, u32[]{:S(2)}, u32[]{:S(2)}) collective-permute-start(bf16[1,256,256]{2,1,0:T(8,128)(2,1)S(1)} %merge.2), channel_id=1, source_target_pairs={{0,2},{2,4},{4,6},{6,0},{1,3},{3,5},{5,7},{7,1},{8,10},{10,12},{12... | collective-permute-start | bytes 393224 | tf_op jit(solution)/shard_map/ppermute | solution.py:519
  143.6 15.8 %collective-permute-start.4 = (bf16[1,256,256]{2,1,0:T(8,128)(2,1)S(1)}, bf16[1,256,256]{2,1,0:T(8,128)(2,1)S(1)}, u32[]{:S(2)}, u32[]{:S(2)}) collective-permute-start(bf16[1,256,256]{2,1,0:T(8,128)(2,1)S(1)} %merge.2), channel_id=1, source_target_pairs={{0,4},{2,6},{4,0},{6,2},{1,5},{3,7},{5,1},{7,3},{8,12},{10,14},{12... | collective-permute-start | bytes 393224 | tf_op jit(solution)/shard_map/ppermute | solution.py:519
  147.6 11.8 %collective-permute-start.5 = (bf16[1,256,256]{2,1,0:T(8,128)(2,1)S(1)}, bf16[1,256,256]{2,1,0:T(8,128)(2,1)S(1)}, u32[]{:S(2)}, u32[]{:S(2)}) collective-permute-start(bf16[1,256,256]{2,1,0:T(8,128)(2,1)S(1)} %merge.2), channel_id=1, source_target_pairs={{0,6},{2,0},{4,2},{6,4},{1,7},{3,1},{5,3},{7,5},{8,14},{10,8},{12,... | collective-permute-start | bytes 393224 | tf_op jit(solution)/shard_map/ppermute | solution.py:519
  159.5 7.7 %collective-permute-start.6 = (bf16[4,256,256]{2,1,0:T(8,128)(2,1)S(1)}, bf16[4,256,256]{2,1,0:T(8,128)(2,1)S(1)}, u32[]{:S(2)}, u32[]{:S(2)}) collective-permute-start(bf16[4,256,256]{2,1,0:T(8,128)(2,1)S(1)} %pad_maximum_fusion.2.refs_0_), channel_id=1, source_target_pairs={{0,1},{1,0},{2,3},{3,2},{4,5},{5,4},{6,7},{7,6},{8,9},{9,8},{10,11... | collective-permute-start | bytes 1572872 | tf_op jit(solution)/shard_map/ppermute | solution.py:523
  165.3 3.8 %collective-permute-start.8 = (bf16[4,256,256]{2,1,0:T(8,128)(2,1)S(1)}, bf16[4,256,256]{2,1,0:T(8,128)(2,1)S(1)}, u32[]{:S(2)}, u32[]{:S(2)}) collective-permute-start(bf16[4,256,256]{2,1,0:T(8,128)(2,1)S(1)} %all-to-all-done.3.refs_2_), channel_id=1, source_target_pairs={{0,1},{1,0},{2,3},{3,2},{4,5},{5,4},{6,7},{7,6},{8,9},{9,8},{10,11... | collective-permute-start | bytes 1572872 | tf_op jit(solution)/shard_map/ppermute | solution.py:523
  169.1 12.8 %copy-start.11 = (f32[512]{0:T(512)S(1)}, f32[512]{0:T(512)}, u32[]{:S(2)}) copy-start(f32[512]{0:T(512)} %param.18) | copy-start | bytes 6148
  169.1 12.8 %copy-start.12 = (f32[512]{0:T(512)S(1)}, f32[512]{0:T(512)}, u32[]{:S(2)}) copy-start(f32[512]{0:T(512)} %param.17) | copy-start | bytes 6148
Sparse Core Ops, SparseCore 0:
  9.4 71.0 all-gather.2
  94.0 56.2 all-gather.4

commit v10 on v9

--- a/solution.py
+++ b/solution.py
@@ -64,7 +64,7 @@
     return out
 
 
-def serve_kernel(row_ref, mark_ref, zh_ref, q_ref, key_ref, value_ref, out_ref):
+def serve_kernel(value_at, row_ref, mark_ref, zh_ref, q_ref, pool_ref, out_ref):
     n_x, n_zh, rows, wide = q_ref.shape
     listings = row_ref.shape[0] // (pl.num_programs(0) * n_x * n_zh)
     block_of = lax.broadcasted_iota(jnp.int32, (BLOCK, rows), 1) // BLOCK
@@ -75,7 +75,7 @@
             places, listed = [], []
             for i in range(listings):
                 at = peer * listings + i
-                places.append(pl.ds(pl.multiple_of(row_ref[at] * BLOCK, BLOCK), BLOCK))
+                places.append(row_ref[at] * BLOCK)
                 mark = mark_ref[at]
                 listed.append(
                     jnp.logical_or(block_of == mark, jnp.full(block_of.shape, mark) < 0)
@@ -83,10 +83,13 @@
             listed = jnp.concatenate(listed, axis=0)
             jobs += [(x, j, h, places, listed) for h in range(wide // DH)]
 
+    def taken(places, shift, lanes):
+        blocks = [pl.ds(pl.multiple_of(p + shift, BLOCK), BLOCK) for p in places]
+        return jnp.concatenate([pool_ref[b, lanes] for b in blocks], axis=0)
+
     def scores(x, j, h, places, listed):
         lanes = slice(h * DH, (h + 1) * DH)
-        keys = jnp.concatenate([key_ref[p, lanes] for p in places], axis=0)
-        return dot_t(keys, q_ref[x, j, :, lanes])
+        return dot_t(taken(places, 0, lanes), q_ref[x, j, :, lanes])
 
     stats = []
     coming = scores(*jobs[0])
@@ -95,8 +98,7 @@
         if k + 1 < len(jobs):
             coming = scores(*jobs[k + 1])
         lanes = slice(h * DH, (h + 1) * DH)
-        values = jnp.concatenate([value_ref[p, lanes] for p in places], axis=0)
-        top, total, got = partial(now, listed, values)
+        top, total, got = partial(now, listed, taken(places, value_at, lanes))
         peer = x * n_zh + lax.rem(j + zh_ref[0], n_zh)
         out_ref[peer, lanes, :] = got.astype(BF)
         stats += split(top, 3) + split(total, 2)
@@ -115,26 +117,25 @@
     out = (peers, wide + STAT_ROWS, rows)
     steps = n_x // 2
     return pl.pallas_call(
-        serve_kernel,
+        functools.partial(serve_kernel, rows),
         grid_spec=pltpu.PrefetchScalarGridSpec(
             num_scalar_prefetch=3,
             grid=(steps,),
             in_specs=[
                 pl.BlockSpec((n_x // steps, 2, rows, wide), lambda i, a, b, c: (i, 0, 0, part)),
                 pl.BlockSpec((pool.shape[0], wide), lambda i, a, b, c: (0, part)),
-                pl.BlockSpec((pool.shape[0], wide), lambda i, a, b, c: (0, PARTS + part)),
             ],
             out_specs=pl.BlockSpec((peers // steps,) + out[1:], lambda i, a, b, c: (i, 0, 0)),
         ),
         out_shape=jax.ShapeDtypeStruct(out, BF),
-        compiler_params=params(),
+        compiler_params=params(56 << 20),
         cost_estimate=pl.CostEstimate(
             flops=4 * peers * rows * 320 * wide,
             transcendentals=peers * rows * 320 * wide // DH,
             bytes_accessed=4 << 20,
         ),
         name="serve",
-    )(row, mark, zh, q, pool, pool)
+    )(row, mark, zh, q, pool)
 
 
 def local_kernel(q_ref, k_ref, v_ref, out_ref, stat_ref):
@@ -402,8 +403,8 @@
     zh_at = lax.axis_index("zh")
     wide = width_here // PARTS
 
-    paired = jnp.concatenate([key_rows, value_rows], axis=1)
-    pool = lax.all_gather(paired, "y", axis=0, tiled=True)
+    pool = lax.all_gather(jnp.stack([key_rows, value_rows]), "y", axis=0, tiled=True)
+    pool = pool.reshape(n_y * 2 * row_count, width_here)
 
     def moves(flip):
         return [
@@ -456,25 +457,23 @@
     asked = over_x(jnp.stack([near_q, far_q]))
     after = asked[0, 0, row_count, 0] * 0
     shards = over_x(shards + after)
-    weight = lax.all_gather(
-        shards.reshape(plane * cols_here, width_here), "y", axis=0, tiled=True
-    )
-    weight = weight.reshape(tp_count, plane * cols_here, width_here)
+    shards = shards.reshape(plane * cols_here, width_here)
+    weight = lax.all_gather(shards, "y", axis=0, tiled=True)
 
     lists = asked[:, :, row_count, : cells.shape[0]].reshape(plane, plane, 2 * slots)
     lists = lax.dynamic_index_in_dim(lists, plane_at, 1, keepdims=False).astype(jnp.int32)
-    base = (jnp.arange(slots, dtype=jnp.int32) // CAP) * block_count
+    base = (jnp.arange(slots, dtype=jnp.int32) // CAP) * (2 * block_count)
     order = jnp.arange(plane, dtype=jnp.int32)
     peer = jnp.bitwise_xor(order, zh_at)
     nothing = jnp.int32(block_count)
     owner = global_list // block_count
-    glob_row = (owner // plane) * block_count + global_list % block_count
+    glob_row = (owner // plane) * (2 * block_count) + global_list % block_count
     glob_mark = jnp.where(owner % plane == plane_at, -1, nothing)
     here = y_at * plane + peer
     low = (here + seq_count - 1) % seq_count
     high = (here + 1) % seq_count
-    low_row = (low // plane) * block_count + block_count - 1
-    high_row = (high // plane) * block_count
+    low_row = (low // plane) * (2 * block_count) + block_count - 1
+    high_row = (high // plane) * (2 * block_count)
     low_mark = jnp.where(low % plane == plane_at, 0, nothing)
     high_mark = jnp.where(high % plane == plane_at, block_count - 1, nothing)
     marks = lists[:, slots:] - 1
@@ -511,7 +510,7 @@
     contexts = []
     for part in range(PARTS):
         copies = n_zl if part else 1
-        context = merge(zh, *folded[part], *near[part], gone[1 - part], copies)
+        context = merge(zh, *folded[part], *near[part], (weight, gone[0])[part], copies)
         if part:
             mine = lax.all_to_all(context, "zl", split_axis=0, concat_axis=0, tiled=True)
         else:
@@ -521,7 +520,7 @@
             ]
             mine = jnp.concatenate([context] + shifted, axis=0)
         contexts += [mine, lax.ppermute(mine, "core", flip)]
-    summed, stats = project(where, contexts, weight, kept, residual)
+    summed, stats = project(where, contexts, weight.reshape(tp_count, -1, width_here), kept, residual)
     stats = lax.all_to_all(stats, TP, split_axis=0, concat_axis=0, tiled=True)
     means, spreads = stats[:, 0], stats[:, 1]
     mean = jnp.sum(means, axis=0) / tp_count

time: 191 us -> 188 us (0.984)
  waiting for transfers between devices: 50.9 us -> 34.9 us
  blocking collectives: 9.01 us -> 19.2 us
    all_to_all x0 -> x1, blocking collectives: none -> 10 us  [over_x(): return lax.all_to_all(x, 'x', split_axis=0, concat_axis=0, tiled=True)]
    ppermute x3, waiting for transfers between devices: 8.7 us -> 0.01 us  [on_device(): lax.ppermute(context, 'zl', [(z, (z + by) % n_zl) for z in range(n_zl)])]
    all_gather x2, waiting for transfers between devices: 13.7 us -> 6.85 us  [the longest x1 6.47 us: on_device(): lax.all_gather(jnp.stack([key_rows, value_rows]), 'y', axis=0, tiled=True)]
    ppermute x2, starting transfers between devices: 7.72 us -> 12.8 us  [on_device(): contexts += [mine, lax.ppermute(mine, 'core', flip)]]
    ppermute x1, waiting for transfers between devices: 3.78 us -> 0.01 us  [on_device(): same_zh = lax.ppermute(out_weight.T, SEQ + TP, moves(0))]
    ppermute x1, starting transfers between devices: 1.92 us -> 5.6 us  [on_device(): same_zh = lax.ppermute(out_weight.T, SEQ + TP, moves(0))]
    ppermute x1, starting transfers between devices: 11.4 us -> 7.73 us  [on_device(): other_zh = lax.ppermute(out_weight.T, SEQ + TP, moves(1))]
    ppermute x1, waiting for transfers between devices: 1.56 us -> 5.06 us  [on_device(): other_zh = lax.ppermute(out_weight.T, SEQ + TP, moves(1))]
  transfers between devices with their start and end apart: 18 -> 17, of which waited for: 9 -> 8; matrix products, arithmetic and copies ran while one was open for 4% -> 4% of each run, Pallas kernels for 9% -> 10%
where the time goes in v10:
time: 188 us; the launch traced here: 187 us
  starting transfers between devices  80.7 us (43%)
  waiting for transfers between devices  34.9 us (19%)
  Pallas kernels  22.5 us (12%)
  blocking collectives  19.2 us (10%)
  between operations  15.2 us (8%)
  local copies, waits for them, and re-layouts  9.99 us (5%)
  other arithmetic  4.68 us (2%)
    ppermute x2, starting transfers between devices, on_device(): folded.append((got, lax.ppermute(gone[part], 'zh', flip)))  15.5 us
    ppermute x2, starting transfers between devices, on_device(): contexts += [mine, lax.ppermute(mine, 'core', flip)]  12.8 us
    pallas_call x2, Pallas kernels, serve(): pl.pallas_call(functools.partial(serve_kernel, rows), grid_spec=pltpu.Pre...  12.3 us
    ppermute x1, starting transfers between devices, on_device(): lax.ppermute(queries, 'zh', flip)  11.5 us
    ppermute x3, starting transfers between devices, on_device(): lax.ppermute(context, 'zl', [(z, (z + by) % n_zl) for z in range(n_zl)])  10.5 us
    all_to_all x1, blocking collectives, over_x(): return lax.all_to_all(x, 'x', split_axis=0, concat_axis=0, tiled=True)  10 us
    all_to_all x2, waiting for transfers between devices, on_device(): got = lax.all_to_all(partials, 'x', split_axis=0, concat_axis=0, tiled=True)  9.82 us
    all_to_all x1, blocking collectives, on_device(): stats = lax.all_to_all(stats, TP, split_axis=0, concat_axis=0, tiled=True)  9.19 us
  transfers between devices with their start and end apart: 17, of which 8 were waited for; matrix products, arithmetic and copies ran while one was open for 4% of the time, Pallas kernels for 10%

profile of v10, /device:TPU:1, one launch (start us, length us, event | category | flops | bytes accessed | tf_op | source)
XLA Modules:
  0.0 187.2 jit_solution(4411290851851643171)
XLA Ops:
  6.5 1.9 %pad_maximum_fusion.1 = bf16[2,256,512]{2,1,0:T(8,128)(2,1)} fusion(bf16[1,256,512]{2,1,0:T(8,128)(2,1)} %bitcast.24, bf16[1,256,512]{2,1,0:T(8,128)(2,1)} %bitcast.25), kind=kLoop, calls=%fused_computation.1 | loop fusion | flops 262144 | bytes 1048576 | tf_op jit(solution)/shard_map/stack | solution.py:406
  8.4 0.0 all-gather.3.cloned.1.call-update
  8.4 11.5 %collective-permute-start = (bf16[256,512]{1,0:T(8,128)(2,1)}, bf16[256,512]{1,0:T(8,128)(2,1)S(1)}, u32[]{:S(2)}, u32[]{:S(2)}) collective-permute-start(bf16[256,512]{1,0:T(8,128)(2,1)} %q_ref.3), channel_id=1, source_target_pairs={{0,8},{8,0},{1,9},{9,1},{2,10},{10,2},{3,11},{11,3},{4,12},{12,4},... | collective-permute-start | bytes 786440 | tf_op jit(solution)/shard_map/ppermute | solution.py:455
  19.9 0.8 copy.19
  20.7 0.1 reshape.409
  20.8 0.2 convert_reduce_fusion
  21.0 0.8 copy.20
  21.7 0.1 broadcast_in_dim.47
  21.8 0.1 select_reduce_fusion
  22.0 1.9 %collective-permute-start.1 = (bf16[8,512]{1,0:T(8,128)(2,1)S(1)}, bf16[8,512]{1,0:T(8,128)(2,1)S(1)}, u32[]{:S(2)}, u32[]{:S(2)}) collective-permute-start(bf16[8,512]{1,0:T(8,128)(2,1)S(1)} %pad.4), channel_id=1, source_target_pairs={{0,8},{8,0},{1,9},{9,1},{2,10},{10,2},{3,11},{11,3},{4,12},{12,4},... | collective-permute-start | bytes 24584 | tf_op jit(solution)/shard_map/ppermute | solution.py:455
  23.9 1.0 maximum_bitcast_fusion
  24.9 5.5 %collective-permute-done.1 = bf16[8,512]{1,0:T(8,128)(2,1)S(1)} collective-permute-done((bf16[8,512]{1,0:T(8,128)(2,1)S(1)}, bf16[8,512]{1,0:T(8,128)(2,1)S(1)}, u32[]{:S(2)}, u32[]{:S(2)}) %collective-permute-start.1) | collective-permute-done | bytes 8224 | tf_op jit(solution)/shard_map/ppermute | solution.py:455
  30.4 0.1 pad_maximum_fusion
  30.5 1.5 broadcast_in_dim.51
  32.1 4.1 %all-to-all-start = ((bf16[4,2,264,512]{3,2,1,0:T(8,128)(2,1)}), bf16[4,2,264,512]{3,2,1,0:T(8,128)(2,1)S(1)}, u32[]{:S(2)}, u32[]{:S(2)}) async-start(bf16[4,2,264,512]{3,2,1,0:T(8,128)(2,1)} %broadcast_in_dim.51), calls=%async_computation | async-start | bytes 4325376 | tf_op jit(solution)/shard_map/all_to_all | solution.py:451
  36.2 5.6 %collective-permute-start.3 = (bf16[64,512]{1,0:T(8,128)(2,1)S(1)}, bf16[64,512]{1,0:T(8,128)(2,1)S(1)}, u32[]{:S(2)}, u32[]{:S(2)}) collective-permute-start(bf16[64,512]{1,0:T(8,128)(2,1)S(1)} %bitcast.32), channel_id=1, source_target_pairs={{0,0},{1,64},{2,128},{3,192},{4,256},{5,320},{6,384},{7,448},{8,8}... | collective-permute-start | bytes 196616 | tf_op jit(solution)/shard_map/ppermute | solution.py:417
  41.8 7.7 %collective-permute-start.4 = (bf16[64,512]{1,0:T(8,128)(2,1)S(1)}, bf16[64,512]{1,0:T(8,128)(2,1)S(1)}, u32[]{:S(2)}, u32[]{:S(2)}) collective-permute-start(bf16[64,512]{1,0:T(8,128)(2,1)S(1)} %bitcast.33), channel_id=1, source_target_pairs={{0,8},{1,72},{2,136},{3,200},{4,264},{5,328},{6,392},{7,456},{8,0}... | collective-permute-start | bytes 196616 | tf_op jit(solution)/shard_map/ppermute | solution.py:418
  49.5 5.1 %collective-permute-done.4 = bf16[64,512]{1,0:T(8,128)(2,1)S(1)} collective-permute-done((bf16[64,512]{1,0:T(8,128)(2,1)S(1)}, bf16[64,512]{1,0:T(8,128)(2,1)S(1)}, u32[]{:S(2)}, u32[]{:S(2)}) %collective-permute-start.4) | collective-permute-done | bytes 65568 | tf_op jit(solution)/shard_map/ppermute | solution.py:418
  54.6 6.1 %all-to-all-done.q_ref = bf16[4,2,264,512]{3,2,1,0:T(8,128)(2,1)S(1)} async-done(((bf16[4,2,264,512]{3,2,1,0:T(8,128)(2,1)}), bf16[4,2,264,512]{3,2,1,0:T(8,128)(2,1)S(1)}, u32[]{:S(2)}, u32[]{:S(2)}) %all-to-all-start) | async-done | bytes 2162720 | tf_op jit(solution)/shard_map/all_to_all | solution.py:451
  60.7 0.5 slice.25
  62.0 10.0 %all_to_all.30 = bf16[4,128,512]{2,1,0:T(8,128)(2,1)} all-to-all(bf16[4,128,512]{2,1,0:T(8,128)(2,1)S(1)} %broadcast_in_dim.55), channel_id=1, replica_groups=mesh['y'=8,'x'=4,'zh'=2,'zl'=4,'core'=2] {'x'}, dimensions={0} | all-to-all | bytes 1048576 | tf_op jit(solution)/shard_map/all_to_all | solution.py:451
  72.1 0.0 all-gather.5.cloned.1.call-update
  72.1 0.1 pad.14.clone
  72.2 0.1 pad.18.clone
  72.4 0.1 reshape_squeeze.3
  72.5 0.1 compare_select_fusion
  72.6 0.1 pad_add_fusion.1
  72.6 0.7 reshape.411.mark_ref
  73.3 0.1 pad_add_fusion
  73.4 0.6 reshape.410.row_ref
  74.0 6.5 %all-gather.3.cloned.1.call-done = bf16[16,256,512]{2,1,0:T(8,128)(2,1)} async-done(((bf16[2,256,512]{2,1,0:T(8,128)(2,1)}), bf16[16,256,512]{2,1,0:T(8,128)(2,1)}) %all-gather.3.cloned.1.call-update) | async-done | bytes 4194320 | tf_op jit(solution)/shard_map/all_gather | solution.py:406
  80.5 6.2 %serve.3 = bf16[8,272,256]{2,1,0:T(8,128)(2,1)} custom-call(s32[160]{0:T(256)} %reshape.410.row_ref, s32[160]{0:T(256)} %reshape.411.mark_ref, s32[1]{0:T(128)} %bitcast.2.zh_ref, bf16[4,2,264,512]{3,2,1,0:T(8,128)(2,1)} %copy-done.10, bf16[4096,512]{1,0:T(8,128)(2,1)} %bitcast.26), custom_call_target="tpu_custom_call" | custom-call | flops 671088640 | bytes 4194304 | tf_op jit(solution)/shard_map/serve/pallas_call | solution.py:119
  86.7 4.0 %all-to-all-start.3 = ((bf16[4,2,272,256]{3,2,1,0:T(8,128)(2,1)}), bf16[4,2,272,256]{3,2,1,0:T(8,128)(2,1)S(1)}, u32[]{:S(2)}, u32[]{:S(2)}) async-start(bf16[4,2,272,256]{3,2,1,0:T(8,128)(2,1)} %bitcast.29), calls=%async_computation.3 | async-start | bytes 2228224 | tf_op jit(solution)/shard_map/all_to_all | solution.py:507
  90.7 6.1 %serve.2 = bf16[8,272,256]{2,1,0:T(8,128)(2,1)} custom-call(s32[160]{0:T(256)} %reshape.410.row_ref, s32[160]{0:T(256)} %reshape.411.mark_ref, s32[1]{0:T(128)} %bitcast.2.zh_ref, bf16[4,2,264,512]{3,2,1,0:T(8,128)(2,1)} %copy-done.10, bf16[4096,512]{1,0:T(8,128)(2,1)} %bitcast.27), custom_call_target="tpu_custom_call" | custom-call | flops 671088640 | bytes 4194304 | tf_op jit(solution)/shard_map/serve/pallas_call | solution.py:119
  96.8 8.7 %all-to-all-done.3.got_ref = bf16[4,2,272,256]{3,2,1,0:T(8,128)(2,1)S(1)} async-done(((bf16[4,2,272,256]{3,2,1,0:T(8,128)(2,1)}), bf16[4,2,272,256]{3,2,1,0:T(8,128)(2,1)S(1)}, u32[]{:S(2)}, u32[]{:S(2)}) %all-to-all-start.3) | async-done | bytes 1114144 | tf_op jit(solution)/shard_map/all_to_all | solution.py:507
  105.5 3.7 %all-to-all-start.1 = ((bf16[4,2,272,256]{3,2,1,0:T(8,128)(2,1)}), bf16[4,2,272,256]{3,2,1,0:T(8,128)(2,1)S(1)}, u32[]{:S(2)}, u32[]{:S(2)}) async-start(bf16[4,2,272,256]{3,2,1,0:T(8,128)(2,1)} %bitcast.28), calls=%async_computation.1 | async-start | bytes 2228224 | tf_op jit(solution)/shard_map/all_to_all | solution.py:507
  109.9 0.1 pad_add_fusion.2.where_ref
  110.0 0.8 keep.1._.refs_5_
  110.7 0.8 fold.3
  111.5 7.7 %collective-permute-start.9 = (bf16[272,256]{1,0:T(8,128)(2,1)}, bf16[272,256]{1,0:T(8,128)(2,1)}, u32[]{:S(2)}, u32[]{:S(2)}) collective-permute-start(bf16[272,256]{1,0:T(8,128)(2,1)} %fold.3), channel_id=1, source_target_pairs={{0,8},{8,0},{1,9},{9,1},{2,10},{10,2},{3,11},{11,3},{4,12},{12,4},... | collective-permute-start | bytes 417800 | tf_op jit(solution)/shard_map/ppermute | solution.py:509
  119.3 0.7 local.3
  120.0 0.7 copy-done.8
  120.7 0.7 local.2
  121.5 0.0 copy-start.6
  121.5 0.7 copy-done.6
  122.2 1.1 all-to-all-done.1.got_ref
  123.2 0.1 fold.2._
  123.4 7.7 %collective-permute-start.2 = (bf16[272,256]{1,0:T(8,128)(2,1)S(1)}, bf16[272,256]{1,0:T(8,128)(2,1)}, u32[]{:S(2)}, u32[]{:S(2)}) collective-permute-start(bf16[272,256]{1,0:T(8,128)(2,1)S(1)} %fold.2._), channel_id=1, source_target_pairs={{0,8},{8,0},{1,9},{9,1},{2,10},{10,2},{3,11},{11,3},{4,12},{12,4},... | collective-permute-start | bytes 417800 | tf_op jit(solution)/shard_map/ppermute | solution.py:509
  131.2 0.9 copy-done.9
  132.1 2.1 %merge.3 = bf16[4,256,256]{2,1,0:T(8,128)(2,1)} custom-call(s32[1]{0:T(128)} %bitcast.2.zh_ref, bf16[4,2,272,256]{3,2,1,0:T(8,128)(2,1)S(1)} %all-to-all-done.3.got_ref, bf16[272,256]{1,0:T(8,128)(2,1)} %collective-permute-done.9.far_ref, f32[256,256]{1,0:T(8,128)S(1)} %copy-done.9, f32[4,256]{1,0:T(4,128)S(1)} %get-tuple-element.14.stat_ref, ...), custom_call_target="tpu_custom_call" | custom-call | flops 30000001024 | bytes 1048576 | tf_op jit(solution)/shard_map/merge/pallas_call | solution.py:252
  134.2 3.5 %all-to-all-start.4 = ((bf16[4,256,256]{2,1,0:T(8,128)(2,1)}), bf16[4,256,256]{2,1,0:T(8,128)(2,1)S(1)}, u32[]{:S(2)}, u32[]{:S(2)}) async-start(bf16[4,256,256]{2,1,0:T(8,128)(2,1)} %merge.3), calls=%async_computation.4 | async-start | bytes 1048576 | tf_op jit(solution)/shard_map/all_to_all | solution.py:515
  137.7 0.4 all-gather.5.cloned.1.call-done._
  138.1 2.2 %copy-done = bf16[4096,512]{1,0:T(8,128)(2,1)S(1)} copy-done((bf16[4096,512]{1,0:T(8,128)(2,1)S(1)}, bf16[4096,512]{1,0:T(8,128)(2,1)}, u32[]{:S(2)}) %copy-start) | copy-done | bytes 4194328
  140.2 1.2 merge.2
  141.5 3.3 %collective-permute-start.5 = (bf16[1,256,256]{2,1,0:T(8,128)(2,1)S(1)}, bf16[1,256,256]{2,1,0:T(8,128)(2,1)S(1)}, u32[]{:S(2)}, u32[]{:S(2)}) collective-permute-start(bf16[1,256,256]{2,1,0:T(8,128)(2,1)S(1)} %merge.2), channel_id=1, source_target_pairs={{0,2},{2,4},{4,6},{6,0},{1,3},{3,5},{5,7},{7,1},{8,10},{10,12},{12... | collective-permute-start | bytes 393224 | tf_op jit(solution)/shard_map/ppermute | solution.py:518
  144.8 4.4 %collective-permute-start.6 = (bf16[1,256,256]{2,1,0:T(8,128)(2,1)S(1)}, bf16[1,256,256]{2,1,0:T(8,128)(2,1)S(1)}, u32[]{:S(2)}, u32[]{:S(2)}) collective-permute-start(bf16[1,256,256]{2,1,0:T(8,128)(2,1)S(1)} %merge.2), channel_id=1, source_target_pairs={{0,4},{2,6},{4,0},{6,2},{1,5},{3,7},{5,1},{7,3},{8,12},{10,14},{12... | collective-permute-start | bytes 393224 | tf_op jit(solution)/shard_map/ppermute | solution.py:518
  149.1 2.9 %collective-permute-start.7 = (bf16[1,256,256]{2,1,0:T(8,128)(2,1)S(1)}, bf16[1,256,256]{2,1,0:T(8,128)(2,1)S(1)}, u32[]{:S(2)}, u32[]{:S(2)}) collective-permute-start(bf16[1,256,256]{2,1,0:T(8,128)(2,1)S(1)} %merge.2), channel_id=1, source_target_pairs={{0,6},{2,0},{4,2},{6,4},{1,7},{3,1},{5,3},{7,5},{8,14},{10,8},{12,... | collective-permute-start | bytes 393224 | tf_op jit(solution)/shard_map/ppermute | solution.py:518
  152.1 10.5 %collective-permute-start.10 = (bf16[4,256,256]{2,1,0:T(8,128)(2,1)S(1)}, bf16[4,256,256]{2,1,0:T(8,128)(2,1)S(1)}, u32[]{:S(2)}, u32[]{:S(2)}) collective-permute-start(bf16[4,256,256]{2,1,0:T(8,128)(2,1)S(1)} %all-to-all-done.4.refs_2_), channel_id=1, source_target_pairs={{0,1},{1,0},{2,3},{3,2},{4,5},{5,4},{6,7},{7,6},{8,9},{9,8},{10,11... | collective-permute-start | bytes 1572872 | tf_op jit(solution)/shard_map/ppermute | solution.py:522
  162.6 0.1 pad_maximum_fusion.2.refs_0_
  162.7 2.3 %collective-permute-start.8 = (bf16[4,256,256]{2,1,0:T(8,128)(2,1)S(1)}, bf16[4,256,256]{2,1,0:T(8,128)(2,1)S(1)}, u32[]{:S(2)}, u32[]{:S(2)}) collective-permute-start(bf16[4,256,256]{2,1,0:T(8,128)(2,1)S(1)} %pad_maximum_fusion.2.refs_0_), channel_id=1, source_target_pairs={{0,1},{1,0},{2,3},{3,2},{4,5},{5,4},{6,7},{7,6},{8,9},{9,8},{10,11... | collective-permute-start | bytes 1572872 | tf_op jit(solution)/shard_map/ppermute | solution.py:522
  165.0 1.5 collective-permute-done.8.refs_1_
  166.5 3.7 %project.1 = (f32[256,512]{1,0:T(8,128)S(1)}, f32[8,2,256]{2,1,0:T(2,128)S(1)}) custom-call(s32[3]{0:T(128)S(1)} %pad_add_fusion.2.where_ref, bf16[4,256,256]{2,1,0:T(8,128)(2,1)S(1)} %pad_maximum_fusion.2.refs_0_, bf16[4,256,256]{2,1,0:T(8,128)(2,1)S(1)} %collective-permute-done.8.refs_1_, bf16[4,256,256]{2,1,0:T(8,128)(2,1)S(1)} %all-to-all-done.4.refs_2_, ...), custom_call_target="tpu_custom_call" | custom-call | flops 1073741824 | bytes 6291456 | tf_op jit(solution)/shard_map/project/pallas_call | solution.py:353
  170.2 9.2 %all_to_all.31 = f32[8,2,256]{2,1,0:T(2,128)S(1)} all-to-all(f32[8,2,256]{2,1,0:T(2,128)S(1)} %get-tuple-element.16), channel_id=1, replica_groups=mesh['y'=8,'x'=4,'zh'=2,'zl'=4,'core'=2] {'zl','core'}, dimensions={0} | all-to-all | bytes 32768 | tf_op jit(solution)/shard_map/all_to_all | solution.py:524
  179.5 0.9 add_convert_fusion
  (55 shorter events, 0.4 us)
Async XLA Ops:
  6.5 74.0 %all-gather.3.cloned.1.call-start = ((), (), s32[]{:S(2)}) async-start(), calls=%async_computation.6 | async-start | bytes 4718592 | tf_op jit(solution)/shard_map/all_gather | solution.py:406
  8.4 22.0 %collective-permute-start = (bf16[256,512]{1,0:T(8,128)(2,1)}, bf16[256,512]{1,0:T(8,128)(2,1)S(1)}, u32[]{:S(2)}, u32[]{:S(2)}) collective-permute-start(bf16[256,512]{1,0:T(8,128)(2,1)} %q_ref.3), channel_id=1, source_target_pairs={{0,8},{8,0},{1,9},{9,1},{2,10},{10,2},{3,11},{11,3},{4,12},{12,4},... | collective-permute-start | bytes 786440 | tf_op jit(solution)/shard_map/ppermute | solution.py:455
  22.0 8.4 %collective-permute-start.1 = (bf16[8,512]{1,0:T(8,128)(2,1)S(1)}, bf16[8,512]{1,0:T(8,128)(2,1)S(1)}, u32[]{:S(2)}, u32[]{:S(2)}) collective-permute-start(bf16[8,512]{1,0:T(8,128)(2,1)S(1)} %pad.4), channel_id=1, source_target_pairs={{0,8},{8,0},{1,9},{9,1},{2,10},{10,2},{3,11},{11,3},{4,12},{12,4},... | collective-permute-start | bytes 24584 | tf_op jit(solution)/shard_map/ppermute | solution.py:455
  32.1 4.1 %copy-start.14 = (bf16[512,64]{0,1:T(8,128)(2,1)S(1)}, bf16[512,64]{0,1:T(8,128)(2,1)}, u32[]{:S(2)}) copy-start(bf16[512,64]{0,1:T(8,128)(2,1)} %param.16) | copy-start | bytes 196612
  32.1 28.7 %all-to-all-start = ((bf16[4,2,264,512]{3,2,1,0:T(8,128)(2,1)}), bf16[4,2,264,512]{3,2,1,0:T(8,128)(2,1)S(1)}, u32[]{:S(2)}, u32[]{:S(2)}) async-start(bf16[4,2,264,512]{3,2,1,0:T(8,128)(2,1)} %broadcast_in_dim.51), calls=%async_computation | async-start | bytes 4325376 | tf_op jit(solution)/shard_map/all_to_all | solution.py:451
  36.2 35.9 %copy-start.13 = (s32[2]{0:T(128)S(1)}, s32[2]{0:T(128)}, u32[]{:S(2)}) copy-start(s32[2]{0:T(128)} %param.19) | copy-start | bytes 28
  36.2 101.9 %all-gather.5.cloned.1.call-start = ((), (), s32[]{:S(2)}) async-start(), calls=%async_computation.7 | async-start | bytes 4718592 | tf_op jit(solution)/shard_map/all_gather | solution.py:461
  36.2 13.4 %collective-permute-start.3 = (bf16[64,512]{1,0:T(8,128)(2,1)S(1)}, bf16[64,512]{1,0:T(8,128)(2,1)S(1)}, u32[]{:S(2)}, u32[]{:S(2)}) collective-permute-start(bf16[64,512]{1,0:T(8,128)(2,1)S(1)} %bitcast.32), channel_id=1, source_target_pairs={{0,0},{1,64},{2,128},{3,192},{4,256},{5,320},{6,384},{7,448},{8,8}... | collective-permute-start | bytes 196616 | tf_op jit(solution)/shard_map/ppermute | solution.py:417
  41.8 12.8 %collective-permute-start.4 = (bf16[64,512]{1,0:T(8,128)(2,1)S(1)}, bf16[64,512]{1,0:T(8,128)(2,1)S(1)}, u32[]{:S(2)}, u32[]{:S(2)}) collective-permute-start(bf16[64,512]{1,0:T(8,128)(2,1)S(1)} %bitcast.33), channel_id=1, source_target_pairs={{0,8},{1,72},{2,136},{3,200},{4,264},{5,328},{6,392},{7,456},{8,0}... | collective-permute-start | bytes 196616 | tf_op jit(solution)/shard_map/ppermute | solution.py:418
  60.7 19.8 %copy-start.10 = (bf16[4,2,264,512]{3,2,1,0:T(8,128)(2,1)}, bf16[4,2,264,512]{3,2,1,0:T(8,128)(2,1)S(1)}, u32[]{:S(2)}) copy-start(bf16[4,2,264,512]{3,2,1,0:T(8,128)(2,1)S(1)} %all-to-all-done.q_ref) | copy-start | bytes 6488068
  86.7 18.9 %all-to-all-start.3 = ((bf16[4,2,272,256]{3,2,1,0:T(8,128)(2,1)}), bf16[4,2,272,256]{3,2,1,0:T(8,128)(2,1)S(1)}, u32[]{:S(2)}, u32[]{:S(2)}) async-start(bf16[4,2,272,256]{3,2,1,0:T(8,128)(2,1)} %bitcast.29), calls=%async_computation.3 | async-start | bytes 2228224 | tf_op jit(solution)/shard_map/all_to_all | solution.py:507
  96.8 13.2 %copy-start.5 = (s32[16]{0:T(128)S(1)}, s32[16]{0:T(128)}, u32[]{:S(2)}) copy-start(s32[16]{0:T(128)} %drop_ref.1) | copy-start | bytes 196
  105.5 13.7 %copy-start.1 = (bf16[256,512]{1,0:T(8,128)(2,1)S(1)}, bf16[256,512]{1,0:T(8,128)(2,1)}, u32[]{:S(2)}) copy-start(bf16[256,512]{1,0:T(8,128)(2,1)} %q_ref.3) | copy-start | bytes 786436
  105.5 13.7 %copy-start.2 = (bf16[256,512]{1,0:T(8,128)(2,1)S(1)}, bf16[256,512]{1,0:T(8,128)(2,1)}, u32[]{:S(2)}) copy-start(bf16[256,512]{1,0:T(8,128)(2,1)} %v_ref.3) | copy-start | bytes 786436
  105.5 13.7 %copy-start.3 = (bf16[256,512]{1,0:T(8,128)(2,1)S(1)}, bf16[256,512]{1,0:T(8,128)(2,1)}, u32[]{:S(2)}) copy-start(bf16[256,512]{1,0:T(8,128)(2,1)} %k_ref.3) | copy-start | bytes 786436
  105.5 17.7 %all-to-all-start.1 = ((bf16[4,2,272,256]{3,2,1,0:T(8,128)(2,1)}), bf16[4,2,272,256]{3,2,1,0:T(8,128)(2,1)S(1)}, u32[]{:S(2)}, u32[]{:S(2)}) async-start(bf16[4,2,272,256]{3,2,1,0:T(8,128)(2,1)} %bitcast.28), calls=%async_computation.1 | async-start | bytes 2228224 | tf_op jit(solution)/shard_map/all_to_all | solution.py:507
  111.5 19.6 %collective-permute-start.9 = (bf16[272,256]{1,0:T(8,128)(2,1)}, bf16[272,256]{1,0:T(8,128)(2,1)}, u32[]{:S(2)}, u32[]{:S(2)}) collective-permute-start(bf16[272,256]{1,0:T(8,128)(2,1)} %fold.3), channel_id=1, source_target_pairs={{0,8},{8,0},{1,9},{9,1},{2,10},{10,2},{3,11},{11,3},{4,12},{12,4},... | collective-permute-start | bytes 417800 | tf_op jit(solution)/shard_map/ppermute | solution.py:509
  120.0 0.7 copy-start.8
  121.5 0.7 copy-start.6
  123.4 14.3 %collective-permute-start.2 = (bf16[272,256]{1,0:T(8,128)(2,1)S(1)}, bf16[272,256]{1,0:T(8,128)(2,1)}, u32[]{:S(2)}, u32[]{:S(2)}) collective-permute-start(bf16[272,256]{1,0:T(8,128)(2,1)S(1)} %fold.2._), channel_id=1, source_target_pairs={{0,8},{8,0},{1,9},{9,1},{2,10},{10,2},{3,11},{11,3},{4,12},{12,4},... | collective-permute-start | bytes 417800 | tf_op jit(solution)/shard_map/ppermute | solution.py:509
  131.1 1.0 copy-start.9
  132.1 6.0 %copy-start.7 = (f32[256,256]{1,0:T(8,128)S(1)}, f32[256,256]{1,0:T(8,128)}, u32[]{:S(2)}) copy-start(f32[256,256]{1,0:T(8,128)} %copy-done.6) | copy-start | bytes 786436
  134.2 17.9 %all-to-all-start.4 = ((bf16[4,256,256]{2,1,0:T(8,128)(2,1)}), bf16[4,256,256]{2,1,0:T(8,128)(2,1)S(1)}, u32[]{:S(2)}, u32[]{:S(2)}) async-start(bf16[4,256,256]{2,1,0:T(8,128)(2,1)} %merge.3), calls=%async_computation.4 | async-start | bytes 1048576 | tf_op jit(solution)/shard_map/all_to_all | solution.py:515
  138.1 2.2 %copy-start = (bf16[4096,512]{1,0:T(8,128)(2,1)S(1)}, bf16[4096,512]{1,0:T(8,128)(2,1)}, u32[]{:S(2)}) copy-start(bf16[4096,512]{1,0:T(8,128)(2,1)} %all-gather.5.cloned.1.call-done._) | copy-start | bytes 12582916
  140.2 26.2 %copy-start.4 = (bf16[256,512]{1,0:T(8,128)(2,1)S(1)}, bf16[256,512]{1,0:T(8,128)(2,1)}, u32[]{:S(2)}) copy-start(bf16[256,512]{1,0:T(8,128)(2,1)} %refs_6_.1) | copy-start | bytes 786436
  141.5 21.1 %collective-permute-start.5 = (bf16[1,256,256]{2,1,0:T(8,128)(2,1)S(1)}, bf16[1,256,256]{2,1,0:T(8,128)(2,1)S(1)}, u32[]{:S(2)}, u32[]{:S(2)}) collective-permute-start(bf16[1,256,256]{2,1,0:T(8,128)(2,1)S(1)} %merge.2), channel_id=1, source_target_pairs={{0,2},{2,4},{4,6},{6,0},{1,3},{3,5},{5,7},{7,1},{8,10},{10,12},{12... | collective-permute-start | bytes 393224 | tf_op jit(solution)/shard_map/ppermute | solution.py:518
  144.8 17.8 %collective-permute-start.6 = (bf16[1,256,256]{2,1,0:T(8,128)(2,1)S(1)}, bf16[1,256,256]{2,1,0:T(8,128)(2,1)S(1)}, u32[]{:S(2)}, u32[]{:S(2)}) collective-permute-start(bf16[1,256,256]{2,1,0:T(8,128)(2,1)S(1)} %merge.2), channel_id=1, source_target_pairs={{0,4},{2,6},{4,0},{6,2},{1,5},{3,7},{5,1},{7,3},{8,12},{10,14},{12... | collective-permute-start | bytes 393224 | tf_op jit(solution)/shard_map/ppermute | solution.py:518
  149.1 13.4 %collective-permute-start.7 = (bf16[1,256,256]{2,1,0:T(8,128)(2,1)S(1)}, bf16[1,256,256]{2,1,0:T(8,128)(2,1)S(1)}, u32[]{:S(2)}, u32[]{:S(2)}) collective-permute-start(bf16[1,256,256]{2,1,0:T(8,128)(2,1)S(1)} %merge.2), channel_id=1, source_target_pairs={{0,6},{2,0},{4,2},{6,4},{1,7},{3,1},{5,3},{7,5},{8,14},{10,8},{12,... | collective-permute-start | bytes 393224 | tf_op jit(solution)/shard_map/ppermute | solution.py:518
  152.1 12.9 %collective-permute-start.10 = (bf16[4,256,256]{2,1,0:T(8,128)(2,1)S(1)}, bf16[4,256,256]{2,1,0:T(8,128)(2,1)S(1)}, u32[]{:S(2)}, u32[]{:S(2)}) collective-permute-start(bf16[4,256,256]{2,1,0:T(8,128)(2,1)S(1)} %all-to-all-done.4.refs_2_), channel_id=1, source_target_pairs={{0,1},{1,0},{2,3},{3,2},{4,5},{5,4},{6,7},{7,6},{8,9},{9,8},{10,11... | collective-permute-start | bytes 1572872 | tf_op jit(solution)/shard_map/ppermute | solution.py:522
  162.7 3.8 %collective-permute-start.8 = (bf16[4,256,256]{2,1,0:T(8,128)(2,1)S(1)}, bf16[4,256,256]{2,1,0:T(8,128)(2,1)S(1)}, u32[]{:S(2)}, u32[]{:S(2)}) collective-permute-start(bf16[4,256,256]{2,1,0:T(8,128)(2,1)S(1)} %pad_maximum_fusion.2.refs_0_), channel_id=1, source_target_pairs={{0,1},{1,0},{2,3},{3,2},{4,5},{5,4},{6,7},{7,6},{8,9},{9,8},{10,11... | collective-permute-start | bytes 1572872 | tf_op jit(solution)/shard_map/ppermute | solution.py:522
  166.5 13.0 %copy-start.11 = (f32[512]{0:T(512)S(1)}, f32[512]{0:T(512)}, u32[]{:S(2)}) copy-start(f32[512]{0:T(512)} %param.18) | copy-start | bytes 6148
  166.5 13.0 %copy-start.12 = (f32[512]{0:T(512)S(1)}, f32[512]{0:T(512)}, u32[]{:S(2)}) copy-start(f32[512]{0:T(512)} %param.17) | copy-start | bytes 6148
Sparse Core Ops, SparseCore 0:
  9.4 71.0 all-gather.2
  82.6 55.4 all-gather.4

commit v11 on v10

--- a/solution.py
+++ b/solution.py
@@ -245,7 +245,7 @@
             out_ref[copy, :, lines] = context
 
 
-def merge(zh, got, far, near, stat, after, copies):
+def merge(zh, got, far, near, stat, after, copies, flops):
     peers, _, lines, rows = got.shape
     wide = lines - STAT_ROWS
     out = (copies, rows, wide)
@@ -266,10 +266,31 @@
         out_shape=jax.ShapeDtypeStruct(out, BF),
         compiler_params=params(),
         cost_estimate=pl.CostEstimate(
-            flops=MERGE_HINT, transcendentals=0, bytes_accessed=1 << 20
+            flops=flops, transcendentals=0, bytes_accessed=1 << 20
         ),
         name="merge",
     )(zh, got, far, near, stat, after)
+
+
+def spread_kernel(x_ref, _, out_ref):
+    for copy in range(out_ref.shape[0]):
+        out_ref[copy] = x_ref[0]
+
+
+def spread_out(x, after, copies):
+    out = (copies,) + x.shape[1:]
+    return pl.pallas_call(
+        spread_kernel,
+        grid=(1,),
+        in_specs=[whole(x.shape), pl.BlockSpec((BLOCK, DH), lambda i: (0, 0))],
+        out_specs=whole(out),
+        out_shape=jax.ShapeDtypeStruct(out, BF),
+        compiler_params=params(),
+        cost_estimate=pl.CostEstimate(
+            flops=MERGE_HINT, transcendentals=0, bytes_accessed=1 << 20
+        ),
+        name="spread",
+    )(x, after)
 
 
 def keep_kernel(where_ref, drop_ref, out_ref):
@@ -500,26 +521,26 @@
     near = [local(part, queries, key_rows, value_rows) for part in range(PARTS)]
     where = jnp.stack([tp_at % 2, drop_seed[0], tp_at]).astype(jnp.int32)
     kept = keep(where, drop_offsets, residual.shape)
-    folded, gone = [], []
-    for part in range(PARTS):
+    contexts, after = [], kept
+    for part in (1, 0):
         partials = serve(part, row, mark, zh, asked, pool, row_count)
         partials = partials.reshape((n_x, 2) + partials.shape[1:])
         got = lax.all_to_all(partials, "x", split_axis=0, concat_axis=0, tiled=True)
-        gone.append(fold(zh, got, kept))
-        folded.append((got, lax.ppermute(gone[part], "zh", flip)))
-    contexts = []
-    for part in range(PARTS):
-        copies = n_zl if part else 1
-        context = merge(zh, *folded[part], *near[part], (weight, gone[0])[part], copies)
-        if part:
-            mine = lax.all_to_all(context, "zl", split_axis=0, concat_axis=0, tiled=True)
-        else:
-            shifted = [
-                lax.ppermute(context, "zl", [(z, (z + by) % n_zl) for z in range(n_zl)])
-                for by in range(1, n_zl)
-            ]
-            mine = jnp.concatenate([context] + shifted, axis=0)
-        contexts += [mine, lax.ppermute(mine, "core", flip)]
+        gone = fold(zh, got, after)
+        far = lax.ppermute(gone, "zh", flip)
+        cost = 2 * row_count * width_here if part else MERGE_HINT
+        context = merge(zh, got, far, *near[part], kept if part else weight, 1, cost)
+        contexts.append(context)
+        after = context[0]
+    first, second = contexts
+    shifted = [
+        lax.ppermute(second, "zl", [(z, (z + by) % n_zl) for z in range(n_zl)])
+        for by in range(1, n_zl)
+    ]
+    late = jnp.concatenate([second] + shifted, axis=0)
+    early = spread_out(first, gone, n_zl)
+    early = lax.all_to_all(early, "zl", split_axis=0, concat_axis=0, tiled=True)
+    contexts = [x for half in (late, early) for x in (half, lax.ppermute(half, "core", flip))]
     summed, stats = project(where, contexts, weight.reshape(tp_count, -1, width_here), kept, residual)
     stats = lax.all_to_all(stats, TP, split_axis=0, concat_axis=0, tiled=True)
     means, spreads = stats[:, 0], stats[:, 1]

time: 188 us -> 186 us (0.989)
  waiting for transfers between devices: 34.9 us -> 38.7 us
  Pallas kernels: 22.5 us -> 19.9 us
    pallas_call x2, Pallas kernels: 3.32 us -> 0.52 us  [merge(): pl.pallas_call(merge_kernel, grid_spec=pltpu.PrefetchScalarGridSpec(num_s...]
    ppermute x7, waiting for transfers between devices: 1.52 us -> 4.23 us  [the longest x2 2.72 us: on_device(): far = lax.ppermute(gone, 'zh', flip)]
    all_gather x1, waiting for transfers between devices: 0.38 us -> 2.51 us  [on_device(): weight = lax.all_gather(shards, 'y', axis=0, tiled=True)]
    unnamed x32 -> x28, local copies, waits for them, and re-layouts: 6.09 us -> 4.45 us
  transfers between devices with their start and end apart: 17 -> 17, of which waited for: 8 -> 8; matrix products, arithmetic and copies ran while one was open for 4% -> 4% of each run, Pallas kernels for 10% -> 9%
where the time goes in v11:
time: 186 us; the launch traced here: 185 us
  starting transfers between devices  79 us (42%)
  waiting for transfers between devices  38.7 us (21%)
  Pallas kernels  19.9 us (11%)
  blocking collectives  19.2 us (10%)
  between operations  15.2 us (8%)
  local copies, waits for them, and re-layouts  8.34 us (4%)
  other arithmetic  4.68 us (3%)
    ppermute x2, starting transfers between devices, on_device(): far = lax.ppermute(gone, 'zh', flip)  14.9 us
    pallas_call x2, Pallas kernels, serve(): pl.pallas_call(functools.partial(serve_kernel, rows), grid_spec=pltpu.Pre...  12.3 us
    ppermute x2, starting transfers between devices, on_device(): lax.ppermute(half, 'core', flip)  11.6 us
    ppermute x1, starting transfers between devices, on_device(): lax.ppermute(queries, 'zh', flip)  11.5 us
    ppermute x3, starting transfers between devices, on_device(): lax.ppermute(second, 'zl', [(z, (z + by) % n_zl) for z in range(n_zl)])  10.5 us
    all_to_all x1, blocking collectives, over_x(): return lax.all_to_all(x, 'x', split_axis=0, concat_axis=0, tiled=True)  10 us
    all_to_all x1, blocking collectives, on_device(): stats = lax.all_to_all(stats, TP, split_axis=0, concat_axis=0, tiled=True)  9.18 us
    all_to_all x2, waiting for transfers between devices, on_device(): got = lax.all_to_all(partials, 'x', split_axis=0, concat_axis=0, tiled=True)  8.77 us
  transfers between devices with their start and end apart: 17, of which 8 were waited for; matrix products, arithmetic and copies ran while one was open for 4% of the time, Pallas kernels for 9%

profile of v11, /device:TPU:1, one launch (start us, length us, event | category | flops | bytes accessed | tf_op | source)
XLA Modules:
  0.0 185.1 jit_solution(9526076068495450342)
XLA Ops:
  6.5 1.9 %pad_maximum_fusion.1 = bf16[2,256,512]{2,1,0:T(8,128)(2,1)} fusion(bf16[1,256,512]{2,1,0:T(8,128)(2,1)} %bitcast.25, bf16[1,256,512]{2,1,0:T(8,128)(2,1)} %bitcast.26), kind=kLoop, calls=%fused_computation.1 | loop fusion | flops 262144 | bytes 1048576 | tf_op jit(solution)/shard_map/stack | solution.py:427
  8.4 0.0 all-gather.3.cloned.1.call-update
  8.4 11.5 %collective-permute-start = (bf16[256,512]{1,0:T(8,128)(2,1)}, bf16[256,512]{1,0:T(8,128)(2,1)S(1)}, u32[]{:S(2)}, u32[]{:S(2)}) collective-permute-start(bf16[256,512]{1,0:T(8,128)(2,1)} %q_ref.3), channel_id=1, source_target_pairs={{0,8},{8,0},{1,9},{9,1},{2,10},{10,2},{3,11},{11,3},{4,12},{12,4},... | collective-permute-start | bytes 786440 | tf_op jit(solution)/shard_map/ppermute | solution.py:476
  19.9 0.8 copy.19
  20.7 0.1 reshape.409
  20.8 0.2 convert_reduce_fusion
  21.0 0.8 copy.20
  21.7 0.1 broadcast_in_dim.47
  21.8 0.1 select_reduce_fusion
  22.0 1.9 %collective-permute-start.1 = (bf16[8,512]{1,0:T(8,128)(2,1)S(1)}, bf16[8,512]{1,0:T(8,128)(2,1)S(1)}, u32[]{:S(2)}, u32[]{:S(2)}) collective-permute-start(bf16[8,512]{1,0:T(8,128)(2,1)S(1)} %pad.4), channel_id=1, source_target_pairs={{0,8},{8,0},{1,9},{9,1},{2,10},{10,2},{3,11},{11,3},{4,12},{12,4},... | collective-permute-start | bytes 24584 | tf_op jit(solution)/shard_map/ppermute | solution.py:476
  23.9 1.0 maximum_bitcast_fusion
  24.9 5.5 %collective-permute-done.1 = bf16[8,512]{1,0:T(8,128)(2,1)S(1)} collective-permute-done((bf16[8,512]{1,0:T(8,128)(2,1)S(1)}, bf16[8,512]{1,0:T(8,128)(2,1)S(1)}, u32[]{:S(2)}, u32[]{:S(2)}) %collective-permute-start.1) | collective-permute-done | bytes 8224 | tf_op jit(solution)/shard_map/ppermute | solution.py:476
  30.4 0.1 pad_maximum_fusion
  30.5 1.6 broadcast_in_dim.51
  32.1 4.1 %all-to-all-start = ((bf16[4,2,264,512]{3,2,1,0:T(8,128)(2,1)}), bf16[4,2,264,512]{3,2,1,0:T(8,128)(2,1)S(1)}, u32[]{:S(2)}, u32[]{:S(2)}) async-start(bf16[4,2,264,512]{3,2,1,0:T(8,128)(2,1)} %broadcast_in_dim.51), calls=%async_computation | async-start | bytes 4325376 | tf_op jit(solution)/shard_map/all_to_all | solution.py:472
  36.2 5.6 %collective-permute-start.4 = (bf16[64,512]{1,0:T(8,128)(2,1)S(1)}, bf16[64,512]{1,0:T(8,128)(2,1)S(1)}, u32[]{:S(2)}, u32[]{:S(2)}) collective-permute-start(bf16[64,512]{1,0:T(8,128)(2,1)S(1)} %bitcast.34), channel_id=1, source_target_pairs={{0,0},{1,64},{2,128},{3,192},{4,256},{5,320},{6,384},{7,448},{8,8}... | collective-permute-start | bytes 196616 | tf_op jit(solution)/shard_map/ppermute | solution.py:438
  41.8 7.7 %collective-permute-start.5 = (bf16[64,512]{1,0:T(8,128)(2,1)S(1)}, bf16[64,512]{1,0:T(8,128)(2,1)S(1)}, u32[]{:S(2)}, u32[]{:S(2)}) collective-permute-start(bf16[64,512]{1,0:T(8,128)(2,1)S(1)} %bitcast.35), channel_id=1, source_target_pairs={{0,8},{1,72},{2,136},{3,200},{4,264},{5,328},{6,392},{7,456},{8,0}... | collective-permute-start | bytes 196616 | tf_op jit(solution)/shard_map/ppermute | solution.py:439
  49.5 5.0 %collective-permute-done.5 = bf16[64,512]{1,0:T(8,128)(2,1)S(1)} collective-permute-done((bf16[64,512]{1,0:T(8,128)(2,1)S(1)}, bf16[64,512]{1,0:T(8,128)(2,1)S(1)}, u32[]{:S(2)}, u32[]{:S(2)}) %collective-permute-start.5) | collective-permute-done | bytes 65568 | tf_op jit(solution)/shard_map/ppermute | solution.py:439
  54.6 6.1 %all-to-all-done.q_ref = bf16[4,2,264,512]{3,2,1,0:T(8,128)(2,1)S(1)} async-done(((bf16[4,2,264,512]{3,2,1,0:T(8,128)(2,1)}), bf16[4,2,264,512]{3,2,1,0:T(8,128)(2,1)S(1)}, u32[]{:S(2)}, u32[]{:S(2)}) %all-to-all-start) | async-done | bytes 2162720 | tf_op jit(solution)/shard_map/all_to_all | solution.py:472
  60.7 0.5 slice.25
  62.0 10.0 %all_to_all.30 = bf16[4,128,512]{2,1,0:T(8,128)(2,1)} all-to-all(bf16[4,128,512]{2,1,0:T(8,128)(2,1)S(1)} %broadcast_in_dim.55), channel_id=1, replica_groups=mesh['y'=8,'x'=4,'zh'=2,'zl'=4,'core'=2] {'x'}, dimensions={0} | all-to-all | bytes 1048576 | tf_op jit(solution)/shard_map/all_to_all | solution.py:472
  72.1 0.0 all-gather.5.cloned.1.call-update
  72.1 0.1 pad.14.clone
  72.2 0.1 pad.18.clone
  72.4 0.1 reshape_squeeze.3
  72.5 0.1 compare_select_fusion
  72.6 0.1 pad_add_fusion.1
  72.6 0.7 reshape.411.mark_ref
  73.3 0.1 pad_add_fusion
  73.4 0.6 reshape.410.row_ref
  74.0 6.5 %all-gather.3.cloned.1.call-done = bf16[16,256,512]{2,1,0:T(8,128)(2,1)} async-done(((bf16[2,256,512]{2,1,0:T(8,128)(2,1)}), bf16[16,256,512]{2,1,0:T(8,128)(2,1)}) %all-gather.3.cloned.1.call-update) | async-done | bytes 4194320 | tf_op jit(solution)/shard_map/all_gather | solution.py:427
  80.5 6.1 %serve.3 = bf16[8,272,256]{2,1,0:T(8,128)(2,1)} custom-call(s32[160]{0:T(256)} %reshape.410.row_ref, s32[160]{0:T(256)} %reshape.411.mark_ref, s32[1]{0:T(128)} %bitcast.2.zh_ref, bf16[4,2,264,512]{3,2,1,0:T(8,128)(2,1)} %copy-done.8, bf16[4096,512]{1,0:T(8,128)(2,1)} %bitcast.28), custom_call_target="tpu_custom_call" | custom-call | flops 671088640 | bytes 4194304 | tf_op jit(solution)/shard_map/serve/pallas_call | solution.py:119
  86.7 4.0 %all-to-all-start.2 = ((bf16[4,2,272,256]{3,2,1,0:T(8,128)(2,1)}), bf16[4,2,272,256]{3,2,1,0:T(8,128)(2,1)S(1)}, u32[]{:S(2)}, u32[]{:S(2)}) async-start(bf16[4,2,272,256]{3,2,1,0:T(8,128)(2,1)} %bitcast.31), calls=%async_computation.2 | async-start | bytes 2228224 | tf_op jit(solution)/shard_map/all_to_all | solution.py:528
  90.6 6.1 %serve.2 = bf16[8,272,256]{2,1,0:T(8,128)(2,1)} custom-call(s32[160]{0:T(256)} %reshape.410.row_ref, s32[160]{0:T(256)} %reshape.411.mark_ref, s32[1]{0:T(128)} %bitcast.2.zh_ref, bf16[4,2,264,512]{3,2,1,0:T(8,128)(2,1)} %copy-done.8, bf16[4096,512]{1,0:T(8,128)(2,1)} %bitcast.29), custom_call_target="tpu_custom_call" | custom-call | flops 671088640 | bytes 4194304 | tf_op jit(solution)/shard_map/serve/pallas_call | solution.py:119
  96.8 8.8 %all-to-all-done.2.got_ref = bf16[4,2,272,256]{3,2,1,0:T(8,128)(2,1)S(1)} async-done(((bf16[4,2,272,256]{3,2,1,0:T(8,128)(2,1)}), bf16[4,2,272,256]{3,2,1,0:T(8,128)(2,1)S(1)}, u32[]{:S(2)}, u32[]{:S(2)}) %all-to-all-start.2) | async-done | bytes 1114144 | tf_op jit(solution)/shard_map/all_to_all | solution.py:528
  105.5 3.7 %all-to-all-start.1 = ((bf16[4,2,272,256]{3,2,1,0:T(8,128)(2,1)}), bf16[4,2,272,256]{3,2,1,0:T(8,128)(2,1)S(1)}, u32[]{:S(2)}, u32[]{:S(2)}) async-start(bf16[4,2,272,256]{3,2,1,0:T(8,128)(2,1)} %bitcast.30), calls=%async_computation.1 | async-start | bytes 2228224 | tf_op jit(solution)/shard_map/all_to_all | solution.py:528
  109.9 0.1 pad_add_fusion.2.where_ref
  109.9 0.8 keep.1._.refs_5_
  110.7 0.1 fold.2
  110.9 7.7 %collective-permute-start.2 = (bf16[272,256]{1,0:T(8,128)(2,1)S(1)}, bf16[272,256]{1,0:T(8,128)(2,1)S(1)}, u32[]{:S(2)}, u32[]{:S(2)}) collective-permute-start(bf16[272,256]{1,0:T(8,128)(2,1)S(1)} %fold.2), channel_id=1, source_target_pairs={{0,8},{8,0},{1,9},{9,1},{2,10},{10,2},{3,11},{11,3},{4,12},{12,4},... | collective-permute-start | bytes 417800 | tf_op jit(solution)/shard_map/ppermute | solution.py:530
  118.6 0.7 local.2
  119.4 0.7 local.3
  120.1 0.0 copy-start.6
  120.1 0.7 copy-done.6
  120.8 2.7 %collective-permute-done.2.far_ref = bf16[272,256]{1,0:T(8,128)(2,1)S(1)} collective-permute-done((bf16[272,256]{1,0:T(8,128)(2,1)S(1)}, bf16[272,256]{1,0:T(8,128)(2,1)S(1)}, u32[]{:S(2)}, u32[]{:S(2)}) %collective-permute-start.2) | collective-permute-done | bytes 139296 | tf_op jit(solution)/shard_map/ppermute | solution.py:530
  123.5 0.3 merge.2.x_ref
  123.8 0.1 fold.3._
  123.9 0.0 copy-start.7
  124.0 7.2 %collective-permute-start.3 = (bf16[272,256]{1,0:T(8,128)(2,1)S(1)}, bf16[272,256]{1,0:T(8,128)(2,1)S(1)}, u32[]{:S(2)}, u32[]{:S(2)}) collective-permute-start(bf16[272,256]{1,0:T(8,128)(2,1)S(1)} %fold.3._), channel_id=1, source_target_pairs={{0,8},{8,0},{1,9},{9,1},{2,10},{10,2},{3,11},{11,3},{4,12},{12,4},... | collective-permute-start | bytes 417800 | tf_op jit(solution)/shard_map/ppermute | solution.py:530
  131.2 0.9 spread.1
  132.1 3.5 %all-to-all-start.4 = ((bf16[4,256,256]{2,1,0:T(8,128)(2,1)}), bf16[4,256,256]{2,1,0:T(8,128)(2,1)S(1)}, u32[]{:S(2)}, u32[]{:S(2)}) async-start(bf16[4,256,256]{2,1,0:T(8,128)(2,1)} %spread.1), calls=%async_computation.4 | async-start | bytes 1048576 | tf_op jit(solution)/shard_map/all_to_all | solution.py:542
  135.5 2.5 %all-gather.5.cloned.1.call-done._ = bf16[4096,512]{1,0:T(8,128)(2,1)} async-done(((bf16[512,512]{1,0:T(8,128)(2,1)}), bf16[4096,512]{1,0:T(8,128)(2,1)}) %all-gather.5.cloned.1.call-update) | async-done | bytes 4194320 | tf_op jit(solution)/shard_map/all_gather | solution.py:482
  138.1 2.2 %copy-done = bf16[4096,512]{1,0:T(8,128)(2,1)S(1)} copy-done((bf16[4096,512]{1,0:T(8,128)(2,1)S(1)}, bf16[4096,512]{1,0:T(8,128)(2,1)}, u32[]{:S(2)}) %copy-start) | copy-done | bytes 4194328
  140.2 0.3 merge.3
  140.5 3.3 %collective-permute-start.6 = (bf16[1,256,256]{2,1,0:T(8,128)(2,1)S(1)}, bf16[1,256,256]{2,1,0:T(8,128)(2,1)S(1)}, u32[]{:S(2)}, u32[]{:S(2)}) collective-permute-start(bf16[1,256,256]{2,1,0:T(8,128)(2,1)S(1)} %merge.3), channel_id=1, source_target_pairs={{0,2},{2,4},{4,6},{6,0},{1,3},{3,5},{5,7},{7,1},{8,10},{10,12},{12... | collective-permute-start | bytes 393224 | tf_op jit(solution)/shard_map/ppermute | solution.py:537
  143.8 4.4 %collective-permute-start.7 = (bf16[1,256,256]{2,1,0:T(8,128)(2,1)S(1)}, bf16[1,256,256]{2,1,0:T(8,128)(2,1)S(1)}, u32[]{:S(2)}, u32[]{:S(2)}) collective-permute-start(bf16[1,256,256]{2,1,0:T(8,128)(2,1)S(1)} %merge.3), channel_id=1, source_target_pairs={{0,4},{2,6},{4,0},{6,2},{1,5},{3,7},{5,1},{7,3},{8,12},{10,14},{12... | collective-permute-start | bytes 393224 | tf_op jit(solution)/shard_map/ppermute | solution.py:537
  148.2 2.9 %collective-permute-start.8 = (bf16[1,256,256]{2,1,0:T(8,128)(2,1)S(1)}, bf16[1,256,256]{2,1,0:T(8,128)(2,1)S(1)}, u32[]{:S(2)}, u32[]{:S(2)}) collective-permute-start(bf16[1,256,256]{2,1,0:T(8,128)(2,1)S(1)} %merge.3), channel_id=1, source_target_pairs={{0,6},{2,0},{4,2},{6,4},{1,7},{3,1},{5,3},{7,5},{8,14},{10,8},{12,... | collective-permute-start | bytes 393224 | tf_op jit(solution)/shard_map/ppermute | solution.py:537
  151.1 9.1 %collective-permute-start.10 = (bf16[4,256,256]{2,1,0:T(8,128)(2,1)S(1)}, bf16[4,256,256]{2,1,0:T(8,128)(2,1)S(1)}, u32[]{:S(2)}, u32[]{:S(2)}) collective-permute-start(bf16[4,256,256]{2,1,0:T(8,128)(2,1)S(1)} %all-to-all-done.4.refs_2_), channel_id=1, source_target_pairs={{0,1},{1,0},{2,3},{3,2},{4,5},{5,4},{6,7},{7,6},{8,9},{9,8},{10,11... | collective-permute-start | bytes 1572872 | tf_op jit(solution)/shard_map/ppermute | solution.py:543
  160.2 0.1 pad_maximum_fusion.2.refs_0_
  160.3 2.5 %collective-permute-start.9 = (bf16[4,256,256]{2,1,0:T(8,128)(2,1)S(1)}, bf16[4,256,256]{2,1,0:T(8,128)(2,1)S(1)}, u32[]{:S(2)}, u32[]{:S(2)}) collective-permute-start(bf16[4,256,256]{2,1,0:T(8,128)(2,1)S(1)} %pad_maximum_fusion.2.refs_0_), channel_id=1, source_target_pairs={{0,1},{1,0},{2,3},{3,2},{4,5},{5,4},{6,7},{7,6},{8,9},{9,8},{10,11... | collective-permute-start | bytes 1572872 | tf_op jit(solution)/shard_map/ppermute | solution.py:543
  162.8 1.5 collective-permute-done.9.refs_1_
  164.3 3.7 %project.1 = (f32[256,512]{1,0:T(8,128)S(1)}, f32[8,2,256]{2,1,0:T(2,128)S(1)}) custom-call(s32[3]{0:T(128)S(1)} %pad_add_fusion.2.where_ref, bf16[4,256,256]{2,1,0:T(8,128)(2,1)S(1)} %pad_maximum_fusion.2.refs_0_, bf16[4,256,256]{2,1,0:T(8,128)(2,1)S(1)} %collective-permute-done.9.refs_1_, bf16[4,256,256]{2,1,0:T(8,128)(2,1)S(1)} %all-to-all-done.4.refs_2_, ...), custom_call_target="tpu_custom_call" | custom-call | flops 1073741824 | bytes 6291456 | tf_op jit(solution)/shard_map/project/pallas_call | solution.py:374
  168.1 9.2 %all_to_all.31 = f32[8,2,256]{2,1,0:T(2,128)S(1)} all-to-all(f32[8,2,256]{2,1,0:T(2,128)S(1)} %get-tuple-element.16), channel_id=1, replica_groups=mesh['y'=8,'x'=4,'zh'=2,'zl'=4,'core'=2] {'zl','core'}, dimensions={0} | all-to-all | bytes 32768 | tf_op jit(solution)/shard_map/all_to_all | solution.py:545
  177.4 0.9 add_convert_fusion
  (52 shorter events, 0.4 us)
Async XLA Ops:
  6.5 74.0 %all-gather.3.cloned.1.call-start = ((), (), s32[]{:S(2)}) async-start(), calls=%async_computation.6 | async-start | bytes 4718592 | tf_op jit(solution)/shard_map/all_gather | solution.py:427
  8.4 22.0 %collective-permute-start = (bf16[256,512]{1,0:T(8,128)(2,1)}, bf16[256,512]{1,0:T(8,128)(2,1)S(1)}, u32[]{:S(2)}, u32[]{:S(2)}) collective-permute-start(bf16[256,512]{1,0:T(8,128)(2,1)} %q_ref.3), channel_id=1, source_target_pairs={{0,8},{8,0},{1,9},{9,1},{2,10},{10,2},{3,11},{11,3},{4,12},{12,4},... | collective-permute-start | bytes 786440 | tf_op jit(solution)/shard_map/ppermute | solution.py:476
  22.0 8.4 %collective-permute-start.1 = (bf16[8,512]{1,0:T(8,128)(2,1)S(1)}, bf16[8,512]{1,0:T(8,128)(2,1)S(1)}, u32[]{:S(2)}, u32[]{:S(2)}) collective-permute-start(bf16[8,512]{1,0:T(8,128)(2,1)S(1)} %pad.4), channel_id=1, source_target_pairs={{0,8},{8,0},{1,9},{9,1},{2,10},{10,2},{3,11},{11,3},{4,12},{12,4},... | collective-permute-start | bytes 24584 | tf_op jit(solution)/shard_map/ppermute | solution.py:476
  32.1 4.1 %copy-start.12 = (bf16[512,64]{0,1:T(8,128)(2,1)S(1)}, bf16[512,64]{0,1:T(8,128)(2,1)}, u32[]{:S(2)}) copy-start(bf16[512,64]{0,1:T(8,128)(2,1)} %param.16) | copy-start | bytes 196612
  32.1 28.7 %all-to-all-start = ((bf16[4,2,264,512]{3,2,1,0:T(8,128)(2,1)}), bf16[4,2,264,512]{3,2,1,0:T(8,128)(2,1)S(1)}, u32[]{:S(2)}, u32[]{:S(2)}) async-start(bf16[4,2,264,512]{3,2,1,0:T(8,128)(2,1)} %broadcast_in_dim.51), calls=%async_computation | async-start | bytes 4325376 | tf_op jit(solution)/shard_map/all_to_all | solution.py:472
  36.2 35.9 %copy-start.11 = (s32[2]{0:T(128)S(1)}, s32[2]{0:T(128)}, u32[]{:S(2)}) copy-start(s32[2]{0:T(128)} %param.19) | copy-start | bytes 28
  36.2 101.9 %all-gather.5.cloned.1.call-start = ((), (), s32[]{:S(2)}) async-start(), calls=%async_computation.7 | async-start | bytes 4718592 | tf_op jit(solution)/shard_map/all_gather | solution.py:482
  36.2 13.4 %collective-permute-start.4 = (bf16[64,512]{1,0:T(8,128)(2,1)S(1)}, bf16[64,512]{1,0:T(8,128)(2,1)S(1)}, u32[]{:S(2)}, u32[]{:S(2)}) collective-permute-start(bf16[64,512]{1,0:T(8,128)(2,1)S(1)} %bitcast.34), channel_id=1, source_target_pairs={{0,0},{1,64},{2,128},{3,192},{4,256},{5,320},{6,384},{7,448},{8,8}... | collective-permute-start | bytes 196616 | tf_op jit(solution)/shard_map/ppermute | solution.py:438
  41.8 12.8 %collective-permute-start.5 = (bf16[64,512]{1,0:T(8,128)(2,1)S(1)}, bf16[64,512]{1,0:T(8,128)(2,1)S(1)}, u32[]{:S(2)}, u32[]{:S(2)}) collective-permute-start(bf16[64,512]{1,0:T(8,128)(2,1)S(1)} %bitcast.35), channel_id=1, source_target_pairs={{0,8},{1,72},{2,136},{3,200},{4,264},{5,328},{6,392},{7,456},{8,0}... | collective-permute-start | bytes 196616 | tf_op jit(solution)/shard_map/ppermute | solution.py:439
  60.7 19.8 %copy-start.8 = (bf16[4,2,264,512]{3,2,1,0:T(8,128)(2,1)}, bf16[4,2,264,512]{3,2,1,0:T(8,128)(2,1)S(1)}, u32[]{:S(2)}) copy-start(bf16[4,2,264,512]{3,2,1,0:T(8,128)(2,1)S(1)} %all-to-all-done.q_ref) | copy-start | bytes 6488068
  86.7 18.9 %all-to-all-start.2 = ((bf16[4,2,272,256]{3,2,1,0:T(8,128)(2,1)}), bf16[4,2,272,256]{3,2,1,0:T(8,128)(2,1)S(1)}, u32[]{:S(2)}, u32[]{:S(2)}) async-start(bf16[4,2,272,256]{3,2,1,0:T(8,128)(2,1)} %bitcast.31), calls=%async_computation.2 | async-start | bytes 2228224 | tf_op jit(solution)/shard_map/all_to_all | solution.py:528
  96.8 13.2 %copy-start.5 = (s32[16]{0:T(128)S(1)}, s32[16]{0:T(128)}, u32[]{:S(2)}) copy-start(s32[16]{0:T(128)} %drop_ref.1) | copy-start | bytes 196
  105.5 13.1 %copy-start.1 = (bf16[256,512]{1,0:T(8,128)(2,1)S(1)}, bf16[256,512]{1,0:T(8,128)(2,1)}, u32[]{:S(2)}) copy-start(bf16[256,512]{1,0:T(8,128)(2,1)} %q_ref.3) | copy-start | bytes 786436
  105.5 13.1 %copy-start.2 = (bf16[256,512]{1,0:T(8,128)(2,1)S(1)}, bf16[256,512]{1,0:T(8,128)(2,1)}, u32[]{:S(2)}) copy-start(bf16[256,512]{1,0:T(8,128)(2,1)} %v_ref.3) | copy-start | bytes 786436
  105.5 13.1 %copy-start.3 = (bf16[256,512]{1,0:T(8,128)(2,1)S(1)}, bf16[256,512]{1,0:T(8,128)(2,1)}, u32[]{:S(2)}) copy-start(bf16[256,512]{1,0:T(8,128)(2,1)} %k_ref.3) | copy-start | bytes 786436
  105.5 18.2 %all-to-all-start.1 = ((bf16[4,2,272,256]{3,2,1,0:T(8,128)(2,1)}), bf16[4,2,272,256]{3,2,1,0:T(8,128)(2,1)S(1)}, u32[]{:S(2)}, u32[]{:S(2)}) async-start(bf16[4,2,272,256]{3,2,1,0:T(8,128)(2,1)} %bitcast.30), calls=%async_computation.1 | async-start | bytes 2228224 | tf_op jit(solution)/shard_map/all_to_all | solution.py:528
  110.9 12.7 %collective-permute-start.2 = (bf16[272,256]{1,0:T(8,128)(2,1)S(1)}, bf16[272,256]{1,0:T(8,128)(2,1)S(1)}, u32[]{:S(2)}, u32[]{:S(2)}) collective-permute-start(bf16[272,256]{1,0:T(8,128)(2,1)S(1)} %fold.2), channel_id=1, source_target_pairs={{0,8},{8,0},{1,9},{9,1},{2,10},{10,2},{3,11},{11,3},{4,12},{12,4},... | collective-permute-start | bytes 417800 | tf_op jit(solution)/shard_map/ppermute | solution.py:530
  120.1 0.7 copy-start.6
  123.9 14.1 %copy-start.7 = (f32[256,256]{1,0:T(8,128)S(1)}, f32[256,256]{1,0:T(8,128)}, u32[]{:S(2)}) copy-start(f32[256,256]{1,0:T(8,128)} %copy-done.6) | copy-start | bytes 786436
  124.0 11.6 %collective-permute-start.3 = (bf16[272,256]{1,0:T(8,128)(2,1)S(1)}, bf16[272,256]{1,0:T(8,128)(2,1)S(1)}, u32[]{:S(2)}, u32[]{:S(2)}) collective-permute-start(bf16[272,256]{1,0:T(8,128)(2,1)S(1)} %fold.3._), channel_id=1, source_target_pairs={{0,8},{8,0},{1,9},{9,1},{2,10},{10,2},{3,11},{11,3},{4,12},{12,4},... | collective-permute-start | bytes 417800 | tf_op jit(solution)/shard_map/ppermute | solution.py:530
  132.1 19.0 %all-to-all-start.4 = ((bf16[4,256,256]{2,1,0:T(8,128)(2,1)}), bf16[4,256,256]{2,1,0:T(8,128)(2,1)S(1)}, u32[]{:S(2)}, u32[]{:S(2)}) async-start(bf16[4,256,256]{2,1,0:T(8,128)(2,1)} %spread.1), calls=%async_computation.4 | async-start | bytes 1048576 | tf_op jit(solution)/shard_map/all_to_all | solution.py:542
  138.1 2.2 %copy-start = (bf16[4096,512]{1,0:T(8,128)(2,1)S(1)}, bf16[4096,512]{1,0:T(8,128)(2,1)}, u32[]{:S(2)}) copy-start(bf16[4096,512]{1,0:T(8,128)(2,1)} %all-gather.5.cloned.1.call-done._) | copy-start | bytes 12582916
  140.2 24.1 %copy-start.4 = (bf16[256,512]{1,0:T(8,128)(2,1)S(1)}, bf16[256,512]{1,0:T(8,128)(2,1)}, u32[]{:S(2)}) copy-start(bf16[256,512]{1,0:T(8,128)(2,1)} %refs_6_.1) | copy-start | bytes 786436
  140.5 19.7 %collective-permute-start.6 = (bf16[1,256,256]{2,1,0:T(8,128)(2,1)S(1)}, bf16[1,256,256]{2,1,0:T(8,128)(2,1)S(1)}, u32[]{:S(2)}, u32[]{:S(2)}) collective-permute-start(bf16[1,256,256]{2,1,0:T(8,128)(2,1)S(1)} %merge.3), channel_id=1, source_target_pairs={{0,2},{2,4},{4,6},{6,0},{1,3},{3,5},{5,7},{7,1},{8,10},{10,12},{12... | collective-permute-start | bytes 393224 | tf_op jit(solution)/shard_map/ppermute | solution.py:537
  143.8 16.4 %collective-permute-start.7 = (bf16[1,256,256]{2,1,0:T(8,128)(2,1)S(1)}, bf16[1,256,256]{2,1,0:T(8,128)(2,1)S(1)}, u32[]{:S(2)}, u32[]{:S(2)}) collective-permute-start(bf16[1,256,256]{2,1,0:T(8,128)(2,1)S(1)} %merge.3), channel_id=1, source_target_pairs={{0,4},{2,6},{4,0},{6,2},{1,5},{3,7},{5,1},{7,3},{8,12},{10,14},{12... | collective-permute-start | bytes 393224 | tf_op jit(solution)/shard_map/ppermute | solution.py:537
  148.2 12.0 %collective-permute-start.8 = (bf16[1,256,256]{2,1,0:T(8,128)(2,1)S(1)}, bf16[1,256,256]{2,1,0:T(8,128)(2,1)S(1)}, u32[]{:S(2)}, u32[]{:S(2)}) collective-permute-start(bf16[1,256,256]{2,1,0:T(8,128)(2,1)S(1)} %merge.3), channel_id=1, source_target_pairs={{0,6},{2,0},{4,2},{6,4},{1,7},{3,1},{5,3},{7,5},{8,14},{10,8},{12,... | collective-permute-start | bytes 393224 | tf_op jit(solution)/shard_map/ppermute | solution.py:537
  151.1 11.7 %collective-permute-start.10 = (bf16[4,256,256]{2,1,0:T(8,128)(2,1)S(1)}, bf16[4,256,256]{2,1,0:T(8,128)(2,1)S(1)}, u32[]{:S(2)}, u32[]{:S(2)}) collective-permute-start(bf16[4,256,256]{2,1,0:T(8,128)(2,1)S(1)} %all-to-all-done.4.refs_2_), channel_id=1, source_target_pairs={{0,1},{1,0},{2,3},{3,2},{4,5},{5,4},{6,7},{7,6},{8,9},{9,8},{10,11... | collective-permute-start | bytes 1572872 | tf_op jit(solution)/shard_map/ppermute | solution.py:543
  160.3 4.1 %collective-permute-start.9 = (bf16[4,256,256]{2,1,0:T(8,128)(2,1)S(1)}, bf16[4,256,256]{2,1,0:T(8,128)(2,1)S(1)}, u32[]{:S(2)}, u32[]{:S(2)}) collective-permute-start(bf16[4,256,256]{2,1,0:T(8,128)(2,1)S(1)} %pad_maximum_fusion.2.refs_0_), channel_id=1, source_target_pairs={{0,1},{1,0},{2,3},{3,2},{4,5},{5,4},{6,7},{7,6},{8,9},{9,8},{10,11... | collective-permute-start | bytes 1572872 | tf_op jit(solution)/shard_map/ppermute | solution.py:543
  164.3 13.0 %copy-start.9 = (f32[512]{0:T(512)S(1)}, f32[512]{0:T(512)}, u32[]{:S(2)}) copy-start(f32[512]{0:T(512)} %param.18) | copy-start | bytes 6148
  164.3 13.0 %copy-start.10 = (f32[512]{0:T(512)S(1)}, f32[512]{0:T(512)}, u32[]{:S(2)}) copy-start(f32[512]{0:T(512)} %param.17) | copy-start | bytes 6148
Sparse Core Ops, SparseCore 0:
  9.4 71.0 all-gather.2
  82.6 55.4 all-gather.4
